TPU v7x, 256 devices: a whole 4x4x8 slice. The times are simulated.
256 devices in a mesh: dp: 8 (over x, z_lo), seq: 32 (over y, z_hi, core).
Axes of the slice: x: 4, y: 4, z: 8 (z_hi: 4, z_lo: 2; z = z_hi * 2 + z_lo), core: 2. Of those that a mesh axis runs over, the one named last changes fastest.
Arguments:
- queries: bfloat16 [8, 32, 512, 1024], P('dp', 'seq'), may hold values from -16 to 16
- keys: bfloat16 [8, 32, 512, 1024], P('dp', 'seq'), may hold values from -12 to 12
- values: bfloat16 [8, 32, 512, 1024], P('dp', 'seq'), may hold values from -24 to 24
- out_proj: bfloat16 [1024, 2048], P(('dp', 'seq')), may hold values from -0.1875 to 0.1875
- out_grad: bfloat16 [8, 32, 512, 2048], P('dp', 'seq'), may hold values from -48 to 48
- block_pattern: int32 [4, 4], replicated, may hold values from 0 to 3, as said below
- col_offset: int32 [4], replicated, may hold values from 0 to 511
Outputs:
- layer_out: bfloat16 [8, 32, 512, 2048], P('dp', 'seq')
- q_grad: bfloat16 [8, 32, 512, 1024], P('dp', 'seq')
- k_grad: bfloat16 [8, 32, 512, 1024], P('dp', 'seq')
- v_grad: bfloat16 [8, 32, 512, 1024], P('dp', 'seq')
- w_grad: float32 [1024, 2048], P(('dp', 'seq'))
Inputs may be any that keep to these rules, and one draw needn't show every extreme that they name: `block_pattern`: for each row head, the entries name each of the 4 blocks of a grid row once, and entry j is never j.
All inputs are finite; a program needn't handle non-finite values.
Results may differ from a plain program's by a relative error of at most 0.006.
Values may be sent and summed in bfloat16 or wider, within the bound.
No kernel may reach another device: no remote copies, remote signals or barrier semaphores. Data moves between devices by JAX's collectives and lax.ppermute only.
A program may use at most 128 MiB of HBM per device.

v0:
```python
import jax
import jax.numpy as jnp
from jax import lax
from jax.sharding import PartitionSpec as P

HD = 128
HR = 4
HC = 4
BLK = 128
NB = 4


def block_selector(block_pattern):
    numbers = jnp.arange(NB, dtype=jnp.int32)
    return (block_pattern.T[:, :, None] == numbers[None, None, :]).astype(jnp.bfloat16)


def roll_columns(tensor, col_offset, direction):
    moved_heads = [
        jnp.roll(tensor[:, :, head_idx], direction * col_offset[head_idx], axis=1)
        for head_idx in range(HC)
    ]
    return jnp.stack(moved_heads, axis=2)


def column_forward(parts):
    query_cols, key_cols, value_cols = parts
    score_scale = HD ** (-0.5)
    scores = (
        jnp.einsum("rchd,schd->rchs", query_cols, key_cols, preferred_element_type=jnp.float32)
        * score_scale
    )
    col_probs = jax.nn.softmax(scores, axis=-1)
    col_out = jnp.einsum(
        "rchs,schd->rchd",
        col_probs.astype(jnp.bfloat16),
        value_cols,
        preferred_element_type=jnp.float32,
    ).astype(jnp.bfloat16)
    return (col_out, col_probs, query_cols, key_cols, value_cols)


def column_backward(query_cols, key_cols, value_cols, col_probs, grad_cols):
    score_scale = HD ** (-0.5)
    prob_half = col_probs.astype(jnp.bfloat16)
    value_grad = jnp.einsum(
        "rchs,rchd->schd", prob_half, grad_cols, preferred_element_type=jnp.float32
    ).astype(jnp.bfloat16)
    prob_grad = jnp.einsum(
        "rchd,schd->rchs", grad_cols, value_cols, preferred_element_type=jnp.float32
    )
    delta_sum = jnp.sum(col_probs * prob_grad, axis=-1, keepdims=True)
    score_grad = (col_probs * (prob_grad - delta_sum)).astype(jnp.bfloat16)
    query_grad = (
        jnp.einsum("rchs,schd->rchd", score_grad, key_cols, preferred_element_type=jnp.float32)
        * score_scale
    ).astype(jnp.bfloat16)
    key_grad = (
        jnp.einsum("rchs,rchd->schd", score_grad, query_cols, preferred_element_type=jnp.float32)
        * score_scale
    ).astype(jnp.bfloat16)
    return (query_grad, key_grad, value_grad)


def row_forward(query_rows, key_rows, value_rows, selector):
    score_scale = HD ** (-0.5)
    key_other = jnp.einsum(
        "jhm,rmbhd->rjbhd", selector, key_rows, preferred_element_type=jnp.float32
    ).astype(jnp.bfloat16)
    value_other = jnp.einsum(
        "jhm,rmbhd->rjbhd", selector, value_rows, preferred_element_type=jnp.float32
    ).astype(jnp.bfloat16)
    key_joined = jnp.concatenate([key_other, key_rows], axis=2)
    value_joined = jnp.concatenate([value_other, value_rows], axis=2)
    scores = (
        jnp.einsum("rjqhd,rjkhd->rjhqk", query_rows, key_joined, preferred_element_type=jnp.float32)
        * score_scale
    )
    row_probs = jax.nn.softmax(scores, axis=-1)
    row_out = jnp.einsum(
        "rjhqk,rjkhd->rjqhd",
        row_probs.astype(jnp.bfloat16),
        value_joined,
        preferred_element_type=jnp.float32,
    ).astype(jnp.bfloat16)
    return (row_out, row_probs, key_joined, value_joined)


def fold_back(term_sums, selector):
    own_part = term_sums[:, :, BLK:]
    moved_part = jnp.einsum(
        "jhm,rjbhd->rmbhd",
        selector.astype(jnp.float32),
        term_sums[:, :, :BLK],
        precision=lax.Precision.HIGHEST,
    )
    return (own_part + moved_part).astype(jnp.bfloat16)


def row_backward(query_rows, key_joined, value_joined, row_probs, grad_rows, selector):
    score_scale = HD ** (-0.5)
    prob_half = row_probs.astype(jnp.bfloat16)
    value_terms = jnp.einsum(
        "rjhqk,rjqhd->rjkhd", prob_half, grad_rows, preferred_element_type=jnp.float32
    )
    prob_grad = jnp.einsum(
        "rjqhd,rjkhd->rjhqk", grad_rows, value_joined, preferred_element_type=jnp.float32
    )
    delta_sum = jnp.sum(row_probs * prob_grad, axis=-1, keepdims=True)
    score_grad = (row_probs * (prob_grad - delta_sum)).astype(jnp.bfloat16)
    query_grad = (
        jnp.einsum("rjhqk,rjkhd->rjqhd", score_grad, key_joined, preferred_element_type=jnp.float32)
        * score_scale
    ).astype(jnp.bfloat16)
    key_terms = (
        jnp.einsum("rjhqk,rjqhd->rjkhd", score_grad, query_rows, preferred_element_type=jnp.float32)
        * score_scale
    )
    return (query_grad, fold_back(key_terms, selector), fold_back(value_terms, selector))


def shards(queries, keys, values, out_proj, out_grad, block_pattern, col_offset):
    row_count = queries.shape[1]
    col_count = queries.shape[2]
    feat_width = queries.shape[3]
    model_width = out_grad.shape[3]
    head_count = feat_width // HD
    token_count = row_count * col_count
    query_heads = queries.reshape(row_count, col_count, head_count, HD)
    key_heads = keys.reshape(row_count, col_count, head_count, HD)
    value_heads = values.reshape(row_count, col_count, head_count, HD)
    selector = block_selector(block_pattern)
    grad_flat = out_grad.reshape(token_count, model_width)
    attn_grad = lax.dot_general(
        grad_flat,
        lax.all_gather(out_proj, ("dp", "seq"), axis=0, tiled=True),
        (((1,), (1,)), ((), ())),
        preferred_element_type=jnp.float32,
    ).astype(jnp.bfloat16)
    grad_heads = attn_grad.reshape(row_count, col_count, head_count, HD)
    key_shift = roll_columns(key_heads[:, :, HR:], col_offset, 1)
    value_shift = roll_columns(value_heads[:, :, HR:], col_offset, 1)
    row_shape = (row_count, NB, BLK, HR, HD)
    query_rows = query_heads[:, :, :HR].reshape(row_shape)
    col_out, col_probs, query_cols, key_cols, value_cols = column_forward(
        (
            lax.all_to_all(query_heads[:, :, HR:], "seq", split_axis=1, concat_axis=0, tiled=True),
            lax.all_to_all(key_shift, "seq", split_axis=1, concat_axis=0, tiled=True),
            lax.all_to_all(value_shift, "seq", split_axis=1, concat_axis=0, tiled=True),
        )
    )
    row_out, row_probs, key_joined, value_joined = row_forward(
        query_rows,
        key_heads[:, :, :HR].reshape(row_shape),
        value_heads[:, :, :HR].reshape(row_shape),
        selector,
    )
    col_back = lax.all_to_all(col_out, "seq", split_axis=0, concat_axis=1, tiled=True)
    grad_cols = lax.all_to_all(
        grad_heads[:, :, HR:], "seq", split_axis=1, concat_axis=0, tiled=True
    )
    col_query_grad, col_key_grad, col_value_grad = column_backward(
        query_cols, key_cols, value_cols, col_probs, grad_cols
    )
    query_back, key_back, value_back = (
        lax.all_to_all(col_query_grad, "seq", split_axis=0, concat_axis=1, tiled=True),
        lax.all_to_all(col_key_grad, "seq", split_axis=0, concat_axis=1, tiled=True),
        lax.all_to_all(col_value_grad, "seq", split_axis=0, concat_axis=1, tiled=True),
    )
    attention = jnp.concatenate(
        [row_out.reshape(row_count, col_count, HR, HD), col_back], axis=2
    ).reshape(token_count, feat_width)
    attn_part = attention
    layer_sum = jnp.dot(
        attn_part,
        lax.all_gather(out_proj, ("dp", "seq"), axis=0, tiled=True),
        preferred_element_type=jnp.float32,
    )
    data_count = lax.axis_size("dp")
    seq_count = lax.axis_size("seq")
    attn_part = attention
    summed_grad = lax.psum_scatter(
        lax.dot_general(
            attn_part, grad_flat, (((0,), (0,)), ((), ())), preferred_element_type=jnp.float32
        ),
        ("dp", "seq"),
        scatter_dimension=0,
        tiled=True,
    )
    w_grad = summed_grad * (data_count * seq_count * token_count) ** (-0.5)
    key_back = roll_columns(key_back, col_offset, -1)
    value_back = roll_columns(value_back, col_offset, -1)
    row_query_grad, row_key_grad, row_value_grad = row_backward(
        query_rows,
        key_joined,
        value_joined,
        row_probs,
        grad_heads[:, :, :HR].reshape(row_shape),
        selector,
    )

    def assemble(row_part, col_part):
        return jnp.concatenate(
            [row_part.reshape(row_count, col_count, HR, HD), col_part], axis=2
        ).reshape(1, row_count, col_count, feat_width)

    layer_out = layer_sum.astype(jnp.bfloat16).reshape(1, row_count, col_count, model_width)
    return (
        layer_out,
        assemble(row_query_grad, query_back),
        assemble(row_key_grad, key_back),
        assemble(row_value_grad, value_back),
        w_grad,
    )


def solution(mesh):
    in_specs = (
        P("dp", "seq", None, None),
        P("dp", "seq", None, None),
        P("dp", "seq", None, None),
        P(("dp", "seq"), None),
        P("dp", "seq", None, None),
        P(),
        P(),
    )
    out_specs = (
        P("dp", "seq", None, None),
        P("dp", "seq", None, None),
        P("dp", "seq", None, None),
        P("dp", "seq", None, None),
        P(("dp", "seq"), None),
    )
    return jax.shard_map(shards, mesh=mesh, in_specs=in_specs, out_specs=out_specs, check_vma=False)
```

profile of v0, /device:TPU:1, one launch (start us, length us, event | category | flops | bytes accessed | tf_op | source)
XLA Modules:
  0.0 978.7 jit_solution(12304957022160518582)
XLA Ops:
  9.9 2.1 copy.246
  12.0 12.8 %all-to-all-start.2 = ((bf16[1,512,4,128]{3,2,0,1:T(4,128)(2,1)}), bf16[1,512,4,128]{3,2,0,1:T(4,128)(2,1)}, u32[]{:S(2)}, u32[]{:S(2)}) async-start(bf16[1,512,4,128]{3,2,0,1:T(4,128)(2,1)} %copy.246), calls=%async_computation.2 | async-start | bytes 1048576 | tf_op jit(solution)/shard_map/all_to_all | solution.py:147
  36.3 2.3 copy.215
  53.0 2.1 fusion.90
  58.4 9.8 %all-to-all-start.1 = ((bf16[1,512,4,128]{3,2,0,1:T(4,128)(2,1)}), bf16[1,512,4,128]{3,2,0,1:T(4,128)(2,1)}, u32[]{:S(2)}, u32[]{:S(2)}) async-start(bf16[1,512,4,128]{3,2,0,1:T(4,128)(2,1)} %copy.244), calls=%async_computation.1 | async-start | bytes 1048576 | tf_op jit(solution)/shard_map/all_to_all | solution.py:148
  70.5 15.7 %all-to-all-done.1 = bf16[1,512,4,128]{3,2,0,1:T(4,128)(2,1)} async-done(((bf16[1,512,4,128]{3,2,0,1:T(4,128)(2,1)}), bf16[1,512,4,128]{3,2,0,1:T(4,128)(2,1)}, u32[]{:S(2)}, u32[]{:S(2)}) %all-to-all-start.1) | async-done | bytes 524320 | tf_op jit(solution)/shard_map/all_to_all | solution.py:148
  86.2 6.0 all-to-all-start
  102.6 2.7 maximum_bitcast_fusion
  110.4 2.8 fusion.122
  117.2 10.0 %all-to-all-start.3 = ((bf16[32,16,4,128]{3,2,1,0:T(4,128)(2,1)}), bf16[32,16,4,128]{3,2,1,0:T(4,128)(2,1)}, u32[]{:S(2)}, u32[]{:S(2)}) async-start(bf16[32,16,4,128]{3,2,1,0:T(4,128)(2,1)} %copy.252), calls=%async_computation.3 | async-start | bytes 1048576 | tf_op jit(solution)/shard_map/all_to_all | solution.py:158
  132.5 12.5 %all-to-all-done.3 = bf16[32,16,4,128]{3,2,1,0:T(4,128)(2,1)} async-done(((bf16[32,16,4,128]{3,2,1,0:T(4,128)(2,1)}), bf16[32,16,4,128]{3,2,1,0:T(4,128)(2,1)}, u32[]{:S(2)}, u32[]{:S(2)}) %all-to-all-start.3) | async-done | bytes 524320 | tf_op jit(solution)/shard_map/all_to_all | solution.py:158
  146.2 2.1 pad_maximum_fusion
  148.3 2.3 copy.254
  150.6 6.8 fusion.3
  160.8 270.3 %all-reduce.3.cloned.1.call-done = f32[1024,2048]{1,0:T(8,128)} async-done(((f32[1024,2048]{1,0:T(8,128)}), f32[1024,2048]{1,0:T(8,128)}) %all-reduce.3.cloned.1.call-update) | async-done | bytes 8388624
  432.6 413.8 %all-gather.3.cloned.1.call-done = bf16[256,4,2048]{2,1,0:T(4,128)(2,1)} async-done(((bf16[1,4,2048]{2,1,0:T(4,128)(2,1)}), bf16[256,4,2048]{2,1,0:T(4,128)(2,1)}) %all-gather.3.cloned.1.call-update) | async-done | bytes 4194320 | tf_op jit(solution)/shard_map/all_gather | solution.py:176
  846.4 6.9 reshape.197
  853.3 4.5 fusion.16
  860.3 8.3 all-to-all-start.4
  877.8 8.8 all-to-all-done.4
  891.9 5.3 all-to-all-start.5
  897.3 2.3 slice_bitcast_fusion
  899.6 2.5 copy.282
  902.1 3.3 fusion.113
  905.4 2.6 copy.283
  908.0 2.5 fusion.32
  911.8 3.5 all-to-all-done.5
  915.3 6.5 all-to-all-start.6
  923.1 6.0 fusion.2
  930.6 9.3 all-to-all-done.6
  939.9 4.8 all-to-all-start.7
  953.8 9.0 all-to-all-done.7
  (153 shorter events, 93.0 us)
Async XLA Ops:
  7.2 143.4 %copy-start = (bf16[1,1,512,2048]{3,2,1,0:T(8,128)(2,1)S(1)}, bf16[1,1,512,2048]{3,2,1,0:T(8,128)(2,1)}, u32[]{:S(2)}) copy-start(bf16[1,1,512,2048]{3,2,1,0:T(8,128)(2,1)} %param.13) | copy-start | bytes 6291460
  8.8 16.0 %copy-start.28 = (s32[4]{0:T(128)S(1)}, s32[4]{0:T(128)}, u32[]{:S(2)}) copy-start(s32[4]{0:T(128)} %param.15) | copy-start | bytes 52
  12.0 46.5 %all-to-all-start.2 = ((bf16[1,512,4,128]{3,2,0,1:T(4,128)(2,1)}), bf16[1,512,4,128]{3,2,0,1:T(4,128)(2,1)}, u32[]{:S(2)}, u32[]{:S(2)}) async-start(bf16[1,512,4,128]{3,2,0,1:T(4,128)(2,1)} %copy.246), calls=%async_computation.2 | async-start | bytes 1048576 | tf_op jit(solution)/shard_map/all_to_all | solution.py:147
  53.0 15.3 %copy-start.24 = (bf16[1,512,1,128]{3,1,2,0:T(8,128)(2,1)S(1)}, bf16[1,512,1,128]{3,1,2,0:T(8,128)(2,1)}, u32[]{:S(2)}) copy-start(bf16[1,512,1,128]{3,1,2,0:T(8,128)(2,1)} %get-tuple-element.52) | copy-start | bytes 393220
  55.1 13.2 %copy-start.25 = (bf16[1,512,1,128]{3,1,2,0:T(8,128)(2,1)S(1)}, bf16[1,512,1,128]{3,1,2,0:T(8,128)(2,1)}, u32[]{:S(2)}) copy-start(bf16[1,512,1,128]{3,1,2,0:T(8,128)(2,1)} %get-tuple-element.54) | copy-start | bytes 393220
  57.2 11.1 %copy-start.26 = (bf16[1,512,1,128]{3,1,2,0:T(8,128)(2,1)S(1)}, bf16[1,512,1,128]{3,1,2,0:T(8,128)(2,1)}, u32[]{:S(2)}) copy-start(bf16[1,512,1,128]{3,1,2,0:T(8,128)(2,1)} %get-tuple-element.56) | copy-start | bytes 393220
  58.4 27.8 %all-to-all-start.1 = ((bf16[1,512,4,128]{3,2,0,1:T(4,128)(2,1)}), bf16[1,512,4,128]{3,2,0,1:T(4,128)(2,1)}, u32[]{:S(2)}, u32[]{:S(2)}) async-start(bf16[1,512,4,128]{3,2,0,1:T(4,128)(2,1)} %copy.244), calls=%async_computation.1 | async-start | bytes 1048576 | tf_op jit(solution)/shard_map/all_to_all | solution.py:148
  86.2 27.0 %all-to-all-start = ((bf16[1,512,4,128]{3,2,0,1:T(4,128)(2,1)}), bf16[1,512,4,128]{3,2,0,1:T(4,128)(2,1)}, u32[]{:S(2)}, u32[]{:S(2)}) async-start(bf16[1,512,4,128]{3,2,0,1:T(4,128)(2,1)} %copy.238), calls=%async_computation | async-start | bytes 1048576 | tf_op jit(solution)/shard_map/all_to_all | solution.py:149
  96.2 5.8 copy-start.27
  102.0 3.9 copy-start.13
  114.3 1.8 copy-start.21
  117.2 27.9 %all-to-all-start.3 = ((bf16[32,16,4,128]{3,2,1,0:T(4,128)(2,1)}), bf16[32,16,4,128]{3,2,1,0:T(4,128)(2,1)}, u32[]{:S(2)}, u32[]{:S(2)}) async-start(bf16[32,16,4,128]{3,2,1,0:T(4,128)(2,1)} %copy.252), calls=%async_computation.3 | async-start | bytes 1048576 | tf_op jit(solution)/shard_map/all_to_all | solution.py:158
  127.2 303.9 %all-reduce.3.cloned.1.call-start = ((), (), s32[]{:S(2)}) async-start(), calls=%async_computation.9 | async-start | bytes 16777216
  128.7 1.7 copy-start.16
  157.5 688.9 %all-gather.3.cloned.1.call-start = ((), (), s32[]{:S(2)}) async-start(), calls=%async_computation.8 | async-start | bytes 4210688 | tf_op jit(solution)/shard_map/all_gather | solution.py:176
  859.2 11.0 %copy-start.3 = (f32[4,4,128,256]{2,3,1,0:T(8,128)S(1)}, f32[4,4,128,256]{2,3,1,0:T(8,128)}, u32[]{:S(2)}) copy-start(f32[4,4,128,256]{2,3,1,0:T(8,128)} %copy-done.2) | copy-start | bytes 6291460
  860.3 26.3 %all-to-all-start.4 = ((bf16[1,512,4,128]{3,2,0,1:T(4,128)(2,1)}), bf16[1,512,4,128]{3,2,0,1:T(4,128)(2,1)}, u32[]{:S(2)}, u32[]{:S(2)}) async-start(bf16[1,512,4,128]{3,2,0,1:T(4,128)(2,1)} %slice.155), calls=%async_computation.4 | async-start | bytes 1048576 | tf_op jit(solution)/shard_map/all_to_all | solution.py:159
  870.2 1.6 copy-start.4
  876.0 11.7 %copy-start.18 = (f32[32,16,4,32]{0,3,2,1:T(8,128)S(1)}, f32[32,16,4,32]{0,3,2,1:T(8,128)}, u32[]{:S(2)}) copy-start(f32[32,16,4,32]{0,3,2,1:T(8,128)} %get-tuple-element.44) | copy-start | bytes 786436
  887.7 1.8 copy-start.22
  887.7 1.8 copy-start.19
  891.9 23.4 %all-to-all-start.5 = ((bf16[32,16,4,128]{3,2,1,0:T(4,128)(2,1)}), bf16[32,16,4,128]{3,2,1,0:T(4,128)(2,1)}, u32[]{:S(2)}, u32[]{:S(2)}) async-start(bf16[32,16,4,128]{3,2,1,0:T(4,128)(2,1)} %copy.269), calls=%async_computation.5 | async-start | bytes 1048576 | tf_op jit(solution)/shard_map/all_to_all | solution.py:166
  905.4 5.1 copy-start.7
  915.3 24.5 %all-to-all-start.6 = ((bf16[32,16,4,128]{3,2,1,0:T(4,128)(2,1)}), bf16[32,16,4,128]{3,2,1,0:T(4,128)(2,1)S(1)}, u32[]{:S(2)}, u32[]{:S(2)}) async-start(bf16[32,16,4,128]{3,2,1,0:T(4,128)(2,1)} %copy.277), calls=%async_computation.6 | async-start | bytes 1048576 | tf_op jit(solution)/shard_map/all_to_all | solution.py:167
  923.1 6.0 copy-start.20
  923.1 6.0 copy-start.23
  929.5 15.2 %copy-start.10 = (bf16[1,4,128,4,128]{4,2,1,3,0:T(8,128)(2,1)S(1)}, bf16[1,4,128,4,128]{4,2,1,3,0:T(8,128)(2,1)}, u32[]{:S(2)}) copy-start(bf16[1,4,128,4,128]{4,2,1,3,0:T(8,128)(2,1)} %copy.275) | copy-start | bytes 1572868
  929.5 16.1 %copy-start.9 = (bf16[1,4,128,4,128]{2,4,3,1,0:T(8,128)(2,1)S(1)}, bf16[1,4,128,4,128]{2,4,3,1,0:T(8,128)(2,1)}, u32[]{:S(2)}) copy-start(bf16[1,4,128,4,128]{2,4,3,1,0:T(8,128)(2,1)} %fusion.32) | copy-start | bytes 1572868
  939.9 6.0 copy-start.11
  939.9 22.9 %all-to-all-start.7 = ((bf16[32,16,4,128]{3,2,1,0:T(4,128)(2,1)}), bf16[32,16,4,128]{3,2,1,0:T(4,128)(2,1)}, u32[]{:S(2)}, u32[]{:S(2)}) async-start(bf16[32,16,4,128]{3,2,1,0:T(4,128)(2,1)} %copy.286), calls=%async_computation.7 | async-start | bytes 1048576 | tf_op jit(solution)/shard_map/all_to_all | solution.py:168
  945.6 2.2 copy-start.14
  967.4 4.0 copy-start.1
  (7 other events, 8.5 us)
Sparse Core Ops, SparseCore 0:
  157.6 273.4 all-reduce.2
  433.1 413.1 all-gather.2
where the time goes:
time: 986 us; the launch traced here: 979 us
  waiting for transfers between devices  743 us (75%)
  local copies, waits for them, and re-layouts  82 us (8%)
  starting transfers between devices  63.8 us (6%)
  matrix products  36.2 us (4%)
  other arithmetic  27.8 us (3%)
  between operations  25.3 us (3%)
    all_gather x1, waiting for transfers between devices, shards(): lax.all_gather(out_proj, ('dp', 'seq'), axis=0, tiled=True)  414 us
    unnamed x3, waiting for transfers between devices  271 us
    unnamed x69, local copies, waits for them, and re-layouts  22.3 us
  transfers between devices with their start and end apart: 10, of which 8 were waited for; matrix products, arithmetic and copies ran while one was open for 10% of the time, Pallas kernels for 0%

commit v1 on v0

v1 whole, which is shorter than its diff:
```python
import jax
import jax.numpy as jnp
from jax import lax
from jax.experimental import pallas as pl
from jax.experimental.pallas import tpu as pltpu
from jax.sharding import Mesh, PartitionSpec as P

HD = 128
HR = 4
HC = 4
BLK = 128
NB = 4
COLS = 512
HALF = HR * HD
D = 2048
DH = D // 2
SCALE = HD ** (-0.5)
BF = jnp.bfloat16
F32 = jnp.float32
GRP = 8
ROWS = 32
TILE = GRP * ROWS
VMEM_LIMIT = 50 * 1024 * 1024

DP = ("x", "zl")
SEQ = ("y", "zh", "c")


def mm(a, b):
    return lax.dot_general(a, b, (((1,), (0,)), ((), ())), preferred_element_type=F32)


def mm_t(a, b):
    return lax.dot_general(a, b, (((1,), (1,)), ((), ())), preferred_element_type=F32)


def t_mm(a, b):
    return lax.dot_general(a, b, (((0,), (0,)), ((), ())), preferred_element_type=F32)


def params():
    return pltpu.CompilerParams(vmem_limit_bytes=VMEM_LIMIT)


def cost(flops, nbytes, trans=0):
    return pl.CostEstimate(flops=int(flops), transcendentals=int(trans), bytes_accessed=int(nbytes))


SMEM_SPEC = pl.BlockSpec(memory_space=pltpu.SMEM)
VMEM_SPEC = pl.BlockSpec(memory_space=pltpu.VMEM)


def head(index):
    return slice(index * HD, (index + 1) * HD)


def shift_selector(offset):
    row = lax.broadcasted_iota(jnp.int32, (COLS, COLS), 0)
    col = lax.broadcasted_iota(jnp.int32, (COLS, COLS), 1)
    source = row - offset
    source = jnp.where(source < 0, source + COLS, source)
    return jnp.where(source == col, 1.0, 0.0).astype(BF)


def pack_kernel(off_ref, q_ref, k_ref, v_ref, o_ref):
    o_ref[:, :HALF] = q_ref[...]
    for h in range(HC):
        pair = jnp.concatenate([k_ref[:, head(h)], v_ref[:, head(h)]], axis=1)
        moved = mm(shift_selector(off_ref[h]), pair).astype(BF)
        o_ref[:, head(HC + h)] = moved[:, :HD]
        o_ref[:, head(2 * HC + h)] = moved[:, HD:]


def pack(q, k, v, offset):
    half = pl.BlockSpec((COLS, HALF), lambda i: (0, 1))
    return pl.pallas_call(
        pack_kernel,
        grid=(1,),
        out_shape=jax.ShapeDtypeStruct((COLS, 3 * HALF), BF),
        in_specs=[SMEM_SPEC, half, half, half],
        out_specs=pl.BlockSpec((COLS, 3 * HALF), lambda i: (0, 0)),
        compiler_params=params(),
        cost_estimate=cost(2 * COLS * COLS * 2 * HALF, 6 * COLS * HALF * 2),
        name="pack",
    )(offset, q, k, v)


def tile_of(ref, group, lane):
    tile = ref[:, group, :, lane * HD : (lane + 1) * HD]
    return tile.astype(F32).reshape(TILE, HD).astype(BF)


def store_tile(ref, group, lane, value):
    ref[:, group, :, lane * HD : (lane + 1) * HD] = value.reshape(ROWS, GRP, HD).astype(BF)


def column_mask():
    row = lax.broadcasted_iota(jnp.int32, (TILE, TILE), 0)
    col = lax.broadcasted_iota(jnp.int32, (TILE, TILE), 1)
    return lax.rem(row, GRP) == lax.rem(col, GRP)


def softmax(scores):
    e = jnp.exp(scores - jnp.max(scores, axis=-1, keepdims=True))
    return e / jnp.sum(e, axis=-1, keepdims=True)


def column_probs(r_ref, group, h, mask):
    q = tile_of(r_ref, group, h)
    k = tile_of(r_ref, group, HC + h)
    v = tile_of(r_ref, group, 2 * HC + h)
    return q, k, v, softmax(jnp.where(mask, mm_t(q, k) * SCALE, -1e30))


def column_forward_kernel(r_ref, o_ref):
    mask = column_mask()
    for group in range(2):
        for h in range(HC):
            _, _, v, probs = column_probs(r_ref, group, h, mask)
            store_tile(o_ref, group, h, mm(probs.astype(BF), v))


def column_forward(received):
    return pl.pallas_call(
        column_forward_kernel,
        out_shape=jax.ShapeDtypeStruct((ROWS, 2, GRP, HALF), BF),
        in_specs=[VMEM_SPEC],
        out_specs=VMEM_SPEC,
        compiler_params=params(),
        cost_estimate=cost(8 * 4 * TILE * TILE * HD, 4 * COLS * HALF * 2, 8 * TILE * TILE),
        name="column_forward",
    )(received)


def column_backward_kernel(r_ref, g_ref, o_ref):
    mask = column_mask()
    for group in range(2):
        for h in range(HC):
            q, k, v, probs = column_probs(r_ref, group, h, mask)
            g = tile_of(g_ref, group, h)
            store_tile(o_ref, group, 2 * HC + h, t_mm(probs.astype(BF), g))
            prob_grad = mm_t(g, v)
            delta = jnp.sum(probs * prob_grad, axis=-1, keepdims=True)
            score_grad = (probs * (prob_grad - delta)).astype(BF)
            store_tile(o_ref, group, h, mm(score_grad, k) * SCALE)
            store_tile(o_ref, group, HC + h, t_mm(score_grad, q) * SCALE)


def column_backward(received, grads):
    return pl.pallas_call(
        column_backward_kernel,
        out_shape=jax.ShapeDtypeStruct((ROWS, 2, GRP, 3 * HALF), BF),
        in_specs=[VMEM_SPEC, VMEM_SPEC],
        out_specs=VMEM_SPEC,
        compiler_params=params(),
        cost_estimate=cost(8 * 10 * TILE * TILE * HD, 7 * COLS * HALF * 2, 8 * TILE * TILE),
        name="column_backward",
    )(received, grads)


def row_tile(pat_ref, q_ref, k_ref, v_ref, h, j):
    block = slice(j * BLK, (j + 1) * BLK)
    other = pl.ds(pl.multiple_of(pat_ref[h, j] * BLK, BLK), BLK)
    q = q_ref[block, head(h)]
    k = jnp.concatenate([k_ref[other, head(h)], k_ref[block, head(h)]], axis=0)
    v = jnp.concatenate([v_ref[other, head(h)], v_ref[block, head(h)]], axis=0)
    return block, other, q, k, v, softmax(mm_t(q, k) * SCALE)


def row_forward_kernel(pat_ref, q_ref, k_ref, v_ref, o_ref):
    for h in range(HR):
        for j in range(NB):
            block, _, _, _, v, probs = row_tile(pat_ref, q_ref, k_ref, v_ref, h, j)
            o_ref[block, head(h)] = mm(probs.astype(BF), v).astype(BF)


def first_half():
    return pl.BlockSpec((COLS, HALF), lambda i: (0, 0))


def row_forward(q, k, v, pattern):
    return pl.pallas_call(
        row_forward_kernel,
        grid=(1,),
        out_shape=jax.ShapeDtypeStruct((COLS, HALF), BF),
        in_specs=[SMEM_SPEC, first_half(), first_half(), first_half()],
        out_specs=first_half(),
        compiler_params=params(),
        cost_estimate=cost(16 * 4 * BLK * 2 * BLK * HD, 4 * COLS * HALF * 2, 16 * BLK * 2 * BLK),
        name="row_forward",
    )(pattern, q, k, v)


def row_backward_kernel(pat_ref, q_ref, k_ref, v_ref, g_ref, dq_ref, dk_ref, dv_ref, own, moved):
    for h in range(HR):
        for j in range(NB):
            block, other, q, k, v, probs = row_tile(pat_ref, q_ref, k_ref, v_ref, h, j)
            g = g_ref[block, head(h)]
            value_terms = t_mm(probs.astype(BF), g)
            prob_grad = mm_t(g, v)
            delta = jnp.sum(probs * prob_grad, axis=-1, keepdims=True)
            score_grad = (probs * (prob_grad - delta)).astype(BF)
            dq_ref[block, head(h)] = (mm(score_grad, k) * SCALE).astype(BF)
            key_terms = t_mm(score_grad, q) * SCALE
            moved[0, other, :] = key_terms[:BLK]
            own[0, block, :] = key_terms[BLK:]
            moved[1, other, :] = value_terms[:BLK]
            own[1, block, :] = value_terms[BLK:]
        dk_ref[:, head(h)] = (own[0] + moved[0]).astype(BF)
        dv_ref[:, head(h)] = (own[1] + moved[1]).astype(BF)


def row_backward(q, k, v, g, pattern):
    whole = jax.ShapeDtypeStruct((COLS, 2 * HALF), BF)
    return pl.pallas_call(
        row_backward_kernel,
        grid=(1,),
        out_shape=(whole, whole, whole),
        in_specs=[SMEM_SPEC] + [first_half()] * 4,
        out_specs=(first_half(),) * 3,
        scratch_shapes=[pltpu.VMEM((2, COLS, HD), F32), pltpu.VMEM((2, COLS, HD), F32)],
        compiler_params=params(),
        cost_estimate=cost(16 * 10 * BLK * 2 * BLK * HD, 7 * COLS * HALF * 2, 16 * BLK * 2 * BLK),
        name="row_backward",
    )(pattern, q, k, v, g)


def finish_kernel(off_ref, b_ref, dq_in, dk_in, dv_in, dq_ref, dk_ref, dv_ref):
    dq_ref[...] = b_ref[:, :HALF]
    for h in range(HC):
        pair = jnp.concatenate([b_ref[:, head(HC + h)], b_ref[:, head(2 * HC + h)]], axis=1)
        back = t_mm(shift_selector(off_ref[h]), pair).astype(BF)
        dk_ref[:, head(h)] = back[:, :HD]
        dv_ref[:, head(h)] = back[:, HD:]


def finish(back, dq, dk, dv, offset):
    whole = jax.ShapeDtypeStruct((COLS, 2 * HALF), BF)
    kept = pl.BlockSpec(memory_space=pl.ANY)
    second = pl.BlockSpec((COLS, HALF), lambda i: (0, 1))
    return pl.pallas_call(
        finish_kernel,
        grid=(1,),
        out_shape=(whole, whole, whole),
        in_specs=[SMEM_SPEC, pl.BlockSpec((COLS, 3 * HALF), lambda i: (0, 0)), kept, kept, kept],
        out_specs=(second, second, second),
        input_output_aliases={2: 0, 3: 1, 4: 2},
        compiler_params=params(),
        cost_estimate=cost(2 * COLS * COLS * 2 * HALF, 6 * COLS * HALF * 2),
        name="finish",
    )(offset, back, dq, dk, dv)


def attn_grad_kernel(core_ref, og_mine, og_theirs, mine_ref, theirs_ref, o_ref):
    total = mm_t(og_mine[...], mine_ref[...]) + mm_t(og_theirs[...], theirs_ref[...])
    o_ref[...] = total.astype(BF)


def attn_grad_of(og, mine, theirs, core):
    steps = 4
    rows = 2 * HALF // steps
    return pl.pallas_call(
        attn_grad_kernel,
        grid_spec=pltpu.PrefetchScalarGridSpec(
            num_scalar_prefetch=1,
            grid=(steps,),
            in_specs=[
                pl.BlockSpec((COLS, DH), lambda i, c: (0, c[0])),
                pl.BlockSpec((COLS, DH), lambda i, c: (0, 1 - c[0])),
                pl.BlockSpec((rows, DH), lambda i, c: (i, 0)),
                pl.BlockSpec((rows, DH), lambda i, c: (i, 0)),
            ],
            out_specs=pl.BlockSpec((COLS, rows), lambda i, c: (0, i)),
        ),
        out_shape=jax.ShapeDtypeStruct((COLS, 2 * HALF), BF),
        compiler_params=params(),
        cost_estimate=cost(2 * COLS * 2 * HALF * D, 7 * 2**20),
        name="attn_grad",
    )(core, og, og, mine, theirs)


def layer_out_kernel(core_ref, row_ref, col_ref, mine_ref, theirs_ref, o_ref):
    def product(w_ref):
        total = mm(row_ref[...], w_ref[:HALF, :]) + mm(col_ref[...], w_ref[HALF:, :])
        o_ref[...] = total.astype(BF)

    pl.when(pl.program_id(0) == 0)(lambda: product(mine_ref))
    pl.when(pl.program_id(0) == 1)(lambda: product(theirs_ref))


def layer_out_of(row_out, col_out, mine, theirs, core):
    steps = 2
    width = DH // steps

    def place(half, i, c):
        which = jnp.where(half == 0, c[0], 1 - c[0])
        return (0, which * steps + i)

    return pl.pallas_call(
        layer_out_kernel,
        grid_spec=pltpu.PrefetchScalarGridSpec(
            num_scalar_prefetch=1,
            grid=(2, steps),
            in_specs=[
                pl.BlockSpec((COLS, HALF), lambda half, i, c: (0, 0)),
                pl.BlockSpec((COLS, HALF), lambda half, i, c: (0, 0)),
                pl.BlockSpec((2 * HALF, width), lambda half, i, c: (0, jnp.where(half == 0, i, steps - 1))),
                pl.BlockSpec((2 * HALF, width), lambda half, i, c: (0, jnp.where(half == 0, 0, i))),
            ],
            out_specs=pl.BlockSpec((COLS, width), place),
        ),
        out_shape=jax.ShapeDtypeStruct((COLS, D), BF),
        compiler_params=params(),
        cost_estimate=cost(2 * COLS * 2 * HALF * D, 7 * 2**20),
        name="layer_out",
    )(core, row_out, col_out, mine, theirs)


def weight_grad_kernel(core_ref, row_mine, row_theirs, col_mine, col_theirs, og_mine, og_theirs, o_ref):
    def product(a_ref, b_ref):
        o_ref[...] = (t_mm(a_ref[...], og_mine[...]) + t_mm(b_ref[...], og_theirs[...])).astype(BF)

    pl.when(pl.program_id(0) == 0)(lambda: product(row_mine, row_theirs))
    pl.when(pl.program_id(0) == 1)(lambda: product(col_mine, col_theirs))


def weight_grad_of(row_mine, row_theirs, col_mine, col_theirs, og, og_theirs, core):
    part = pl.BlockSpec((COLS, HALF), lambda i, c: (0, 0))
    return pl.pallas_call(
        weight_grad_kernel,
        grid_spec=pltpu.PrefetchScalarGridSpec(
            num_scalar_prefetch=1,
            grid=(2,),
            in_specs=[part] * 4
            + [
                pl.BlockSpec((COLS, DH), lambda i, c: (0, c[0])),
                pl.BlockSpec((COLS, DH), lambda i, c: (0, 0)),
            ],
            out_specs=pl.BlockSpec((HALF, DH), lambda i, c: (i, 0)),
        ),
        out_shape=jax.ShapeDtypeStruct((2 * HALF, DH), BF),
        compiler_params=params(),
        cost_estimate=cost(4 * COLS * 2 * HALF * DH, 6 * 2**20),
        name="weight_grad",
    )(core, row_mine, row_theirs, col_mine, col_theirs, og, og_theirs)


def exchange(tensor, axes):
    return lax.all_to_all(tensor, axes, split_axis=0, concat_axis=0, tiled=True)


def other_core(tensor):
    return lax.ppermute(tensor, "c", [(0, 1), (1, 0)])


def dp_shift(step, dx, dz):
    return [(x * dz + z, (x + step // dz) % dx * dz + (z + step % dz) % dz) for x in range(dx) for z in range(dz)]


def shards(queries, keys, values, out_proj, out_grad, block_pattern, col_offset):
    q, k, v = (t.reshape(COLS, 2 * HALF) for t in (queries, keys, values))
    og = out_grad.reshape(COLS, D)
    rows_of = out_proj.shape[0]
    seq = ROWS
    chips = seq // 2
    dp = lax.axis_size("x") * lax.axis_size("zl")
    core_index = lax.axis_index("c")
    core = core_index.astype(jnp.int32).reshape(1)

    halves = out_proj.reshape(rows_of, 2, DH).transpose(1, 0, 2)
    spread = jnp.broadcast_to(halves[None], (chips, 2, rows_of, DH)).reshape(seq, rows_of, DH)
    own_rows = exchange(spread, SEQ).reshape(seq * rows_of, DH)
    mine = lax.all_gather(own_rows, DP, axis=0, tiled=True)
    theirs = other_core(mine)

    packed = pack(q, k, v, col_offset)
    received = exchange(packed.reshape(seq, COLS // seq, 3 * HALF), SEQ)
    received = received.reshape(ROWS, 2, GRP, 3 * HALF)

    og_sent = lax.dynamic_slice(og, (0, (1 - core_index) * DH), (COLS, DH))
    og_theirs = other_core(og_sent)
    row_out = row_forward(q, k, v, block_pattern)
    row_theirs = other_core(row_out)

    col_sent = column_forward(received).reshape(seq, COLS // seq, HALF)
    col_out = exchange(col_sent, SEQ).reshape(COLS, HALF)
    col_theirs = other_core(col_out)

    grads = attn_grad_of(og, mine, theirs, core)
    col_grads = exchange(grads[:, HALF:].reshape(seq, COLS // seq, HALF), SEQ)
    col_grads = col_grads.reshape(ROWS, 2, GRP, HALF)

    weight_part = weight_grad_of(row_out, row_theirs, col_out, col_theirs, og, og_theirs, core)
    weight_dp = exchange(weight_part.reshape(dp, 2 * HALF // dp, DH), DP)
    weight_dp = jnp.sum(weight_dp.astype(F32), axis=0).astype(BF)
    weight_seq = exchange(weight_dp.reshape(seq, rows_of, DH), SEQ)
    weight_sum = jnp.sum(weight_seq.astype(F32).reshape(chips, 2, rows_of, DH), axis=0)
    tokens = COLS * seq * dp
    w_grad = weight_sum.transpose(1, 0, 2).reshape(rows_of, D) * tokens ** (-0.5)

    dq, dk, dv = row_backward(q, k, v, grads, block_pattern)
    col_back = column_backward(received, col_grads).reshape(seq, COLS // seq, 3 * HALF)
    back = exchange(col_back, SEQ).reshape(COLS, 3 * HALF)
    dq, dk, dv = finish(back, dq, dk, dv, col_offset)

    layer = layer_out_of(row_out, col_out, mine, theirs, core)
    lead = (1, 1, COLS)
    return (
        layer.reshape(lead + (D,)),
        dq.reshape(lead + (2 * HALF,)),
        dk.reshape(lead + (2 * HALF,)),
        dv.reshape(lead + (2 * HALF,)),
        w_grad,
    )


def solution(mesh):
    fine = Mesh(mesh.devices.reshape(4, 2, 4, 4, 2), DP + SEQ)
    token = P(DP, SEQ, None, None)
    rows = P(DP + SEQ, None)
    in_specs = (token, token, token, rows, token, P(), P())
    out_specs = (token, token, token, token, rows)
    return jax.shard_map(shards, mesh=fine, in_specs=in_specs, out_specs=out_specs, check_vma=False)
```

time: 986 us -> 257 us (0.26)
  waiting for transfers between devices: 743 us -> 137 us
  local copies, waits for them, and re-layouts: 82 us -> 17.1 us
  Pallas kernels: 0 us -> 41.3 us
  matrix products: 36.2 us -> 0 us
  other arithmetic: 27.8 us -> 2.71 us
  starting transfers between devices: 63.8 us -> 43.6 us
  between operations: 25.3 us -> 14.2 us
    all_gather x1, waiting for transfers between devices: 414 us -> 0.02 us  [shards(): mine = lax.all_gather(own_rows, DP, axis=0, tiled=True)]
    unnamed x3 -> x1, waiting for transfers between devices: 271 us -> 0.02 us
    all_to_all x8 -> x7, waiting for transfers between devices: 58.9 us -> 131 us  [exchange(): return lax.all_to_all(tensor, axes, split_axis=0, concat_axis=0, tiled=True)]
    pallas_call x0 -> x9, Pallas kernels: none -> 41.3 us  [the longest x1 9.88 us: row_backward(): pl.pallas_call(row_backward_kernel, grid=(1,), out_shape=(whole, whole, w...]
    dot_general x18 -> x0, matrix products: 33.5 us -> none  [the longest x1 6.82 us: shards(): lax.dot_general(attn_part, grad_flat, (((0,), (0,)), ((), ())), preferred...]
    slice x20 -> x1, local copies, waits for them, and re-layouts: 25.9 us -> 0.83 us  [shards(): col_grads = exchange(grads[:, HALF:].reshape(seq, COLS // seq, HALF), SEQ)]
    all_to_all x8 -> x7, starting transfers between devices: 63.5 us -> 40.8 us  [exchange(): return lax.all_to_all(tensor, axes, split_axis=0, concat_axis=0, tiled=True)]
    another operation x8 -> x0, other arithmetic: 12.5 us -> none  [the longest x6 9.13 us: roll_columns(): return jnp.stack(moved_heads, axis=2)]
  transfers between devices with their start and end apart: 10 -> 12, of which waited for: 8 -> 9; matrix products, arithmetic and copies ran while one was open for 10% -> 3% of each run, Pallas kernels for 0% -> 15%
where the time goes in v1:
time: 257 us; the launch traced here: 256 us
  waiting for transfers between devices  137 us (53%)
  starting transfers between devices  43.6 us (17%)
  Pallas kernels  41.3 us (16%)
  local copies, waits for them, and re-layouts  17.1 us (7%)
  between operations  14.2 us (6%)
  other arithmetic  2.71 us (1%)
    all_to_all x7, waiting for transfers between devices, exchange(): return lax.all_to_all(tensor, axes, split_axis=0, concat_axis=0, tiled=True)  131 us
    all_to_all x7, starting transfers between devices, exchange(): return lax.all_to_all(tensor, axes, split_axis=0, concat_axis=0, tiled=True)  40.8 us
    unnamed x36, local copies, waits for them, and re-layouts  10.7 us
    pallas_call x1, Pallas kernels, row_backward(): pl.pallas_call(row_backward_kernel, grid=(1,), out_shape=(whole, whole, w...  9.88 us
    pallas_call x1, Pallas kernels, layer_out_of(): pl.pallas_call(layer_out_kernel, grid_spec=pltpu.PrefetchScalarGridSpec(n...  5.89 us
    ppermute x4, waiting for transfers between devices, other_core(): return lax.ppermute(tensor, 'c', [(0, 1), (1, 0)])  5.75 us
    pallas_call x1, Pallas kernels, weight_grad_of(): pl.pallas_call(weight_grad_kernel, grid_spec=pltpu.PrefetchScalarGridSpec...  5.46 us
  transfers between devices with their start and end apart: 12, of which 9 were waited for; matrix products, arithmetic and copies ran while one was open for 3% of the time, Pallas kernels for 15%

profile of v1, /device:TPU:1, one launch (start us, length us, event | category | flops | bytes accessed | tf_op | source)
XLA Modules:
  0.0 256.2 jit_solution(4522026758438252513)
XLA Ops:
  8.7 12.8 %all-to-all-start.2 = ((bf16[32,4,1024]{2,1,0:T(4,128)(2,1)}), bf16[32,4,1024]{2,1,0:T(4,128)(2,1)S(1)}, u32[]{:S(2)}, u32[]{:S(2)}) async-start(bf16[32,4,1024]{2,1,0:T(4,128)(2,1)} %bitcast.9), calls=%async_computation.2 | async-start | bytes 524288 | tf_op jit(solution)/shard_map/all_to_all | solution.py:349
  22.7 1.2 copy-done.3
  23.9 1.2 copy-done.6
  25.8 2.5 pack.1
  28.3 6.6 %all-to-all-done.2 = bf16[32,4,1024]{2,1,0:T(4,128)(2,1)S(1)} async-done(((bf16[32,4,1024]{2,1,0:T(4,128)(2,1)}), bf16[32,4,1024]{2,1,0:T(4,128)(2,1)S(1)}, u32[]{:S(2)}, u32[]{:S(2)}) %all-to-all-start.2) | async-done | bytes 262176 | tf_op jit(solution)/shard_map/all_to_all | solution.py:349
  34.9 4.0 %all-to-all-start = ((bf16[32,16,1536]{2,1,0:T(8,128)(2,1)}), bf16[32,16,1536]{2,1,0:T(8,128)(2,1)S(1)}, u32[]{:S(2)}, u32[]{:S(2)}) async-start(bf16[32,16,1536]{2,1,0:T(8,128)(2,1)} %bitcast.43), calls=%async_computation | async-start | bytes 3145728 | tf_op jit(solution)/shard_map/all_to_all | solution.py:349
  39.8 50.6 %all-to-all-done = bf16[32,16,1536]{2,1,0:T(8,128)(2,1)S(1)} async-done(((bf16[32,16,1536]{2,1,0:T(8,128)(2,1)}), bf16[32,16,1536]{2,1,0:T(8,128)(2,1)S(1)}, u32[]{:S(2)}, u32[]{:S(2)}) %all-to-all-start) | async-done | bytes 1572896 | tf_op jit(solution)/shard_map/all_to_all | solution.py:349
  90.4 2.4 column_forward.1
  92.7 4.7 %all-to-all-start.1 = ((bf16[32,16,512]{2,1,0:T(8,128)(2,1)}), bf16[32,16,512]{2,1,0:T(8,128)(2,1)}, u32[]{:S(2)}, u32[]{:S(2)}) async-start(bf16[32,16,512]{2,1,0:T(8,128)(2,1)} %bitcast.6), calls=%async_computation.1 | async-start | bytes 1048576 | tf_op jit(solution)/shard_map/all_to_all | solution.py:349
  97.5 2.4 dynamic-slice_bitcast_fusion
  100.4 2.2 row_forward.1.row_ref.row_mine
  102.7 16.3 %all-to-all-done.1 = bf16[32,16,512]{2,1,0:T(8,128)(2,1)} async-done(((bf16[32,16,512]{2,1,0:T(8,128)(2,1)}), bf16[32,16,512]{2,1,0:T(8,128)(2,1)}, u32[]{:S(2)}, u32[]{:S(2)}) %all-to-all-start.1) | async-done | bytes 524320 | tf_op jit(solution)/shard_map/all_to_all | solution.py:349
  119.0 1.7 collective-permute-start.2
  120.7 1.7 collective-permute-done.2.col_theirs
  122.5 5.5 %weight_grad.1 = bf16[1024,1024]{1,0:T(8,128)(2,1)} custom-call(s32[1]{0:T(128)} %bitcast.core_ref, bf16[512,512]{1,0:T(8,128)(2,1)S(1)} %row_forward.1.row_ref.row_mine, bf16[512,512]{1,0:T(8,128)(2,1)} %collective-permute-done.1.row_theirs, bf16[512,512]{1,0:T(8,128)(2,1)} %bitcast.7.col_ref.col_mine, ...), custom_call_target="tpu_custom_call" | custom-call | flops 2147483648 | bytes 6291456 | tf_op jit(solution)/shard_map/weight_grad/pallas_call | solution.py:329
  127.9 4.4 %all-to-all-start.5 = ((bf16[8,128,1024]{2,1,0:T(8,128)(2,1)}), bf16[8,128,1024]{2,1,0:T(8,128)(2,1)}, u32[]{:S(2)}, u32[]{:S(2)}) async-start(bf16[8,128,1024]{2,1,0:T(8,128)(2,1)} %bitcast.44), calls=%async_computation.5 | async-start | bytes 4194304 | tf_op jit(solution)/shard_map/all_to_all | solution.py:349
  132.8 4.0 %collective-permute-done.theirs_ref = bf16[1024,1024]{1,0:T(8,128)(2,1)S(1)} collective-permute-done((bf16[1024,1024]{1,0:T(8,128)(2,1)}, bf16[1024,1024]{1,0:T(8,128)(2,1)S(1)}, u32[]{:S(2)}, u32[]{:S(2)}) %collective-permute-start) | collective-permute-done | bytes 2097184 | tf_op jit(solution)/shard_map/ppermute | solution.py:353
  136.8 1.3 copy-done.17
  138.1 1.6 copy-done
  139.7 4.8 %attn_grad.1.g_ref = bf16[512,1024]{1,0:T(8,128)(2,1)S(1)} custom-call(s32[1]{0:T(128)} %bitcast.core_ref, bf16[512,2048]{1,0:T(8,128)(2,1)S(1)} %bitcast.30, bf16[512,2048]{1,0:T(8,128)(2,1)S(1)} %bitcast.31, bf16[1024,1024]{1,0:T(8,128)(2,1)} %all-gather.2.cloned.1.call-done.mine_ref, bf16[1024,1024]{1,0:T(8,128)(2,1)} %copy-done.17), custom_call_target="tpu_custom_call" | custom-call | flops 2147483648 | bytes 7340032 | tf_op jit(solution)/shard_map/attn_grad/pallas_call | solution.py:262
  146.4 12.6 %all-to-all-done.5 = bf16[8,128,1024]{2,1,0:T(8,128)(2,1)} async-done(((bf16[8,128,1024]{2,1,0:T(8,128)(2,1)}), bf16[8,128,1024]{2,1,0:T(8,128)(2,1)}, u32[]{:S(2)}, u32[]{:S(2)}) %all-to-all-start.5) | async-done | bytes 2097184 | tf_op jit(solution)/shard_map/all_to_all | solution.py:349
  159.0 5.4 %all-to-all-start.3 = ((bf16[32,16,512]{2,1,0:T(8,128)(2,1)}), bf16[32,16,512]{2,1,0:T(8,128)(2,1)S(1)}, u32[]{:S(2)}, u32[]{:S(2)}) async-start(bf16[32,16,512]{2,1,0:T(8,128)(2,1)} %bitcast.45), calls=%async_computation.3 | async-start | bytes 1048576 | tf_op jit(solution)/shard_map/all_to_all | solution.py:349
  164.5 2.0 reduce_sum.21
  167.2 15.4 %all-to-all-done.3 = bf16[32,16,512]{2,1,0:T(8,128)(2,1)S(1)} async-done(((bf16[32,16,512]{2,1,0:T(8,128)(2,1)}), bf16[32,16,512]{2,1,0:T(8,128)(2,1)S(1)}, u32[]{:S(2)}, u32[]{:S(2)}) %all-to-all-start.3) | async-done | bytes 524320 | tf_op jit(solution)/shard_map/all_to_all | solution.py:349
  182.7 4.8 %all-to-all-start.6 = ((bf16[32,4,1024]{2,1,0:T(4,128)(2,1)}), bf16[32,4,1024]{2,1,0:T(4,128)(2,1)S(1)}, u32[]{:S(2)}, u32[]{:S(2)}) async-start(bf16[32,4,1024]{2,1,0:T(4,128)(2,1)} %reshape.108), calls=%async_computation.6 | async-start | bytes 524288 | tf_op jit(solution)/shard_map/all_to_all | solution.py:349
  187.5 4.8 %column_backward.1 = bf16[32,2,8,1536]{3,2,1,0:T(8,128)(2,1)S(1)} custom-call(bf16[32,2,8,1536]{3,2,1,0:T(8,128)(2,1)S(1)} %bitcast.28, bf16[32,2,8,512]{3,2,1,0:T(8,128)(2,1)S(1)} %bitcast.42), custom_call_target="tpu_custom_call" | custom-call | flops 671088640 | bytes 3670016 | tf_op jit(solution)/shard_map/column_backward/pallas_call | solution.py:150
  193.4 7.0 %all-to-all-done.6 = bf16[32,4,1024]{2,1,0:T(4,128)(2,1)S(1)} async-done(((bf16[32,4,1024]{2,1,0:T(4,128)(2,1)}), bf16[32,4,1024]{2,1,0:T(4,128)(2,1)S(1)}, u32[]{:S(2)}, u32[]{:S(2)}) %all-to-all-start.6) | async-done | bytes 262176 | tf_op jit(solution)/shard_map/all_to_all | solution.py:349
  200.5 4.7 %all-to-all-start.4 = ((bf16[32,16,1536]{2,1,0:T(8,128)(2,1)}), bf16[32,16,1536]{2,1,0:T(8,128)(2,1)}, u32[]{:S(2)}, u32[]{:S(2)}) async-start(bf16[32,16,1536]{2,1,0:T(8,128)(2,1)} %bitcast.41), calls=%async_computation.4 | async-start | bytes 3145728 | tf_op jit(solution)/shard_map/all_to_all | solution.py:349
  206.4 9.9 %row_backward.1 = (bf16[512,1024]{1,0:T(8,128)(2,1)}, bf16[512,1024]{1,0:T(8,128)(2,1)}, bf16[512,1024]{1,0:T(8,128)(2,1)}) custom-call(s32[4,4]{1,0:T(4,128)S(1)} %copy-done.14, bf16[512,1024]{1,0:T(8,128)(2,1)S(1)} %bitcast.34, bf16[512,1024]{1,0:T(8,128)(2,1)S(1)} %bitcast.37, bf16[512,1024]{1,0:T(8,128)(2,1)S(1)} %bitcast.40, bf16[512,1024]{1,0:T(8,128)(2,1)} %copy-done.9), custom_call_target="tpu_custom_call" | custom-call | flops 671088640 | bytes 3670016 | tf_op jit(solution)/shard_map/row_backward/pallas_call | solution.py:215
  216.3 5.9 %layer_out.1 = bf16[512,2048]{1,0:T(8,128)(2,1)} custom-call(s32[1]{0:T(128)} %bitcast.core_ref, bf16[512,512]{1,0:T(8,128)(2,1)S(1)} %copy-done.13, bf16[512,512]{1,0:T(8,128)(2,1)} %bitcast.7.col_ref.col_mine, bf16[1024,1024]{1,0:T(8,128)(2,1)S(1)} %copy-done.11, bf16[1024,1024]{1,0:T(8,128)(2,1)} %copy-done.17), custom_call_target="tpu_custom_call" | custom-call | flops 2147483648 | bytes 7340032 | tf_op jit(solution)/shard_map/layer_out/pallas_call | solution.py:299
  223.0 23.0 %all-to-all-done.4 = bf16[32,16,1536]{2,1,0:T(8,128)(2,1)} async-done(((bf16[32,16,1536]{2,1,0:T(8,128)(2,1)}), bf16[32,16,1536]{2,1,0:T(8,128)(2,1)}, u32[]{:S(2)}, u32[]{:S(2)}) %all-to-all-start.4) | async-done | bytes 1572896 | tf_op jit(solution)/shard_map/all_to_all | solution.py:349
  245.9 3.4 %finish.1 = (bf16[512,1024]{1,0:T(8,128)(2,1)}, bf16[512,1024]{1,0:T(8,128)(2,1)}, bf16[512,1024]{1,0:T(8,128)(2,1)}) custom-call(s32[4]{0:T(128)S(1)} %copy-done.16, bf16[512,1536]{1,0:T(8,128)(2,1)} %bitcast.15.b_ref, bf16[512,1024]{1,0:T(8,128)(2,1)} %get-tuple-element.11.dq_in, ...), custom_call_target="tpu_custom_call", output_to_operand_aliasing={{0}: (2, {}), {1}: (3, {}), {2}: (4, {})} | custom-call | flops 536870912 | bytes 3145728 | tf_op jit(solution)/shard_map/finish/pallas_call | solution.py:241
  (48 shorter events, 11.2 us)
Async XLA Ops:
  8.7 26.2 %all-to-all-start.2 = ((bf16[32,4,1024]{2,1,0:T(4,128)(2,1)}), bf16[32,4,1024]{2,1,0:T(4,128)(2,1)S(1)}, u32[]{:S(2)}, u32[]{:S(2)}) async-start(bf16[32,4,1024]{2,1,0:T(4,128)(2,1)} %bitcast.9), calls=%async_computation.2 | async-start | bytes 524288 | tf_op jit(solution)/shard_map/all_to_all | solution.py:349
  21.5 1.2 copy-start.1
  22.7 1.2 copy-start.3
  23.9 1.2 copy-start.6
  25.2 0.7 copy-start.15
  34.9 55.5 %all-to-all-start = ((bf16[32,16,1536]{2,1,0:T(8,128)(2,1)}), bf16[32,16,1536]{2,1,0:T(8,128)(2,1)S(1)}, u32[]{:S(2)}, u32[]{:S(2)}) async-start(bf16[32,16,1536]{2,1,0:T(8,128)(2,1)} %bitcast.43), calls=%async_computation | async-start | bytes 3145728 | tf_op jit(solution)/shard_map/all_to_all | solution.py:349
  38.9 93.4 %all-gather.2.cloned.1.call-start = ((), (), s32[]{:S(2)}) async-start(), calls=%async_computation.7 | async-start | bytes 2359296 | tf_op jit(solution)/shard_map/all_gather | solution.py:373
  92.7 7.6 %copy-start.2 = (bf16[1,1,512,1024]{3,2,1,0:T(8,128)(2,1)S(1)}, bf16[1,1,512,1024]{3,2,1,0:T(8,128)(2,1)}, u32[]{:S(2)}) copy-start(bf16[1,1,512,1024]{3,2,1,0:T(8,128)(2,1)} %param.7) | copy-start | bytes 3145732
  92.7 7.6 %copy-start.14 = (s32[4,4]{1,0:T(4,128)S(1)}, s32[4,4]{1,0:T(4,128)}, u32[]{:S(2)}) copy-start(s32[4,4]{1,0:T(4,128)} %pat_ref.3) | copy-start | bytes 196
  92.7 26.3 %all-to-all-start.1 = ((bf16[32,16,512]{2,1,0:T(8,128)(2,1)}), bf16[32,16,512]{2,1,0:T(8,128)(2,1)}, u32[]{:S(2)}, u32[]{:S(2)}) async-start(bf16[32,16,512]{2,1,0:T(8,128)(2,1)} %bitcast.6), calls=%async_computation.1 | async-start | bytes 1048576 | tf_op jit(solution)/shard_map/all_to_all | solution.py:349
  97.5 2.9 %copy-start.4 = (bf16[1,1,512,1024]{3,2,1,0:T(8,128)(2,1)S(1)}, bf16[1,1,512,1024]{3,2,1,0:T(8,128)(2,1)}, u32[]{:S(2)}) copy-start(bf16[1,1,512,1024]{3,2,1,0:T(8,128)(2,1)} %param.8) | copy-start | bytes 3145732
  97.5 2.9 %copy-start.7 = (bf16[1,1,512,1024]{3,2,1,0:T(8,128)(2,1)S(1)}, bf16[1,1,512,1024]{3,2,1,0:T(8,128)(2,1)}, u32[]{:S(2)}) copy-start(bf16[1,1,512,1024]{3,2,1,0:T(8,128)(2,1)} %param.9) | copy-start | bytes 3145732
  99.9 20.8 %collective-permute-start.3 = (bf16[512,1024]{1,0:T(8,128)(2,1)}, bf16[512,1024]{1,0:T(8,128)(2,1)}, u32[]{:S(2)}, u32[]{:S(2)}) collective-permute-start(bf16[512,1024]{1,0:T(8,128)(2,1)} %dynamic-slice_bitcast_fusion), channel_id=1, source_target_pairs={{0,1},{1,0},{2,3},{3,2},{4,5},{5,4},{6,7},{7,6},{8,9},{9,8},{10,11... | collective-permute-start | bytes 3145736 | tf_op jit(solution)/shard_map/ppermute | solution.py:353
  102.6 25.4 %copy-start.12 = (bf16[512,512]{1,0:T(8,128)(2,1)}, bf16[512,512]{1,0:T(8,128)(2,1)S(1)}, u32[]{:S(2)}) copy-start(bf16[512,512]{1,0:T(8,128)(2,1)S(1)} %row_forward.1.row_ref.row_mine) | copy-start | bytes 1572868
  102.6 18.2 %collective-permute-start.1 = (bf16[512,512]{1,0:T(8,128)(2,1)S(1)}, bf16[512,512]{1,0:T(8,128)(2,1)}, u32[]{:S(2)}, u32[]{:S(2)}) collective-permute-start(bf16[512,512]{1,0:T(8,128)(2,1)S(1)} %row_forward.1.row_ref.row_mine), channel_id=1, source_target_pairs={{0,1},{1,0},{2,3},{3,2},{4,5},{5,4},{6,7},{7,6},{8,9},{9,8},{10,11... | collective-permute-start | bytes 1572872 | tf_op jit(solution)/shard_map/ppermute | solution.py:353
  119.0 3.5 %collective-permute-start.2 = (bf16[512,512]{1,0:T(8,128)(2,1)}, bf16[512,512]{1,0:T(8,128)(2,1)S(1)}, u32[]{:S(2)}, u32[]{:S(2)}) collective-permute-start(bf16[512,512]{1,0:T(8,128)(2,1)} %bitcast.7.col_ref.col_mine), channel_id=1, source_target_pairs={{0,1},{1,0},{2,3},{3,2},{4,5},{5,4},{6,7},{7,6},{8,9},{9,8},{10,11... | collective-permute-start | bytes 1572872 | tf_op jit(solution)/shard_map/ppermute | solution.py:353
  127.9 31.1 %all-to-all-start.5 = ((bf16[8,128,1024]{2,1,0:T(8,128)(2,1)}), bf16[8,128,1024]{2,1,0:T(8,128)(2,1)}, u32[]{:S(2)}, u32[]{:S(2)}) async-start(bf16[8,128,1024]{2,1,0:T(8,128)(2,1)} %bitcast.44), calls=%async_computation.5 | async-start | bytes 4194304 | tf_op jit(solution)/shard_map/all_to_all | solution.py:349
  132.3 4.5 %collective-permute-start = (bf16[1024,1024]{1,0:T(8,128)(2,1)}, bf16[1024,1024]{1,0:T(8,128)(2,1)S(1)}, u32[]{:S(2)}, u32[]{:S(2)}) collective-permute-start(bf16[1024,1024]{1,0:T(8,128)(2,1)} %all-gather.2.cloned.1.call-done.mine_ref), channel_id=1, source_target_pairs={{0,1},{1,0},{2,3},{3,2},{4,5},{5,4},{6,7},{7,6},{8,9},{9,8},{10,11... | collective-permute-start | bytes 6291464 | tf_op jit(solution)/shard_map/ppermute | solution.py:353
  136.8 1.3 copy-start.17
  138.1 1.6 copy-start
  144.5 1.1 copy-start.9
  159.0 23.6 %all-to-all-start.3 = ((bf16[32,16,512]{2,1,0:T(8,128)(2,1)}), bf16[32,16,512]{2,1,0:T(8,128)(2,1)S(1)}, u32[]{:S(2)}, u32[]{:S(2)}) async-start(bf16[32,16,512]{2,1,0:T(8,128)(2,1)} %bitcast.45), calls=%async_computation.3 | async-start | bytes 1048576 | tf_op jit(solution)/shard_map/all_to_all | solution.py:349
  182.7 17.8 %all-to-all-start.6 = ((bf16[32,4,1024]{2,1,0:T(4,128)(2,1)}), bf16[32,4,1024]{2,1,0:T(4,128)(2,1)S(1)}, u32[]{:S(2)}, u32[]{:S(2)}) async-start(bf16[32,4,1024]{2,1,0:T(4,128)(2,1)} %reshape.108), calls=%async_computation.6 | async-start | bytes 524288 | tf_op jit(solution)/shard_map/all_to_all | solution.py:349
  192.3 1.1 copy-start.10
  193.4 11.7 %copy-start.5 = (bf16[1,1,512,1024]{3,2,1,0:T(8,128)(2,1)S(1)}, bf16[1,1,512,1024]{3,2,1,0:T(8,128)(2,1)}, u32[]{:S(2)}) copy-start(bf16[1,1,512,1024]{3,2,1,0:T(8,128)(2,1)} %param.8) | copy-start | bytes 3145732
  200.5 45.4 %all-to-all-start.4 = ((bf16[32,16,1536]{2,1,0:T(8,128)(2,1)}), bf16[32,16,1536]{2,1,0:T(8,128)(2,1)}, u32[]{:S(2)}, u32[]{:S(2)}) async-start(bf16[32,16,1536]{2,1,0:T(8,128)(2,1)} %bitcast.41), calls=%async_computation.4 | async-start | bytes 3145728 | tf_op jit(solution)/shard_map/all_to_all | solution.py:349
  205.2 1.2 copy-start.8
  206.4 9.9 %copy-start.11 = (bf16[1024,1024]{1,0:T(8,128)(2,1)S(1)}, bf16[1024,1024]{1,0:T(8,128)(2,1)}, u32[]{:S(2)}) copy-start(bf16[1024,1024]{1,0:T(8,128)(2,1)} %all-gather.2.cloned.1.call-done.mine_ref) | copy-start | bytes 6291460
  206.4 9.9 %copy-start.13 = (bf16[512,512]{1,0:T(8,128)(2,1)S(1)}, bf16[512,512]{1,0:T(8,128)(2,1)}, u32[]{:S(2)}) copy-start(bf16[512,512]{1,0:T(8,128)(2,1)} %copy-done.12) | copy-start | bytes 1572868
  216.3 29.6 %copy-start.16 = (s32[4]{0:T(128)S(1)}, s32[4]{0:T(128)}, u32[]{:S(2)}) copy-start(s32[4]{0:T(128)} %off_ref.3) | copy-start | bytes 52
Sparse Core Ops, SparseCore 0:
  42.1 85.0 all-gather.1

commit v2 on v1

--- a/solution.py
+++ b/solution.py
@@ -112,7 +112,7 @@
     return q, k, v, softmax(jnp.where(mask, mm_t(q, k) * SCALE, -1e30))
 
 
-def column_forward_kernel(r_ref, o_ref):
+def column_forward_kernel(r_ref, kept_ref, o_ref):
     mask = column_mask()
     for group in range(2):
         for h in range(HC):
@@ -120,16 +120,21 @@
             store_tile(o_ref, group, h, mm(probs.astype(BF), v))
 
 
-def column_forward(received):
+def column_forward(received, send):
     return pl.pallas_call(
         column_forward_kernel,
-        out_shape=jax.ShapeDtypeStruct((ROWS, 2, GRP, HALF), BF),
-        in_specs=[VMEM_SPEC],
-        out_specs=VMEM_SPEC,
+        grid=(1,),
+        out_shape=jax.ShapeDtypeStruct((ROWS, 2, GRP, 2 * HALF), BF),
+        in_specs=[
+            pl.BlockSpec((ROWS, 2, GRP, 3 * HALF), lambda i: (0, 0, 0, 0)),
+            pl.BlockSpec(memory_space=pl.ANY),
+        ],
+        out_specs=pl.BlockSpec((ROWS, 2, GRP, HALF), lambda i: (0, 0, 0, 0)),
+        input_output_aliases={1: 0},
         compiler_params=params(),
         cost_estimate=cost(8 * 4 * TILE * TILE * HD, 4 * COLS * HALF * 2, 8 * TILE * TILE),
         name="column_forward",
-    )(received)
+    )(received, send)
 
 
 def column_backward_kernel(r_ref, g_ref, o_ref):
@@ -149,9 +154,13 @@
 def column_backward(received, grads):
     return pl.pallas_call(
         column_backward_kernel,
+        grid=(1,),
         out_shape=jax.ShapeDtypeStruct((ROWS, 2, GRP, 3 * HALF), BF),
-        in_specs=[VMEM_SPEC, VMEM_SPEC],
-        out_specs=VMEM_SPEC,
+        in_specs=[
+            pl.BlockSpec((ROWS, 2, GRP, 3 * HALF), lambda i: (0, 0, 0, 0)),
+            pl.BlockSpec((ROWS, 2, GRP, HALF), lambda i: (0, 0, 0, 1)),
+        ],
+        out_specs=pl.BlockSpec((ROWS, 2, GRP, 3 * HALF), lambda i: (0, 0, 0, 0)),
         compiler_params=params(),
         cost_estimate=cost(8 * 10 * TILE * TILE * HD, 7 * COLS * HALF * 2, 8 * TILE * TILE),
         name="column_backward",
@@ -251,12 +260,19 @@
     )(offset, back, dq, dk, dv)
 
 
-def attn_grad_kernel(core_ref, og_mine, og_theirs, mine_ref, theirs_ref, o_ref):
-    total = mm_t(og_mine[...], mine_ref[...]) + mm_t(og_theirs[...], theirs_ref[...])
-    o_ref[...] = total.astype(BF)
-
-
-def attn_grad_of(og, mine, theirs, core):
+def attn_grad_kernel(place, og_mine, og_theirs, mine_ref, theirs_ref, row_ref, send_ref):
+    total = (mm_t(og_mine[...], mine_ref[...]) + mm_t(og_theirs[...], theirs_ref[...])).astype(BF)
+
+    @pl.when(pl.program_id(0) < 2)
+    def _():
+        row_ref[...] = total
+
+    @pl.when(pl.program_id(0) >= 2)
+    def _():
+        send_ref[...] = total
+
+
+def attn_grad_of(og, mine, theirs, place):
     steps = 4
     rows = 2 * HALF // steps
     return pl.pallas_call(
@@ -265,18 +281,21 @@
             num_scalar_prefetch=1,
             grid=(steps,),
             in_specs=[
-                pl.BlockSpec((COLS, DH), lambda i, c: (0, c[0])),
-                pl.BlockSpec((COLS, DH), lambda i, c: (0, 1 - c[0])),
-                pl.BlockSpec((rows, DH), lambda i, c: (i, 0)),
-                pl.BlockSpec((rows, DH), lambda i, c: (i, 0)),
+                pl.BlockSpec((COLS, DH), lambda i, at: (0, at[0])),
+                pl.BlockSpec((COLS, DH), lambda i, at: (0, 1 - at[0])),
+                pl.BlockSpec((rows, DH), lambda i, at: (i, 0)),
+                pl.BlockSpec((rows, DH), lambda i, at: (i, 0)),
             ],
-            out_specs=pl.BlockSpec((COLS, rows), lambda i, c: (0, i)),
+            out_specs=(
+                pl.BlockSpec((COLS, rows), lambda i, at: (0, jnp.minimum(i, 1))),
+                pl.BlockSpec((COLS, rows), lambda i, at: (0, jnp.maximum(i, 2))),
+            ),
         ),
-        out_shape=jax.ShapeDtypeStruct((COLS, 2 * HALF), BF),
+        out_shape=(jax.ShapeDtypeStruct((COLS, HALF), BF), jax.ShapeDtypeStruct((COLS, 2 * HALF), BF)),
         compiler_params=params(),
         cost_estimate=cost(2 * COLS * 2 * HALF * D, 7 * 2**20),
         name="attn_grad",
-    )(core, og, og, mine, theirs)
+    )(place, og, og, mine, theirs)
 
 
 def layer_out_kernel(core_ref, row_ref, col_ref, mine_ref, theirs_ref, o_ref):
@@ -316,33 +335,77 @@
     )(core, row_out, col_out, mine, theirs)
 
 
-def weight_grad_kernel(core_ref, row_mine, row_theirs, col_mine, col_theirs, og_mine, og_theirs, o_ref):
+def weight_grad_kernel(place, row_mine, row_theirs, col_mine, col_theirs, og_mine, og_theirs, *refs):
+    outs, total = refs[:4], refs[4]
+    step = pl.program_id(0)
+    block = lax.rem(place[1] + step, 4)
+
     def product(a_ref, b_ref):
-        o_ref[...] = (t_mm(a_ref[...], og_mine[...]) + t_mm(b_ref[...], og_theirs[...])).astype(BF)
-
-    pl.when(pl.program_id(0) == 0)(lambda: product(row_mine, row_theirs))
-    pl.when(pl.program_id(0) == 1)(lambda: product(col_mine, col_theirs))
-
-
-def weight_grad_of(row_mine, row_theirs, col_mine, col_theirs, og, og_theirs, core):
-    part = pl.BlockSpec((COLS, HALF), lambda i, c: (0, 0))
+        total[...] = t_mm(a_ref[...], og_mine[...]) + t_mm(b_ref[...], og_theirs[...])
+
+    pl.when(block < 2)(lambda: product(row_mine, row_theirs))
+    pl.when(block >= 2)(lambda: product(col_mine, col_theirs))
+    for target, out in enumerate(outs):
+
+        @pl.when(step == target)
+        def _(out=out):
+            out[...] = total[...].astype(out.dtype)
+
+
+def weight_grad_of(row_mine, row_theirs, col_mine, col_theirs, og, og_theirs, place):
+    rows = 2 * HALF // 4
+
+    def row_block(i, at):
+        return (0, jnp.minimum(lax.rem(at[1] + i, 4), 1))
+
+    def col_block(i, at):
+        return (0, jnp.maximum(lax.rem(at[1] + i, 4), 2) - 2)
+
     return pl.pallas_call(
         weight_grad_kernel,
         grid_spec=pltpu.PrefetchScalarGridSpec(
             num_scalar_prefetch=1,
-            grid=(2,),
-            in_specs=[part] * 4
-            + [
-                pl.BlockSpec((COLS, DH), lambda i, c: (0, c[0])),
-                pl.BlockSpec((COLS, DH), lambda i, c: (0, 0)),
+            grid=(4,),
+            in_specs=[
+                pl.BlockSpec((COLS, rows), row_block),
+                pl.BlockSpec((COLS, rows), row_block),
+                pl.BlockSpec((COLS, rows), col_block),
+                pl.BlockSpec((COLS, rows), col_block),
+                pl.BlockSpec((COLS, DH), lambda i, at: (0, at[0])),
+                pl.BlockSpec((COLS, DH), lambda i, at: (0, 0)),
             ],
-            out_specs=pl.BlockSpec((HALF, DH), lambda i, c: (i, 0)),
+            out_specs=(pl.BlockSpec((rows, DH), lambda i, at: (0, 0)),) * 4,
+            scratch_shapes=[pltpu.VMEM((rows, DH), F32)],
         ),
-        out_shape=jax.ShapeDtypeStruct((2 * HALF, DH), BF),
-        compiler_params=params(),
-        cost_estimate=cost(4 * COLS * 2 * HALF * DH, 6 * 2**20),
+        out_shape=(jax.ShapeDtypeStruct((rows, DH), F32),) + (jax.ShapeDtypeStruct((rows, DH), BF),) * 3,
+        compiler_params=params(),
+        cost_estimate=cost(4 * COLS * 2 * HALF * DH, 7 * 2**20),
         name="weight_grad",
-    )(core, row_mine, row_theirs, col_mine, col_theirs, og, og_theirs)
+    )(place, row_mine, row_theirs, col_mine, col_theirs, og, og_theirs)
+
+
+def weight_sum_kernel(place, a_ref, b_ref, c_ref, d_ref, keep_ref, send_ref):
+    half = keep_ref.shape[0]
+
+    def total(index):
+        rows = pl.ds(pl.multiple_of(index * half, half), half)
+        return (a_ref[rows, :] + b_ref[rows, :].astype(F32)) + (c_ref[rows, :].astype(F32) + d_ref[rows, :].astype(F32))
+
+    keep_ref[...] = total(place[2])
+    send_ref[...] = total(1 - place[2]).astype(BF)
+
+
+def weight_sum(parts, place):
+    half = parts[0].shape[0] // 2
+    return pl.pallas_call(
+        weight_sum_kernel,
+        out_shape=(jax.ShapeDtypeStruct((half, DH), F32), jax.ShapeDtypeStruct((half, DH), BF)),
+        in_specs=[SMEM_SPEC] + [VMEM_SPEC] * 4,
+        out_specs=(VMEM_SPEC, VMEM_SPEC),
+        compiler_params=params(),
+        cost_estimate=cost(8 * half * DH, 4 * 2**20),
+        name="weight_sum",
+    )(place, *parts)
 
 
 def exchange(tensor, axes):
@@ -353,8 +416,16 @@
     return lax.ppermute(tensor, "c", [(0, 1), (1, 0)])
 
 
-def dp_shift(step, dx, dz):
-    return [(x * dz + z, (x + step // dz) % dx * dz + (z + step % dz) % dz) for x in range(dx) for z in range(dz)]
+def together(*values):
+    return lax.optimization_barrier(values)
+
+
+def other_z(tensor):
+    return lax.ppermute(tensor, "zl", [(0, 1), (1, 0)])
+
+
+def along_x(tensor, step):
+    return lax.ppermute(tensor, "x", [(i, (i + step) % 4) for i in range(4)])
 
 
 def shards(queries, keys, values, out_proj, out_grad, block_pattern, col_offset):
@@ -364,46 +435,54 @@
     seq = ROWS
     chips = seq // 2
     dp = lax.axis_size("x") * lax.axis_size("zl")
-    core_index = lax.axis_index("c")
-    core = core_index.astype(jnp.int32).reshape(1)
-
-    halves = out_proj.reshape(rows_of, 2, DH).transpose(1, 0, 2)
-    spread = jnp.broadcast_to(halves[None], (chips, 2, rows_of, DH)).reshape(seq, rows_of, DH)
-    own_rows = exchange(spread, SEQ).reshape(seq * rows_of, DH)
-    mine = lax.all_gather(own_rows, DP, axis=0, tiled=True)
+    core, at_x, at_z = (lax.axis_index(name).astype(jnp.int32) for name in ("c", "x", "zl"))
+    place = jnp.stack([core, at_x, at_z])
+
+    z_proj = other_z(out_proj)
+    first = at_z == 0
+    pair = jnp.stack([jnp.where(first, out_proj, z_proj), jnp.where(first, z_proj, out_proj)])
+    halves = pair.reshape(2 * rows_of, 2, DH).transpose(1, 0, 2)
+    spread = jnp.broadcast_to(halves[None], (chips, 2, 2 * rows_of, DH)).reshape(seq, 2 * rows_of, DH)
+    own_rows = exchange(spread, SEQ)
+    packed = pack(q, k, v, col_offset)
+    own_rows, packed = together(own_rows, packed)
+    own_rows = own_rows.reshape(seq, 2, rows_of, DH).transpose(1, 0, 2, 3).reshape(2 * seq * rows_of, DH)
+    mine = lax.all_gather(own_rows, "x", axis=0, tiled=True)
     theirs = other_core(mine)
 
-    packed = pack(q, k, v, col_offset)
     received = exchange(packed.reshape(seq, COLS // seq, 3 * HALF), SEQ)
-    received = received.reshape(ROWS, 2, GRP, 3 * HALF)
-
-    og_sent = lax.dynamic_slice(og, (0, (1 - core_index) * DH), (COLS, DH))
+    og_sent = lax.dynamic_slice(og, (0, (1 - core) * DH), (COLS, DH))
     og_theirs = other_core(og_sent)
     row_out = row_forward(q, k, v, block_pattern)
     row_theirs = other_core(row_out)
-
-    col_sent = column_forward(received).reshape(seq, COLS // seq, HALF)
-    col_out = exchange(col_sent, SEQ).reshape(COLS, HALF)
-    col_theirs = other_core(col_out)
-
-    grads = attn_grad_of(og, mine, theirs, core)
-    col_grads = exchange(grads[:, HALF:].reshape(seq, COLS // seq, HALF), SEQ)
-    col_grads = col_grads.reshape(ROWS, 2, GRP, HALF)
-
-    weight_part = weight_grad_of(row_out, row_theirs, col_out, col_theirs, og, og_theirs, core)
-    weight_dp = exchange(weight_part.reshape(dp, 2 * HALF // dp, DH), DP)
-    weight_dp = jnp.sum(weight_dp.astype(F32), axis=0).astype(BF)
-    weight_seq = exchange(weight_dp.reshape(seq, rows_of, DH), SEQ)
-    weight_sum = jnp.sum(weight_seq.astype(F32).reshape(chips, 2, rows_of, DH), axis=0)
+    grad_rows, send = attn_grad_of(og, mine, theirs, place)
+    received, row_out, row_theirs, og_theirs, send = together(received, row_out, row_theirs, og_theirs, send)
+    received = received.reshape(ROWS, 2, GRP, 3 * HALF)
+
+    send = column_forward(received, send.reshape(ROWS, 2, GRP, 2 * HALF))
+    mixed = exchange(send.reshape(seq, COLS // seq, 2 * HALF), SEQ)
+    dq, dk, dv = row_backward(q, k, v, grad_rows, block_pattern)
+    mixed, dq, dk, dv = together(mixed, dq, dk, dv)
+
+    col_mine = mixed.reshape(COLS, 2 * HALF)
+    col_theirs = other_core(col_mine)
+    col_back = column_backward(received, mixed.reshape(ROWS, 2, GRP, 2 * HALF)).reshape(seq, COLS // seq, 3 * HALF)
+    col_back, col_mine, col_theirs = together(col_back, col_mine, col_theirs)
+    back = exchange(col_back, SEQ).reshape(COLS, 3 * HALF)
+
+    parts = weight_grad_of(row_out, row_theirs, col_mine, col_theirs, og, og_theirs, place)
+    parts = [parts[0]] + [along_x(parts[step], step) for step in (1, 2, 3)]
+    keep, give = weight_sum(parts, place)
+    weight_part = (keep + other_z(give).astype(F32)).astype(BF).reshape(seq, rows_of, DH)
+    weight_part, back = together(weight_part, back)
+    weight_seq = exchange(weight_part, SEQ)
+    weight_total = jnp.sum(weight_seq.astype(F32).reshape(chips, 2, rows_of, DH), axis=0)
     tokens = COLS * seq * dp
-    w_grad = weight_sum.transpose(1, 0, 2).reshape(rows_of, D) * tokens ** (-0.5)
-
-    dq, dk, dv = row_backward(q, k, v, grads, block_pattern)
-    col_back = column_backward(received, col_grads).reshape(seq, COLS // seq, 3 * HALF)
-    back = exchange(col_back, SEQ).reshape(COLS, 3 * HALF)
+    w_grad = weight_total.transpose(1, 0, 2).reshape(rows_of, D) * tokens ** (-0.5)
+
     dq, dk, dv = finish(back, dq, dk, dv, col_offset)
 
-    layer = layer_out_of(row_out, col_out, mine, theirs, core)
+    layer = layer_out_of(row_out, col_mine, mine, theirs, place)
     lead = (1, 1, COLS)
     return (
         layer.reshape(lead + (D,)),

time: 257 us -> 220 us (0.86)
  waiting for transfers between devices: 137 us -> 89.8 us
  starting transfers between devices: 43.6 us -> 48.7 us
  Pallas kernels: 41.3 us -> 44.2 us
  local copies, waits for them, and re-layouts: 17.1 us -> 20 us
    all_to_all x7 -> x5, waiting for transfers between devices: 131 us -> 32.1 us  [exchange(): return lax.all_to_all(tensor, axes, split_axis=0, concat_axis=0, tiled=True)]
    ppermute x0 -> x5, waiting for transfers between devices: none -> 33.2 us  [the longest x3 22.4 us: along_x(): return lax.ppermute(tensor, 'x', [(i, (i + step) % 4) for i in range(4)])]
    all_gather x1, waiting for transfers between devices: 0.02 us -> 24.5 us  [shards(): mine = lax.all_gather(own_rows, 'x', axis=0, tiled=True)]
    ppermute x0 -> x5, starting transfers between devices: none -> 6.51 us  [the longest x3 3.71 us: along_x(): return lax.ppermute(tensor, 'x', [(i, (i + step) % 4) for i in range(4)])]
    ppermute x4, waiting for transfers between devices: 5.75 us -> 0.01 us  [other_core(): return lax.ppermute(tensor, 'c', [(0, 1), (1, 0)])]
    unnamed x36, local copies, waits for them, and re-layouts: 10.7 us -> 14.3 us
    pallas_call x2 -> x3, Pallas kernels: 7.15 us -> 9.92 us  [the longest x1 7.47 us: column_backward(): pl.pallas_call(column_backward_kernel, grid=(1,), out_shape=jax.ShapeDtyp...]
    all_to_all x7 -> x5, starting transfers between devices: 40.8 us -> 39 us  [exchange(): return lax.all_to_all(tensor, axes, split_axis=0, concat_axis=0, tiled=True)]
  transfers between devices with their start and end apart: 12 -> 15, of which waited for: 9 -> 9; matrix products, arithmetic and copies ran while one was open for 3% -> 2% of each run, Pallas kernels for 15% -> 19%
where the time goes in v2:
time: 220 us; the launch traced here: 219 us
  waiting for transfers between devices  89.8 us (41%)
  starting transfers between devices  48.7 us (22%)
  Pallas kernels  44.2 us (20%)
  local copies, waits for them, and re-layouts  20 us (9%)
  between operations  14.2 us (6%)
    all_to_all x5, starting transfers between devices, exchange(): return lax.all_to_all(tensor, axes, split_axis=0, concat_axis=0, tiled=True)  39 us
    all_to_all x5, waiting for transfers between devices, exchange(): return lax.all_to_all(tensor, axes, split_axis=0, concat_axis=0, tiled=True)  32.1 us
    all_gather x1, waiting for transfers between devices, shards(): mine = lax.all_gather(own_rows, 'x', axis=0, tiled=True)  24.5 us
    ppermute x3, waiting for transfers between devices, along_x(): return lax.ppermute(tensor, 'x', [(i, (i + step) % 4) for i in range(4)])  22.4 us
    unnamed x36, local copies, waits for them, and re-layouts  14.3 us
    ppermute x2, waiting for transfers between devices, other_z(): return lax.ppermute(tensor, 'zl', [(0, 1), (1, 0)])  10.8 us
    pallas_call x1, Pallas kernels, row_backward(): pl.pallas_call(row_backward_kernel, grid=(1,), out_shape=(whole, whole, w...  9.13 us
    pallas_call x1, Pallas kernels, column_backward(): pl.pallas_call(column_backward_kernel, grid=(1,), out_shape=jax.ShapeDtyp...  7.47 us
  transfers between devices with their start and end apart: 15, of which 9 were waited for; matrix products, arithmetic and copies ran while one was open for 2% of the time, Pallas kernels for 19%

profile of v2, /device:TPU:1, one launch (start us, length us, event | category | flops | bytes accessed | tf_op | source)
XLA Modules:
  0.0 218.6 jit_solution(2492038261681247630)
XLA Ops:
  7.2 2.6 %collective-permute-start = (bf16[4,2048]{1,0:T(4,128)(2,1)}, bf16[4,2048]{1,0:T(4,128)(2,1)S(1)}, u32[]{:S(2)}, u32[]{:S(2)}) collective-permute-start(bf16[4,2048]{1,0:T(4,128)(2,1)} %param.10), channel_id=1, source_target_pairs={{0,32},{32,0},{1,33},{33,1},{2,34},{34,2},{3,35},{35,3},{4,36},{36... | collective-permute-start | bytes 49160 | tf_op jit(solution)/shard_map/ppermute | solution.py:424
  9.7 1.3 collective-permute-done
  12.7 12.9 %all-to-all-start = ((bf16[32,8,1024]{2,1,0:T(8,128)(2,1)}), bf16[32,8,1024]{2,1,0:T(8,128)(2,1)S(1)}, u32[]{:S(2)}, u32[]{:S(2)}) async-start(bf16[32,8,1024]{2,1,0:T(8,128)(2,1)} %bitcast.6), calls=%async_computation | async-start | bytes 1048576 | tf_op jit(solution)/shard_map/all_to_all | solution.py:412
  26.9 1.2 copy-done.6
  28.8 2.4 %pack.1 = bf16[512,1536]{1,0:T(8,128)(2,1)} custom-call(s32[4]{0:T(128)S(1)} %copy-done.16, bf16[512,1024]{1,0:T(8,128)(2,1)S(1)} %bitcast.40, bf16[512,1024]{1,0:T(8,128)(2,1)S(1)} %bitcast.43, bf16[512,1024]{1,0:T(8,128)(2,1)S(1)} %bitcast.46), custom_call_target="tpu_custom_call" | custom-call | flops 536870912 | bytes 3145728 | tf_op jit(solution)/shard_map/pack/pallas_call | solution.py:76
  31.3 12.3 %all-to-all-done = bf16[32,8,1024]{2,1,0:T(8,128)(2,1)S(1)} async-done(((bf16[32,8,1024]{2,1,0:T(8,128)(2,1)}), bf16[32,8,1024]{2,1,0:T(8,128)(2,1)S(1)}, u32[]{:S(2)}, u32[]{:S(2)}) %all-to-all-start) | async-done | bytes 524320 | tf_op jit(solution)/shard_map/all_to_all | solution.py:412
  45.2 5.1 %all-to-all-start.1 = ((bf16[32,16,1536]{2,1,0:T(8,128)(2,1)}), bf16[32,16,1536]{2,1,0:T(8,128)(2,1)S(1)}, u32[]{:S(2)}, u32[]{:S(2)}) async-start(bf16[32,16,1536]{2,1,0:T(8,128)(2,1)} %bitcast.52), calls=%async_computation.1 | async-start | bytes 3145728 | tf_op jit(solution)/shard_map/all_to_all | solution.py:412
  50.3 24.5 %all-gather.2.cloned.1.call-done.mine_ref = bf16[1024,1024]{1,0:T(8,128)(2,1)} async-done(((bf16[256,1024]{1,0:T(8,128)(2,1)}), bf16[1024,1024]{1,0:T(8,128)(2,1)}) %all-gather.2.cloned.1.call-update) | async-done | bytes 2097168 | tf_op jit(solution)/shard_map/all_gather | solution.py:450
  75.4 2.4 %dynamic-slice_bitcast_fusion = bf16[512,1024]{1,0:T(8,128)(2,1)} fusion(bf16[1,1,512,2048]{3,2,1,0:T(8,128)(2,1)} %param.11, s32[]{:T(128)S(6)} %select_n.18), kind=kLoop, calls=%fused_computation | loop fusion | bytes 2097156 | tf_op jit(solution)/shard_map/dynamic_slice | solution.py:454
  77.9 2.1 row_forward.1.row_ref.row_mine
  80.7 1.6 copy-done.1
  82.3 5.5 %attn_grad.1 = (bf16[512,512]{1,0:T(8,128)(2,1)S(1)}, bf16[512,1024]{1,0:T(8,128)(2,1)S(1)}) custom-call(s32[3]{0:T(128)S(1)} %pad_add_fusion.place.core_ref, bf16[512,2048]{1,0:T(8,128)(2,1)S(1)} %bitcast.38, bf16[512,2048]{1,0:T(8,128)(2,1)S(1)} %bitcast.39, bf16[1024,1024]{1,0:T(8,128)(2,1)} %all-gather.2.cloned.1.call-done.mine_ref, ...), custom_call_target="tpu_custom_call" | custom-call | flops 2147483648 | bytes 7340032 | tf_op jit(solution)/shard_map/attn_grad/pallas_call | solution.py:278
  89.6 1.5 all-to-all-done.1
  91.0 1.8 copy-done.10
  92.8 1.7 column_forward.1
  95.5 8.4 %all-to-all-start.2 = ((bf16[32,16,1024]{2,1,0:T(8,128)(2,1)}), bf16[32,16,1024]{2,1,0:T(8,128)(2,1)}, u32[]{:S(2)}, u32[]{:S(2)}) async-start(bf16[32,16,1024]{2,1,0:T(8,128)(2,1)} %bitcast.51), calls=%async_computation.2 | async-start | bytes 2097152 | tf_op jit(solution)/shard_map/all_to_all | solution.py:412
  105.1 1.2 copy-done.8
  107.4 9.1 %row_backward.1 = (bf16[512,1024]{1,0:T(8,128)(2,1)}, bf16[512,1024]{1,0:T(8,128)(2,1)}, bf16[512,1024]{1,0:T(8,128)(2,1)}) custom-call(s32[4,4]{1,0:T(4,128)S(1)} %copy-done.15, bf16[512,1024]{1,0:T(8,128)(2,1)S(1)} %bitcast.42, bf16[512,1024]{1,0:T(8,128)(2,1)S(1)} %bitcast.45, bf16[512,1024]{1,0:T(8,128)(2,1)S(1)} %bitcast.48, bf16[512,512]{1,0:T(8,128)(2,1)S(1)} %copy-done.14), custom_call_target="tpu_custom_call" | custom-call | flops 671088640 | bytes 3670016 | tf_op jit(solution)/shard_map/row_backward/pallas_call | solution.py:224
  116.5 15.9 %all-to-all-done.2 = bf16[32,16,1024]{2,1,0:T(8,128)(2,1)} async-done(((bf16[32,16,1024]{2,1,0:T(8,128)(2,1)}), bf16[32,16,1024]{2,1,0:T(8,128)(2,1)}, u32[]{:S(2)}, u32[]{:S(2)}) %all-to-all-start.2) | async-done | bytes 1048608 | tf_op jit(solution)/shard_map/all_to_all | solution.py:412
  132.4 1.9 collective-permute-start.4
  134.3 7.5 %column_backward.1 = bf16[32,2,8,1536]{3,2,1,0:T(8,128)(2,1)} custom-call(bf16[32,2,8,1536]{3,2,1,0:T(8,128)(2,1)} %bitcast.36, bf16[32,2,8,1024]{3,2,1,0:T(8,128)(2,1)} %bitcast.18.g_ref), custom_call_target="tpu_custom_call" | custom-call | flops 671088640 | bytes 3670016 | tf_op jit(solution)/shard_map/column_backward/pallas_call | solution.py:155
  141.8 4.2 %all-to-all-start.3 = ((bf16[32,16,1536]{2,1,0:T(8,128)(2,1)}), bf16[32,16,1536]{2,1,0:T(8,128)(2,1)S(1)}, u32[]{:S(2)}, u32[]{:S(2)}) async-start(bf16[32,16,1536]{2,1,0:T(8,128)(2,1)} %bitcast.19), calls=%async_computation.3 | async-start | bytes 3145728 | tf_op jit(solution)/shard_map/all_to_all | solution.py:412
  146.0 6.0 %weight_grad.1 = (f32[256,1024]{1,0:T(8,128)S(1)}, bf16[256,1024]{1,0:T(8,128)(2,1)S(1)}, bf16[256,1024]{1,0:T(8,128)(2,1)S(1)}, bf16[256,1024]{1,0:T(8,128)(2,1)S(1)}) custom-call(s32[3]{0:T(128)S(1)} %pad_add_fusion.place.core_ref, bf16[512,512]{1,0:T(8,128)(2,1)S(1)} %row_forward.1.row_ref.row_mine, bf16[512,512]{1,0:T(8,128)(2,1)} %collective-permute-done.1.row_theirs, ...), custom_call_target="tpu_custom_call" | custom-call | flops 2147483648 | bytes 7340032 | tf_op jit(solution)/shard_map/weight_grad/pallas_call | solution.py:364
  152.5 1.5 collective-permute-start.6
  154.0 1.8 collective-permute-start.7
  155.8 22.1 %collective-permute-done.5.b_ref = bf16[256,1024]{1,0:T(8,128)(2,1)S(1)} collective-permute-done((bf16[256,1024]{1,0:T(8,128)(2,1)S(1)}, bf16[256,1024]{1,0:T(8,128)(2,1)S(1)}, u32[]{:S(2)}, u32[]{:S(2)}) %collective-permute-start.5) | collective-permute-done | bytes 524320 | tf_op jit(solution)/shard_map/ppermute | solution.py:428
  179.2 9.4 %collective-permute-done.8 = bf16[128,1024]{1,0:T(8,128)(2,1)S(1)} collective-permute-done((bf16[128,1024]{1,0:T(8,128)(2,1)S(1)}, bf16[128,1024]{1,0:T(8,128)(2,1)S(1)}, u32[]{:S(2)}, u32[]{:S(2)}) %collective-permute-start.8) | collective-permute-done | bytes 262176 | tf_op jit(solution)/shard_map/ppermute | solution.py:424
  189.5 8.4 %all-to-all-start.4 = ((bf16[32,4,1024]{2,1,0:T(4,128)(2,1)}), bf16[32,4,1024]{2,1,0:T(4,128)(2,1)S(1)}, u32[]{:S(2)}, u32[]{:S(2)}) async-start(bf16[32,4,1024]{2,1,0:T(4,128)(2,1)} %reshape.100), calls=%async_computation.4 | async-start | bytes 524288 | tf_op jit(solution)/shard_map/all_to_all | solution.py:412
  197.9 1.6 copy-done.12
  199.5 6.4 %layer_out.1 = bf16[512,2048]{1,0:T(8,128)(2,1)} custom-call(s32[3]{0:T(128)S(1)} %pad_add_fusion.place.core_ref, bf16[512,512]{1,0:T(8,128)(2,1)S(1)} %row_forward.1.row_ref.row_mine, bf16[512,1024]{1,0:T(8,128)(2,1)} %bitcast.20.col_ref.col_mine, bf16[1024,1024]{1,0:T(8,128)(2,1)S(1)} %copy-done.12, bf16[1024,1024]{1,0:T(8,128)(2,1)} %collective-permute-done.3.theirs_ref), custom_call_target="tpu_custom_call" | custom-call | flops 2147483648 | bytes 7340032 | tf_op jit(solution)/shard_map/layer_out/pallas_call | solution.py:318
  205.9 2.6 %finish.1 = (bf16[512,1024]{1,0:T(8,128)(2,1)}, bf16[512,1024]{1,0:T(8,128)(2,1)}, bf16[512,1024]{1,0:T(8,128)(2,1)}) custom-call(s32[4]{0:T(128)S(1)} %copy-done.17, bf16[512,1536]{1,0:T(8,128)(2,1)S(1)} %bitcast.49, bf16[512,1024]{1,0:T(8,128)(2,1)} %get-tuple-element.58.dq_in, ...), custom_call_target="tpu_custom_call", output_to_operand_aliasing={{0}: (2, {}), {1}: (3, {}), {2}: (4, {})} | custom-call | flops 536870912 | bytes 3145728 | tf_op jit(solution)/shard_map/finish/pallas_call | solution.py:250
  208.5 2.5 %all-to-all-done.4 = bf16[32,4,1024]{2,1,0:T(4,128)(2,1)S(1)} async-done(((bf16[32,4,1024]{2,1,0:T(4,128)(2,1)}), bf16[32,4,1024]{2,1,0:T(4,128)(2,1)S(1)}, u32[]{:S(2)}, u32[]{:S(2)}) %all-to-all-start.4) | async-done | bytes 262176 | tf_op jit(solution)/shard_map/all_to_all | solution.py:412
  (59 shorter events, 15.0 us)
Async XLA Ops:
  7.2 18.5 %copy-start.2 = (bf16[1,1,512,1024]{3,2,1,0:T(8,128)(2,1)S(1)}, bf16[1,1,512,1024]{3,2,1,0:T(8,128)(2,1)}, u32[]{:S(2)}) copy-start(bf16[1,1,512,1024]{3,2,1,0:T(8,128)(2,1)} %param.7) | copy-start | bytes 3145732
  7.2 3.9 %collective-permute-start = (bf16[4,2048]{1,0:T(4,128)(2,1)}, bf16[4,2048]{1,0:T(4,128)(2,1)S(1)}, u32[]{:S(2)}, u32[]{:S(2)}) collective-permute-start(bf16[4,2048]{1,0:T(4,128)(2,1)} %param.10), channel_id=1, source_target_pairs={{0,32},{32,0},{1,33},{33,1},{2,34},{34,2},{3,35},{35,3},{4,36},{36... | collective-permute-start | bytes 49160 | tf_op jit(solution)/shard_map/ppermute | solution.py:424
  12.7 30.8 %all-to-all-start = ((bf16[32,8,1024]{2,1,0:T(8,128)(2,1)}), bf16[32,8,1024]{2,1,0:T(8,128)(2,1)S(1)}, u32[]{:S(2)}, u32[]{:S(2)}) async-start(bf16[32,8,1024]{2,1,0:T(8,128)(2,1)} %bitcast.6), calls=%async_computation | async-start | bytes 1048576 | tf_op jit(solution)/shard_map/all_to_all | solution.py:412
  25.7 49.1 %all-gather.2.cloned.1.call-start = ((), (), s32[]{:S(2)}) async-start(), calls=%async_computation.5 | async-start | bytes 2621440 | tf_op jit(solution)/shard_map/all_gather | solution.py:450
  25.7 1.2 copy-start.3
  26.9 1.2 copy-start.6
  45.2 32.7 %copy-start.15 = (s32[4,4]{1,0:T(4,128)S(1)}, s32[4,4]{1,0:T(4,128)}, u32[]{:S(2)}) copy-start(s32[4,4]{1,0:T(4,128)} %pat_ref.3) | copy-start | bytes 196
  45.2 45.8 %all-to-all-start.1 = ((bf16[32,16,1536]{2,1,0:T(8,128)(2,1)}), bf16[32,16,1536]{2,1,0:T(8,128)(2,1)S(1)}, u32[]{:S(2)}, u32[]{:S(2)}) async-start(bf16[32,16,1536]{2,1,0:T(8,128)(2,1)} %bitcast.52), calls=%async_computation.1 | async-start | bytes 3145728 | tf_op jit(solution)/shard_map/all_to_all | solution.py:412
  74.8 5.9 %collective-permute-start.3 = (bf16[1024,1024]{1,0:T(8,128)(2,1)}, bf16[1024,1024]{1,0:T(8,128)(2,1)}, u32[]{:S(2)}, u32[]{:S(2)}) collective-permute-start(bf16[1024,1024]{1,0:T(8,128)(2,1)} %all-gather.2.cloned.1.call-done.mine_ref), channel_id=1, source_target_pairs={{0,1},{1,0},{2,3},{3,2},{4,5},{5,4},{6,7},{7,6},{8,9},{9,8},{10,11... | collective-permute-start | bytes 6291464 | tf_op jit(solution)/shard_map/ppermute | solution.py:416
  75.4 2.4 %copy-start.4 = (bf16[1,1,512,1024]{3,2,1,0:T(8,128)(2,1)S(1)}, bf16[1,1,512,1024]{3,2,1,0:T(8,128)(2,1)}, u32[]{:S(2)}) copy-start(bf16[1,1,512,1024]{3,2,1,0:T(8,128)(2,1)} %param.8) | copy-start | bytes 3145732
  75.4 2.4 %copy-start.7 = (bf16[1,1,512,1024]{3,2,1,0:T(8,128)(2,1)S(1)}, bf16[1,1,512,1024]{3,2,1,0:T(8,128)(2,1)}, u32[]{:S(2)}) copy-start(bf16[1,1,512,1024]{3,2,1,0:T(8,128)(2,1)} %param.9) | copy-start | bytes 3145732
  77.8 11.7 %collective-permute-start.2 = (bf16[512,1024]{1,0:T(8,128)(2,1)}, bf16[512,1024]{1,0:T(8,128)(2,1)}, u32[]{:S(2)}, u32[]{:S(2)}) collective-permute-start(bf16[512,1024]{1,0:T(8,128)(2,1)} %dynamic-slice_bitcast_fusion), channel_id=1, source_target_pairs={{0,1},{1,0},{2,3},{3,2},{4,5},{5,4},{6,7},{7,6},{8,9},{9,8},{10,11... | collective-permute-start | bytes 3145736 | tf_op jit(solution)/shard_map/ppermute | solution.py:416
  80.0 9.6 %collective-permute-start.1 = (bf16[512,512]{1,0:T(8,128)(2,1)S(1)}, bf16[512,512]{1,0:T(8,128)(2,1)}, u32[]{:S(2)}, u32[]{:S(2)}) collective-permute-start(bf16[512,512]{1,0:T(8,128)(2,1)S(1)} %row_forward.1.row_ref.row_mine), channel_id=1, source_target_pairs={{0,1},{1,0},{2,3},{3,2},{4,5},{5,4},{6,7},{7,6},{8,9},{9,8},{10,11... | collective-permute-start | bytes 1572872 | tf_op jit(solution)/shard_map/ppermute | solution.py:416
  80.7 1.6 copy-start.1
  87.8 1.0 copy-start.9
  88.8 0.8 copy-start.13
  91.0 4.5 %copy-start = (bf16[32,16,1536]{2,1,0:T(8,128)(2,1)}, bf16[32,16,1536]{2,1,0:T(8,128)(2,1)S(1)}, u32[]{:S(2)}) copy-start(bf16[32,16,1536]{2,1,0:T(8,128)(2,1)S(1)} %all-to-all-done.1) | copy-start | bytes 4718596
  91.0 1.8 copy-start.10
  94.5 1.0 copy-start.11
  95.5 36.9 %all-to-all-start.2 = ((bf16[32,16,1024]{2,1,0:T(8,128)(2,1)}), bf16[32,16,1024]{2,1,0:T(8,128)(2,1)}, u32[]{:S(2)}, u32[]{:S(2)}) async-start(bf16[32,16,1024]{2,1,0:T(8,128)(2,1)} %bitcast.51), calls=%async_computation.2 | async-start | bytes 2097152 | tf_op jit(solution)/shard_map/all_to_all | solution.py:412
  103.9 1.2 copy-start.5
  105.1 1.2 copy-start.8
  106.3 1.0 copy-start.14
  132.4 9.4 %collective-permute-start.4 = (bf16[512,1024]{1,0:T(8,128)(2,1)}, bf16[512,1024]{1,0:T(8,128)(2,1)}, u32[]{:S(2)}, u32[]{:S(2)}) collective-permute-start(bf16[512,1024]{1,0:T(8,128)(2,1)} %bitcast.20.col_ref.col_mine), channel_id=1, source_target_pairs={{0,1},{1,0},{2,3},{3,2},{4,5},{5,4},{6,7},{7,6},{8,9},{9,8},{10,11... | collective-permute-start | bytes 3145736 | tf_op jit(solution)/shard_map/ppermute | solution.py:416
  141.8 47.7 %all-to-all-start.3 = ((bf16[32,16,1536]{2,1,0:T(8,128)(2,1)}), bf16[32,16,1536]{2,1,0:T(8,128)(2,1)S(1)}, u32[]{:S(2)}, u32[]{:S(2)}) async-start(bf16[32,16,1536]{2,1,0:T(8,128)(2,1)} %bitcast.19), calls=%async_computation.3 | async-start | bytes 3145728 | tf_op jit(solution)/shard_map/all_to_all | solution.py:412
  152.1 25.8 %collective-permute-start.5 = (bf16[256,1024]{1,0:T(8,128)(2,1)S(1)}, bf16[256,1024]{1,0:T(8,128)(2,1)S(1)}, u32[]{:S(2)}, u32[]{:S(2)}) collective-permute-start(bf16[256,1024]{1,0:T(8,128)(2,1)S(1)} %get-tuple-element.51), channel_id=1, source_target_pairs={{0,64},{64,128},{128,192},{192,0},{1,65},{65,129},{129,193},{193,1... | collective-permute-start | bytes 1572872 | tf_op jit(solution)/shard_map/ppermute | solution.py:428
  152.5 25.3 %collective-permute-start.6 = (bf16[256,1024]{1,0:T(8,128)(2,1)S(1)}, bf16[256,1024]{1,0:T(8,128)(2,1)S(1)}, u32[]{:S(2)}, u32[]{:S(2)}) collective-permute-start(bf16[256,1024]{1,0:T(8,128)(2,1)S(1)} %get-tuple-element.52), channel_id=1, source_target_pairs={{0,128},{64,192},{128,0},{192,64},{1,129},{65,193},{129,1},{193,65... | collective-permute-start | bytes 1572872 | tf_op jit(solution)/shard_map/ppermute | solution.py:428
  154.0 24.2 %collective-permute-start.7 = (bf16[256,1024]{1,0:T(8,128)(2,1)S(1)}, bf16[256,1024]{1,0:T(8,128)(2,1)S(1)}, u32[]{:S(2)}, u32[]{:S(2)}) collective-permute-start(bf16[256,1024]{1,0:T(8,128)(2,1)S(1)} %get-tuple-element.53), channel_id=1, source_target_pairs={{0,192},{64,0},{128,64},{192,128},{1,193},{65,1},{129,65},{193,129... | collective-permute-start | bytes 1572872 | tf_op jit(solution)/shard_map/ppermute | solution.py:428
  178.9 9.7 %collective-permute-start.8 = (bf16[128,1024]{1,0:T(8,128)(2,1)S(1)}, bf16[128,1024]{1,0:T(8,128)(2,1)S(1)}, u32[]{:S(2)}, u32[]{:S(2)}) collective-permute-start(bf16[128,1024]{1,0:T(8,128)(2,1)S(1)} %get-tuple-element.55), channel_id=1, source_target_pairs={{0,32},{32,0},{1,33},{33,1},{2,34},{34,2},{3,35},{35,3},{4,36},{36... | collective-permute-start | bytes 786440 | tf_op jit(solution)/shard_map/ppermute | solution.py:424
  189.5 21.5 %all-to-all-start.4 = ((bf16[32,4,1024]{2,1,0:T(4,128)(2,1)}), bf16[32,4,1024]{2,1,0:T(4,128)(2,1)S(1)}, u32[]{:S(2)}, u32[]{:S(2)}) async-start(bf16[32,4,1024]{2,1,0:T(4,128)(2,1)} %reshape.100), calls=%async_computation.4 | async-start | bytes 524288 | tf_op jit(solution)/shard_map/all_to_all | solution.py:412
  197.9 1.6 copy-start.12
  199.5 6.4 %copy-start.17 = (s32[4]{0:T(128)S(1)}, s32[4]{0:T(128)}, u32[]{:S(2)}) copy-start(s32[4]{0:T(128)} %off_ref.3) | copy-start | bytes 52
  (1 other events, 0.7 us)
Sparse Core Ops, SparseCore 0:
  45.3 29.3 all-gather.1

commit v3 on v2

--- a/solution.py
+++ b/solution.py
@@ -24,6 +24,7 @@
 
 DP = ("x", "zl")
 SEQ = ("y", "zh", "c")
+NEAR = ("zl", "zh", "c")
 
 
 def mm(a, b):
@@ -85,13 +86,13 @@
     )(offset, q, k, v)
 
 
-def tile_of(ref, group, lane):
-    tile = ref[:, group, :, lane * HD : (lane + 1) * HD]
+def tile_of(ref, lane):
+    tile = ref[:, 0, :, lane * HD : (lane + 1) * HD]
     return tile.astype(F32).reshape(TILE, HD).astype(BF)
 
 
-def store_tile(ref, group, lane, value):
-    ref[:, group, :, lane * HD : (lane + 1) * HD] = value.reshape(ROWS, GRP, HD).astype(BF)
+def store_tile(ref, lane, value):
+    ref[:, 0, :, lane * HD : (lane + 1) * HD] = value.reshape(ROWS, GRP, HD).astype(BF)
 
 
 def column_mask():
@@ -105,66 +106,62 @@
     return e / jnp.sum(e, axis=-1, keepdims=True)
 
 
-def column_probs(r_ref, group, h, mask):
-    q = tile_of(r_ref, group, h)
-    k = tile_of(r_ref, group, HC + h)
-    v = tile_of(r_ref, group, 2 * HC + h)
+def column_probs(r_ref, h, mask):
+    q = tile_of(r_ref, h)
+    k = tile_of(r_ref, HC + h)
+    v = tile_of(r_ref, 2 * HC + h)
     return q, k, v, softmax(jnp.where(mask, mm_t(q, k) * SCALE, -1e30))
 
 
-def column_forward_kernel(r_ref, kept_ref, o_ref):
+def column_forward_kernel(r_ref, g_ref, o_ref):
     mask = column_mask()
-    for group in range(2):
-        for h in range(HC):
-            _, _, v, probs = column_probs(r_ref, group, h, mask)
-            store_tile(o_ref, group, h, mm(probs.astype(BF), v))
-
-
-def column_forward(received, send):
+    o_ref[:, :, :, HALF:] = g_ref[...]
+    for h in range(HC):
+        _, _, v, probs = column_probs(r_ref, h, mask)
+        store_tile(o_ref, h, mm(probs.astype(BF), v))
+
+
+def group_block(lanes, part=0):
+    return pl.BlockSpec((ROWS, 1, GRP, lanes), lambda i: (0, i, 0, part))
+
+
+def column_forward(received, grads):
     return pl.pallas_call(
         column_forward_kernel,
-        grid=(1,),
+        grid=(2,),
         out_shape=jax.ShapeDtypeStruct((ROWS, 2, GRP, 2 * HALF), BF),
-        in_specs=[
-            pl.BlockSpec((ROWS, 2, GRP, 3 * HALF), lambda i: (0, 0, 0, 0)),
-            pl.BlockSpec(memory_space=pl.ANY),
-        ],
-        out_specs=pl.BlockSpec((ROWS, 2, GRP, HALF), lambda i: (0, 0, 0, 0)),
-        input_output_aliases={1: 0},
+        in_specs=[group_block(3 * HALF), group_block(HALF)],
+        out_specs=group_block(2 * HALF),
         compiler_params=params(),
         cost_estimate=cost(8 * 4 * TILE * TILE * HD, 4 * COLS * HALF * 2, 8 * TILE * TILE),
         name="column_forward",
-    )(received, send)
+    )(received, grads)
 
 
 def column_backward_kernel(r_ref, g_ref, o_ref):
     mask = column_mask()
-    for group in range(2):
-        for h in range(HC):
-            q, k, v, probs = column_probs(r_ref, group, h, mask)
-            g = tile_of(g_ref, group, h)
-            store_tile(o_ref, group, 2 * HC + h, t_mm(probs.astype(BF), g))
-            prob_grad = mm_t(g, v)
-            delta = jnp.sum(probs * prob_grad, axis=-1, keepdims=True)
-            score_grad = (probs * (prob_grad - delta)).astype(BF)
-            store_tile(o_ref, group, h, mm(score_grad, k) * SCALE)
-            store_tile(o_ref, group, HC + h, t_mm(score_grad, q) * SCALE)
-
-
-def column_backward(received, grads):
+    for h in range(HC):
+        q, k, v, probs = column_probs(r_ref, h, mask)
+        g = tile_of(g_ref, h)
+        store_tile(o_ref, 2 * HC + h, t_mm(probs.astype(BF), g))
+        prob_grad = mm_t(g, v)
+        delta = jnp.sum(probs * prob_grad, axis=-1, keepdims=True)
+        score_grad = (probs * (prob_grad - delta)).astype(BF)
+        store_tile(o_ref, h, mm(score_grad, k) * SCALE)
+        store_tile(o_ref, HC + h, t_mm(score_grad, q) * SCALE)
+
+
+def column_backward(received, mixed):
     return pl.pallas_call(
         column_backward_kernel,
-        grid=(1,),
+        grid=(2,),
         out_shape=jax.ShapeDtypeStruct((ROWS, 2, GRP, 3 * HALF), BF),
-        in_specs=[
-            pl.BlockSpec((ROWS, 2, GRP, 3 * HALF), lambda i: (0, 0, 0, 0)),
-            pl.BlockSpec((ROWS, 2, GRP, HALF), lambda i: (0, 0, 0, 1)),
-        ],
-        out_specs=pl.BlockSpec((ROWS, 2, GRP, 3 * HALF), lambda i: (0, 0, 0, 0)),
+        in_specs=[group_block(3 * HALF), group_block(HALF, 1)],
+        out_specs=group_block(3 * HALF),
         compiler_params=params(),
         cost_estimate=cost(8 * 10 * TILE * TILE * HD, 7 * COLS * HALF * 2, 8 * TILE * TILE),
         name="column_backward",
-    )(received, grads)
+    )(received, mixed)
 
 
 def row_tile(pat_ref, q_ref, k_ref, v_ref, h, j):
@@ -260,8 +257,15 @@
     )(offset, back, dq, dk, dv)
 
 
+def pair_rows(ref, pair):
+    chunk = 2 * HD // 8
+    starts = [2 * HD * pair + (2 * at_y + at_z) * chunk for at_z in range(2) for at_y in range(4)]
+    return jnp.concatenate([ref[start : start + chunk, :] for start in starts], axis=0)
+
+
 def attn_grad_kernel(place, og_mine, og_theirs, mine_ref, theirs_ref, row_ref, send_ref):
-    total = (mm_t(og_mine[...], mine_ref[...]) + mm_t(og_theirs[...], theirs_ref[...])).astype(BF)
+    total = mm_t(og_mine[...], pair_rows(mine_ref, 0)) + mm_t(og_theirs[...], pair_rows(theirs_ref, 0))
+    total = total.astype(BF)
 
     @pl.when(pl.program_id(0) < 2)
     def _():
@@ -288,10 +292,10 @@
             ],
             out_specs=(
                 pl.BlockSpec((COLS, rows), lambda i, at: (0, jnp.minimum(i, 1))),
-                pl.BlockSpec((COLS, rows), lambda i, at: (0, jnp.maximum(i, 2))),
+                pl.BlockSpec((COLS, rows), lambda i, at: (0, jnp.maximum(i, 2) - 2)),
             ),
         ),
-        out_shape=(jax.ShapeDtypeStruct((COLS, HALF), BF), jax.ShapeDtypeStruct((COLS, 2 * HALF), BF)),
+        out_shape=(jax.ShapeDtypeStruct((COLS, HALF), BF),) * 2,
         compiler_params=params(),
         cost_estimate=cost(2 * COLS * 2 * HALF * D, 7 * 2**20),
         name="attn_grad",
@@ -300,7 +304,9 @@
 
 def layer_out_kernel(core_ref, row_ref, col_ref, mine_ref, theirs_ref, o_ref):
     def product(w_ref):
-        total = mm(row_ref[...], w_ref[:HALF, :]) + mm(col_ref[...], w_ref[HALF:, :])
+        two = 2 * HD
+        total = mm(row_ref[:, :two], pair_rows(w_ref, 0)) + mm(row_ref[:, two:], pair_rows(w_ref, 1))
+        total += mm(col_ref[:, :two], pair_rows(w_ref, 2)) + mm(col_ref[:, two:], pair_rows(w_ref, 3))
         o_ref[...] = total.astype(BF)
 
     pl.when(pl.program_id(0) == 0)(lambda: product(mine_ref))
@@ -384,26 +390,26 @@
     )(place, row_mine, row_theirs, col_mine, col_theirs, og, og_theirs)
 
 
-def weight_sum_kernel(place, a_ref, b_ref, c_ref, d_ref, keep_ref, send_ref):
-    half = keep_ref.shape[0]
-
-    def total(index):
-        rows = pl.ds(pl.multiple_of(index * half, half), half)
-        return (a_ref[rows, :] + b_ref[rows, :].astype(F32)) + (c_ref[rows, :].astype(F32) + d_ref[rows, :].astype(F32))
-
-    keep_ref[...] = total(place[2])
-    send_ref[...] = total(1 - place[2]).astype(BF)
+def weight_sum_kernel(place, a_ref, b_ref, c_ref, d_ref, *outs):
+    chunk = 2 * HD // 8
+    for step, out in enumerate(outs):
+        at_y = lax.rem(place[3] + step, 4)
+        for at_z in range(2):
+            rows = pl.ds(pl.multiple_of(at_z * HD + at_y * chunk, chunk), chunk)
+            near = a_ref[rows, :] + b_ref[rows, :].astype(F32)
+            far = c_ref[rows, :].astype(F32) + d_ref[rows, :].astype(F32)
+            out[at_z * chunk : (at_z + 1) * chunk, :] = (near + far).astype(out.dtype)
 
 
 def weight_sum(parts, place):
-    half = parts[0].shape[0] // 2
+    rows = parts[0].shape[0] // 4
     return pl.pallas_call(
         weight_sum_kernel,
-        out_shape=(jax.ShapeDtypeStruct((half, DH), F32), jax.ShapeDtypeStruct((half, DH), BF)),
+        out_shape=(jax.ShapeDtypeStruct((rows, DH), F32),) + (jax.ShapeDtypeStruct((rows, DH), BF),) * 3,
         in_specs=[SMEM_SPEC] + [VMEM_SPEC] * 4,
-        out_specs=(VMEM_SPEC, VMEM_SPEC),
-        compiler_params=params(),
-        cost_estimate=cost(8 * half * DH, 4 * 2**20),
+        out_specs=(VMEM_SPEC,) * 4,
+        compiler_params=params(),
+        cost_estimate=cost(16 * rows * DH, 4 * 2**20),
         name="weight_sum",
     )(place, *parts)
 
@@ -420,12 +426,8 @@
     return lax.optimization_barrier(values)
 
 
-def other_z(tensor):
-    return lax.ppermute(tensor, "zl", [(0, 1), (1, 0)])
-
-
-def along_x(tensor, step):
-    return lax.ppermute(tensor, "x", [(i, (i + step) % 4) for i in range(4)])
+def along(tensor, axis, step):
+    return lax.ppermute(tensor, axis, [(i, (i + step) % 4) for i in range(4)])
 
 
 def shards(queries, keys, values, out_proj, out_grad, block_pattern, col_offset):
@@ -435,31 +437,26 @@
     seq = ROWS
     chips = seq // 2
     dp = lax.axis_size("x") * lax.axis_size("zl")
-    core, at_x, at_z = (lax.axis_index(name).astype(jnp.int32) for name in ("c", "x", "zl"))
-    place = jnp.stack([core, at_x, at_z])
-
-    z_proj = other_z(out_proj)
-    first = at_z == 0
-    pair = jnp.stack([jnp.where(first, out_proj, z_proj), jnp.where(first, z_proj, out_proj)])
-    halves = pair.reshape(2 * rows_of, 2, DH).transpose(1, 0, 2)
-    spread = jnp.broadcast_to(halves[None], (chips, 2, 2 * rows_of, DH)).reshape(seq, 2 * rows_of, DH)
-    own_rows = exchange(spread, SEQ)
+    core = lax.axis_index("c").astype(jnp.int32)
+    place = jnp.stack([core] + [lax.axis_index(name).astype(jnp.int32) for name in ("x", "zl", "y")])
+
+    halves = out_proj.reshape(rows_of, 2, DH).transpose(1, 0, 2)
+    spread = jnp.broadcast_to(halves[None], (chips // 2, 2, rows_of, DH)).reshape(chips, rows_of, DH)
+    own_rows = exchange(spread, NEAR)
     packed = pack(q, k, v, col_offset)
     own_rows, packed = together(own_rows, packed)
-    own_rows = own_rows.reshape(seq, 2, rows_of, DH).transpose(1, 0, 2, 3).reshape(2 * seq * rows_of, DH)
-    mine = lax.all_gather(own_rows, "x", axis=0, tiled=True)
-    theirs = other_core(mine)
+    mine = lax.all_gather(own_rows.reshape(chips * rows_of, DH), ("x", "y"), axis=0, tiled=True)
 
     received = exchange(packed.reshape(seq, COLS // seq, 3 * HALF), SEQ)
     og_sent = lax.dynamic_slice(og, (0, (1 - core) * DH), (COLS, DH))
-    og_theirs = other_core(og_sent)
     row_out = row_forward(q, k, v, block_pattern)
-    row_theirs = other_core(row_out)
-    grad_rows, send = attn_grad_of(og, mine, theirs, place)
-    received, row_out, row_theirs, og_theirs, send = together(received, row_out, row_theirs, og_theirs, send)
+    mine, row_out, og_sent = together(mine, row_out, og_sent)
+    theirs, row_theirs, og_theirs = other_core(mine), other_core(row_out), other_core(og_sent)
+    grad_rows, grad_cols = attn_grad_of(og, mine, theirs, place)
+    received, row_theirs, og_theirs, grad_cols = together(received, row_theirs, og_theirs, grad_cols)
     received = received.reshape(ROWS, 2, GRP, 3 * HALF)
 
-    send = column_forward(received, send.reshape(ROWS, 2, GRP, 2 * HALF))
+    send = column_forward(received, grad_cols.reshape(ROWS, 2, GRP, HALF))
     mixed = exchange(send.reshape(seq, COLS // seq, 2 * HALF), SEQ)
     dq, dk, dv = row_backward(q, k, v, grad_rows, block_pattern)
     mixed, dq, dk, dv = together(mixed, dq, dk, dv)
@@ -471,12 +468,15 @@
     back = exchange(col_back, SEQ).reshape(COLS, 3 * HALF)
 
     parts = weight_grad_of(row_out, row_theirs, col_mine, col_theirs, og, og_theirs, place)
-    parts = [parts[0]] + [along_x(parts[step], step) for step in (1, 2, 3)]
-    keep, give = weight_sum(parts, place)
-    weight_part = (keep + other_z(give).astype(F32)).astype(BF).reshape(seq, rows_of, DH)
-    weight_part, back = together(weight_part, back)
-    weight_seq = exchange(weight_part, SEQ)
-    weight_total = jnp.sum(weight_seq.astype(F32).reshape(chips, 2, rows_of, DH), axis=0)
+    parts = [parts[0]] + [along(parts[step], "x", step) for step in (1, 2, 3)]
+    parts = weight_sum(parts, place)
+    part = parts[0]
+    for step in (1, 2, 3):
+        part = part + along(parts[step], "y", step).astype(F32)
+    part = part.astype(BF).reshape(chips, rows_of, DH)
+    part, back = together(part, back)
+    part = exchange(part, NEAR).astype(F32).reshape(chips // 2, 2, rows_of, DH)
+    weight_total = jnp.sum(part, axis=0)
     tokens = COLS * seq * dp
     w_grad = weight_total.transpose(1, 0, 2).reshape(rows_of, D) * tokens ** (-0.5)
 

time: 220 us -> 226 us (1.027)
  waiting for transfers between devices: 89.8 us -> 94.9 us
    all_gather x1, waiting for transfers between devices: 24.5 us -> 44.5 us  [shards(): lax.all_gather(own_rows.reshape(chips * rows_of, DH), ('x', 'y'), axis=0,...]
    all_to_all x5, waiting for transfers between devices: 32.1 us -> 18.2 us  [exchange(): return lax.all_to_all(tensor, axes, split_axis=0, concat_axis=0, tiled=True)]
    ppermute x5 -> x6, waiting for transfers between devices: 33.2 us -> 28.5 us  [along(): return lax.ppermute(tensor, axis, [(i, (i + step) % 4) for i in range(4)])]
    ppermute x4, waiting for transfers between devices: 0.01 us -> 3.55 us  [other_core(): return lax.ppermute(tensor, 'c', [(0, 1), (1, 0)])]
    all_to_all x5, starting transfers between devices: 39 us -> 35.5 us  [exchange(): return lax.all_to_all(tensor, axes, split_axis=0, concat_axis=0, tiled=True)]
    unnamed x36 -> x42, local copies, waits for them, and re-layouts: 14.3 us -> 17.5 us
    ppermute x5 -> x6, starting transfers between devices: 6.51 us -> 8.83 us  [along(): return lax.ppermute(tensor, axis, [(i, (i + step) % 4) for i in range(4)])]
  transfers between devices with their start and end apart: 15 -> 16, of which waited for: 9 -> 9; matrix products, arithmetic and copies ran while one was open for 2% -> 1% of each run, Pallas kernels for 19% -> 19%
where the time goes in v3:
time: 226 us; the launch traced here: 224 us
  waiting for transfers between devices  94.9 us (42%)
  starting transfers between devices  48.3 us (21%)
  Pallas kernels  44.8 us (20%)
  local copies, waits for them, and re-layouts  21.4 us (9%)
  between operations  14.2 us (6%)
    all_gather x1, waiting for transfers between devices, shards(): lax.all_gather(own_rows.reshape(chips * rows_of, DH), ('x', 'y'), axis=0,...  44.5 us
    all_to_all x5, starting transfers between devices, exchange(): return lax.all_to_all(tensor, axes, split_axis=0, concat_axis=0, tiled=True)  35.5 us
    ppermute x6, waiting for transfers between devices, along(): return lax.ppermute(tensor, axis, [(i, (i + step) % 4) for i in range(4)])  28.5 us
    all_to_all x5, waiting for transfers between devices, exchange(): return lax.all_to_all(tensor, axes, split_axis=0, concat_axis=0, tiled=True)  18.2 us
    unnamed x42, local copies, waits for them, and re-layouts  17.5 us
    pallas_call x1, Pallas kernels, row_backward(): pl.pallas_call(row_backward_kernel, grid=(1,), out_shape=(whole, whole, w...  9.14 us
    ppermute x6, starting transfers between devices, along(): return lax.ppermute(tensor, axis, [(i, (i + step) % 4) for i in range(4)])  8.83 us
    pallas_call x1, Pallas kernels, column_backward(): pl.pallas_call(column_backward_kernel, grid=(2,), out_shape=jax.ShapeDtyp...  7.3 us
  transfers between devices with their start and end apart: 16, of which 9 were waited for; matrix products, arithmetic and copies ran while one was open for 1% of the time, Pallas kernels for 19%

profile of v3, /device:TPU:1, one launch (start us, length us, event | category | flops | bytes accessed | tf_op | source)
XLA Modules:
  0.0 224.4 jit_solution(9118027259869306721)
XLA Ops:
  8.6 10.0 %all-to-all-start = ((bf16[16,4,1024]{2,1,0:T(4,128)(2,1)}), bf16[16,4,1024]{2,1,0:T(4,128)(2,1)S(1)}, u32[]{:S(2)}, u32[]{:S(2)}) async-start(bf16[16,4,1024]{2,1,0:T(4,128)(2,1)} %bitcast.5), calls=%async_computation | async-start | bytes 262144 | tf_op jit(solution)/shard_map/all_to_all | solution.py:418
  23.0 2.4 %pack.1 = bf16[512,1536]{1,0:T(8,128)(2,1)} custom-call(s32[4]{0:T(128)S(1)} %copy-done.18, bf16[512,1024]{1,0:T(8,128)(2,1)S(1)} %bitcast.34, bf16[512,1024]{1,0:T(8,128)(2,1)S(1)} %bitcast.37, bf16[512,1024]{1,0:T(8,128)(2,1)S(1)} %bitcast.40), custom_call_target="tpu_custom_call" | custom-call | flops 536870912 | bytes 3145728 | tf_op jit(solution)/shard_map/pack/pallas_call | solution.py:77
  25.4 2.3 %all-to-all-done = bf16[16,4,1024]{2,1,0:T(4,128)(2,1)S(1)} async-done(((bf16[16,4,1024]{2,1,0:T(4,128)(2,1)}), bf16[16,4,1024]{2,1,0:T(4,128)(2,1)S(1)}, u32[]{:S(2)}, u32[]{:S(2)}) %all-to-all-start) | async-done | bytes 131104 | tf_op jit(solution)/shard_map/all_to_all | solution.py:418
  28.5 7.7 %all-to-all-start.1 = ((bf16[32,16,1536]{2,1,0:T(8,128)(2,1)}), bf16[32,16,1536]{2,1,0:T(8,128)(2,1)S(1)}, u32[]{:S(2)}, u32[]{:S(2)}) async-start(bf16[32,16,1536]{2,1,0:T(8,128)(2,1)} %bitcast.46), calls=%async_computation.1 | async-start | bytes 3145728 | tf_op jit(solution)/shard_map/all_to_all | solution.py:418
  37.4 1.2 copy-done.9
  38.6 2.1 row_forward.1.row_ref.row_mine
  41.9 44.5 %all-gather.2.cloned.1.call-done.mine_ref = bf16[1024,1024]{1,0:T(8,128)(2,1)} async-done(((bf16[64,1024]{1,0:T(8,128)(2,1)}), bf16[1024,1024]{1,0:T(8,128)(2,1)}) %all-gather.2.cloned.1.call-update) | async-done | bytes 2097168 | tf_op jit(solution)/shard_map/all_gather | solution.py:448
  86.4 1.5 collective-permute-start.2
  88.5 3.5 %collective-permute-done.2.theirs_ref = bf16[1024,1024]{1,0:T(8,128)(2,1)} collective-permute-done((bf16[1024,1024]{1,0:T(8,128)(2,1)}, bf16[1024,1024]{1,0:T(8,128)(2,1)}, u32[]{:S(2)}, u32[]{:S(2)}) %collective-permute-start.2) | collective-permute-done | bytes 2097184 | tf_op jit(solution)/shard_map/ppermute | solution.py:422
  92.0 1.6 copy-done.2
  93.6 5.5 %attn_grad.1 = (bf16[512,512]{1,0:T(8,128)(2,1)S(1)}, bf16[512,512]{1,0:T(8,128)(2,1)S(1)}) custom-call(s32[4]{0:T(128)S(1)} %pad_add_fusion.place.core_ref, bf16[512,2048]{1,0:T(8,128)(2,1)S(1)} %bitcast.32, bf16[512,2048]{1,0:T(8,128)(2,1)S(1)} %bitcast.33, bf16[1024,1024]{1,0:T(8,128)(2,1)} %all-gather.2.cloned.1.call-done.mine_ref, ...), custom_call_target="tpu_custom_call" | custom-call | flops 2147483648 | bytes 7340032 | tf_op jit(solution)/shard_map/attn_grad/pallas_call | solution.py:282
  100.8 1.4 copy-done.16
  102.2 2.5 %column_forward.1 = bf16[32,2,8,1024]{3,2,1,0:T(8,128)(2,1)S(1)} custom-call(bf16[32,2,8,1536]{3,2,1,0:T(8,128)(2,1)S(1)} %bitcast.29, bf16[32,2,8,512]{3,2,1,0:T(8,128)(2,1)S(1)} %bitcast.45), custom_call_target="tpu_custom_call" | custom-call | flops 268435456 | bytes 2097152 | tf_op jit(solution)/shard_map/column_forward/pallas_call | solution.py:129
  105.7 6.9 %all-to-all-start.2 = ((bf16[32,16,1024]{2,1,0:T(8,128)(2,1)}), bf16[32,16,1024]{2,1,0:T(8,128)(2,1)}, u32[]{:S(2)}, u32[]{:S(2)}) async-start(bf16[32,16,1024]{2,1,0:T(8,128)(2,1)} %bitcast.44), calls=%async_computation.2 | async-start | bytes 2097152 | tf_op jit(solution)/shard_map/all_to_all | solution.py:418
  116.1 9.1 %row_backward.1 = (bf16[512,1024]{1,0:T(8,128)(2,1)}, bf16[512,1024]{1,0:T(8,128)(2,1)}, bf16[512,1024]{1,0:T(8,128)(2,1)}) custom-call(s32[4,4]{1,0:T(4,128)S(1)} %copy-done.17, bf16[512,1024]{1,0:T(8,128)(2,1)S(1)} %bitcast.36, bf16[512,1024]{1,0:T(8,128)(2,1)S(1)} %bitcast.39, bf16[512,1024]{1,0:T(8,128)(2,1)S(1)} %bitcast.42, bf16[512,512]{1,0:T(8,128)(2,1)S(1)} %copy-done.14), custom_call_target="tpu_custom_call" | custom-call | flops 671088640 | bytes 3670016 | tf_op jit(solution)/shard_map/row_backward/pallas_call | solution.py:221
  125.2 15.9 %all-to-all-done.2 = bf16[32,16,1024]{2,1,0:T(8,128)(2,1)} async-done(((bf16[32,16,1024]{2,1,0:T(8,128)(2,1)}), bf16[32,16,1024]{2,1,0:T(8,128)(2,1)}, u32[]{:S(2)}, u32[]{:S(2)}) %all-to-all-start.2) | async-done | bytes 1048608 | tf_op jit(solution)/shard_map/all_to_all | solution.py:418
  141.1 1.9 collective-permute-start.3
  143.0 7.3 %column_backward.1 = bf16[32,2,8,1536]{3,2,1,0:T(8,128)(2,1)} custom-call(bf16[32,2,8,1536]{3,2,1,0:T(8,128)(2,1)} %bitcast.30, bf16[32,2,8,1024]{3,2,1,0:T(8,128)(2,1)} %bitcast.15.g_ref), custom_call_target="tpu_custom_call" | custom-call | flops 671088640 | bytes 3670016 | tf_op jit(solution)/shard_map/column_backward/pallas_call | solution.py:155
  150.3 4.2 %all-to-all-start.3 = ((bf16[32,16,1536]{2,1,0:T(8,128)(2,1)}), bf16[32,16,1536]{2,1,0:T(8,128)(2,1)S(1)}, u32[]{:S(2)}, u32[]{:S(2)}) async-start(bf16[32,16,1536]{2,1,0:T(8,128)(2,1)} %bitcast.16), calls=%async_computation.3 | async-start | bytes 3145728 | tf_op jit(solution)/shard_map/all_to_all | solution.py:418
  154.6 6.0 %weight_grad.1 = (f32[256,1024]{1,0:T(8,128)S(1)}, bf16[256,1024]{1,0:T(8,128)(2,1)S(1)}, bf16[256,1024]{1,0:T(8,128)(2,1)S(1)}, bf16[256,1024]{1,0:T(8,128)(2,1)S(1)}) custom-call(s32[4]{0:T(128)S(1)} %pad_add_fusion.place.core_ref, bf16[512,512]{1,0:T(8,128)(2,1)S(1)} %row_forward.1.row_ref.row_mine, bf16[512,512]{1,0:T(8,128)(2,1)} %collective-permute-done.row_theirs, ...), custom_call_target="tpu_custom_call" | custom-call | flops 2147483648 | bytes 7340032 | tf_op jit(solution)/shard_map/weight_grad/pallas_call | solution.py:370
  160.9 2.2 collective-permute-start.5
  163.1 1.2 collective-permute-start.6
  164.3 11.1 %collective-permute-done.4.b_ref = bf16[256,1024]{1,0:T(8,128)(2,1)S(1)} collective-permute-done((bf16[256,1024]{1,0:T(8,128)(2,1)S(1)}, bf16[256,1024]{1,0:T(8,128)(2,1)S(1)}, u32[]{:S(2)}, u32[]{:S(2)}) %collective-permute-start.4) | collective-permute-done | bytes 524320 | tf_op jit(solution)/shard_map/ppermute | solution.py:430
  175.5 10.7 %collective-permute-done.5.c_ref = bf16[256,1024]{1,0:T(8,128)(2,1)S(1)} collective-permute-done((bf16[256,1024]{1,0:T(8,128)(2,1)S(1)}, bf16[256,1024]{1,0:T(8,128)(2,1)S(1)}, u32[]{:S(2)}, u32[]{:S(2)}) %collective-permute-start.5) | collective-permute-done | bytes 524320 | tf_op jit(solution)/shard_map/ppermute | solution.py:430
  187.5 1.5 collective-permute-start.7
  189.0 2.4 %collective-permute-start.8 = (bf16[64,1024]{1,0:T(8,128)(2,1)S(1)}, bf16[64,1024]{1,0:T(8,128)(2,1)S(1)}, u32[]{:S(2)}, u32[]{:S(2)}) collective-permute-start(bf16[64,1024]{1,0:T(8,128)(2,1)S(1)} %get-tuple-element.62), channel_id=1, source_target_pairs={{0,16},{8,24},{16,0},{24,8},{1,17},{9,25},{17,1},{25,9},{2,18},{10... | collective-permute-start | bytes 393224 | tf_op jit(solution)/shard_map/ppermute | solution.py:430
  192.6 4.2 %collective-permute-done.7 = bf16[64,1024]{1,0:T(8,128)(2,1)S(1)} collective-permute-done((bf16[64,1024]{1,0:T(8,128)(2,1)S(1)}, bf16[64,1024]{1,0:T(8,128)(2,1)S(1)}, u32[]{:S(2)}, u32[]{:S(2)}) %collective-permute-start.7) | collective-permute-done | bytes 131104 | tf_op jit(solution)/shard_map/ppermute | solution.py:430
  196.8 1.9 collective-permute-done.8
  199.5 6.8 %all-to-all-start.4 = ((bf16[16,4,1024]{2,1,0:T(4,128)(2,1)}), bf16[16,4,1024]{2,1,0:T(4,128)(2,1)S(1)}, u32[]{:S(2)}, u32[]{:S(2)}) async-start(bf16[16,4,1024]{2,1,0:T(4,128)(2,1)} %reshape.96), calls=%async_computation.4 | async-start | bytes 262144 | tf_op jit(solution)/shard_map/all_to_all | solution.py:418
  206.3 1.6 copy-done.12
  207.8 6.4 %layer_out.1 = bf16[512,2048]{1,0:T(8,128)(2,1)} custom-call(s32[4]{0:T(128)S(1)} %pad_add_fusion.place.core_ref, bf16[512,512]{1,0:T(8,128)(2,1)S(1)} %row_forward.1.row_ref.row_mine, bf16[512,1024]{1,0:T(8,128)(2,1)} %bitcast.17.col_ref.col_mine, bf16[1024,1024]{1,0:T(8,128)(2,1)S(1)} %copy-done.12, bf16[1024,1024]{1,0:T(8,128)(2,1)} %collective-permute-done.2.theirs_ref), custom_call_target="tpu_custom_call" | custom-call | flops 2147483648 | bytes 7340032 | tf_op jit(solution)/shard_map/layer_out/pallas_call | solution.py:324
  214.3 2.6 %finish.1 = (bf16[512,1024]{1,0:T(8,128)(2,1)}, bf16[512,1024]{1,0:T(8,128)(2,1)}, bf16[512,1024]{1,0:T(8,128)(2,1)}) custom-call(s32[4]{0:T(128)S(1)} %copy-done.19, bf16[512,1536]{1,0:T(8,128)(2,1)S(1)} %bitcast.43, bf16[512,1024]{1,0:T(8,128)(2,1)} %get-tuple-element.66.dq_in, ...), custom_call_target="tpu_custom_call", output_to_operand_aliasing={{0}: (2, {}), {1}: (3, {}), {2}: (4, {})} | custom-call | flops 536870912 | bytes 3145728 | tf_op jit(solution)/shard_map/finish/pallas_call | solution.py:247
  (63 shorter events, 19.7 us)
Async XLA Ops:
  8.6 19.1 %all-to-all-start = ((bf16[16,4,1024]{2,1,0:T(4,128)(2,1)}), bf16[16,4,1024]{2,1,0:T(4,128)(2,1)S(1)}, u32[]{:S(2)}, u32[]{:S(2)}) async-start(bf16[16,4,1024]{2,1,0:T(4,128)(2,1)} %bitcast.5), calls=%async_computation | async-start | bytes 262144 | tf_op jit(solution)/shard_map/all_to_all | solution.py:418
  18.6 67.8 %all-gather.2.cloned.1.call-start = ((), (), s32[]{:S(2)}) async-start(), calls=%async_computation.5 | async-start | bytes 2228224 | tf_op jit(solution)/shard_map/all_gather | solution.py:448
  18.6 1.2 copy-start.3
  19.9 1.2 copy-start.5
  21.1 1.2 copy-start.8
  25.4 10.7 %copy-start.4 = (bf16[1,1,512,1024]{3,2,1,0:T(8,128)(2,1)S(1)}, bf16[1,1,512,1024]{3,2,1,0:T(8,128)(2,1)}, u32[]{:S(2)}) copy-start(bf16[1,1,512,1024]{3,2,1,0:T(8,128)(2,1)} %param.7) | copy-start | bytes 3145732
  25.4 10.7 %copy-start.17 = (s32[4,4]{1,0:T(4,128)S(1)}, s32[4,4]{1,0:T(4,128)}, u32[]{:S(2)}) copy-start(s32[4,4]{1,0:T(4,128)} %pat_ref.3) | copy-start | bytes 196
  28.5 72.3 %all-to-all-start.1 = ((bf16[32,16,1536]{2,1,0:T(8,128)(2,1)}), bf16[32,16,1536]{2,1,0:T(8,128)(2,1)S(1)}, u32[]{:S(2)}, u32[]{:S(2)}) async-start(bf16[32,16,1536]{2,1,0:T(8,128)(2,1)} %bitcast.46), calls=%async_computation.1 | async-start | bytes 3145728 | tf_op jit(solution)/shard_map/all_to_all | solution.py:418
  36.2 1.2 copy-start.6
  37.4 1.2 copy-start.9
  38.6 2.2 copy-start.1
  86.4 5.6 %collective-permute-start.2 = (bf16[1024,1024]{1,0:T(8,128)(2,1)}, bf16[1024,1024]{1,0:T(8,128)(2,1)}, u32[]{:S(2)}, u32[]{:S(2)}) collective-permute-start(bf16[1024,1024]{1,0:T(8,128)(2,1)} %all-gather.2.cloned.1.call-done.mine_ref), channel_id=1, source_target_pairs={{0,1},{1,0},{2,3},{3,2},{4,5},{5,4},{6,7},{7,6},{8,9},{9,8},{10,11... | collective-permute-start | bytes 6291464 | tf_op jit(solution)/shard_map/ppermute | solution.py:422
  87.9 12.8 %collective-permute-start.1 = (bf16[512,1024]{1,0:T(8,128)(2,1)}, bf16[512,1024]{1,0:T(8,128)(2,1)}, u32[]{:S(2)}, u32[]{:S(2)}) collective-permute-start(bf16[512,1024]{1,0:T(8,128)(2,1)} %dynamic-slice_bitcast_fusion), channel_id=1, source_target_pairs={{0,1},{1,0},{2,3},{3,2},{4,5},{5,4},{6,7},{7,6},{8,9},{9,8},{10,11... | collective-permute-start | bytes 3145736 | tf_op jit(solution)/shard_map/ppermute | solution.py:422
  87.9 12.8 %collective-permute-start = (bf16[512,512]{1,0:T(8,128)(2,1)S(1)}, bf16[512,512]{1,0:T(8,128)(2,1)}, u32[]{:S(2)}, u32[]{:S(2)}) collective-permute-start(bf16[512,512]{1,0:T(8,128)(2,1)S(1)} %row_forward.1.row_ref.row_mine), channel_id=1, source_target_pairs={{0,1},{1,0},{2,3},{3,2},{4,5},{5,4},{6,7},{7,6},{8,9},{9,8},{10,11... | collective-permute-start | bytes 1572872 | tf_op jit(solution)/shard_map/ppermute | solution.py:422
  92.0 1.6 copy-start.2
  100.7 5.0 %copy-start = (bf16[32,16,1536]{2,1,0:T(8,128)(2,1)}, bf16[32,16,1536]{2,1,0:T(8,128)(2,1)S(1)}, u32[]{:S(2)}) copy-start(bf16[32,16,1536]{2,1,0:T(8,128)(2,1)S(1)} %all-to-all-done.1) | copy-start | bytes 4718596
  100.8 1.4 copy-start.16
  105.7 35.4 %all-to-all-start.2 = ((bf16[32,16,1024]{2,1,0:T(8,128)(2,1)}), bf16[32,16,1024]{2,1,0:T(8,128)(2,1)}, u32[]{:S(2)}, u32[]{:S(2)}) async-start(bf16[32,16,1024]{2,1,0:T(8,128)(2,1)} %bitcast.44), calls=%async_computation.2 | async-start | bytes 2097152 | tf_op jit(solution)/shard_map/all_to_all | solution.py:418
  112.6 1.2 copy-start.7
  113.8 1.2 copy-start.10
  141.1 9.2 %collective-permute-start.3 = (bf16[512,1024]{1,0:T(8,128)(2,1)}, bf16[512,1024]{1,0:T(8,128)(2,1)S(1)}, u32[]{:S(2)}, u32[]{:S(2)}) collective-permute-start(bf16[512,1024]{1,0:T(8,128)(2,1)} %bitcast.17.col_ref.col_mine), channel_id=1, source_target_pairs={{0,1},{1,0},{2,3},{3,2},{4,5},{5,4},{6,7},{7,6},{8,9},{9,8},{10,11... | collective-permute-start | bytes 3145736 | tf_op jit(solution)/shard_map/ppermute | solution.py:422
  150.3 4.3 %copy-start.20 = (bf16[512,1024]{1,0:T(8,128)(2,1)}, bf16[512,1024]{1,0:T(8,128)(2,1)S(1)}, u32[]{:S(2)}) copy-start(bf16[512,1024]{1,0:T(8,128)(2,1)S(1)} %collective-permute-done.3.col_theirs) | copy-start | bytes 3145732
  150.3 49.2 %all-to-all-start.3 = ((bf16[32,16,1536]{2,1,0:T(8,128)(2,1)}), bf16[32,16,1536]{2,1,0:T(8,128)(2,1)S(1)}, u32[]{:S(2)}, u32[]{:S(2)}) async-start(bf16[32,16,1536]{2,1,0:T(8,128)(2,1)} %bitcast.16), calls=%async_computation.3 | async-start | bytes 3145728 | tf_op jit(solution)/shard_map/all_to_all | solution.py:418
  160.6 14.8 %collective-permute-start.4 = (bf16[256,1024]{1,0:T(8,128)(2,1)S(1)}, bf16[256,1024]{1,0:T(8,128)(2,1)S(1)}, u32[]{:S(2)}, u32[]{:S(2)}) collective-permute-start(bf16[256,1024]{1,0:T(8,128)(2,1)S(1)} %get-tuple-element.57), channel_id=1, source_target_pairs={{0,64},{64,128},{128,192},{192,0},{1,65},{65,129},{129,193},{193,1... | collective-permute-start | bytes 1572872 | tf_op jit(solution)/shard_map/ppermute | solution.py:430
  160.9 25.3 %collective-permute-start.5 = (bf16[256,1024]{1,0:T(8,128)(2,1)S(1)}, bf16[256,1024]{1,0:T(8,128)(2,1)S(1)}, u32[]{:S(2)}, u32[]{:S(2)}) collective-permute-start(bf16[256,1024]{1,0:T(8,128)(2,1)S(1)} %get-tuple-element.58), channel_id=1, source_target_pairs={{0,128},{64,192},{128,0},{192,64},{1,129},{65,193},{129,1},{193,65... | collective-permute-start | bytes 1572872 | tf_op jit(solution)/shard_map/ppermute | solution.py:430
  163.1 23.6 %collective-permute-start.6 = (bf16[256,1024]{1,0:T(8,128)(2,1)S(1)}, bf16[256,1024]{1,0:T(8,128)(2,1)S(1)}, u32[]{:S(2)}, u32[]{:S(2)}) collective-permute-start(bf16[256,1024]{1,0:T(8,128)(2,1)S(1)} %get-tuple-element.59), channel_id=1, source_target_pairs={{0,192},{64,0},{128,64},{192,128},{1,193},{65,1},{129,65},{193,129... | collective-permute-start | bytes 1572872 | tf_op jit(solution)/shard_map/ppermute | solution.py:430
  187.5 9.3 %collective-permute-start.7 = (bf16[64,1024]{1,0:T(8,128)(2,1)S(1)}, bf16[64,1024]{1,0:T(8,128)(2,1)S(1)}, u32[]{:S(2)}, u32[]{:S(2)}) collective-permute-start(bf16[64,1024]{1,0:T(8,128)(2,1)S(1)} %get-tuple-element.61), channel_id=1, source_target_pairs={{0,8},{8,16},{16,24},{24,0},{1,9},{9,17},{17,25},{25,1},{2,10},{10... | collective-permute-start | bytes 393224 | tf_op jit(solution)/shard_map/ppermute | solution.py:430
  189.0 9.7 %collective-permute-start.8 = (bf16[64,1024]{1,0:T(8,128)(2,1)S(1)}, bf16[64,1024]{1,0:T(8,128)(2,1)S(1)}, u32[]{:S(2)}, u32[]{:S(2)}) collective-permute-start(bf16[64,1024]{1,0:T(8,128)(2,1)S(1)} %get-tuple-element.62), channel_id=1, source_target_pairs={{0,16},{8,24},{16,0},{24,8},{1,17},{9,25},{17,1},{25,9},{2,18},{10... | collective-permute-start | bytes 393224 | tf_op jit(solution)/shard_map/ppermute | solution.py:430
  191.5 7.3 %collective-permute-start.9 = (bf16[64,1024]{1,0:T(8,128)(2,1)S(1)}, bf16[64,1024]{1,0:T(8,128)(2,1)S(1)}, u32[]{:S(2)}, u32[]{:S(2)}) collective-permute-start(bf16[64,1024]{1,0:T(8,128)(2,1)S(1)} %get-tuple-element.63), channel_id=1, source_target_pairs={{0,24},{8,0},{16,8},{24,16},{1,25},{9,1},{17,9},{25,17},{2,26},{10... | collective-permute-start | bytes 393224 | tf_op jit(solution)/shard_map/ppermute | solution.py:430
  199.5 17.3 %all-to-all-start.4 = ((bf16[16,4,1024]{2,1,0:T(4,128)(2,1)}), bf16[16,4,1024]{2,1,0:T(4,128)(2,1)S(1)}, u32[]{:S(2)}, u32[]{:S(2)}) async-start(bf16[16,4,1024]{2,1,0:T(4,128)(2,1)} %reshape.96), calls=%async_computation.4 | async-start | bytes 262144 | tf_op jit(solution)/shard_map/all_to_all | solution.py:418
  206.3 1.6 copy-start.12
  207.8 6.4 %copy-start.19 = (s32[4]{0:T(128)S(1)}, s32[4]{0:T(128)}, u32[]{:S(2)}) copy-start(s32[4]{0:T(128)} %off_ref.3) | copy-start | bytes 52
  (5 other events, 4.3 us)
Sparse Core Ops, SparseCore 0:
  28.6 57.7 all-gather.1

commit v4 on v3

--- a/solution.py
+++ b/solution.py
@@ -1,3 +1,5 @@
+import functools
+
 import jax
 import jax.numpy as jnp
 from jax import lax
@@ -113,29 +115,28 @@
     return q, k, v, softmax(jnp.where(mask, mm_t(q, k) * SCALE, -1e30))
 
 
-def column_forward_kernel(r_ref, g_ref, o_ref):
+def column_forward_kernel(r_ref, o_ref):
     mask = column_mask()
-    o_ref[:, :, :, HALF:] = g_ref[...]
     for h in range(HC):
         _, _, v, probs = column_probs(r_ref, h, mask)
         store_tile(o_ref, h, mm(probs.astype(BF), v))
 
 
-def group_block(lanes, part=0):
-    return pl.BlockSpec((ROWS, 1, GRP, lanes), lambda i: (0, i, 0, part))
-
-
-def column_forward(received, grads):
+def group_block(lanes):
+    return pl.BlockSpec((ROWS, 1, GRP, lanes), lambda i: (0, i, 0, 0))
+
+
+def column_forward(received):
     return pl.pallas_call(
         column_forward_kernel,
         grid=(2,),
-        out_shape=jax.ShapeDtypeStruct((ROWS, 2, GRP, 2 * HALF), BF),
-        in_specs=[group_block(3 * HALF), group_block(HALF)],
-        out_specs=group_block(2 * HALF),
+        out_shape=jax.ShapeDtypeStruct((ROWS, 2, GRP, HALF), BF),
+        in_specs=[group_block(3 * HALF)],
+        out_specs=group_block(HALF),
         compiler_params=params(),
         cost_estimate=cost(8 * 4 * TILE * TILE * HD, 4 * COLS * HALF * 2, 8 * TILE * TILE),
         name="column_forward",
-    )(received, grads)
+    )(received)
 
 
 def column_backward_kernel(r_ref, g_ref, o_ref):
@@ -151,17 +152,17 @@
         store_tile(o_ref, HC + h, t_mm(score_grad, q) * SCALE)
 
 
-def column_backward(received, mixed):
+def column_backward(received, grads):
     return pl.pallas_call(
         column_backward_kernel,
         grid=(2,),
         out_shape=jax.ShapeDtypeStruct((ROWS, 2, GRP, 3 * HALF), BF),
-        in_specs=[group_block(3 * HALF), group_block(HALF, 1)],
+        in_specs=[group_block(3 * HALF), group_block(HALF)],
         out_specs=group_block(3 * HALF),
         compiler_params=params(),
         cost_estimate=cost(8 * 10 * TILE * TILE * HD, 7 * COLS * HALF * 2, 8 * TILE * TILE),
         name="column_backward",
-    )(received, mixed)
+    )(received, grads)
 
 
 def row_tile(pat_ref, q_ref, k_ref, v_ref, h, j):
@@ -257,14 +258,8 @@
     )(offset, back, dq, dk, dv)
 
 
-def pair_rows(ref, pair):
-    chunk = 2 * HD // 8
-    starts = [2 * HD * pair + (2 * at_y + at_z) * chunk for at_z in range(2) for at_y in range(4)]
-    return jnp.concatenate([ref[start : start + chunk, :] for start in starts], axis=0)
-
-
 def attn_grad_kernel(place, og_mine, og_theirs, mine_ref, theirs_ref, row_ref, send_ref):
-    total = mm_t(og_mine[...], pair_rows(mine_ref, 0)) + mm_t(og_theirs[...], pair_rows(theirs_ref, 0))
+    total = mm_t(og_mine[...], mine_ref[...]) + mm_t(og_theirs[...], theirs_ref[...])
     total = total.astype(BF)
 
     @pl.when(pl.program_id(0) < 2)
@@ -304,9 +299,7 @@
 
 def layer_out_kernel(core_ref, row_ref, col_ref, mine_ref, theirs_ref, o_ref):
     def product(w_ref):
-        two = 2 * HD
-        total = mm(row_ref[:, :two], pair_rows(w_ref, 0)) + mm(row_ref[:, two:], pair_rows(w_ref, 1))
-        total += mm(col_ref[:, :two], pair_rows(w_ref, 2)) + mm(col_ref[:, two:], pair_rows(w_ref, 3))
+        total = mm(row_ref[...], w_ref[:HALF, :]) + mm(col_ref[...], w_ref[HALF:, :])
         o_ref[...] = total.astype(BF)
 
     pl.when(pl.program_id(0) == 0)(lambda: product(mine_ref))
@@ -390,6 +383,28 @@
     )(place, row_mine, row_theirs, col_mine, col_theirs, og, og_theirs)
 
 
+def gather_kernel(axis, pieces, place, own_ref, a_ref, b_ref, c_ref, o_ref):
+    chunk = own_ref.shape[0] // pieces
+    for step, ref in enumerate((own_ref, a_ref, b_ref, c_ref)):
+        source = lax.rem(place[axis] + 4 - step, 4)
+        for piece in range(pieces):
+            rows = pl.ds(pl.multiple_of((piece * 4 + source) * chunk, chunk), chunk)
+            o_ref[rows, :] = ref[piece * chunk : (piece + 1) * chunk, :]
+
+
+def gather_of(own, place, axis, index, pieces):
+    blocks = [own] + [along(own, axis, step) for step in (1, 2, 3)]
+    return pl.pallas_call(
+        functools.partial(gather_kernel, index, pieces),
+        out_shape=jax.ShapeDtypeStruct((4 * own.shape[0], DH), BF),
+        in_specs=[SMEM_SPEC] + [VMEM_SPEC] * 4,
+        out_specs=VMEM_SPEC,
+        compiler_params=params(),
+        cost_estimate=cost(0, 16 * own.shape[0] * DH),
+        name="gather_" + axis,
+    )(place, *blocks)
+
+
 def weight_sum_kernel(place, a_ref, b_ref, c_ref, d_ref, *outs):
     chunk = 2 * HD // 8
     for step, out in enumerate(outs):
@@ -414,6 +429,54 @@
     )(place, *parts)
 
 
+def y_sum_kernel(place, a_ref, b_ref, c_ref, d_ref, *refs):
+    outs, total = refs[:-1], refs[-1]
+    near = a_ref[...] + b_ref[...].astype(F32)
+    total[...] = near + (c_ref[...].astype(F32) + d_ref[...].astype(F32))
+    rows = outs[0].shape[0]
+    for step, out in enumerate(outs):
+        target = lax.rem(place[2] + step // 4, 2) * 4 + lax.rem(place[4] + step % 4, 4)
+        out[...] = total[pl.ds(pl.multiple_of(target * rows, rows), rows), :].astype(out.dtype)
+
+
+def y_sum(parts, place):
+    rows = parts[0].shape[0] // 8
+    return pl.pallas_call(
+        y_sum_kernel,
+        out_shape=(jax.ShapeDtypeStruct((rows, DH), F32),) + (jax.ShapeDtypeStruct((rows, DH), BF),) * 7,
+        in_specs=[SMEM_SPEC] + [VMEM_SPEC] * 4,
+        out_specs=(VMEM_SPEC,) * 8,
+        scratch_shapes=[pltpu.VMEM(parts[0].shape, F32)],
+        compiler_params=params(),
+        cost_estimate=cost(32 * rows * DH, 2**20),
+        name="y_sum",
+    )(place, *parts)
+
+
+def z_sum_kernel(place, *refs):
+    ins, (keep_ref, send_ref) = refs[:8], refs[8:]
+    total = ins[0][...]
+    for ref in ins[1:]:
+        total = total + ref[...].astype(F32)
+    half = keep_ref.shape[0]
+    first = jnp.broadcast_to(place[0], (half, DH)) == 0
+    keep_ref[...] = jnp.where(first, total[:half], total[half:])
+    send_ref[...] = jnp.where(first, total[half:], total[:half])
+
+
+def z_sum(parts, place):
+    out = jax.ShapeDtypeStruct((parts[0].shape[0] // 2, DH), F32)
+    return pl.pallas_call(
+        z_sum_kernel,
+        out_shape=(out, out),
+        in_specs=[SMEM_SPEC] + [VMEM_SPEC] * 8,
+        out_specs=(VMEM_SPEC, VMEM_SPEC),
+        compiler_params=params(),
+        cost_estimate=cost(8 * 8 * DH, 2**18),
+        name="z_sum",
+    )(place, *parts)
+
+
 def exchange(tensor, axes):
     return lax.all_to_all(tensor, axes, split_axis=0, concat_axis=0, tiled=True)
 
@@ -428,6 +491,11 @@
 
 def along(tensor, axis, step):
     return lax.ppermute(tensor, axis, [(i, (i + step) % 4) for i in range(4)])
+
+
+def along_z(tensor, step):
+    turns = [(z * 4 + h, (z + step // 4) % 2 * 4 + (h + step % 4) % 4) for z in range(2) for h in range(4)]
+    return lax.ppermute(tensor, ("zl", "zh"), turns)
 
 
 def shards(queries, keys, values, out_proj, out_grad, block_pattern, col_offset):
@@ -435,53 +503,57 @@
     og = out_grad.reshape(COLS, D)
     rows_of = out_proj.shape[0]
     seq = ROWS
-    chips = seq // 2
+    near = seq // 2
     dp = lax.axis_size("x") * lax.axis_size("zl")
     core = lax.axis_index("c").astype(jnp.int32)
-    place = jnp.stack([core] + [lax.axis_index(name).astype(jnp.int32) for name in ("x", "zl", "y")])
+    place = jnp.stack([core] + [lax.axis_index(name).astype(jnp.int32) for name in ("x", "zl", "y", "zh")])
 
     halves = out_proj.reshape(rows_of, 2, DH).transpose(1, 0, 2)
-    spread = jnp.broadcast_to(halves[None], (chips // 2, 2, rows_of, DH)).reshape(chips, rows_of, DH)
+    spread = jnp.broadcast_to(halves[None], (near // 2, 2, rows_of, DH)).reshape(near, rows_of, DH)
     own_rows = exchange(spread, NEAR)
     packed = pack(q, k, v, col_offset)
     own_rows, packed = together(own_rows, packed)
-    mine = lax.all_gather(own_rows.reshape(chips * rows_of, DH), ("x", "y"), axis=0, tiled=True)
+    own_rows = own_rows.reshape(near * rows_of, DH)
+    mine = gather_of(gather_of(own_rows, place, "y", 3, 2), place, "x", 1, 1)
 
     received = exchange(packed.reshape(seq, COLS // seq, 3 * HALF), SEQ)
     og_sent = lax.dynamic_slice(og, (0, (1 - core) * DH), (COLS, DH))
+    og_theirs = other_core(og_sent)
     row_out = row_forward(q, k, v, block_pattern)
-    mine, row_out, og_sent = together(mine, row_out, og_sent)
-    theirs, row_theirs, og_theirs = other_core(mine), other_core(row_out), other_core(og_sent)
+    row_theirs = other_core(row_out)
+    received, row_out, row_theirs, og_theirs = together(received, row_out, row_theirs, og_theirs)
+    received = received.reshape(ROWS, 2, GRP, 3 * HALF)
+
+    col_sent = column_forward(received).reshape(seq, COLS // seq, HALF)
+    col_sent, mine = together(col_sent, mine)
+    col_mine = exchange(col_sent, SEQ)
+    theirs = other_core(mine)
     grad_rows, grad_cols = attn_grad_of(og, mine, theirs, place)
-    received, row_theirs, og_theirs, grad_cols = together(received, row_theirs, og_theirs, grad_cols)
-    received = received.reshape(ROWS, 2, GRP, 3 * HALF)
-
-    send = column_forward(received, grad_cols.reshape(ROWS, 2, GRP, HALF))
-    mixed = exchange(send.reshape(seq, COLS // seq, 2 * HALF), SEQ)
+    col_mine, grad_rows, grad_cols = together(col_mine, grad_rows, grad_cols)
+    col_mine = col_mine.reshape(COLS, HALF)
+
+    col_grads = exchange(grad_cols.reshape(seq, COLS // seq, HALF), SEQ)
+    col_theirs = other_core(col_mine)
+    parts = weight_grad_of(row_out, row_theirs, col_mine, col_theirs, og, og_theirs, place)
     dq, dk, dv = row_backward(q, k, v, grad_rows, block_pattern)
-    mixed, dq, dk, dv = together(mixed, dq, dk, dv)
-
-    col_mine = mixed.reshape(COLS, 2 * HALF)
-    col_theirs = other_core(col_mine)
-    col_back = column_backward(received, mixed.reshape(ROWS, 2, GRP, 2 * HALF)).reshape(seq, COLS // seq, 3 * HALF)
-    col_back, col_mine, col_theirs = together(col_back, col_mine, col_theirs)
+    next_x, last_x = along(parts[1], "x", 1), along(parts[3], "x", 3)
+    col_grads, dq, dk, dv, next_x, last_x = together(col_grads, dq, dk, dv, next_x, last_x)
+
+    col_back = column_backward(received, col_grads.reshape(ROWS, 2, GRP, HALF)).reshape(seq, COLS // seq, 3 * HALF)
     back = exchange(col_back, SEQ).reshape(COLS, 3 * HALF)
 
-    parts = weight_grad_of(row_out, row_theirs, col_mine, col_theirs, og, og_theirs, place)
-    parts = [parts[0]] + [along(parts[step], "x", step) for step in (1, 2, 3)]
-    parts = weight_sum(parts, place)
-    part = parts[0]
-    for step in (1, 2, 3):
-        part = part + along(parts[step], "y", step).astype(F32)
-    part = part.astype(BF).reshape(chips, rows_of, DH)
-    part, back = together(part, back)
-    part = exchange(part, NEAR).astype(F32).reshape(chips // 2, 2, rows_of, DH)
-    weight_total = jnp.sum(part, axis=0)
+    parts = weight_sum([parts[0], next_x, along(parts[2], "x", 2), last_x], place)
+    parts = [parts[0]] + [along(parts[step], "y", step) for step in (1, 2, 3)]
+    parts = y_sum(parts, place)
+    parts = [parts[0]] + [along_z(parts[step], step) for step in range(1, 8)]
+    keep, give = z_sum(parts, place)
+    taken = other_core(give)
+    first = core == 0
     tokens = COLS * seq * dp
-    w_grad = weight_total.transpose(1, 0, 2).reshape(rows_of, D) * tokens ** (-0.5)
+    w_grad = jnp.concatenate([jnp.where(first, keep, taken), jnp.where(first, taken, keep)], axis=1)
+    w_grad = w_grad * tokens ** (-0.5)
 
     dq, dk, dv = finish(back, dq, dk, dv, col_offset)
-
     layer = layer_out_of(row_out, col_mine, mine, theirs, place)
     lead = (1, 1, COLS)
     return (

time: 226 us -> 226 us (level)
  starting transfers between devices: 48.3 us -> 87.9 us
  waiting for transfers between devices: 94.9 us -> 66.8 us
  between operations: 14.2 us -> 0.9 us
  Pallas kernels: 44.8 us -> 50.5 us
  local copies, waits for them, and re-layouts: 21.4 us -> 16.9 us
    all_gather x1 -> x0, waiting for transfers between devices: 44.5 us -> none  [shards(): lax.all_gather(own_rows.reshape(chips * rows_of, DH), ('x', 'y'), axis=0,...]
    ppermute x6 -> x12, waiting for transfers between devices: 28.5 us -> 53.4 us  [along(): return lax.ppermute(tensor, axis, [(i, (i + step) % 4) for i in range(4)])]
    ppermute x0 -> x7, starting transfers between devices: none -> 23.8 us  [along_z(): return lax.ppermute(tensor, ('zl', 'zh'), turns)]
    all_to_all x5, waiting for transfers between devices: 18.2 us -> 10.1 us  [exchange(): return lax.all_to_all(tensor, axes, split_axis=0, concat_axis=0, tiled=True)]
    ppermute x6 -> x12, starting transfers between devices: 8.83 us -> 16.7 us  [along(): return lax.ppermute(tensor, axis, [(i, (i + step) % 4) for i in range(4)])]
    all_to_all x5, starting transfers between devices: 35.5 us -> 40.4 us  [exchange(): return lax.all_to_all(tensor, axes, split_axis=0, concat_axis=0, tiled=True)]
    unnamed x42 -> x44, local copies, waits for them, and re-layouts: 17.5 us -> 13 us
    pallas_call x0 -> x4, Pallas kernels: none -> 3.82 us  [the longest x2 2.62 us: gather_of(): pl.pallas_call(functools.partial(gather_kernel, index, pieces), out_shape...]
  transfers between devices with their start and end apart: 16 -> 29, of which waited for: 9 -> 15; matrix products, arithmetic and copies ran while one was open for 1% -> 1% of each run, Pallas kernels for 19% -> 17%
where the time goes in v4:
time: 226 us; the launch traced here: 224 us
  starting transfers between devices  87.9 us (39%)
  waiting for transfers between devices  66.8 us (30%)
  Pallas kernels  50.5 us (22%)
  local copies, waits for them, and re-layouts  16.9 us (7%)
    ppermute x12, waiting for transfers between devices, along(): return lax.ppermute(tensor, axis, [(i, (i + step) % 4) for i in range(4)])  53.4 us
    all_to_all x5, starting transfers between devices, exchange(): return lax.all_to_all(tensor, axes, split_axis=0, concat_axis=0, tiled=True)  40.4 us
    ppermute x7, starting transfers between devices, along_z(): return lax.ppermute(tensor, ('zl', 'zh'), turns)  23.8 us
    ppermute x12, starting transfers between devices, along(): return lax.ppermute(tensor, axis, [(i, (i + step) % 4) for i in range(4)])  16.7 us
    unnamed x44, local copies, waits for them, and re-layouts  13 us
    all_to_all x5, waiting for transfers between devices, exchange(): return lax.all_to_all(tensor, axes, split_axis=0, concat_axis=0, tiled=True)  10.1 us
    pallas_call x1, Pallas kernels, row_backward(): pl.pallas_call(row_backward_kernel, grid=(1,), out_shape=(whole, whole, w...  9.16 us
    pallas_call x1, Pallas kernels, weight_grad_of(): pl.pallas_call(weight_grad_kernel, grid_spec=pltpu.PrefetchScalarGridSpec...  7.27 us
  transfers between devices with their start and end apart: 29, of which 15 were waited for; matrix products, arithmetic and copies ran while one was open for 1% of the time, Pallas kernels for 17%

profile of v4, /device:TPU:1, one launch (start us, length us, event | category | flops | bytes accessed | tf_op | source)
XLA Modules:
  0.0 223.7 jit_solution(18436195388457286451)
XLA Ops:
  2.1 10.0 %all-to-all-start = ((bf16[16,4,1024]{2,1,0:T(4,128)(2,1)}), bf16[16,4,1024]{2,1,0:T(4,128)(2,1)S(1)}, u32[]{:S(2)}, u32[]{:S(2)}) async-start(bf16[16,4,1024]{2,1,0:T(4,128)(2,1)} %bitcast.6), calls=%async_computation | async-start | bytes 262144 | tf_op jit(solution)/shard_map/all_to_all | solution.py:481
  16.4 2.4 %pack.1 = bf16[512,1536]{1,0:T(8,128)(2,1)} custom-call(s32[4]{0:T(128)S(1)} %copy-done.17, bf16[512,1024]{1,0:T(8,128)(2,1)S(1)} %bitcast.30, bf16[512,1024]{1,0:T(8,128)(2,1)S(1)} %bitcast.33, bf16[512,1024]{1,0:T(8,128)(2,1)S(1)} %bitcast.36), custom_call_target="tpu_custom_call" | custom-call | flops 536870912 | bytes 3145728 | tf_op jit(solution)/shard_map/pack/pallas_call | solution.py:79
  18.8 2.4 %all-to-all-done = bf16[16,4,1024]{2,1,0:T(4,128)(2,1)S(1)} async-done(((bf16[16,4,1024]{2,1,0:T(4,128)(2,1)}), bf16[16,4,1024]{2,1,0:T(4,128)(2,1)S(1)}, u32[]{:S(2)}, u32[]{:S(2)}) %all-to-all-start) | async-done | bytes 131104 | tf_op jit(solution)/shard_map/all_to_all | solution.py:481
  21.2 7.6 %all-to-all-start.1 = ((bf16[32,16,1536]{2,1,0:T(8,128)(2,1)}), bf16[32,16,1536]{2,1,0:T(8,128)(2,1)S(1)}, u32[]{:S(2)}, u32[]{:S(2)}) async-start(bf16[32,16,1536]{2,1,0:T(8,128)(2,1)} %bitcast.42), calls=%async_computation.1 | async-start | bytes 3145728 | tf_op jit(solution)/shard_map/all_to_all | solution.py:481
  28.9 2.4 %dynamic-slice_bitcast_fusion = bf16[512,1024]{1,0:T(8,128)(2,1)} fusion(bf16[1,1,512,2048]{3,2,1,0:T(8,128)(2,1)} %param.11, s32[]{:T(128)S(6)} %select_n.15), kind=kLoop, calls=%fused_computation | loop fusion | bytes 2097156 | tf_op jit(solution)/shard_map/dynamic_slice | solution.py:520
  31.5 2.8 %collective-permute-start.4 = (bf16[64,1024]{1,0:T(8,128)(2,1)S(1)}, bf16[64,1024]{1,0:T(8,128)(2,1)S(1)}, u32[]{:S(2)}, u32[]{:S(2)}) collective-permute-start(bf16[64,1024]{1,0:T(8,128)(2,1)S(1)} %reshape.77.own_ref), channel_id=1, source_target_pairs={{0,24},{8,0},{16,8},{24,16},{1,25},{9,1},{17,9},{25,17},{2,26},{10... | collective-permute-start | bytes 393224 | tf_op jit(solution)/shard_map/ppermute | solution.py:493
  35.5 3.8 %collective-permute-done.4.c_ref = bf16[64,1024]{1,0:T(8,128)(2,1)S(1)} collective-permute-done((bf16[64,1024]{1,0:T(8,128)(2,1)S(1)}, bf16[64,1024]{1,0:T(8,128)(2,1)S(1)}, u32[]{:S(2)}, u32[]{:S(2)}) %collective-permute-start.4) | collective-permute-done | bytes 131104 | tf_op jit(solution)/shard_map/ppermute | solution.py:493
  41.1 4.7 %collective-permute-done.2.a_ref = bf16[64,1024]{1,0:T(8,128)(2,1)S(1)} collective-permute-done((bf16[64,1024]{1,0:T(8,128)(2,1)S(1)}, bf16[64,1024]{1,0:T(8,128)(2,1)S(1)}, u32[]{:S(2)}, u32[]{:S(2)}) %collective-permute-start.2) | collective-permute-done | bytes 131104 | tf_op jit(solution)/shard_map/ppermute | solution.py:493
  46.4 2.5 %collective-permute-start.7 = (bf16[256,1024]{1,0:T(8,128)(2,1)S(1)}, bf16[256,1024]{1,0:T(8,128)(2,1)S(1)}, u32[]{:S(2)}, u32[]{:S(2)}) collective-permute-start(bf16[256,1024]{1,0:T(8,128)(2,1)S(1)} %gather_y.1.own_ref), channel_id=1, source_target_pairs={{0,192},{64,0},{128,64},{192,128},{1,193},{65,1},{129,65},{193,129... | collective-permute-start | bytes 1572872 | tf_op jit(solution)/shard_map/ppermute | solution.py:493
  56.1 4.4 %collective-permute-done.7.c_ref = bf16[256,1024]{1,0:T(8,128)(2,1)S(1)} collective-permute-done((bf16[256,1024]{1,0:T(8,128)(2,1)S(1)}, bf16[256,1024]{1,0:T(8,128)(2,1)S(1)}, u32[]{:S(2)}, u32[]{:S(2)}) %collective-permute-start.7) | collective-permute-done | bytes 524320 | tf_op jit(solution)/shard_map/ppermute | solution.py:493
  60.5 2.7 %collective-permute-done.6.b_ref = bf16[256,1024]{1,0:T(8,128)(2,1)S(1)} collective-permute-done((bf16[256,1024]{1,0:T(8,128)(2,1)S(1)}, bf16[256,1024]{1,0:T(8,128)(2,1)S(1)}, u32[]{:S(2)}, u32[]{:S(2)}) %collective-permute-start.6) | collective-permute-done | bytes 524320 | tf_op jit(solution)/shard_map/ppermute | solution.py:493
  63.2 12.3 %collective-permute-done.5.a_ref = bf16[256,1024]{1,0:T(8,128)(2,1)S(1)} collective-permute-done((bf16[256,1024]{1,0:T(8,128)(2,1)S(1)}, bf16[256,1024]{1,0:T(8,128)(2,1)S(1)}, u32[]{:S(2)}, u32[]{:S(2)}) %collective-permute-start.5) | collective-permute-done | bytes 524320 | tf_op jit(solution)/shard_map/ppermute | solution.py:493
  77.6 3.1 %column_forward.1 = bf16[32,2,8,512]{3,2,1,0:T(8,128)(2,1)} custom-call(bf16[32,2,8,1536]{3,2,1,0:T(8,128)(2,1)S(1)} %bitcast.25), custom_call_target="tpu_custom_call" | custom-call | flops 268435456 | bytes 2097152 | tf_op jit(solution)/shard_map/column_forward/pallas_call | solution.py:130
  81.2 7.5 %all-to-all-start.2 = ((bf16[32,16,512]{2,1,0:T(8,128)(2,1)}), bf16[32,16,512]{2,1,0:T(8,128)(2,1)}, u32[]{:S(2)}, u32[]{:S(2)}) async-start(bf16[32,16,512]{2,1,0:T(8,128)(2,1)} %bitcast.13), calls=%async_computation.2 | async-start | bytes 1048576 | tf_op jit(solution)/shard_map/all_to_all | solution.py:481
  90.2 5.5 %attn_grad.1 = (bf16[512,512]{1,0:T(8,128)(2,1)S(1)}, bf16[512,512]{1,0:T(8,128)(2,1)S(1)}) custom-call(s32[5]{0:T(128)S(1)} %stack.23.place.core_ref, bf16[512,2048]{1,0:T(8,128)(2,1)S(1)} %bitcast.28, bf16[512,2048]{1,0:T(8,128)(2,1)S(1)} %bitcast.29, bf16[1024,1024]{1,0:T(8,128)(2,1)} %gather_x.1.mine_ref, ...), custom_call_target="tpu_custom_call" | custom-call | flops 2147483648 | bytes 7340032 | tf_op jit(solution)/shard_map/attn_grad/pallas_call | solution.py:277
  97.4 7.8 %all-to-all-done.2 = bf16[32,16,512]{2,1,0:T(8,128)(2,1)} async-done(((bf16[32,16,512]{2,1,0:T(8,128)(2,1)}), bf16[32,16,512]{2,1,0:T(8,128)(2,1)}, u32[]{:S(2)}, u32[]{:S(2)}) %all-to-all-start.2) | async-done | bytes 524320 | tf_op jit(solution)/shard_map/all_to_all | solution.py:481
  106.5 4.7 %all-to-all-start.3 = ((bf16[32,16,512]{2,1,0:T(8,128)(2,1)}), bf16[32,16,512]{2,1,0:T(8,128)(2,1)S(1)}, u32[]{:S(2)}, u32[]{:S(2)}) async-start(bf16[32,16,512]{2,1,0:T(8,128)(2,1)} %bitcast.41), calls=%async_computation.3 | async-start | bytes 1048576 | tf_op jit(solution)/shard_map/all_to_all | solution.py:481
  113.4 7.3 %weight_grad.1 = (f32[256,1024]{1,0:T(8,128)}, bf16[256,1024]{1,0:T(8,128)(2,1)}, bf16[256,1024]{1,0:T(8,128)(2,1)S(1)}, bf16[256,1024]{1,0:T(8,128)(2,1)}) custom-call(s32[5]{0:T(128)S(1)} %stack.23.place.core_ref, bf16[512,512]{1,0:T(8,128)(2,1)S(1)} %copy-done.11, bf16[512,512]{1,0:T(8,128)(2,1)S(1)} %copy-done.20, ...), custom_call_target="tpu_custom_call" | custom-call | flops 2147483648 | bytes 7340032 | tf_op jit(solution)/shard_map/weight_grad/pallas_call | solution.py:363
  121.5 2.7 %collective-permute-start.11 = (bf16[256,1024]{1,0:T(8,128)(2,1)}, bf16[256,1024]{1,0:T(8,128)(2,1)}, u32[]{:S(2)}, u32[]{:S(2)}) collective-permute-start(bf16[256,1024]{1,0:T(8,128)(2,1)} %get-tuple-element.65), channel_id=1, source_target_pairs={{0,192},{64,0},{128,64},{192,128},{1,193},{65,1},{129,65},{193,129... | collective-permute-start | bytes 1572872 | tf_op jit(solution)/shard_map/ppermute | solution.py:493
  124.2 9.2 %row_backward.1 = (bf16[512,1024]{1,0:T(8,128)(2,1)}, bf16[512,1024]{1,0:T(8,128)(2,1)}, bf16[512,1024]{1,0:T(8,128)(2,1)}) custom-call(s32[4,4]{1,0:T(4,128)S(1)} %copy-done.16, bf16[512,1024]{1,0:T(8,128)(2,1)S(1)} %bitcast.32, bf16[512,1024]{1,0:T(8,128)(2,1)S(1)} %bitcast.35, bf16[512,1024]{1,0:T(8,128)(2,1)S(1)} %bitcast.38, bf16[512,512]{1,0:T(8,128)(2,1)S(1)} %copy-done.14), custom_call_target="tpu_custom_call" | custom-call | flops 671088640 | bytes 3670016 | tf_op jit(solution)/shard_map/row_backward/pallas_call | solution.py:222
  133.4 3.0 %collective-permute-done.10.b_ref = bf16[256,1024]{1,0:T(8,128)(2,1)} collective-permute-done((bf16[256,1024]{1,0:T(8,128)(2,1)}, bf16[256,1024]{1,0:T(8,128)(2,1)}, u32[]{:S(2)}, u32[]{:S(2)}) %collective-permute-start.10) | collective-permute-done | bytes 524320 | tf_op jit(solution)/shard_map/ppermute | solution.py:493
  136.3 6.3 %column_backward.1 = bf16[32,2,8,1536]{3,2,1,0:T(8,128)(2,1)} custom-call(bf16[32,2,8,1536]{3,2,1,0:T(8,128)(2,1)S(1)} %bitcast.26, bf16[32,2,8,512]{3,2,1,0:T(8,128)(2,1)S(1)} %bitcast.40), custom_call_target="tpu_custom_call" | custom-call | flops 671088640 | bytes 3670016 | tf_op jit(solution)/shard_map/column_backward/pallas_call | solution.py:156
  142.7 10.6 %all-to-all-start.4 = ((bf16[32,16,1536]{2,1,0:T(8,128)(2,1)}), bf16[32,16,1536]{2,1,0:T(8,128)(2,1)S(1)}, u32[]{:S(2)}, u32[]{:S(2)}) async-start(bf16[32,16,1536]{2,1,0:T(8,128)(2,1)} %bitcast.19), calls=%async_computation.4 | async-start | bytes 3145728 | tf_op jit(solution)/shard_map/all_to_all | solution.py:481
  154.6 13.8 %collective-permute-done.12.c_ref = bf16[256,1024]{1,0:T(8,128)(2,1)S(1)} collective-permute-done((bf16[256,1024]{1,0:T(8,128)(2,1)}, bf16[256,1024]{1,0:T(8,128)(2,1)S(1)}, u32[]{:S(2)}, u32[]{:S(2)}) %collective-permute-start.12) | collective-permute-done | bytes 524320 | tf_op jit(solution)/shard_map/ppermute | solution.py:493
  171.4 2.4 %collective-permute-start.14 = (bf16[64,1024]{1,0:T(8,128)(2,1)S(1)}, bf16[64,1024]{1,0:T(8,128)(2,1)S(1)}, u32[]{:S(2)}, u32[]{:S(2)}) collective-permute-start(bf16[64,1024]{1,0:T(8,128)(2,1)S(1)} %get-tuple-element.79), channel_id=1, source_target_pairs={{0,16},{8,24},{16,0},{24,8},{1,17},{9,25},{17,1},{25,9},{2,18},{10... | collective-permute-start | bytes 393224 | tf_op jit(solution)/shard_map/ppermute | solution.py:493
  176.7 5.2 %collective-permute-done.14.c_ref = bf16[64,1024]{1,0:T(8,128)(2,1)S(1)} collective-permute-done((bf16[64,1024]{1,0:T(8,128)(2,1)S(1)}, bf16[64,1024]{1,0:T(8,128)(2,1)S(1)}, u32[]{:S(2)}, u32[]{:S(2)}) %collective-permute-start.14) | collective-permute-done | bytes 131104 | tf_op jit(solution)/shard_map/ppermute | solution.py:493
  182.6 2.3 %collective-permute-start.16 = (bf16[8,1024]{1,0:T(8,128)(2,1)S(1)}, bf16[8,1024]{1,0:T(8,128)(2,1)S(1)}, u32[]{:S(2)}, u32[]{:S(2)}) collective-permute-start(bf16[8,1024]{1,0:T(8,128)(2,1)S(1)} %get-tuple-element.82), channel_id=1, source_target_pairs={{0,2},{2,4},{4,6},{6,0},{32,34},{34,36},{36,38},{38,32},{1,3},{3,5... | collective-permute-start | bytes 49160 | tf_op jit(solution)/shard_map/ppermute | solution.py:498
  184.9 4.2 %collective-permute-start.17 = (bf16[8,1024]{1,0:T(8,128)(2,1)S(1)}, bf16[8,1024]{1,0:T(8,128)(2,1)S(1)}, u32[]{:S(2)}, u32[]{:S(2)}) collective-permute-start(bf16[8,1024]{1,0:T(8,128)(2,1)S(1)} %get-tuple-element.83), channel_id=1, source_target_pairs={{0,4},{2,6},{4,0},{6,2},{32,36},{34,38},{36,32},{38,34},{1,5},{3,7... | collective-permute-start | bytes 49160 | tf_op jit(solution)/shard_map/ppermute | solution.py:498
  190.8 12.3 %collective-permute-start.19 = (bf16[8,1024]{1,0:T(8,128)(2,1)S(1)}, bf16[8,1024]{1,0:T(8,128)(2,1)S(1)}, u32[]{:S(2)}, u32[]{:S(2)}) collective-permute-start(bf16[8,1024]{1,0:T(8,128)(2,1)S(1)} %get-tuple-element.85), channel_id=1, source_target_pairs={{0,32},{2,34},{4,36},{6,38},{32,0},{34,2},{36,4},{38,6},{1,33},{3,... | collective-permute-start | bytes 49160 | tf_op jit(solution)/shard_map/ppermute | solution.py:498
  210.2 3.6 %collective-permute-start.23 = (f32[4,1024]{1,0:T(4,128)S(1)}, f32[4,1024]{1,0:T(4,128)S(1)}, u32[]{:S(2)}, u32[]{:S(2)}) collective-permute-start(f32[4,1024]{1,0:T(4,128)S(1)} %get-tuple-element.90), channel_id=1, source_target_pairs={{0,1},{1,0},{2,3},{3,2},{4,5},{5,4},{6,7},{7,6},{8,9},{9,8},{10,11... | collective-permute-start | bytes 49160 | tf_op jit(solution)/shard_map/ppermute | solution.py:485
  213.8 6.7 %layer_out.1 = bf16[512,2048]{1,0:T(8,128)(2,1)} custom-call(s32[5]{0:T(128)S(1)} %stack.23.place.core_ref, bf16[512,512]{1,0:T(8,128)(2,1)S(1)} %copy-done.12, bf16[512,512]{1,0:T(8,128)(2,1)} %bitcast.15.col_ref.col_mine, bf16[1024,1024]{1,0:T(8,128)(2,1)} %gather_x.1.mine_ref, bf16[1024,1024]{1,0:T(8,128)(2,1)} %collective-permute-done.8.theirs_ref), custom_call_target="tpu_custom_call" | custom-call | flops 2147483648 | bytes 7340032 | tf_op jit(solution)/shard_map/layer_out/pallas_call | solution.py:317
  221.1 2.6 %finish.1 = (bf16[512,1024]{1,0:T(8,128)(2,1)}, bf16[512,1024]{1,0:T(8,128)(2,1)}, bf16[512,1024]{1,0:T(8,128)(2,1)}) custom-call(s32[4]{0:T(128)S(1)} %copy-done.18, bf16[512,1536]{1,0:T(8,128)(2,1)S(1)} %bitcast.39, bf16[512,1024]{1,0:T(8,128)(2,1)} %get-tuple-element.67.dq_in, ...), custom_call_target="tpu_custom_call", output_to_operand_aliasing={{0}: (2, {}), {1}: (3, {}), {2}: (4, {})} | custom-call | flops 536870912 | bytes 3145728 | tf_op jit(solution)/shard_map/finish/pallas_call | solution.py:248
  (92 shorter events, 44.1 us)
Async XLA Ops:
  2.1 19.1 %all-to-all-start = ((bf16[16,4,1024]{2,1,0:T(4,128)(2,1)}), bf16[16,4,1024]{2,1,0:T(4,128)(2,1)S(1)}, u32[]{:S(2)}, u32[]{:S(2)}) async-start(bf16[16,4,1024]{2,1,0:T(4,128)(2,1)} %bitcast.6), calls=%async_computation | async-start | bytes 262144 | tf_op jit(solution)/shard_map/all_to_all | solution.py:481
  21.2 56.3 %all-to-all-start.1 = ((bf16[32,16,1536]{2,1,0:T(8,128)(2,1)}), bf16[32,16,1536]{2,1,0:T(8,128)(2,1)S(1)}, u32[]{:S(2)}, u32[]{:S(2)}) async-start(bf16[32,16,1536]{2,1,0:T(8,128)(2,1)} %bitcast.42), calls=%async_computation.1 | async-start | bytes 3145728 | tf_op jit(solution)/shard_map/all_to_all | solution.py:481
  31.2 46.3 %collective-permute-start.1 = (bf16[512,1024]{1,0:T(8,128)(2,1)}, bf16[512,1024]{1,0:T(8,128)(2,1)}, u32[]{:S(2)}, u32[]{:S(2)}) collective-permute-start(bf16[512,1024]{1,0:T(8,128)(2,1)} %dynamic-slice_bitcast_fusion), channel_id=1, source_target_pairs={{0,1},{1,0},{2,3},{3,2},{4,5},{5,4},{6,7},{7,6},{8,9},{9,8},{10,11... | collective-permute-start | bytes 3145736 | tf_op jit(solution)/shard_map/ppermute | solution.py:485
  31.5 7.8 %collective-permute-start.4 = (bf16[64,1024]{1,0:T(8,128)(2,1)S(1)}, bf16[64,1024]{1,0:T(8,128)(2,1)S(1)}, u32[]{:S(2)}, u32[]{:S(2)}) collective-permute-start(bf16[64,1024]{1,0:T(8,128)(2,1)S(1)} %reshape.77.own_ref), channel_id=1, source_target_pairs={{0,24},{8,0},{16,8},{24,16},{1,25},{9,1},{17,9},{25,17},{2,26},{10... | collective-permute-start | bytes 393224 | tf_op jit(solution)/shard_map/ppermute | solution.py:493
  34.3 6.7 %collective-permute-start.3 = (bf16[64,1024]{1,0:T(8,128)(2,1)S(1)}, bf16[64,1024]{1,0:T(8,128)(2,1)S(1)}, u32[]{:S(2)}, u32[]{:S(2)}) collective-permute-start(bf16[64,1024]{1,0:T(8,128)(2,1)S(1)} %reshape.77.own_ref), channel_id=1, source_target_pairs={{0,16},{8,24},{16,0},{24,8},{1,17},{9,25},{17,1},{25,9},{2,18},{10... | collective-permute-start | bytes 393224 | tf_op jit(solution)/shard_map/ppermute | solution.py:493
  34.9 10.9 %collective-permute-start.2 = (bf16[64,1024]{1,0:T(8,128)(2,1)S(1)}, bf16[64,1024]{1,0:T(8,128)(2,1)S(1)}, u32[]{:S(2)}, u32[]{:S(2)}) collective-permute-start(bf16[64,1024]{1,0:T(8,128)(2,1)S(1)} %reshape.77.own_ref), channel_id=1, source_target_pairs={{0,8},{8,16},{16,24},{24,0},{1,9},{9,17},{17,25},{25,1},{2,10},{10... | collective-permute-start | bytes 393224 | tf_op jit(solution)/shard_map/ppermute | solution.py:493
  46.4 14.1 %collective-permute-start.7 = (bf16[256,1024]{1,0:T(8,128)(2,1)S(1)}, bf16[256,1024]{1,0:T(8,128)(2,1)S(1)}, u32[]{:S(2)}, u32[]{:S(2)}) collective-permute-start(bf16[256,1024]{1,0:T(8,128)(2,1)S(1)} %gather_y.1.own_ref), channel_id=1, source_target_pairs={{0,192},{64,0},{128,64},{192,128},{1,193},{65,1},{129,65},{193,129... | collective-permute-start | bytes 1572872 | tf_op jit(solution)/shard_map/ppermute | solution.py:493
  48.9 14.3 %collective-permute-start.6 = (bf16[256,1024]{1,0:T(8,128)(2,1)S(1)}, bf16[256,1024]{1,0:T(8,128)(2,1)S(1)}, u32[]{:S(2)}, u32[]{:S(2)}) collective-permute-start(bf16[256,1024]{1,0:T(8,128)(2,1)S(1)} %gather_y.1.own_ref), channel_id=1, source_target_pairs={{0,128},{64,192},{128,0},{192,64},{1,129},{65,193},{129,1},{193,65... | collective-permute-start | bytes 1572872 | tf_op jit(solution)/shard_map/ppermute | solution.py:493
  49.4 26.1 %collective-permute-start.5 = (bf16[256,1024]{1,0:T(8,128)(2,1)S(1)}, bf16[256,1024]{1,0:T(8,128)(2,1)S(1)}, u32[]{:S(2)}, u32[]{:S(2)}) collective-permute-start(bf16[256,1024]{1,0:T(8,128)(2,1)S(1)} %gather_y.1.own_ref), channel_id=1, source_target_pairs={{0,64},{64,128},{128,192},{192,0},{1,65},{65,129},{129,193},{193,1... | collective-permute-start | bytes 1572872 | tf_op jit(solution)/shard_map/ppermute | solution.py:493
  54.7 22.8 %copy-start.10 = (bf16[512,512]{1,0:T(8,128)(2,1)}, bf16[512,512]{1,0:T(8,128)(2,1)S(1)}, u32[]{:S(2)}) copy-start(bf16[512,512]{1,0:T(8,128)(2,1)S(1)} %row_forward.1.row_ref.row_mine) | copy-start | bytes 1572868
  54.7 22.8 %collective-permute-start = (bf16[512,512]{1,0:T(8,128)(2,1)S(1)}, bf16[512,512]{1,0:T(8,128)(2,1)S(1)}, u32[]{:S(2)}, u32[]{:S(2)}) collective-permute-start(bf16[512,512]{1,0:T(8,128)(2,1)S(1)} %row_forward.1.row_ref.row_mine), channel_id=1, source_target_pairs={{0,1},{1,0},{2,3},{3,2},{4,5},{5,4},{6,7},{7,6},{8,9},{9,8},{10,11... | collective-permute-start | bytes 1572872 | tf_op jit(solution)/shard_map/ppermute | solution.py:485
  80.7 8.0 %collective-permute-start.8 = (bf16[1024,1024]{1,0:T(8,128)(2,1)}, bf16[1024,1024]{1,0:T(8,128)(2,1)}, u32[]{:S(2)}, u32[]{:S(2)}) collective-permute-start(bf16[1024,1024]{1,0:T(8,128)(2,1)} %gather_x.1.mine_ref), channel_id=1, source_target_pairs={{0,1},{1,0},{2,3},{3,2},{4,5},{5,4},{6,7},{7,6},{8,9},{9,8},{10,11... | collective-permute-start | bytes 6291464 | tf_op jit(solution)/shard_map/ppermute | solution.py:485
  81.2 24.0 %all-to-all-start.2 = ((bf16[32,16,512]{2,1,0:T(8,128)(2,1)}), bf16[32,16,512]{2,1,0:T(8,128)(2,1)}, u32[]{:S(2)}, u32[]{:S(2)}) async-start(bf16[32,16,512]{2,1,0:T(8,128)(2,1)} %bitcast.13), calls=%async_computation.2 | async-start | bytes 1048576 | tf_op jit(solution)/shard_map/all_to_all | solution.py:481
  105.1 6.1 %collective-permute-start.9 = (bf16[512,512]{1,0:T(8,128)(2,1)}, bf16[512,512]{1,0:T(8,128)(2,1)}, u32[]{:S(2)}, u32[]{:S(2)}) collective-permute-start(bf16[512,512]{1,0:T(8,128)(2,1)} %bitcast.15.col_ref.col_mine), channel_id=1, source_target_pairs={{0,1},{1,0},{2,3},{3,2},{4,5},{5,4},{6,7},{7,6},{8,9},{9,8},{10,11... | collective-permute-start | bytes 1572872 | tf_op jit(solution)/shard_map/ppermute | solution.py:485
  106.5 26.9 %all-to-all-start.3 = ((bf16[32,16,512]{2,1,0:T(8,128)(2,1)}), bf16[32,16,512]{2,1,0:T(8,128)(2,1)S(1)}, u32[]{:S(2)}, u32[]{:S(2)}) async-start(bf16[32,16,512]{2,1,0:T(8,128)(2,1)} %bitcast.41), calls=%async_computation.3 | async-start | bytes 1048576 | tf_op jit(solution)/shard_map/all_to_all | solution.py:481
  121.5 14.8 %collective-permute-start.10 = (bf16[256,1024]{1,0:T(8,128)(2,1)}, bf16[256,1024]{1,0:T(8,128)(2,1)}, u32[]{:S(2)}, u32[]{:S(2)}) collective-permute-start(bf16[256,1024]{1,0:T(8,128)(2,1)} %get-tuple-element.64), channel_id=1, source_target_pairs={{0,64},{64,128},{128,192},{192,0},{1,65},{65,129},{129,193},{193,1... | collective-permute-start | bytes 1572872 | tf_op jit(solution)/shard_map/ppermute | solution.py:493
  121.5 14.8 %collective-permute-start.11 = (bf16[256,1024]{1,0:T(8,128)(2,1)}, bf16[256,1024]{1,0:T(8,128)(2,1)}, u32[]{:S(2)}, u32[]{:S(2)}) collective-permute-start(bf16[256,1024]{1,0:T(8,128)(2,1)} %get-tuple-element.65), channel_id=1, source_target_pairs={{0,192},{64,0},{128,64},{192,128},{1,193},{65,1},{129,65},{193,129... | collective-permute-start | bytes 1572872 | tf_op jit(solution)/shard_map/ppermute | solution.py:493
  142.7 25.7 %copy-start.9 = (f32[256,1024]{1,0:T(8,128)S(1)}, f32[256,1024]{1,0:T(8,128)}, u32[]{:S(2)}) copy-start(f32[256,1024]{1,0:T(8,128)} %get-tuple-element.73.a_ref) | copy-start | bytes 3145732
  142.7 78.4 %all-to-all-start.4 = ((bf16[32,16,1536]{2,1,0:T(8,128)(2,1)}), bf16[32,16,1536]{2,1,0:T(8,128)(2,1)S(1)}, u32[]{:S(2)}, u32[]{:S(2)}) async-start(bf16[32,16,1536]{2,1,0:T(8,128)(2,1)} %bitcast.19), calls=%async_computation.4 | async-start | bytes 3145728 | tf_op jit(solution)/shard_map/all_to_all | solution.py:481
  153.3 60.5 %copy-start.12 = (bf16[512,512]{1,0:T(8,128)(2,1)S(1)}, bf16[512,512]{1,0:T(8,128)(2,1)}, u32[]{:S(2)}) copy-start(bf16[512,512]{1,0:T(8,128)(2,1)} %copy-done.10) | copy-start | bytes 1572868
  153.3 15.1 %collective-permute-start.12 = (bf16[256,1024]{1,0:T(8,128)(2,1)}, bf16[256,1024]{1,0:T(8,128)(2,1)S(1)}, u32[]{:S(2)}, u32[]{:S(2)}) collective-permute-start(bf16[256,1024]{1,0:T(8,128)(2,1)} %copy-done.21), channel_id=1, source_target_pairs={{0,128},{64,192},{128,0},{192,64},{1,129},{65,193},{129,1},{193,65... | collective-permute-start | bytes 1572872 | tf_op jit(solution)/shard_map/ppermute | solution.py:493
  169.8 6.9 %collective-permute-start.13 = (bf16[64,1024]{1,0:T(8,128)(2,1)S(1)}, bf16[64,1024]{1,0:T(8,128)(2,1)S(1)}, u32[]{:S(2)}, u32[]{:S(2)}) collective-permute-start(bf16[64,1024]{1,0:T(8,128)(2,1)S(1)} %get-tuple-element.78), channel_id=1, source_target_pairs={{0,8},{8,16},{16,24},{24,0},{1,9},{9,17},{17,25},{25,1},{2,10},{10... | collective-permute-start | bytes 393224 | tf_op jit(solution)/shard_map/ppermute | solution.py:493
  171.4 10.5 %collective-permute-start.14 = (bf16[64,1024]{1,0:T(8,128)(2,1)S(1)}, bf16[64,1024]{1,0:T(8,128)(2,1)S(1)}, u32[]{:S(2)}, u32[]{:S(2)}) collective-permute-start(bf16[64,1024]{1,0:T(8,128)(2,1)S(1)} %get-tuple-element.79), channel_id=1, source_target_pairs={{0,16},{8,24},{16,0},{24,8},{1,17},{9,25},{17,1},{25,9},{2,18},{10... | collective-permute-start | bytes 393224 | tf_op jit(solution)/shard_map/ppermute | solution.py:493
  173.8 8.1 %collective-permute-start.15 = (bf16[64,1024]{1,0:T(8,128)(2,1)S(1)}, bf16[64,1024]{1,0:T(8,128)(2,1)S(1)}, u32[]{:S(2)}, u32[]{:S(2)}) collective-permute-start(bf16[64,1024]{1,0:T(8,128)(2,1)S(1)} %get-tuple-element.80), channel_id=1, source_target_pairs={{0,24},{8,0},{16,8},{24,16},{1,25},{9,1},{17,9},{25,17},{2,26},{10... | collective-permute-start | bytes 393224 | tf_op jit(solution)/shard_map/ppermute | solution.py:493
  182.6 20.6 %collective-permute-start.16 = (bf16[8,1024]{1,0:T(8,128)(2,1)S(1)}, bf16[8,1024]{1,0:T(8,128)(2,1)S(1)}, u32[]{:S(2)}, u32[]{:S(2)}) collective-permute-start(bf16[8,1024]{1,0:T(8,128)(2,1)S(1)} %get-tuple-element.82), channel_id=1, source_target_pairs={{0,2},{2,4},{4,6},{6,0},{32,34},{34,36},{36,38},{38,32},{1,3},{3,5... | collective-permute-start | bytes 49160 | tf_op jit(solution)/shard_map/ppermute | solution.py:498
  184.9 20.1 %collective-permute-start.17 = (bf16[8,1024]{1,0:T(8,128)(2,1)S(1)}, bf16[8,1024]{1,0:T(8,128)(2,1)S(1)}, u32[]{:S(2)}, u32[]{:S(2)}) collective-permute-start(bf16[8,1024]{1,0:T(8,128)(2,1)S(1)} %get-tuple-element.83), channel_id=1, source_target_pairs={{0,4},{2,6},{4,0},{6,2},{32,36},{34,38},{36,32},{38,34},{1,5},{3,7... | collective-permute-start | bytes 49160 | tf_op jit(solution)/shard_map/ppermute | solution.py:498
  189.0 17.3 %collective-permute-start.18 = (bf16[8,1024]{1,0:T(8,128)(2,1)S(1)}, bf16[8,1024]{1,0:T(8,128)(2,1)S(1)}, u32[]{:S(2)}, u32[]{:S(2)}) collective-permute-start(bf16[8,1024]{1,0:T(8,128)(2,1)S(1)} %get-tuple-element.84), channel_id=1, source_target_pairs={{0,6},{2,0},{4,2},{6,4},{32,38},{34,32},{36,34},{38,36},{1,7},{3,1... | collective-permute-start | bytes 49160 | tf_op jit(solution)/shard_map/ppermute | solution.py:498
  190.8 15.6 %collective-permute-start.19 = (bf16[8,1024]{1,0:T(8,128)(2,1)S(1)}, bf16[8,1024]{1,0:T(8,128)(2,1)S(1)}, u32[]{:S(2)}, u32[]{:S(2)}) collective-permute-start(bf16[8,1024]{1,0:T(8,128)(2,1)S(1)} %get-tuple-element.85), channel_id=1, source_target_pairs={{0,32},{2,34},{4,36},{6,38},{32,0},{34,2},{36,4},{38,6},{1,33},{3,... | collective-permute-start | bytes 49160 | tf_op jit(solution)/shard_map/ppermute | solution.py:498
  203.1 3.8 %collective-permute-start.20 = (bf16[8,1024]{1,0:T(8,128)(2,1)S(1)}, bf16[8,1024]{1,0:T(8,128)(2,1)S(1)}, u32[]{:S(2)}, u32[]{:S(2)}) collective-permute-start(bf16[8,1024]{1,0:T(8,128)(2,1)S(1)} %get-tuple-element.86), channel_id=1, source_target_pairs={{0,34},{2,36},{4,38},{6,32},{32,2},{34,4},{36,6},{38,0},{1,35},{3,... | collective-permute-start | bytes 49160 | tf_op jit(solution)/shard_map/ppermute | solution.py:498
  203.1 5.7 %collective-permute-start.21 = (bf16[8,1024]{1,0:T(8,128)(2,1)S(1)}, bf16[8,1024]{1,0:T(8,128)(2,1)S(1)}, u32[]{:S(2)}, u32[]{:S(2)}) collective-permute-start(bf16[8,1024]{1,0:T(8,128)(2,1)S(1)} %get-tuple-element.87), channel_id=1, source_target_pairs={{0,36},{2,38},{4,32},{6,34},{32,4},{34,6},{36,0},{38,2},{1,37},{3,... | collective-permute-start | bytes 49160 | tf_op jit(solution)/shard_map/ppermute | solution.py:498
  205.0 4.6 %collective-permute-start.22 = (bf16[8,1024]{1,0:T(8,128)(2,1)S(1)}, bf16[8,1024]{1,0:T(8,128)(2,1)S(1)}, u32[]{:S(2)}, u32[]{:S(2)}) collective-permute-start(bf16[8,1024]{1,0:T(8,128)(2,1)S(1)} %get-tuple-element.88), channel_id=1, source_target_pairs={{0,38},{2,32},{4,34},{6,36},{32,6},{34,0},{36,2},{38,4},{1,39},{3,... | collective-permute-start | bytes 49160 | tf_op jit(solution)/shard_map/ppermute | solution.py:498
  210.2 10.2 %collective-permute-start.23 = (f32[4,1024]{1,0:T(4,128)S(1)}, f32[4,1024]{1,0:T(4,128)S(1)}, u32[]{:S(2)}, u32[]{:S(2)}) collective-permute-start(f32[4,1024]{1,0:T(4,128)S(1)} %get-tuple-element.90), channel_id=1, source_target_pairs={{0,1},{1,0},{2,3},{3,2},{4,5},{5,4},{6,7},{7,6},{8,9},{9,8},{10,11... | collective-permute-start | bytes 49160 | tf_op jit(solution)/shard_map/ppermute | solution.py:485
  (19 other events, 121.3 us)

commit v5 on v4

--- a/solution.py
+++ b/solution.py
@@ -134,7 +134,7 @@
         in_specs=[group_block(3 * HALF)],
         out_specs=group_block(HALF),
         compiler_params=params(),
-        cost_estimate=cost(8 * 4 * TILE * TILE * HD, 4 * COLS * HALF * 2, 8 * TILE * TILE),
+        cost_estimate=cost(10**11, 4 * COLS * HALF * 2, 8 * TILE * TILE),
         name="column_forward",
     )(received)
 
@@ -383,25 +383,25 @@
     )(place, row_mine, row_theirs, col_mine, col_theirs, og, og_theirs)
 
 
-def gather_kernel(axis, pieces, place, own_ref, a_ref, b_ref, c_ref, o_ref):
-    chunk = own_ref.shape[0] // pieces
+def gather_kernel(place, own_ref, a_ref, b_ref, c_ref, o_ref):
+    chunk = own_ref.shape[0] // 2
     for step, ref in enumerate((own_ref, a_ref, b_ref, c_ref)):
-        source = lax.rem(place[axis] + 4 - step, 4)
-        for piece in range(pieces):
-            rows = pl.ds(pl.multiple_of((piece * 4 + source) * chunk, chunk), chunk)
-            o_ref[rows, :] = ref[piece * chunk : (piece + 1) * chunk, :]
-
-
-def gather_of(own, place, axis, index, pieces):
-    blocks = [own] + [along(own, axis, step) for step in (1, 2, 3)]
-    return pl.pallas_call(
-        functools.partial(gather_kernel, index, pieces),
+        source = lax.rem(place[3] + 4 - step, 4)
+        for at_z in range(2):
+            rows = pl.ds(pl.multiple_of((at_z * 4 + source) * chunk, chunk), chunk)
+            o_ref[rows, :] = ref[at_z * chunk : (at_z + 1) * chunk, :]
+
+
+def gather_y(own, place):
+    blocks = [own] + [along(own, "y", step) for step in (1, 2, 3)]
+    return pl.pallas_call(
+        gather_kernel,
         out_shape=jax.ShapeDtypeStruct((4 * own.shape[0], DH), BF),
         in_specs=[SMEM_SPEC] + [VMEM_SPEC] * 4,
         out_specs=VMEM_SPEC,
         compiler_params=params(),
-        cost_estimate=cost(0, 16 * own.shape[0] * DH),
-        name="gather_" + axis,
+        cost_estimate=cost(0, 2**20),
+        name="gather_y",
     )(place, *blocks)
 
 
@@ -512,37 +512,38 @@
     spread = jnp.broadcast_to(halves[None], (near // 2, 2, rows_of, DH)).reshape(near, rows_of, DH)
     own_rows = exchange(spread, NEAR)
     packed = pack(q, k, v, col_offset)
-    own_rows, packed = together(own_rows, packed)
+    og_sent = lax.dynamic_slice(og, (0, (1 - core) * DH), (COLS, DH))
+    own_rows, packed, og_sent = together(own_rows, packed, og_sent)
     own_rows = own_rows.reshape(near * rows_of, DH)
-    mine = gather_of(gather_of(own_rows, place, "y", 3, 2), place, "x", 1, 1)
+    mine = lax.all_gather(gather_y(own_rows, place), "x", axis=0, tiled=True)
 
     received = exchange(packed.reshape(seq, COLS // seq, 3 * HALF), SEQ)
-    og_sent = lax.dynamic_slice(og, (0, (1 - core) * DH), (COLS, DH))
-    og_theirs = other_core(og_sent)
     row_out = row_forward(q, k, v, block_pattern)
     row_theirs = other_core(row_out)
-    received, row_out, row_theirs, og_theirs = together(received, row_out, row_theirs, og_theirs)
     received = received.reshape(ROWS, 2, GRP, 3 * HALF)
 
     col_sent = column_forward(received).reshape(seq, COLS // seq, HALF)
-    col_sent, mine = together(col_sent, mine)
+    col_sent, mine, row_out, row_theirs = together(col_sent, mine, row_out, row_theirs)
     col_mine = exchange(col_sent, SEQ)
     theirs = other_core(mine)
     grad_rows, grad_cols = attn_grad_of(og, mine, theirs, place)
-    col_mine, grad_rows, grad_cols = together(col_mine, grad_rows, grad_cols)
+    dq, dk, dv = row_backward(q, k, v, grad_rows, block_pattern)
+    og_theirs = other_core(og_sent)
+    col_mine, grad_cols, og_theirs, dq, dk, dv = together(col_mine, grad_cols, og_theirs, dq, dk, dv)
     col_mine = col_mine.reshape(COLS, HALF)
 
     col_grads = exchange(grad_cols.reshape(seq, COLS // seq, HALF), SEQ)
     col_theirs = other_core(col_mine)
     parts = weight_grad_of(row_out, row_theirs, col_mine, col_theirs, og, og_theirs, place)
-    dq, dk, dv = row_backward(q, k, v, grad_rows, block_pattern)
     next_x, last_x = along(parts[1], "x", 1), along(parts[3], "x", 3)
-    col_grads, dq, dk, dv, next_x, last_x = together(col_grads, dq, dk, dv, next_x, last_x)
+    col_grads, next_x, last_x = together(col_grads, next_x, last_x)
 
     col_back = column_backward(received, col_grads.reshape(ROWS, 2, GRP, HALF)).reshape(seq, COLS // seq, 3 * HALF)
     back = exchange(col_back, SEQ).reshape(COLS, 3 * HALF)
 
-    parts = weight_sum([parts[0], next_x, along(parts[2], "x", 2), last_x], place)
+    layer = layer_out_of(row_out, col_mine, mine, theirs, place)
+    far_x, layer = together(along(parts[2], "x", 2), layer)
+    parts = weight_sum([parts[0], next_x, far_x, last_x], place)
     parts = [parts[0]] + [along(parts[step], "y", step) for step in (1, 2, 3)]
     parts = y_sum(parts, place)
     parts = [parts[0]] + [along_z(parts[step], step) for step in range(1, 8)]
@@ -554,7 +555,6 @@
     w_grad = w_grad * tokens ** (-0.5)
 
     dq, dk, dv = finish(back, dq, dk, dv, col_offset)
-    layer = layer_out_of(row_out, col_mine, mine, theirs, place)
     lead = (1, 1, COLS)
     return (
         layer.reshape(lead + (D,)),

time: 226 us -> 235 us (1.040)
  between operations: 0.9 us -> 14.2 us
  starting transfers between devices: 87.9 us -> 80.3 us
  waiting for transfers between devices: 66.8 us -> 74.3 us
  local copies, waits for them, and re-layouts: 16.9 us -> 12.6 us
    ppermute x12 -> x9, waiting for transfers between devices: 53.4 us -> 20 us  [along(): return lax.ppermute(tensor, axis, [(i, (i + step) % 4) for i in range(4)])]
    all_to_all x5, waiting for transfers between devices: 10.1 us -> 35.5 us  [exchange(): return lax.all_to_all(tensor, axes, split_axis=0, concat_axis=0, tiled=True)]
    all_gather x0 -> x1, waiting for transfers between devices: none -> 15.1 us  [shards(): mine = lax.all_gather(gather_y(own_rows, place), 'x', axis=0, tiled=True)]
    ppermute x7, starting transfers between devices: 23.8 us -> 15.3 us  [along_z(): return lax.ppermute(tensor, ('zl', 'zh'), turns)]
    all_to_all x5, starting transfers between devices: 40.4 us -> 45.8 us  [exchange(): return lax.all_to_all(tensor, axes, split_axis=0, concat_axis=0, tiled=True)]
    ppermute x12 -> x9, starting transfers between devices: 16.7 us -> 12.7 us  [along(): return lax.ppermute(tensor, axis, [(i, (i + step) % 4) for i in range(4)])]
    unnamed x44 -> x32, local copies, waits for them, and re-layouts: 13 us -> 9.97 us
  transfers between devices with their start and end apart: 29 -> 27, of which waited for: 15 -> 14; matrix products, arithmetic and copies ran while one was open for 1% -> 1% of each run, Pallas kernels for 17% -> 17%
where the time goes in v5:
time: 235 us; the launch traced here: 232 us
  starting transfers between devices  80.3 us (34%)
  waiting for transfers between devices  74.3 us (32%)
  Pallas kernels  50.4 us (21%)
  between operations  14.2 us (6%)
  local copies, waits for them, and re-layouts  12.6 us (5%)
    all_to_all x5, starting transfers between devices, exchange(): return lax.all_to_all(tensor, axes, split_axis=0, concat_axis=0, tiled=True)  45.8 us
    all_to_all x5, waiting for transfers between devices, exchange(): return lax.all_to_all(tensor, axes, split_axis=0, concat_axis=0, tiled=True)  35.5 us
    ppermute x9, waiting for transfers between devices, along(): return lax.ppermute(tensor, axis, [(i, (i + step) % 4) for i in range(4)])  20 us
    ppermute x7, starting transfers between devices, along_z(): return lax.ppermute(tensor, ('zl', 'zh'), turns)  15.3 us
    all_gather x1, waiting for transfers between devices, shards(): mine = lax.all_gather(gather_y(own_rows, place), 'x', axis=0, tiled=True)  15.1 us
    ppermute x9, starting transfers between devices, along(): return lax.ppermute(tensor, axis, [(i, (i + step) % 4) for i in range(4)])  12.7 us
    unnamed x32, local copies, waits for them, and re-layouts  9.97 us
    pallas_call x1, Pallas kernels, row_backward(): pl.pallas_call(row_backward_kernel, grid=(1,), out_shape=(whole, whole, w...  9.13 us
  transfers between devices with their start and end apart: 27, of which 14 were waited for; matrix products, arithmetic and copies ran while one was open for 1% of the time, Pallas kernels for 17%

profile of v5, /device:TPU:1, one launch (start us, length us, event | category | flops | bytes accessed | tf_op | source)
XLA Modules:
  0.0 232.5 jit_solution(12207642774027263224)
XLA Ops:
  8.6 10.0 %all-to-all-start = ((bf16[16,4,1024]{2,1,0:T(4,128)(2,1)}), bf16[16,4,1024]{2,1,0:T(4,128)(2,1)S(1)}, u32[]{:S(2)}, u32[]{:S(2)}) async-start(bf16[16,4,1024]{2,1,0:T(4,128)(2,1)} %bitcast.6), calls=%async_computation | async-start | bytes 262144 | tf_op jit(solution)/shard_map/all_to_all | solution.py:481
  22.9 2.4 %pack.1 = bf16[512,1536]{1,0:T(8,128)(2,1)} custom-call(s32[4]{0:T(128)S(1)} %copy-done.14, bf16[512,1024]{1,0:T(8,128)(2,1)S(1)} %bitcast.28, bf16[512,1024]{1,0:T(8,128)(2,1)S(1)} %bitcast.31, bf16[512,1024]{1,0:T(8,128)(2,1)S(1)} %bitcast.34), custom_call_target="tpu_custom_call" | custom-call | flops 536870912 | bytes 3145728 | tf_op jit(solution)/shard_map/pack/pallas_call | solution.py:79
  27.8 8.9 %all-to-all-start.1 = ((bf16[32,16,1536]{2,1,0:T(8,128)(2,1)}), bf16[32,16,1536]{2,1,0:T(8,128)(2,1)}, u32[]{:S(2)}, u32[]{:S(2)}) async-start(bf16[32,16,1536]{2,1,0:T(8,128)(2,1)} %bitcast.40), calls=%async_computation.1 | async-start | bytes 3145728 | tf_op jit(solution)/shard_map/all_to_all | solution.py:481
  36.7 2.7 %collective-permute-start.2 = (bf16[64,1024]{1,0:T(8,128)(2,1)S(1)}, bf16[64,1024]{1,0:T(8,128)(2,1)S(1)}, u32[]{:S(2)}, u32[]{:S(2)}) collective-permute-start(bf16[64,1024]{1,0:T(8,128)(2,1)S(1)} %reshape.77.own_ref), channel_id=1, source_target_pairs={{0,24},{8,0},{16,8},{24,16},{1,25},{9,1},{17,9},{25,17},{2,26},{10... | collective-permute-start | bytes 393224 | tf_op jit(solution)/shard_map/ppermute | solution.py:493
  43.0 2.9 %row_forward.1.row_mine.row_ref = bf16[512,512]{1,0:T(8,128)(2,1)} custom-call(s32[4,4]{1,0:T(4,128)S(1)} %copy-done.13, bf16[512,1024]{1,0:T(8,128)(2,1)S(1)} %bitcast.29, bf16[512,1024]{1,0:T(8,128)(2,1)S(1)} %bitcast.32, bf16[512,1024]{1,0:T(8,128)(2,1)S(1)} %bitcast.35), custom_call_target="tpu_custom_call" | custom-call | flops 268435456 | bytes 2097152 | tf_op jit(solution)/shard_map/row_forward/pallas_call | solution.py:189
  48.2 3.8 %collective-permute-done.a_ref = bf16[64,1024]{1,0:T(8,128)(2,1)} collective-permute-done((bf16[64,1024]{1,0:T(8,128)(2,1)S(1)}, bf16[64,1024]{1,0:T(8,128)(2,1)}, u32[]{:S(2)}, u32[]{:S(2)}) %collective-permute-start) | collective-permute-done | bytes 131104 | tf_op jit(solution)/shard_map/ppermute | solution.py:493
  53.7 22.9 %all-to-all-done.1 = bf16[32,16,1536]{2,1,0:T(8,128)(2,1)} async-done(((bf16[32,16,1536]{2,1,0:T(8,128)(2,1)}), bf16[32,16,1536]{2,1,0:T(8,128)(2,1)}, u32[]{:S(2)}, u32[]{:S(2)}) %all-to-all-start.1) | async-done | bytes 1572896 | tf_op jit(solution)/shard_map/all_to_all | solution.py:481
  76.6 3.4 %column_forward.1 = bf16[32,2,8,512]{3,2,1,0:T(8,128)(2,1)S(1)} custom-call(bf16[32,2,8,1536]{3,2,1,0:T(8,128)(2,1)} %bitcast.12.r_ref), custom_call_target="tpu_custom_call" | custom-call | flops 99999997952 | bytes 2097152 | tf_op jit(solution)/shard_map/column_forward/pallas_call | solution.py:130
  80.8 15.1 %all-gather.2.cloned.1.call-done.mine_ref = bf16[1024,1024]{1,0:T(8,128)(2,1)} async-done(((bf16[256,1024]{1,0:T(8,128)(2,1)}), bf16[1024,1024]{1,0:T(8,128)(2,1)}) %all-gather.2.cloned.1.call-update) | async-done | bytes 2097168 | tf_op jit(solution)/shard_map/all_gather | solution.py:518
  96.6 10.2 %all-to-all-start.2 = ((bf16[32,16,512]{2,1,0:T(8,128)(2,1)}), bf16[32,16,512]{2,1,0:T(8,128)(2,1)}, u32[]{:S(2)}, u32[]{:S(2)}) async-start(bf16[32,16,512]{2,1,0:T(8,128)(2,1)} %bitcast.39), calls=%async_computation.2 | async-start | bytes 1048576 | tf_op jit(solution)/shard_map/all_to_all | solution.py:481
  106.9 6.2 %attn_grad.1 = (bf16[512,512]{1,0:T(8,128)(2,1)S(1)}, bf16[512,512]{1,0:T(8,128)(2,1)}) custom-call(s32[5]{0:T(128)S(1)} %stack.23.place.core_ref, bf16[512,2048]{1,0:T(8,128)(2,1)S(1)} %bitcast.26, bf16[512,2048]{1,0:T(8,128)(2,1)S(1)} %bitcast.27, bf16[1024,1024]{1,0:T(8,128)(2,1)} %all-gather.2.cloned.1.call-done.mine_ref, ...), custom_call_target="tpu_custom_call" | custom-call | flops 2147483648 | bytes 7340032 | tf_op jit(solution)/shard_map/attn_grad/pallas_call | solution.py:277
  113.1 9.1 %row_backward.1 = (bf16[512,1024]{1,0:T(8,128)(2,1)}, bf16[512,1024]{1,0:T(8,128)(2,1)}, bf16[512,1024]{1,0:T(8,128)(2,1)}) custom-call(s32[4,4]{1,0:T(4,128)S(1)} %copy-done.13, bf16[512,1024]{1,0:T(8,128)(2,1)S(1)} %bitcast.30, bf16[512,1024]{1,0:T(8,128)(2,1)S(1)} %bitcast.33, bf16[512,1024]{1,0:T(8,128)(2,1)S(1)} %bitcast.36, ...), custom_call_target="tpu_custom_call" | custom-call | flops 671088640 | bytes 3670016 | tf_op jit(solution)/shard_map/row_backward/pallas_call | solution.py:222
  122.2 2.8 %all-to-all-done.2 = bf16[32,16,512]{2,1,0:T(8,128)(2,1)} async-done(((bf16[32,16,512]{2,1,0:T(8,128)(2,1)}), bf16[32,16,512]{2,1,0:T(8,128)(2,1)}, u32[]{:S(2)}, u32[]{:S(2)}) %all-to-all-start.2) | async-done | bytes 524320 | tf_op jit(solution)/shard_map/all_to_all | solution.py:481
  126.0 6.2 %all-to-all-start.3 = ((bf16[32,16,512]{2,1,0:T(8,128)(2,1)}), bf16[32,16,512]{2,1,0:T(8,128)(2,1)S(1)}, u32[]{:S(2)}, u32[]{:S(2)}) async-start(bf16[32,16,512]{2,1,0:T(8,128)(2,1)} %bitcast.17), calls=%async_computation.3 | async-start | bytes 1048576 | tf_op jit(solution)/shard_map/all_to_all | solution.py:481
  132.2 6.9 %weight_grad.1 = (f32[256,1024]{1,0:T(8,128)}, bf16[256,1024]{1,0:T(8,128)(2,1)S(1)}, bf16[256,1024]{1,0:T(8,128)(2,1)S(1)}, bf16[256,1024]{1,0:T(8,128)(2,1)S(1)}) custom-call(s32[5]{0:T(128)S(1)} %stack.23.place.core_ref, bf16[512,512]{1,0:T(8,128)(2,1)} %row_forward.1.row_mine.row_ref, bf16[512,512]{1,0:T(8,128)(2,1)} %collective-permute-done.3.row_theirs, ...), custom_call_target="tpu_custom_call" | custom-call | flops 2147483648 | bytes 7340032 | tf_op jit(solution)/shard_map/weight_grad/pallas_call | solution.py:363
  139.6 2.2 collective-permute-start.9
  141.8 8.6 %all-to-all-done.3 = bf16[32,16,512]{2,1,0:T(8,128)(2,1)S(1)} async-done(((bf16[32,16,512]{2,1,0:T(8,128)(2,1)}), bf16[32,16,512]{2,1,0:T(8,128)(2,1)S(1)}, u32[]{:S(2)}, u32[]{:S(2)}) %all-to-all-start.3) | async-done | bytes 524320 | tf_op jit(solution)/shard_map/all_to_all | solution.py:481
  150.3 3.2 %collective-permute-done.8.b_ref = bf16[256,1024]{1,0:T(8,128)(2,1)S(1)} collective-permute-done((bf16[256,1024]{1,0:T(8,128)(2,1)S(1)}, bf16[256,1024]{1,0:T(8,128)(2,1)S(1)}, u32[]{:S(2)}, u32[]{:S(2)}) %collective-permute-start.8) | collective-permute-done | bytes 524320 | tf_op jit(solution)/shard_map/ppermute | solution.py:493
  153.6 7.2 %column_backward.1 = bf16[32,2,8,1536]{3,2,1,0:T(8,128)(2,1)} custom-call(bf16[32,2,8,1536]{3,2,1,0:T(8,128)(2,1)} %bitcast.12.r_ref, bf16[32,2,8,512]{3,2,1,0:T(8,128)(2,1)S(1)} %bitcast.38), custom_call_target="tpu_custom_call" | custom-call | flops 671088640 | bytes 3670016 | tf_op jit(solution)/shard_map/column_backward/pallas_call | solution.py:156
  160.8 10.5 %all-to-all-start.4 = ((bf16[32,16,1536]{2,1,0:T(8,128)(2,1)}), bf16[32,16,1536]{2,1,0:T(8,128)(2,1)S(1)}, u32[]{:S(2)}, u32[]{:S(2)}) async-start(bf16[32,16,1536]{2,1,0:T(8,128)(2,1)} %bitcast.19), calls=%async_computation.4 | async-start | bytes 3145728 | tf_op jit(solution)/shard_map/all_to_all | solution.py:481
  174.2 6.6 %layer_out.1 = bf16[512,2048]{1,0:T(8,128)(2,1)} custom-call(s32[5]{0:T(128)S(1)} %stack.23.place.core_ref, bf16[512,512]{1,0:T(8,128)(2,1)} %row_forward.1.row_mine.row_ref, bf16[512,512]{1,0:T(8,128)(2,1)} %bitcast.15.col_mine.col_ref, bf16[1024,1024]{1,0:T(8,128)(2,1)S(1)} %copy-done.10, bf16[1024,1024]{1,0:T(8,128)(2,1)} %collective-permute-done.4.theirs_ref), custom_call_target="tpu_custom_call" | custom-call | flops 2147483648 | bytes 7340032 | tf_op jit(solution)/shard_map/layer_out/pallas_call | solution.py:317
  180.8 5.4 %collective-permute-done.7.c_ref = bf16[256,1024]{1,0:T(8,128)(2,1)S(1)} collective-permute-done((bf16[256,1024]{1,0:T(8,128)(2,1)S(1)}, bf16[256,1024]{1,0:T(8,128)(2,1)S(1)}, u32[]{:S(2)}, u32[]{:S(2)}) %collective-permute-start.7) | collective-permute-done | bytes 524320 | tf_op jit(solution)/shard_map/ppermute | solution.py:493
  188.3 2.4 %collective-permute-start.11 = (bf16[64,1024]{1,0:T(8,128)(2,1)S(1)}, bf16[64,1024]{1,0:T(8,128)(2,1)S(1)}, u32[]{:S(2)}, u32[]{:S(2)}) collective-permute-start(bf16[64,1024]{1,0:T(8,128)(2,1)S(1)} %get-tuple-element.81), channel_id=1, source_target_pairs={{0,16},{8,24},{16,0},{24,8},{1,17},{9,25},{17,1},{25,9},{2,18},{10... | collective-permute-start | bytes 393224 | tf_op jit(solution)/shard_map/ppermute | solution.py:493
  191.9 4.1 %collective-permute-done.10.b_ref = bf16[64,1024]{1,0:T(8,128)(2,1)S(1)} collective-permute-done((bf16[64,1024]{1,0:T(8,128)(2,1)S(1)}, bf16[64,1024]{1,0:T(8,128)(2,1)S(1)}, u32[]{:S(2)}, u32[]{:S(2)}) %collective-permute-start.10) | collective-permute-done | bytes 131104 | tf_op jit(solution)/shard_map/ppermute | solution.py:493
  196.0 2.6 %collective-permute-done.11.c_ref = bf16[64,1024]{1,0:T(8,128)(2,1)S(1)} collective-permute-done((bf16[64,1024]{1,0:T(8,128)(2,1)S(1)}, bf16[64,1024]{1,0:T(8,128)(2,1)S(1)}, u32[]{:S(2)}, u32[]{:S(2)}) %collective-permute-start.11) | collective-permute-done | bytes 131104 | tf_op jit(solution)/shard_map/ppermute | solution.py:493
  199.3 2.0 collective-permute-start.13
  201.3 2.9 %collective-permute-start.14 = (bf16[8,1024]{1,0:T(8,128)(2,1)S(1)}, bf16[8,1024]{1,0:T(8,128)(2,1)S(1)}, u32[]{:S(2)}, u32[]{:S(2)}) collective-permute-start(bf16[8,1024]{1,0:T(8,128)(2,1)S(1)} %get-tuple-element.85), channel_id=1, source_target_pairs={{0,4},{2,6},{4,0},{6,2},{32,36},{34,38},{36,32},{38,34},{1,5},{3,7... | collective-permute-start | bytes 49160 | tf_op jit(solution)/shard_map/ppermute | solution.py:498
  204.2 3.4 %collective-permute-start.15 = (bf16[8,1024]{1,0:T(8,128)(2,1)S(1)}, bf16[8,1024]{1,0:T(8,128)(2,1)S(1)}, u32[]{:S(2)}, u32[]{:S(2)}) collective-permute-start(bf16[8,1024]{1,0:T(8,128)(2,1)S(1)} %get-tuple-element.86), channel_id=1, source_target_pairs={{0,6},{2,0},{4,2},{6,4},{32,38},{34,32},{36,34},{38,36},{1,7},{3,1... | collective-permute-start | bytes 49160 | tf_op jit(solution)/shard_map/ppermute | solution.py:498
  207.6 3.2 %collective-permute-start.16 = (bf16[8,1024]{1,0:T(8,128)(2,1)S(1)}, bf16[8,1024]{1,0:T(8,128)(2,1)S(1)}, u32[]{:S(2)}, u32[]{:S(2)}) collective-permute-start(bf16[8,1024]{1,0:T(8,128)(2,1)S(1)} %get-tuple-element.87), channel_id=1, source_target_pairs={{0,32},{2,34},{4,36},{6,38},{32,0},{34,2},{36,4},{38,6},{1,33},{3,... | collective-permute-start | bytes 49160 | tf_op jit(solution)/shard_map/ppermute | solution.py:498
  212.2 2.4 %collective-permute-start.19 = (bf16[8,1024]{1,0:T(8,128)(2,1)S(1)}, bf16[8,1024]{1,0:T(8,128)(2,1)S(1)}, u32[]{:S(2)}, u32[]{:S(2)}) collective-permute-start(bf16[8,1024]{1,0:T(8,128)(2,1)S(1)} %get-tuple-element.90), channel_id=1, source_target_pairs={{0,38},{2,32},{4,34},{6,36},{32,6},{34,0},{36,2},{38,4},{1,39},{3,... | collective-permute-start | bytes 49160 | tf_op jit(solution)/shard_map/ppermute | solution.py:498
  218.0 3.6 %collective-permute-start.20 = (f32[4,1024]{1,0:T(4,128)S(1)}, f32[4,1024]{1,0:T(4,128)S(1)}, u32[]{:S(2)}, u32[]{:S(2)}) collective-permute-start(f32[4,1024]{1,0:T(4,128)S(1)} %get-tuple-element.92), channel_id=1, source_target_pairs={{0,1},{1,0},{2,3},{3,2},{4,5},{5,4},{6,7},{7,6},{8,9},{9,8},{10,11... | collective-permute-start | bytes 49160 | tf_op jit(solution)/shard_map/ppermute | solution.py:485
  223.0 2.6 %finish.1 = (bf16[512,1024]{1,0:T(8,128)(2,1)}, bf16[512,1024]{1,0:T(8,128)(2,1)}, bf16[512,1024]{1,0:T(8,128)(2,1)}) custom-call(s32[4]{0:T(128)S(1)} %copy-done.15, bf16[512,1536]{1,0:T(8,128)(2,1)S(1)} %bitcast.37, bf16[512,1024]{1,0:T(8,128)(2,1)} %get-tuple-element.69.dq_in, ...), custom_call_target="tpu_custom_call", output_to_operand_aliasing={{0}: (2, {}), {1}: (3, {}), {2}: (4, {})} | custom-call | flops 536870912 | bytes 3145728 | tf_op jit(solution)/shard_map/finish/pallas_call | solution.py:248
  (76 shorter events, 31.7 us)
Async XLA Ops:
  8.6 19.1 %all-to-all-start = ((bf16[16,4,1024]{2,1,0:T(4,128)(2,1)}), bf16[16,4,1024]{2,1,0:T(4,128)(2,1)S(1)}, u32[]{:S(2)}, u32[]{:S(2)}) async-start(bf16[16,4,1024]{2,1,0:T(4,128)(2,1)} %bitcast.6), calls=%async_computation | async-start | bytes 262144 | tf_op jit(solution)/shard_map/all_to_all | solution.py:481
  26.5 14.1 %copy-start.2 = (bf16[1,1,512,1024]{3,2,1,0:T(8,128)(2,1)S(1)}, bf16[1,1,512,1024]{3,2,1,0:T(8,128)(2,1)}, u32[]{:S(2)}) copy-start(bf16[1,1,512,1024]{3,2,1,0:T(8,128)(2,1)} %param.7) | copy-start | bytes 3145732
  26.5 14.1 %copy-start.13 = (s32[4,4]{1,0:T(4,128)S(1)}, s32[4,4]{1,0:T(4,128)}, u32[]{:S(2)}) copy-start(s32[4,4]{1,0:T(4,128)} %pat_ref.3) | copy-start | bytes 196
  27.8 48.8 %all-to-all-start.1 = ((bf16[32,16,1536]{2,1,0:T(8,128)(2,1)}), bf16[32,16,1536]{2,1,0:T(8,128)(2,1)}, u32[]{:S(2)}, u32[]{:S(2)}) async-start(bf16[32,16,1536]{2,1,0:T(8,128)(2,1)} %bitcast.40), calls=%async_computation.1 | async-start | bytes 3145728 | tf_op jit(solution)/shard_map/all_to_all | solution.py:481
  36.7 59.3 %all-gather.2.cloned.1.call-start = ((), (), s32[]{:S(2)}) async-start(), calls=%async_computation.5 | async-start | bytes 2621440 | tf_op jit(solution)/shard_map/all_gather | solution.py:518
  36.7 10.5 %collective-permute-start.2 = (bf16[64,1024]{1,0:T(8,128)(2,1)S(1)}, bf16[64,1024]{1,0:T(8,128)(2,1)S(1)}, u32[]{:S(2)}, u32[]{:S(2)}) collective-permute-start(bf16[64,1024]{1,0:T(8,128)(2,1)S(1)} %reshape.77.own_ref), channel_id=1, source_target_pairs={{0,24},{8,0},{16,8},{24,16},{1,25},{9,1},{17,9},{25,17},{2,26},{10... | collective-permute-start | bytes 393224 | tf_op jit(solution)/shard_map/ppermute | solution.py:493
  39.5 8.7 %collective-permute-start.1 = (bf16[64,1024]{1,0:T(8,128)(2,1)S(1)}, bf16[64,1024]{1,0:T(8,128)(2,1)S(1)}, u32[]{:S(2)}, u32[]{:S(2)}) collective-permute-start(bf16[64,1024]{1,0:T(8,128)(2,1)S(1)} %reshape.77.own_ref), channel_id=1, source_target_pairs={{0,16},{8,24},{16,0},{24,8},{1,17},{9,25},{17,1},{25,9},{2,18},{10... | collective-permute-start | bytes 393224 | tf_op jit(solution)/shard_map/ppermute | solution.py:493
  40.0 11.9 %collective-permute-start = (bf16[64,1024]{1,0:T(8,128)(2,1)S(1)}, bf16[64,1024]{1,0:T(8,128)(2,1)}, u32[]{:S(2)}, u32[]{:S(2)}) collective-permute-start(bf16[64,1024]{1,0:T(8,128)(2,1)S(1)} %reshape.77.own_ref), channel_id=1, source_target_pairs={{0,8},{8,16},{16,24},{24,0},{1,9},{9,17},{17,25},{25,1},{2,10},{10... | collective-permute-start | bytes 393224 | tf_op jit(solution)/shard_map/ppermute | solution.py:493
  46.0 34.8 %collective-permute-start.3 = (bf16[512,512]{1,0:T(8,128)(2,1)}, bf16[512,512]{1,0:T(8,128)(2,1)}, u32[]{:S(2)}, u32[]{:S(2)}) collective-permute-start(bf16[512,512]{1,0:T(8,128)(2,1)} %row_forward.1.row_mine.row_ref), channel_id=1, source_target_pairs={{0,1},{1,0},{2,3},{3,2},{4,5},{5,4},{6,7},{7,6},{8,9},{9,8},{10,11... | collective-permute-start | bytes 1572872 | tf_op jit(solution)/shard_map/ppermute | solution.py:485
  95.9 10.9 %collective-permute-start.4 = (bf16[1024,1024]{1,0:T(8,128)(2,1)}, bf16[1024,1024]{1,0:T(8,128)(2,1)}, u32[]{:S(2)}, u32[]{:S(2)}) collective-permute-start(bf16[1024,1024]{1,0:T(8,128)(2,1)} %all-gather.2.cloned.1.call-done.mine_ref), channel_id=1, source_target_pairs={{0,1},{1,0},{2,3},{3,2},{4,5},{5,4},{6,7},{7,6},{8,9},{9,8},{10,11... | collective-permute-start | bytes 6291464 | tf_op jit(solution)/shard_map/ppermute | solution.py:485
  96.6 25.6 %collective-permute-start.5 = (bf16[512,1024]{1,0:T(8,128)(2,1)}, bf16[512,1024]{1,0:T(8,128)(2,1)}, u32[]{:S(2)}, u32[]{:S(2)}) collective-permute-start(bf16[512,1024]{1,0:T(8,128)(2,1)} %dynamic-slice_bitcast_fusion), channel_id=1, source_target_pairs={{0,1},{1,0},{2,3},{3,2},{4,5},{5,4},{6,7},{7,6},{8,9},{9,8},{10,11... | collective-permute-start | bytes 3145736 | tf_op jit(solution)/shard_map/ppermute | solution.py:485
  96.6 28.4 %all-to-all-start.2 = ((bf16[32,16,512]{2,1,0:T(8,128)(2,1)}), bf16[32,16,512]{2,1,0:T(8,128)(2,1)}, u32[]{:S(2)}, u32[]{:S(2)}) async-start(bf16[32,16,512]{2,1,0:T(8,128)(2,1)} %bitcast.39), calls=%async_computation.2 | async-start | bytes 1048576 | tf_op jit(solution)/shard_map/all_to_all | solution.py:481
  106.8 6.3 %copy-start.5 = (bf16[1,1,512,1024]{3,2,1,0:T(8,128)(2,1)S(1)}, bf16[1,1,512,1024]{3,2,1,0:T(8,128)(2,1)}, u32[]{:S(2)}) copy-start(bf16[1,1,512,1024]{3,2,1,0:T(8,128)(2,1)} %param.8) | copy-start | bytes 3145732
  125.0 7.2 %collective-permute-start.6 = (bf16[512,512]{1,0:T(8,128)(2,1)}, bf16[512,512]{1,0:T(8,128)(2,1)S(1)}, u32[]{:S(2)}, u32[]{:S(2)}) collective-permute-start(bf16[512,512]{1,0:T(8,128)(2,1)} %bitcast.15.col_mine.col_ref), channel_id=1, source_target_pairs={{0,1},{1,0},{2,3},{3,2},{4,5},{5,4},{6,7},{7,6},{8,9},{9,8},{10,11... | collective-permute-start | bytes 1572872 | tf_op jit(solution)/shard_map/ppermute | solution.py:485
  126.0 24.3 %all-to-all-start.3 = ((bf16[32,16,512]{2,1,0:T(8,128)(2,1)}), bf16[32,16,512]{2,1,0:T(8,128)(2,1)S(1)}, u32[]{:S(2)}, u32[]{:S(2)}) async-start(bf16[32,16,512]{2,1,0:T(8,128)(2,1)} %bitcast.17), calls=%async_computation.3 | async-start | bytes 1048576 | tf_op jit(solution)/shard_map/all_to_all | solution.py:481
  139.1 14.5 %collective-permute-start.8 = (bf16[256,1024]{1,0:T(8,128)(2,1)S(1)}, bf16[256,1024]{1,0:T(8,128)(2,1)S(1)}, u32[]{:S(2)}, u32[]{:S(2)}) collective-permute-start(bf16[256,1024]{1,0:T(8,128)(2,1)S(1)} %get-tuple-element.66), channel_id=1, source_target_pairs={{0,64},{64,128},{128,192},{192,0},{1,65},{65,129},{129,193},{193,1... | collective-permute-start | bytes 1572872 | tf_op jit(solution)/shard_map/ppermute | solution.py:493
  139.6 14.0 %collective-permute-start.9 = (bf16[256,1024]{1,0:T(8,128)(2,1)S(1)}, bf16[256,1024]{1,0:T(8,128)(2,1)S(1)}, u32[]{:S(2)}, u32[]{:S(2)}) collective-permute-start(bf16[256,1024]{1,0:T(8,128)(2,1)S(1)} %get-tuple-element.67), channel_id=1, source_target_pairs={{0,192},{64,0},{128,64},{192,128},{1,193},{65,1},{129,65},{193,129... | collective-permute-start | bytes 1572872 | tf_op jit(solution)/shard_map/ppermute | solution.py:493
  160.8 62.2 %all-to-all-start.4 = ((bf16[32,16,1536]{2,1,0:T(8,128)(2,1)}), bf16[32,16,1536]{2,1,0:T(8,128)(2,1)S(1)}, u32[]{:S(2)}, u32[]{:S(2)}) async-start(bf16[32,16,1536]{2,1,0:T(8,128)(2,1)} %bitcast.19), calls=%async_computation.4 | async-start | bytes 3145728 | tf_op jit(solution)/shard_map/all_to_all | solution.py:481
  171.3 14.9 %collective-permute-start.7 = (bf16[256,1024]{1,0:T(8,128)(2,1)S(1)}, bf16[256,1024]{1,0:T(8,128)(2,1)S(1)}, u32[]{:S(2)}, u32[]{:S(2)}) collective-permute-start(bf16[256,1024]{1,0:T(8,128)(2,1)S(1)} %get-tuple-element.63), channel_id=1, source_target_pairs={{0,128},{64,192},{128,0},{192,64},{1,129},{65,193},{129,1},{193,65... | collective-permute-start | bytes 1572872 | tf_op jit(solution)/shard_map/ppermute | solution.py:493
  174.2 12.0 %copy-start.11 = (f32[256,1024]{1,0:T(8,128)S(1)}, f32[256,1024]{1,0:T(8,128)}, u32[]{:S(2)}) copy-start(f32[256,1024]{1,0:T(8,128)} %get-tuple-element.75.a_ref) | copy-start | bytes 3145732
  180.8 42.3 %copy-start.15 = (s32[4]{0:T(128)S(1)}, s32[4]{0:T(128)}, u32[]{:S(2)}) copy-start(s32[4]{0:T(128)} %off_ref.3) | copy-start | bytes 52
  187.0 9.0 %collective-permute-start.10 = (bf16[64,1024]{1,0:T(8,128)(2,1)S(1)}, bf16[64,1024]{1,0:T(8,128)(2,1)S(1)}, u32[]{:S(2)}, u32[]{:S(2)}) collective-permute-start(bf16[64,1024]{1,0:T(8,128)(2,1)S(1)} %get-tuple-element.80), channel_id=1, source_target_pairs={{0,8},{8,16},{16,24},{24,0},{1,9},{9,17},{17,25},{25,1},{2,10},{10... | collective-permute-start | bytes 393224 | tf_op jit(solution)/shard_map/ppermute | solution.py:493
  188.3 10.3 %collective-permute-start.11 = (bf16[64,1024]{1,0:T(8,128)(2,1)S(1)}, bf16[64,1024]{1,0:T(8,128)(2,1)S(1)}, u32[]{:S(2)}, u32[]{:S(2)}) collective-permute-start(bf16[64,1024]{1,0:T(8,128)(2,1)S(1)} %get-tuple-element.81), channel_id=1, source_target_pairs={{0,16},{8,24},{16,0},{24,8},{1,17},{9,25},{17,1},{25,9},{2,18},{10... | collective-permute-start | bytes 393224 | tf_op jit(solution)/shard_map/ppermute | solution.py:493
  190.8 7.9 %collective-permute-start.12 = (bf16[64,1024]{1,0:T(8,128)(2,1)S(1)}, bf16[64,1024]{1,0:T(8,128)(2,1)S(1)}, u32[]{:S(2)}, u32[]{:S(2)}) collective-permute-start(bf16[64,1024]{1,0:T(8,128)(2,1)S(1)} %get-tuple-element.82), channel_id=1, source_target_pairs={{0,24},{8,0},{16,8},{24,16},{1,25},{9,1},{17,9},{25,17},{2,26},{10... | collective-permute-start | bytes 393224 | tf_op jit(solution)/shard_map/ppermute | solution.py:493
  199.3 11.6 %collective-permute-start.13 = (bf16[8,1024]{1,0:T(8,128)(2,1)S(1)}, bf16[8,1024]{1,0:T(8,128)(2,1)S(1)}, u32[]{:S(2)}, u32[]{:S(2)}) collective-permute-start(bf16[8,1024]{1,0:T(8,128)(2,1)S(1)} %get-tuple-element.84), channel_id=1, source_target_pairs={{0,2},{2,4},{4,6},{6,0},{32,34},{34,36},{36,38},{38,32},{1,3},{3,5... | collective-permute-start | bytes 49160 | tf_op jit(solution)/shard_map/ppermute | solution.py:498
  201.3 10.9 %collective-permute-start.14 = (bf16[8,1024]{1,0:T(8,128)(2,1)S(1)}, bf16[8,1024]{1,0:T(8,128)(2,1)S(1)}, u32[]{:S(2)}, u32[]{:S(2)}) collective-permute-start(bf16[8,1024]{1,0:T(8,128)(2,1)S(1)} %get-tuple-element.85), channel_id=1, source_target_pairs={{0,4},{2,6},{4,0},{6,2},{32,36},{34,38},{36,32},{38,34},{1,5},{3,7... | collective-permute-start | bytes 49160 | tf_op jit(solution)/shard_map/ppermute | solution.py:498
  204.2 10.4 %collective-permute-start.15 = (bf16[8,1024]{1,0:T(8,128)(2,1)S(1)}, bf16[8,1024]{1,0:T(8,128)(2,1)S(1)}, u32[]{:S(2)}, u32[]{:S(2)}) collective-permute-start(bf16[8,1024]{1,0:T(8,128)(2,1)S(1)} %get-tuple-element.86), channel_id=1, source_target_pairs={{0,6},{2,0},{4,2},{6,4},{32,38},{34,32},{36,34},{38,36},{1,7},{3,1... | collective-permute-start | bytes 49160 | tf_op jit(solution)/shard_map/ppermute | solution.py:498
  207.6 7.1 %collective-permute-start.16 = (bf16[8,1024]{1,0:T(8,128)(2,1)S(1)}, bf16[8,1024]{1,0:T(8,128)(2,1)S(1)}, u32[]{:S(2)}, u32[]{:S(2)}) collective-permute-start(bf16[8,1024]{1,0:T(8,128)(2,1)S(1)} %get-tuple-element.87), channel_id=1, source_target_pairs={{0,32},{2,34},{4,36},{6,38},{32,0},{34,2},{36,4},{38,6},{1,33},{3,... | collective-permute-start | bytes 49160 | tf_op jit(solution)/shard_map/ppermute | solution.py:498
  210.8 3.8 %collective-permute-start.17 = (bf16[8,1024]{1,0:T(8,128)(2,1)S(1)}, bf16[8,1024]{1,0:T(8,128)(2,1)S(1)}, u32[]{:S(2)}, u32[]{:S(2)}) collective-permute-start(bf16[8,1024]{1,0:T(8,128)(2,1)S(1)} %get-tuple-element.88), channel_id=1, source_target_pairs={{0,34},{2,36},{4,38},{6,32},{32,2},{34,4},{36,6},{38,0},{1,35},{3,... | collective-permute-start | bytes 49160 | tf_op jit(solution)/shard_map/ppermute | solution.py:498
  210.9 5.6 %collective-permute-start.18 = (bf16[8,1024]{1,0:T(8,128)(2,1)S(1)}, bf16[8,1024]{1,0:T(8,128)(2,1)S(1)}, u32[]{:S(2)}, u32[]{:S(2)}) collective-permute-start(bf16[8,1024]{1,0:T(8,128)(2,1)S(1)} %get-tuple-element.89), channel_id=1, source_target_pairs={{0,36},{2,38},{4,32},{6,34},{32,4},{34,6},{36,0},{38,2},{1,37},{3,... | collective-permute-start | bytes 49160 | tf_op jit(solution)/shard_map/ppermute | solution.py:498
  212.2 5.2 %collective-permute-start.19 = (bf16[8,1024]{1,0:T(8,128)(2,1)S(1)}, bf16[8,1024]{1,0:T(8,128)(2,1)S(1)}, u32[]{:S(2)}, u32[]{:S(2)}) collective-permute-start(bf16[8,1024]{1,0:T(8,128)(2,1)S(1)} %get-tuple-element.90), channel_id=1, source_target_pairs={{0,38},{2,32},{4,34},{6,36},{32,6},{34,0},{36,2},{38,4},{1,39},{3,... | collective-permute-start | bytes 49160 | tf_op jit(solution)/shard_map/ppermute | solution.py:498
  218.0 4.4 %collective-permute-start.20 = (f32[4,1024]{1,0:T(4,128)S(1)}, f32[4,1024]{1,0:T(4,128)S(1)}, u32[]{:S(2)}, u32[]{:S(2)}) collective-permute-start(f32[4,1024]{1,0:T(4,128)S(1)} %get-tuple-element.92), channel_id=1, source_target_pairs={{0,1},{1,0},{2,3},{3,2},{4,5},{5,4},{6,7},{7,6},{8,9},{9,8},{10,11... | collective-permute-start | bytes 49160 | tf_op jit(solution)/shard_map/ppermute | solution.py:485
  (11 other events, 18.7 us)
Sparse Core Ops, SparseCore 0:
  53.8 42.0 all-gather.1

commit v6 on v4

--- a/solution.py
+++ b/solution.py
@@ -134,7 +134,7 @@
         in_specs=[group_block(3 * HALF)],
         out_specs=group_block(HALF),
         compiler_params=params(),
-        cost_estimate=cost(8 * 4 * TILE * TILE * HD, 4 * COLS * HALF * 2, 8 * TILE * TILE),
+        cost_estimate=cost(10**11, 4 * COLS * HALF * 2, 8 * TILE * TILE),
         name="column_forward",
     )(received)
 
@@ -392,15 +392,18 @@
             o_ref[rows, :] = ref[piece * chunk : (piece + 1) * chunk, :]
 
 
-def gather_of(own, place, axis, index, pieces):
-    blocks = [own] + [along(own, axis, step) for step in (1, 2, 3)]
+def blocks_of(own, axis):
+    return [own] + [along(own, axis, step) for step in (1, 2, 3)]
+
+
+def gather_of(blocks, place, axis, index, pieces):
     return pl.pallas_call(
         functools.partial(gather_kernel, index, pieces),
-        out_shape=jax.ShapeDtypeStruct((4 * own.shape[0], DH), BF),
+        out_shape=jax.ShapeDtypeStruct((4 * blocks[0].shape[0], DH), BF),
         in_specs=[SMEM_SPEC] + [VMEM_SPEC] * 4,
         out_specs=VMEM_SPEC,
         compiler_params=params(),
-        cost_estimate=cost(0, 16 * own.shape[0] * DH),
+        cost_estimate=cost(0, 16 * blocks[0].shape[0] * DH),
         name="gather_" + axis,
     )(place, *blocks)
 
@@ -512,38 +515,41 @@
     spread = jnp.broadcast_to(halves[None], (near // 2, 2, rows_of, DH)).reshape(near, rows_of, DH)
     own_rows = exchange(spread, NEAR)
     packed = pack(q, k, v, col_offset)
-    own_rows, packed = together(own_rows, packed)
+    og_sent = lax.dynamic_slice(og, (0, (1 - core) * DH), (COLS, DH))
+    own_rows, packed, og_sent = together(own_rows, packed, og_sent)
     own_rows = own_rows.reshape(near * rows_of, DH)
-    mine = gather_of(gather_of(own_rows, place, "y", 3, 2), place, "x", 1, 1)
+    blocks = blocks_of(gather_of(blocks_of(own_rows, "y"), place, "y", 3, 2), "x")
 
     received = exchange(packed.reshape(seq, COLS // seq, 3 * HALF), SEQ)
-    og_sent = lax.dynamic_slice(og, (0, (1 - core) * DH), (COLS, DH))
-    og_theirs = other_core(og_sent)
+    received = received.reshape(ROWS, 2, GRP, 3 * HALF)
+
+    col_sent = column_forward(received).reshape(seq, COLS // seq, HALF)
     row_out = row_forward(q, k, v, block_pattern)
     row_theirs = other_core(row_out)
-    received, row_out, row_theirs, og_theirs = together(received, row_out, row_theirs, og_theirs)
-    received = received.reshape(ROWS, 2, GRP, 3 * HALF)
-
-    col_sent = column_forward(received).reshape(seq, COLS // seq, HALF)
-    col_sent, mine = together(col_sent, mine)
+    col_sent, row_out, row_theirs, *blocks = together(col_sent, row_out, row_theirs, *blocks)
     col_mine = exchange(col_sent, SEQ)
+    mine = gather_of(blocks, place, "x", 1, 1)
     theirs = other_core(mine)
+    og_theirs = other_core(og_sent)
     grad_rows, grad_cols = attn_grad_of(og, mine, theirs, place)
-    col_mine, grad_rows, grad_cols = together(col_mine, grad_rows, grad_cols)
+    col_mine, grad_cols, og_theirs = together(col_mine, grad_cols, og_theirs)
     col_mine = col_mine.reshape(COLS, HALF)
 
     col_grads = exchange(grad_cols.reshape(seq, COLS // seq, HALF), SEQ)
     col_theirs = other_core(col_mine)
     parts = weight_grad_of(row_out, row_theirs, col_mine, col_theirs, og, og_theirs, place)
+    x_parts = [parts[0]] + [along(parts[step], "x", step) for step in (1, 3, 2)]
     dq, dk, dv = row_backward(q, k, v, grad_rows, block_pattern)
-    next_x, last_x = along(parts[1], "x", 1), along(parts[3], "x", 3)
-    col_grads, dq, dk, dv, next_x, last_x = together(col_grads, dq, dk, dv, next_x, last_x)
+    col_grads, dq, dk, dv = together(col_grads, dq, dk, dv)
 
     col_back = column_backward(received, col_grads.reshape(ROWS, 2, GRP, HALF)).reshape(seq, COLS // seq, 3 * HALF)
+    col_back, *x_parts = together(col_back, *x_parts)
     back = exchange(col_back, SEQ).reshape(COLS, 3 * HALF)
 
-    parts = weight_sum([parts[0], next_x, along(parts[2], "x", 2), last_x], place)
+    parts = weight_sum(x_parts, place)
+    layer = layer_out_of(row_out, col_mine, mine, theirs, place)
     parts = [parts[0]] + [along(parts[step], "y", step) for step in (1, 2, 3)]
+    layer, *parts = together(layer, *parts)
     parts = y_sum(parts, place)
     parts = [parts[0]] + [along_z(parts[step], step) for step in range(1, 8)]
     keep, give = z_sum(parts, place)
@@ -554,7 +560,6 @@
     w_grad = w_grad * tokens ** (-0.5)
 
     dq, dk, dv = finish(back, dq, dk, dv, col_offset)
-    layer = layer_out_of(row_out, col_mine, mine, theirs, place)
     lead = (1, 1, COLS)
     return (
         layer.reshape(lead + (D,)),

time: 226 us -> 210 us (0.929)
  waiting for transfers between devices: 66.8 us -> 57.8 us
  starting transfers between devices: 87.9 us -> 82.8 us
  local copies, waits for them, and re-layouts: 16.9 us -> 11.8 us
  Pallas kernels: 50.5 us -> 55 us
    ppermute x12, waiting for transfers between devices: 53.4 us -> 22.9 us  [along(): return lax.ppermute(tensor, axis, [(i, (i + step) % 4) for i in range(4)])]
    all_to_all x5, waiting for transfers between devices: 10.1 us -> 30 us  [exchange(): return lax.all_to_all(tensor, axes, split_axis=0, concat_axis=0, tiled=True)]
    ppermute x7, starting transfers between devices: 23.8 us -> 18.4 us  [along_z(): return lax.ppermute(tensor, ('zl', 'zh'), turns)]
    unnamed x44 -> x36, local copies, waits for them, and re-layouts: 13 us -> 9.19 us
    all_to_all x5, starting transfers between devices: 40.4 us -> 43.7 us  [exchange(): return lax.all_to_all(tensor, axes, split_axis=0, concat_axis=0, tiled=True)]
  transfers between devices with their start and end apart: 29 -> 29, of which waited for: 15 -> 12; matrix products, arithmetic and copies ran while one was open for 1% -> 1% of each run, Pallas kernels for 17% -> 24%
where the time goes in v6:
time: 210 us; the launch traced here: 209 us
  starting transfers between devices  82.8 us (39%)
  waiting for transfers between devices  57.8 us (28%)
  Pallas kernels  55 us (26%)
  local copies, waits for them, and re-layouts  11.8 us (6%)
    all_to_all x5, starting transfers between devices, exchange(): return lax.all_to_all(tensor, axes, split_axis=0, concat_axis=0, tiled=True)  43.7 us
    all_to_all x5, waiting for transfers between devices, exchange(): return lax.all_to_all(tensor, axes, split_axis=0, concat_axis=0, tiled=True)  30 us
    ppermute x12, waiting for transfers between devices, along(): return lax.ppermute(tensor, axis, [(i, (i + step) % 4) for i in range(4)])  22.9 us
    ppermute x7, starting transfers between devices, along_z(): return lax.ppermute(tensor, ('zl', 'zh'), turns)  18.4 us
    ppermute x12, starting transfers between devices, along(): return lax.ppermute(tensor, axis, [(i, (i + step) % 4) for i in range(4)])  15.4 us
    unnamed x36, local copies, waits for them, and re-layouts  9.19 us
    pallas_call x1, Pallas kernels, row_backward(): pl.pallas_call(row_backward_kernel, grid=(1,), out_shape=(whole, whole, w...  9.16 us
    pallas_call x1, Pallas kernels, weight_grad_of(): pl.pallas_call(weight_grad_kernel, grid_spec=pltpu.PrefetchScalarGridSpec...  7.57 us
  transfers between devices with their start and end apart: 29, of which 12 were waited for; matrix products, arithmetic and copies ran while one was open for 1% of the time, Pallas kernels for 24%

profile of v6, /device:TPU:1, one launch (start us, length us, event | category | flops | bytes accessed | tf_op | source)
XLA Modules:
  0.0 209.0 jit_solution(5103477280158493766)
XLA Ops:
  2.1 10.0 %all-to-all-start = ((bf16[16,4,1024]{2,1,0:T(4,128)(2,1)}), bf16[16,4,1024]{2,1,0:T(4,128)(2,1)S(1)}, u32[]{:S(2)}, u32[]{:S(2)}) async-start(bf16[16,4,1024]{2,1,0:T(4,128)(2,1)} %bitcast.6), calls=%async_computation | async-start | bytes 262144 | tf_op jit(solution)/shard_map/all_to_all | solution.py:484
  16.4 2.4 %pack.1 = bf16[512,1536]{1,0:T(8,128)(2,1)} custom-call(s32[4]{0:T(128)S(1)} %copy-done.16, bf16[512,1024]{1,0:T(8,128)(2,1)S(1)} %bitcast.28, bf16[512,1024]{1,0:T(8,128)(2,1)S(1)} %bitcast.31, bf16[512,1024]{1,0:T(8,128)(2,1)S(1)} %bitcast.34), custom_call_target="tpu_custom_call" | custom-call | flops 536870912 | bytes 3145728 | tf_op jit(solution)/shard_map/pack/pallas_call | solution.py:79
  21.2 8.9 %all-to-all-start.1 = ((bf16[32,16,1536]{2,1,0:T(8,128)(2,1)}), bf16[32,16,1536]{2,1,0:T(8,128)(2,1)}, u32[]{:S(2)}, u32[]{:S(2)}) async-start(bf16[32,16,1536]{2,1,0:T(8,128)(2,1)} %bitcast.41), calls=%async_computation.1 | async-start | bytes 3145728 | tf_op jit(solution)/shard_map/all_to_all | solution.py:484
  30.1 2.7 %collective-permute-start.3 = (bf16[64,1024]{1,0:T(8,128)(2,1)S(1)}, bf16[64,1024]{1,0:T(8,128)(2,1)S(1)}, u32[]{:S(2)}, u32[]{:S(2)}) collective-permute-start(bf16[64,1024]{1,0:T(8,128)(2,1)S(1)} %reshape.77.own_ref), channel_id=1, source_target_pairs={{0,24},{8,0},{16,8},{24,16},{1,25},{9,1},{17,9},{25,17},{2,26},{10... | collective-permute-start | bytes 393224 | tf_op jit(solution)/shard_map/ppermute | solution.py:496
  36.4 3.0 %row_forward.1.row_ref.row_mine = bf16[512,512]{1,0:T(8,128)(2,1)} custom-call(s32[4,4]{1,0:T(4,128)S(1)} %copy-done.15, bf16[512,1024]{1,0:T(8,128)(2,1)S(1)} %bitcast.29, bf16[512,1024]{1,0:T(8,128)(2,1)S(1)} %bitcast.32, bf16[512,1024]{1,0:T(8,128)(2,1)S(1)} %bitcast.35), custom_call_target="tpu_custom_call" | custom-call | flops 268435456 | bytes 2097152 | tf_op jit(solution)/shard_map/row_forward/pallas_call | solution.py:189
  41.6 3.8 %collective-permute-done.1.a_ref = bf16[64,1024]{1,0:T(8,128)(2,1)} collective-permute-done((bf16[64,1024]{1,0:T(8,128)(2,1)S(1)}, bf16[64,1024]{1,0:T(8,128)(2,1)}, u32[]{:S(2)}, u32[]{:S(2)}) %collective-permute-start.1) | collective-permute-done | bytes 131104 | tf_op jit(solution)/shard_map/ppermute | solution.py:496
  47.1 2.5 %collective-permute-start.6 = (bf16[256,1024]{1,0:T(8,128)(2,1)}, bf16[256,1024]{1,0:T(8,128)(2,1)}, u32[]{:S(2)}, u32[]{:S(2)}) collective-permute-start(bf16[256,1024]{1,0:T(8,128)(2,1)} %gather_y.1.own_ref), channel_id=1, source_target_pairs={{0,192},{64,0},{128,64},{192,128},{1,193},{65,1},{129,65},{193,129... | collective-permute-start | bytes 1572872 | tf_op jit(solution)/shard_map/ppermute | solution.py:496
  50.7 19.3 %all-to-all-done.1 = bf16[32,16,1536]{2,1,0:T(8,128)(2,1)} async-done(((bf16[32,16,1536]{2,1,0:T(8,128)(2,1)}), bf16[32,16,1536]{2,1,0:T(8,128)(2,1)}, u32[]{:S(2)}, u32[]{:S(2)}) %all-to-all-start.1) | async-done | bytes 1572896 | tf_op jit(solution)/shard_map/all_to_all | solution.py:484
  70.0 3.4 %column_forward.1 = bf16[32,2,8,512]{3,2,1,0:T(8,128)(2,1)S(1)} custom-call(bf16[32,2,8,1536]{3,2,1,0:T(8,128)(2,1)} %bitcast.12.r_ref), custom_call_target="tpu_custom_call" | custom-call | flops 99999997952 | bytes 2097152 | tf_op jit(solution)/shard_map/column_forward/pallas_call | solution.py:130
  74.3 2.2 %collective-permute-done.4.a_ref = bf16[256,1024]{1,0:T(8,128)(2,1)} collective-permute-done((bf16[256,1024]{1,0:T(8,128)(2,1)}, bf16[256,1024]{1,0:T(8,128)(2,1)}, u32[]{:S(2)}, u32[]{:S(2)}) %collective-permute-start.4) | collective-permute-done | bytes 524320 | tf_op jit(solution)/shard_map/ppermute | solution.py:496
  76.5 3.0 %gather_x.1.mine_ref = bf16[1024,1024]{1,0:T(8,128)(2,1)} custom-call(s32[5]{0:T(128)S(1)} %stack.23.place.core_ref, bf16[256,1024]{1,0:T(8,128)(2,1)} %gather_y.1.own_ref, bf16[256,1024]{1,0:T(8,128)(2,1)} %collective-permute-done.4.a_ref, bf16[256,1024]{1,0:T(8,128)(2,1)} %collective-permute-done.5.b_ref, bf16[256,1024]{1,0:T(8,128)(2,1)} %collective-permute-done.6.c_ref), custom_call_target="tpu_custom_call" | custom-call | bytes 4194304 | tf_op jit(solution)/shard_map/gather_x/pallas_call | solution.py:400
  80.0 9.4 %all-to-all-start.2 = ((bf16[32,16,512]{2,1,0:T(8,128)(2,1)}), bf16[32,16,512]{2,1,0:T(8,128)(2,1)}, u32[]{:S(2)}, u32[]{:S(2)}) async-start(bf16[32,16,512]{2,1,0:T(8,128)(2,1)} %bitcast.40), calls=%async_computation.2 | async-start | bytes 1048576 | tf_op jit(solution)/shard_map/all_to_all | solution.py:484
  89.4 5.5 %attn_grad.1 = (bf16[512,512]{1,0:T(8,128)(2,1)S(1)}, bf16[512,512]{1,0:T(8,128)(2,1)S(1)}) custom-call(s32[5]{0:T(128)S(1)} %stack.23.place.core_ref, bf16[512,2048]{1,0:T(8,128)(2,1)S(1)} %bitcast.26, bf16[512,2048]{1,0:T(8,128)(2,1)S(1)} %bitcast.27, bf16[1024,1024]{1,0:T(8,128)(2,1)} %gather_x.1.mine_ref, ...), custom_call_target="tpu_custom_call" | custom-call | flops 2147483648 | bytes 7340032 | tf_op jit(solution)/shard_map/attn_grad/pallas_call | solution.py:277
  96.5 9.4 %all-to-all-done.2 = bf16[32,16,512]{2,1,0:T(8,128)(2,1)} async-done(((bf16[32,16,512]{2,1,0:T(8,128)(2,1)}), bf16[32,16,512]{2,1,0:T(8,128)(2,1)}, u32[]{:S(2)}, u32[]{:S(2)}) %all-to-all-start.2) | async-done | bytes 524320 | tf_op jit(solution)/shard_map/all_to_all | solution.py:484
  107.0 5.0 %all-to-all-start.3 = ((bf16[32,16,512]{2,1,0:T(8,128)(2,1)}), bf16[32,16,512]{2,1,0:T(8,128)(2,1)S(1)}, u32[]{:S(2)}, u32[]{:S(2)}) async-start(bf16[32,16,512]{2,1,0:T(8,128)(2,1)} %bitcast.39), calls=%async_computation.3 | async-start | bytes 1048576 | tf_op jit(solution)/shard_map/all_to_all | solution.py:484
  112.0 7.6 %weight_grad.1 = (f32[256,1024]{1,0:T(8,128)}, bf16[256,1024]{1,0:T(8,128)(2,1)}, bf16[256,1024]{1,0:T(8,128)(2,1)}, bf16[256,1024]{1,0:T(8,128)(2,1)}) custom-call(s32[5]{0:T(128)S(1)} %stack.23.place.core_ref, bf16[512,512]{1,0:T(8,128)(2,1)} %row_forward.1.row_ref.row_mine, bf16[512,512]{1,0:T(8,128)(2,1)} %collective-permute-done.row_theirs, ...), custom_call_target="tpu_custom_call" | custom-call | flops 2147483648 | bytes 7340032 | tf_op jit(solution)/shard_map/weight_grad/pallas_call | solution.py:363
  119.6 2.7 %collective-permute-start.11 = (bf16[256,1024]{1,0:T(8,128)(2,1)}, bf16[256,1024]{1,0:T(8,128)(2,1)}, u32[]{:S(2)}, u32[]{:S(2)}) collective-permute-start(bf16[256,1024]{1,0:T(8,128)(2,1)} %get-tuple-element.79), channel_id=1, source_target_pairs={{0,192},{64,0},{128,64},{192,128},{1,193},{65,1},{129,65},{193,129... | collective-permute-start | bytes 1572872 | tf_op jit(solution)/shard_map/ppermute | solution.py:496
  122.3 9.2 %row_backward.1 = (bf16[512,1024]{1,0:T(8,128)(2,1)}, bf16[512,1024]{1,0:T(8,128)(2,1)}, bf16[512,1024]{1,0:T(8,128)(2,1)}) custom-call(s32[4,4]{1,0:T(4,128)S(1)} %copy-done.15, bf16[512,1024]{1,0:T(8,128)(2,1)S(1)} %bitcast.30, bf16[512,1024]{1,0:T(8,128)(2,1)S(1)} %bitcast.33, bf16[512,1024]{1,0:T(8,128)(2,1)S(1)} %bitcast.36, bf16[512,512]{1,0:T(8,128)(2,1)S(1)} %copy-done.12), custom_call_target="tpu_custom_call" | custom-call | flops 671088640 | bytes 3670016 | tf_op jit(solution)/shard_map/row_backward/pallas_call | solution.py:222
  131.5 7.2 %column_backward.1 = bf16[32,2,8,1536]{3,2,1,0:T(8,128)(2,1)} custom-call(bf16[32,2,8,1536]{3,2,1,0:T(8,128)(2,1)} %bitcast.12.r_ref, bf16[32,2,8,512]{3,2,1,0:T(8,128)(2,1)S(1)} %bitcast.38), custom_call_target="tpu_custom_call" | custom-call | flops 671088640 | bytes 3670016 | tf_op jit(solution)/shard_map/column_backward/pallas_call | solution.py:156
  138.7 6.8 %collective-permute-done.10.b_ref = bf16[256,1024]{1,0:T(8,128)(2,1)S(1)} collective-permute-done((bf16[256,1024]{1,0:T(8,128)(2,1)}, bf16[256,1024]{1,0:T(8,128)(2,1)S(1)}, u32[]{:S(2)}, u32[]{:S(2)}) %collective-permute-start.10) | collective-permute-done | bytes 524320 | tf_op jit(solution)/shard_map/ppermute | solution.py:496
  145.5 10.5 %all-to-all-start.4 = ((bf16[32,16,1536]{2,1,0:T(8,128)(2,1)}), bf16[32,16,1536]{2,1,0:T(8,128)(2,1)S(1)}, u32[]{:S(2)}, u32[]{:S(2)}) async-start(bf16[32,16,1536]{2,1,0:T(8,128)(2,1)} %bitcast.18), calls=%async_computation.4 | async-start | bytes 3145728 | tf_op jit(solution)/shard_map/all_to_all | solution.py:484
  159.3 2.4 %collective-permute-start.14 = (bf16[64,1024]{1,0:T(8,128)(2,1)S(1)}, bf16[64,1024]{1,0:T(8,128)(2,1)S(1)}, u32[]{:S(2)}, u32[]{:S(2)}) collective-permute-start(bf16[64,1024]{1,0:T(8,128)(2,1)S(1)} %get-tuple-element.87), channel_id=1, source_target_pairs={{0,16},{8,24},{16,0},{24,8},{1,17},{9,25},{17,1},{25,9},{2,18},{10... | collective-permute-start | bytes 393224 | tf_op jit(solution)/shard_map/ppermute | solution.py:496
  162.9 6.6 %layer_out.1 = bf16[512,2048]{1,0:T(8,128)(2,1)} custom-call(s32[5]{0:T(128)S(1)} %stack.23.place.core_ref, bf16[512,512]{1,0:T(8,128)(2,1)} %row_forward.1.row_ref.row_mine, bf16[512,512]{1,0:T(8,128)(2,1)} %bitcast.15.col_ref.col_mine, bf16[1024,1024]{1,0:T(8,128)(2,1)S(1)} %copy-done.9, bf16[1024,1024]{1,0:T(8,128)(2,1)} %collective-permute-done.7.theirs_ref), custom_call_target="tpu_custom_call" | custom-call | flops 2147483648 | bytes 7340032 | tf_op jit(solution)/shard_map/layer_out/pallas_call | solution.py:317
  169.5 4.9 %collective-permute-done.13.b_ref = bf16[64,1024]{1,0:T(8,128)(2,1)S(1)} collective-permute-done((bf16[64,1024]{1,0:T(8,128)(2,1)S(1)}, bf16[64,1024]{1,0:T(8,128)(2,1)S(1)}, u32[]{:S(2)}, u32[]{:S(2)}) %collective-permute-start.13) | collective-permute-done | bytes 131104 | tf_op jit(solution)/shard_map/ppermute | solution.py:496
  174.3 4.3 %collective-permute-done.14.c_ref = bf16[64,1024]{1,0:T(8,128)(2,1)S(1)} collective-permute-done((bf16[64,1024]{1,0:T(8,128)(2,1)S(1)}, bf16[64,1024]{1,0:T(8,128)(2,1)S(1)}, u32[]{:S(2)}, u32[]{:S(2)}) %collective-permute-start.14) | collective-permute-done | bytes 131104 | tf_op jit(solution)/shard_map/ppermute | solution.py:496
  179.3 3.7 %collective-permute-start.16 = (bf16[8,1024]{1,0:T(8,128)(2,1)S(1)}, bf16[8,1024]{1,0:T(8,128)(2,1)S(1)}, u32[]{:S(2)}, u32[]{:S(2)}) collective-permute-start(bf16[8,1024]{1,0:T(8,128)(2,1)S(1)} %get-tuple-element.102), channel_id=1, source_target_pairs={{0,2},{2,4},{4,6},{6,0},{32,34},{34,36},{36,38},{38,32},{1,3},{3,5... | collective-permute-start | bytes 49160 | tf_op jit(solution)/shard_map/ppermute | solution.py:501
  183.0 4.0 %collective-permute-start.17 = (bf16[8,1024]{1,0:T(8,128)(2,1)S(1)}, bf16[8,1024]{1,0:T(8,128)(2,1)S(1)}, u32[]{:S(2)}, u32[]{:S(2)}) collective-permute-start(bf16[8,1024]{1,0:T(8,128)(2,1)S(1)} %get-tuple-element.103), channel_id=1, source_target_pairs={{0,4},{2,6},{4,0},{6,2},{32,36},{34,38},{36,32},{38,34},{1,5},{3,7... | collective-permute-start | bytes 49160 | tf_op jit(solution)/shard_map/ppermute | solution.py:501
  187.0 3.5 %collective-permute-start.18 = (bf16[8,1024]{1,0:T(8,128)(2,1)S(1)}, bf16[8,1024]{1,0:T(8,128)(2,1)S(1)}, u32[]{:S(2)}, u32[]{:S(2)}) collective-permute-start(bf16[8,1024]{1,0:T(8,128)(2,1)S(1)} %get-tuple-element.104), channel_id=1, source_target_pairs={{0,6},{2,0},{4,2},{6,4},{32,38},{34,32},{36,34},{38,36},{1,7},{3,1... | collective-permute-start | bytes 49160 | tf_op jit(solution)/shard_map/ppermute | solution.py:501
  190.6 6.8 %collective-permute-start.21 = (bf16[8,1024]{1,0:T(8,128)(2,1)S(1)}, bf16[8,1024]{1,0:T(8,128)(2,1)S(1)}, u32[]{:S(2)}, u32[]{:S(2)}) collective-permute-start(bf16[8,1024]{1,0:T(8,128)(2,1)S(1)} %get-tuple-element.107), channel_id=1, source_target_pairs={{0,36},{2,38},{4,32},{6,34},{32,4},{34,6},{36,0},{38,2},{1,37},{3,... | collective-permute-start | bytes 49160 | tf_op jit(solution)/shard_map/ppermute | solution.py:501
  198.7 3.2 %collective-permute-done.22.refs_7_ = bf16[8,1024]{1,0:T(8,128)(2,1)S(1)} collective-permute-done((bf16[8,1024]{1,0:T(8,128)(2,1)S(1)}, bf16[8,1024]{1,0:T(8,128)(2,1)S(1)}, u32[]{:S(2)}, u32[]{:S(2)}) %collective-permute-start.22) | collective-permute-done | bytes 16416 | tf_op jit(solution)/shard_map/ppermute | solution.py:501
  202.4 2.5 %collective-permute-start.23 = (f32[4,1024]{1,0:T(4,128)S(1)}, f32[4,1024]{1,0:T(4,128)S(1)}, u32[]{:S(2)}, u32[]{:S(2)}) collective-permute-start(f32[4,1024]{1,0:T(4,128)S(1)} %get-tuple-element.110), channel_id=1, source_target_pairs={{0,1},{1,0},{2,3},{3,2},{4,5},{5,4},{6,7},{7,6},{8,9},{9,8},{10,11... | collective-permute-start | bytes 49160 | tf_op jit(solution)/shard_map/ppermute | solution.py:488
  206.4 2.6 %finish.1 = (bf16[512,1024]{1,0:T(8,128)(2,1)}, bf16[512,1024]{1,0:T(8,128)(2,1)}, bf16[512,1024]{1,0:T(8,128)(2,1)}) custom-call(s32[4]{0:T(128)S(1)} %copy-done.17, bf16[512,1536]{1,0:T(8,128)(2,1)S(1)} %bitcast.37, bf16[512,1024]{1,0:T(8,128)(2,1)} %get-tuple-element.91.dq_in, ...), custom_call_target="tpu_custom_call", output_to_operand_aliasing={{0}: (2, {}), {1}: (3, {}), {2}: (4, {})} | custom-call | flops 536870912 | bytes 3145728 | tf_op jit(solution)/shard_map/finish/pallas_call | solution.py:248
  (84 shorter events, 29.3 us)
Async XLA Ops:
  2.1 19.1 %all-to-all-start = ((bf16[16,4,1024]{2,1,0:T(4,128)(2,1)}), bf16[16,4,1024]{2,1,0:T(4,128)(2,1)S(1)}, u32[]{:S(2)}, u32[]{:S(2)}) async-start(bf16[16,4,1024]{2,1,0:T(4,128)(2,1)} %bitcast.6), calls=%async_computation | async-start | bytes 262144 | tf_op jit(solution)/shard_map/all_to_all | solution.py:484
  19.9 14.1 %copy-start.15 = (s32[4,4]{1,0:T(4,128)S(1)}, s32[4,4]{1,0:T(4,128)}, u32[]{:S(2)}) copy-start(s32[4,4]{1,0:T(4,128)} %pat_ref.3) | copy-start | bytes 196
  21.2 48.8 %all-to-all-start.1 = ((bf16[32,16,1536]{2,1,0:T(8,128)(2,1)}), bf16[32,16,1536]{2,1,0:T(8,128)(2,1)}, u32[]{:S(2)}, u32[]{:S(2)}) async-start(bf16[32,16,1536]{2,1,0:T(8,128)(2,1)} %bitcast.41), calls=%async_computation.1 | async-start | bytes 3145728 | tf_op jit(solution)/shard_map/all_to_all | solution.py:484
  30.1 10.6 %collective-permute-start.3 = (bf16[64,1024]{1,0:T(8,128)(2,1)S(1)}, bf16[64,1024]{1,0:T(8,128)(2,1)S(1)}, u32[]{:S(2)}, u32[]{:S(2)}) collective-permute-start(bf16[64,1024]{1,0:T(8,128)(2,1)S(1)} %reshape.77.own_ref), channel_id=1, source_target_pairs={{0,24},{8,0},{16,8},{24,16},{1,25},{9,1},{17,9},{25,17},{2,26},{10... | collective-permute-start | bytes 393224 | tf_op jit(solution)/shard_map/ppermute | solution.py:496
  32.9 8.8 %collective-permute-start.2 = (bf16[64,1024]{1,0:T(8,128)(2,1)S(1)}, bf16[64,1024]{1,0:T(8,128)(2,1)S(1)}, u32[]{:S(2)}, u32[]{:S(2)}) collective-permute-start(bf16[64,1024]{1,0:T(8,128)(2,1)S(1)} %reshape.77.own_ref), channel_id=1, source_target_pairs={{0,16},{8,24},{16,0},{24,8},{1,17},{9,25},{17,1},{25,9},{2,18},{10... | collective-permute-start | bytes 393224 | tf_op jit(solution)/shard_map/ppermute | solution.py:496
  33.4 12.0 %collective-permute-start.1 = (bf16[64,1024]{1,0:T(8,128)(2,1)S(1)}, bf16[64,1024]{1,0:T(8,128)(2,1)}, u32[]{:S(2)}, u32[]{:S(2)}) collective-permute-start(bf16[64,1024]{1,0:T(8,128)(2,1)S(1)} %reshape.77.own_ref), channel_id=1, source_target_pairs={{0,8},{8,16},{16,24},{24,0},{1,9},{9,17},{17,25},{25,1},{2,10},{10... | collective-permute-start | bytes 393224 | tf_op jit(solution)/shard_map/ppermute | solution.py:496
  39.4 34.8 %collective-permute-start = (bf16[512,512]{1,0:T(8,128)(2,1)}, bf16[512,512]{1,0:T(8,128)(2,1)}, u32[]{:S(2)}, u32[]{:S(2)}) collective-permute-start(bf16[512,512]{1,0:T(8,128)(2,1)} %row_forward.1.row_ref.row_mine), channel_id=1, source_target_pairs={{0,1},{1,0},{2,3},{3,2},{4,5},{5,4},{6,7},{7,6},{8,9},{9,8},{10,11... | collective-permute-start | bytes 1572872 | tf_op jit(solution)/shard_map/ppermute | solution.py:488
  47.1 27.2 %collective-permute-start.6 = (bf16[256,1024]{1,0:T(8,128)(2,1)}, bf16[256,1024]{1,0:T(8,128)(2,1)}, u32[]{:S(2)}, u32[]{:S(2)}) collective-permute-start(bf16[256,1024]{1,0:T(8,128)(2,1)} %gather_y.1.own_ref), channel_id=1, source_target_pairs={{0,192},{64,0},{128,64},{192,128},{1,193},{65,1},{129,65},{193,129... | collective-permute-start | bytes 1572872 | tf_op jit(solution)/shard_map/ppermute | solution.py:496
  49.6 24.7 %collective-permute-start.5 = (bf16[256,1024]{1,0:T(8,128)(2,1)}, bf16[256,1024]{1,0:T(8,128)(2,1)}, u32[]{:S(2)}, u32[]{:S(2)}) collective-permute-start(bf16[256,1024]{1,0:T(8,128)(2,1)} %gather_y.1.own_ref), channel_id=1, source_target_pairs={{0,128},{64,192},{128,0},{192,64},{1,129},{65,193},{129,1},{193,65... | collective-permute-start | bytes 1572872 | tf_op jit(solution)/shard_map/ppermute | solution.py:496
  50.1 26.4 %collective-permute-start.4 = (bf16[256,1024]{1,0:T(8,128)(2,1)}, bf16[256,1024]{1,0:T(8,128)(2,1)}, u32[]{:S(2)}, u32[]{:S(2)}) collective-permute-start(bf16[256,1024]{1,0:T(8,128)(2,1)} %gather_y.1.own_ref), channel_id=1, source_target_pairs={{0,64},{64,128},{128,192},{192,0},{1,65},{65,129},{129,193},{193,1... | collective-permute-start | bytes 1572872 | tf_op jit(solution)/shard_map/ppermute | solution.py:496
  79.5 9.9 %collective-permute-start.7 = (bf16[1024,1024]{1,0:T(8,128)(2,1)}, bf16[1024,1024]{1,0:T(8,128)(2,1)}, u32[]{:S(2)}, u32[]{:S(2)}) collective-permute-start(bf16[1024,1024]{1,0:T(8,128)(2,1)} %gather_x.1.mine_ref), channel_id=1, source_target_pairs={{0,1},{1,0},{2,3},{3,2},{4,5},{5,4},{6,7},{7,6},{8,9},{9,8},{10,11... | collective-permute-start | bytes 6291464 | tf_op jit(solution)/shard_map/ppermute | solution.py:488
  80.0 16.6 %collective-permute-start.8 = (bf16[512,1024]{1,0:T(8,128)(2,1)}, bf16[512,1024]{1,0:T(8,128)(2,1)}, u32[]{:S(2)}, u32[]{:S(2)}) collective-permute-start(bf16[512,1024]{1,0:T(8,128)(2,1)} %dynamic-slice_bitcast_fusion), channel_id=1, source_target_pairs={{0,1},{1,0},{2,3},{3,2},{4,5},{5,4},{6,7},{7,6},{8,9},{9,8},{10,11... | collective-permute-start | bytes 3145736 | tf_op jit(solution)/shard_map/ppermute | solution.py:488
  80.0 25.9 %all-to-all-start.2 = ((bf16[32,16,512]{2,1,0:T(8,128)(2,1)}), bf16[32,16,512]{2,1,0:T(8,128)(2,1)}, u32[]{:S(2)}, u32[]{:S(2)}) async-start(bf16[32,16,512]{2,1,0:T(8,128)(2,1)} %bitcast.40), calls=%async_computation.2 | async-start | bytes 1048576 | tf_op jit(solution)/shard_map/all_to_all | solution.py:484
  105.9 6.1 %collective-permute-start.9 = (bf16[512,512]{1,0:T(8,128)(2,1)}, bf16[512,512]{1,0:T(8,128)(2,1)S(1)}, u32[]{:S(2)}, u32[]{:S(2)}) collective-permute-start(bf16[512,512]{1,0:T(8,128)(2,1)} %bitcast.15.col_ref.col_mine), channel_id=1, source_target_pairs={{0,1},{1,0},{2,3},{3,2},{4,5},{5,4},{6,7},{7,6},{8,9},{9,8},{10,11... | collective-permute-start | bytes 1572872 | tf_op jit(solution)/shard_map/ppermute | solution.py:488
  107.0 24.5 %all-to-all-start.3 = ((bf16[32,16,512]{2,1,0:T(8,128)(2,1)}), bf16[32,16,512]{2,1,0:T(8,128)(2,1)S(1)}, u32[]{:S(2)}, u32[]{:S(2)}) async-start(bf16[32,16,512]{2,1,0:T(8,128)(2,1)} %bitcast.39), calls=%async_computation.3 | async-start | bytes 1048576 | tf_op jit(solution)/shard_map/all_to_all | solution.py:484
  119.6 25.9 %collective-permute-start.10 = (bf16[256,1024]{1,0:T(8,128)(2,1)}, bf16[256,1024]{1,0:T(8,128)(2,1)S(1)}, u32[]{:S(2)}, u32[]{:S(2)}) collective-permute-start(bf16[256,1024]{1,0:T(8,128)(2,1)} %get-tuple-element.78), channel_id=1, source_target_pairs={{0,64},{64,128},{128,192},{192,0},{1,65},{65,129},{129,193},{193,1... | collective-permute-start | bytes 1572872 | tf_op jit(solution)/shard_map/ppermute | solution.py:496
  119.6 25.9 %collective-permute-start.11 = (bf16[256,1024]{1,0:T(8,128)(2,1)}, bf16[256,1024]{1,0:T(8,128)(2,1)}, u32[]{:S(2)}, u32[]{:S(2)}) collective-permute-start(bf16[256,1024]{1,0:T(8,128)(2,1)} %get-tuple-element.79), channel_id=1, source_target_pairs={{0,192},{64,0},{128,64},{192,128},{1,193},{65,1},{129,65},{193,129... | collective-permute-start | bytes 1572872 | tf_op jit(solution)/shard_map/ppermute | solution.py:496
  122.3 23.3 %collective-permute-start.12 = (bf16[256,1024]{1,0:T(8,128)(2,1)}, bf16[256,1024]{1,0:T(8,128)(2,1)}, u32[]{:S(2)}, u32[]{:S(2)}) collective-permute-start(bf16[256,1024]{1,0:T(8,128)(2,1)} %get-tuple-element.80), channel_id=1, source_target_pairs={{0,128},{64,192},{128,0},{192,64},{1,129},{65,193},{129,1},{193,65... | collective-permute-start | bytes 1572872 | tf_op jit(solution)/shard_map/ppermute | solution.py:496
  138.7 17.3 %copy-start.10 = (f32[256,1024]{1,0:T(8,128)S(1)}, f32[256,1024]{1,0:T(8,128)}, u32[]{:S(2)}) copy-start(f32[256,1024]{1,0:T(8,128)} %get-tuple-element.81.a_ref) | copy-start | bytes 3145732
  145.5 60.8 %all-to-all-start.4 = ((bf16[32,16,1536]{2,1,0:T(8,128)(2,1)}), bf16[32,16,1536]{2,1,0:T(8,128)(2,1)S(1)}, u32[]{:S(2)}, u32[]{:S(2)}) async-start(bf16[32,16,1536]{2,1,0:T(8,128)(2,1)} %bitcast.18), calls=%async_computation.4 | async-start | bytes 3145728 | tf_op jit(solution)/shard_map/all_to_all | solution.py:484
  157.6 16.7 %collective-permute-start.13 = (bf16[64,1024]{1,0:T(8,128)(2,1)S(1)}, bf16[64,1024]{1,0:T(8,128)(2,1)S(1)}, u32[]{:S(2)}, u32[]{:S(2)}) collective-permute-start(bf16[64,1024]{1,0:T(8,128)(2,1)S(1)} %get-tuple-element.86), channel_id=1, source_target_pairs={{0,8},{8,16},{16,24},{24,0},{1,9},{9,17},{17,25},{25,1},{2,10},{10... | collective-permute-start | bytes 393224 | tf_op jit(solution)/shard_map/ppermute | solution.py:496
  159.3 19.3 %collective-permute-start.14 = (bf16[64,1024]{1,0:T(8,128)(2,1)S(1)}, bf16[64,1024]{1,0:T(8,128)(2,1)S(1)}, u32[]{:S(2)}, u32[]{:S(2)}) collective-permute-start(bf16[64,1024]{1,0:T(8,128)(2,1)S(1)} %get-tuple-element.87), channel_id=1, source_target_pairs={{0,16},{8,24},{16,0},{24,8},{1,17},{9,25},{17,1},{25,9},{2,18},{10... | collective-permute-start | bytes 393224 | tf_op jit(solution)/shard_map/ppermute | solution.py:496
  161.8 44.6 %copy-start.17 = (s32[4]{0:T(128)S(1)}, s32[4]{0:T(128)}, u32[]{:S(2)}) copy-start(s32[4]{0:T(128)} %off_ref.3) | copy-start | bytes 52
  161.8 16.9 %collective-permute-start.15 = (bf16[64,1024]{1,0:T(8,128)(2,1)S(1)}, bf16[64,1024]{1,0:T(8,128)(2,1)S(1)}, u32[]{:S(2)}, u32[]{:S(2)}) collective-permute-start(bf16[64,1024]{1,0:T(8,128)(2,1)S(1)} %get-tuple-element.88), channel_id=1, source_target_pairs={{0,24},{8,0},{16,8},{24,16},{1,25},{9,1},{17,9},{25,17},{2,26},{10... | collective-permute-start | bytes 393224 | tf_op jit(solution)/shard_map/ppermute | solution.py:496
  179.3 11.3 %collective-permute-start.16 = (bf16[8,1024]{1,0:T(8,128)(2,1)S(1)}, bf16[8,1024]{1,0:T(8,128)(2,1)S(1)}, u32[]{:S(2)}, u32[]{:S(2)}) collective-permute-start(bf16[8,1024]{1,0:T(8,128)(2,1)S(1)} %get-tuple-element.102), channel_id=1, source_target_pairs={{0,2},{2,4},{4,6},{6,0},{32,34},{34,36},{36,38},{38,32},{1,3},{3,5... | collective-permute-start | bytes 49160 | tf_op jit(solution)/shard_map/ppermute | solution.py:501
  183.0 14.3 %collective-permute-start.17 = (bf16[8,1024]{1,0:T(8,128)(2,1)S(1)}, bf16[8,1024]{1,0:T(8,128)(2,1)S(1)}, u32[]{:S(2)}, u32[]{:S(2)}) collective-permute-start(bf16[8,1024]{1,0:T(8,128)(2,1)S(1)} %get-tuple-element.103), channel_id=1, source_target_pairs={{0,4},{2,6},{4,0},{6,2},{32,36},{34,38},{36,32},{38,34},{1,5},{3,7... | collective-permute-start | bytes 49160 | tf_op jit(solution)/shard_map/ppermute | solution.py:501
  187.0 10.7 %collective-permute-start.18 = (bf16[8,1024]{1,0:T(8,128)(2,1)S(1)}, bf16[8,1024]{1,0:T(8,128)(2,1)S(1)}, u32[]{:S(2)}, u32[]{:S(2)}) collective-permute-start(bf16[8,1024]{1,0:T(8,128)(2,1)S(1)} %get-tuple-element.104), channel_id=1, source_target_pairs={{0,6},{2,0},{4,2},{6,4},{32,38},{34,32},{36,34},{38,36},{1,7},{3,1... | collective-permute-start | bytes 49160 | tf_op jit(solution)/shard_map/ppermute | solution.py:501
  190.5 7.2 %collective-permute-start.19 = (bf16[8,1024]{1,0:T(8,128)(2,1)S(1)}, bf16[8,1024]{1,0:T(8,128)(2,1)S(1)}, u32[]{:S(2)}, u32[]{:S(2)}) collective-permute-start(bf16[8,1024]{1,0:T(8,128)(2,1)S(1)} %get-tuple-element.105), channel_id=1, source_target_pairs={{0,32},{2,34},{4,36},{6,38},{32,0},{34,2},{36,4},{38,6},{1,33},{3,... | collective-permute-start | bytes 49160 | tf_op jit(solution)/shard_map/ppermute | solution.py:501
  190.5 7.2 %collective-permute-start.20 = (bf16[8,1024]{1,0:T(8,128)(2,1)S(1)}, bf16[8,1024]{1,0:T(8,128)(2,1)S(1)}, u32[]{:S(2)}, u32[]{:S(2)}) collective-permute-start(bf16[8,1024]{1,0:T(8,128)(2,1)S(1)} %get-tuple-element.106), channel_id=1, source_target_pairs={{0,34},{2,36},{4,38},{6,32},{32,2},{34,4},{36,6},{38,0},{1,35},{3,... | collective-permute-start | bytes 49160 | tf_op jit(solution)/shard_map/ppermute | solution.py:501
  190.6 8.1 %collective-permute-start.21 = (bf16[8,1024]{1,0:T(8,128)(2,1)S(1)}, bf16[8,1024]{1,0:T(8,128)(2,1)S(1)}, u32[]{:S(2)}, u32[]{:S(2)}) collective-permute-start(bf16[8,1024]{1,0:T(8,128)(2,1)S(1)} %get-tuple-element.107), channel_id=1, source_target_pairs={{0,36},{2,38},{4,32},{6,34},{32,4},{34,6},{36,0},{38,2},{1,37},{3,... | collective-permute-start | bytes 49160 | tf_op jit(solution)/shard_map/ppermute | solution.py:501
  197.4 4.5 %collective-permute-start.22 = (bf16[8,1024]{1,0:T(8,128)(2,1)S(1)}, bf16[8,1024]{1,0:T(8,128)(2,1)S(1)}, u32[]{:S(2)}, u32[]{:S(2)}) collective-permute-start(bf16[8,1024]{1,0:T(8,128)(2,1)S(1)} %get-tuple-element.108), channel_id=1, source_target_pairs={{0,38},{2,32},{4,34},{6,36},{32,6},{34,0},{36,2},{38,4},{1,39},{3,... | collective-permute-start | bytes 49160 | tf_op jit(solution)/shard_map/ppermute | solution.py:501
  202.4 3.3 %collective-permute-start.23 = (f32[4,1024]{1,0:T(4,128)S(1)}, f32[4,1024]{1,0:T(4,128)S(1)}, u32[]{:S(2)}, u32[]{:S(2)}) collective-permute-start(f32[4,1024]{1,0:T(4,128)S(1)} %get-tuple-element.110), channel_id=1, source_target_pairs={{0,1},{1,0},{2,3},{3,2},{4,5},{5,4},{6,7},{7,6},{8,9},{9,8},{10,11... | collective-permute-start | bytes 49160 | tf_op jit(solution)/shard_map/ppermute | solution.py:488
  (15 other events, 63.5 us)

commit v7 on v6

--- a/solution.py
+++ b/solution.py
@@ -532,26 +532,27 @@
     theirs = other_core(mine)
     og_theirs = other_core(og_sent)
     grad_rows, grad_cols = attn_grad_of(og, mine, theirs, place)
-    col_mine, grad_cols, og_theirs = together(col_mine, grad_cols, og_theirs)
+    dq, dk, dv = row_backward(q, k, v, grad_rows, block_pattern)
+    col_mine, grad_cols, og_theirs, dq, dk, dv = together(col_mine, grad_cols, og_theirs, dq, dk, dv)
     col_mine = col_mine.reshape(COLS, HALF)
 
     col_grads = exchange(grad_cols.reshape(seq, COLS // seq, HALF), SEQ)
     col_theirs = other_core(col_mine)
     parts = weight_grad_of(row_out, row_theirs, col_mine, col_theirs, og, og_theirs, place)
-    x_parts = [parts[0]] + [along(parts[step], "x", step) for step in (1, 3, 2)]
-    dq, dk, dv = row_backward(q, k, v, grad_rows, block_pattern)
-    col_grads, dq, dk, dv = together(col_grads, dq, dk, dv)
+    next_x, far_x, last_x = (along(parts[step], "x", step) for step in (1, 2, 3))
 
     col_back = column_backward(received, col_grads.reshape(ROWS, 2, GRP, HALF)).reshape(seq, COLS // seq, 3 * HALF)
-    col_back, *x_parts = together(col_back, *x_parts)
+    col_back, next_x, last_x = together(col_back, next_x, last_x)
     back = exchange(col_back, SEQ).reshape(COLS, 3 * HALF)
 
-    parts = weight_sum(x_parts, place)
+    parts = weight_sum([parts[0], next_x, far_x, last_x], place)
     layer = layer_out_of(row_out, col_mine, mine, theirs, place)
     parts = [parts[0]] + [along(parts[step], "y", step) for step in (1, 2, 3)]
     layer, *parts = together(layer, *parts)
     parts = y_sum(parts, place)
     parts = [parts[0]] + [along_z(parts[step], step) for step in range(1, 8)]
+    dq, dk, dv = finish(back, dq, dk, dv, col_offset)
+    dq, dk, dv, *parts = together(dq, dk, dv, *parts)
     keep, give = z_sum(parts, place)
     taken = other_core(give)
     first = core == 0
@@ -559,7 +560,6 @@
     w_grad = jnp.concatenate([jnp.where(first, keep, taken), jnp.where(first, taken, keep)], axis=1)
     w_grad = w_grad * tokens ** (-0.5)
 
-    dq, dk, dv = finish(back, dq, dk, dv, col_offset)
     lead = (1, 1, COLS)
     return (
         layer.reshape(lead + (D,)),

time: 210 us -> 213 us (1.014)
  starting transfers between devices: 82.8 us -> 93.1 us
  waiting for transfers between devices: 57.8 us -> 49.6 us
    ppermute x7, starting transfers between devices: 18.4 us -> 25.9 us  [along_z(): return lax.ppermute(tensor, ('zl', 'zh'), turns)]
    ppermute x7, waiting for transfers between devices: 4.11 us -> 0.02 us  [along_z(): return lax.ppermute(tensor, ('zl', 'zh'), turns)]
    all_to_all x5, waiting for transfers between devices: 30 us -> 27.5 us  [exchange(): return lax.all_to_all(tensor, axes, split_axis=0, concat_axis=0, tiled=True)]
  transfers between devices with their start and end apart: 29 -> 29, of which waited for: 12 -> 10; matrix products, arithmetic and copies ran while one was open for 1% -> 1% of each run, Pallas kernels for 24% -> 24%
where the time goes in v7:
time: 213 us; the launch traced here: 212 us
  starting transfers between devices  93.1 us (44%)
  Pallas kernels  54.4 us (26%)
  waiting for transfers between devices  49.6 us (23%)
  local copies, waits for them, and re-layouts  12.9 us (6%)
    all_to_all x5, starting transfers between devices, exchange(): return lax.all_to_all(tensor, axes, split_axis=0, concat_axis=0, tiled=True)  45.6 us
    all_to_all x5, waiting for transfers between devices, exchange(): return lax.all_to_all(tensor, axes, split_axis=0, concat_axis=0, tiled=True)  27.5 us
    ppermute x7, starting transfers between devices, along_z(): return lax.ppermute(tensor, ('zl', 'zh'), turns)  25.9 us
    ppermute x12, waiting for transfers between devices, along(): return lax.ppermute(tensor, axis, [(i, (i + step) % 4) for i in range(4)])  21.3 us
    ppermute x12, starting transfers between devices, along(): return lax.ppermute(tensor, axis, [(i, (i + step) % 4) for i in range(4)])  16.1 us
    unnamed x36, local copies, waits for them, and re-layouts  10.3 us
    pallas_call x1, Pallas kernels, row_backward(): pl.pallas_call(row_backward_kernel, grid=(1,), out_shape=(whole, whole, w...  9.13 us
    pallas_call x1, Pallas kernels, column_backward(): pl.pallas_call(column_backward_kernel, grid=(2,), out_shape=jax.ShapeDtyp...  7.24 us
  transfers between devices with their start and end apart: 29, of which 10 were waited for; matrix products, arithmetic and copies ran while one was open for 1% of the time, Pallas kernels for 24%

profile of v7, /device:TPU:1, one launch (start us, length us, event | category | flops | bytes accessed | tf_op | source)
XLA Modules:
  0.0 211.5 jit_solution(764017543668930830)
XLA Ops:
  2.1 10.0 %all-to-all-start = ((bf16[16,4,1024]{2,1,0:T(4,128)(2,1)}), bf16[16,4,1024]{2,1,0:T(4,128)(2,1)S(1)}, u32[]{:S(2)}, u32[]{:S(2)}) async-start(bf16[16,4,1024]{2,1,0:T(4,128)(2,1)} %bitcast.6), calls=%async_computation | async-start | bytes 262144 | tf_op jit(solution)/shard_map/all_to_all | solution.py:484
  16.4 2.4 %pack.1 = bf16[512,1536]{1,0:T(8,128)(2,1)} custom-call(s32[4]{0:T(128)S(1)} %copy-done.15, bf16[512,1024]{1,0:T(8,128)(2,1)S(1)} %bitcast.28, bf16[512,1024]{1,0:T(8,128)(2,1)S(1)} %bitcast.31, bf16[512,1024]{1,0:T(8,128)(2,1)S(1)} %bitcast.34), custom_call_target="tpu_custom_call" | custom-call | flops 536870912 | bytes 3145728 | tf_op jit(solution)/shard_map/pack/pallas_call | solution.py:79
  21.2 8.9 %all-to-all-start.1 = ((bf16[32,16,1536]{2,1,0:T(8,128)(2,1)}), bf16[32,16,1536]{2,1,0:T(8,128)(2,1)}, u32[]{:S(2)}, u32[]{:S(2)}) async-start(bf16[32,16,1536]{2,1,0:T(8,128)(2,1)} %bitcast.40), calls=%async_computation.1 | async-start | bytes 3145728 | tf_op jit(solution)/shard_map/all_to_all | solution.py:484
  30.2 2.7 %collective-permute-start.3 = (bf16[64,1024]{1,0:T(8,128)(2,1)S(1)}, bf16[64,1024]{1,0:T(8,128)(2,1)S(1)}, u32[]{:S(2)}, u32[]{:S(2)}) collective-permute-start(bf16[64,1024]{1,0:T(8,128)(2,1)S(1)} %reshape.77.own_ref), channel_id=1, source_target_pairs={{0,24},{8,0},{16,8},{24,16},{1,25},{9,1},{17,9},{25,17},{2,26},{10... | collective-permute-start | bytes 393224 | tf_op jit(solution)/shard_map/ppermute | solution.py:496
  36.5 3.0 %row_forward.1.row_ref.row_mine = bf16[512,512]{1,0:T(8,128)(2,1)} custom-call(s32[4,4]{1,0:T(4,128)S(1)} %copy-done.14, bf16[512,1024]{1,0:T(8,128)(2,1)S(1)} %bitcast.29, bf16[512,1024]{1,0:T(8,128)(2,1)S(1)} %bitcast.32, bf16[512,1024]{1,0:T(8,128)(2,1)S(1)} %bitcast.35), custom_call_target="tpu_custom_call" | custom-call | flops 268435456 | bytes 2097152 | tf_op jit(solution)/shard_map/row_forward/pallas_call | solution.py:189
  41.6 3.8 %collective-permute-done.1.a_ref = bf16[64,1024]{1,0:T(8,128)(2,1)} collective-permute-done((bf16[64,1024]{1,0:T(8,128)(2,1)S(1)}, bf16[64,1024]{1,0:T(8,128)(2,1)}, u32[]{:S(2)}, u32[]{:S(2)}) %collective-permute-start.1) | collective-permute-done | bytes 131104 | tf_op jit(solution)/shard_map/ppermute | solution.py:496
  45.4 1.7 gather_y.1.own_ref
  47.1 2.5 %collective-permute-start.6 = (bf16[256,1024]{1,0:T(8,128)(2,1)}, bf16[256,1024]{1,0:T(8,128)(2,1)}, u32[]{:S(2)}, u32[]{:S(2)}) collective-permute-start(bf16[256,1024]{1,0:T(8,128)(2,1)} %gather_y.1.own_ref), channel_id=1, source_target_pairs={{0,192},{64,0},{128,64},{192,128},{1,193},{65,1},{129,65},{193,129... | collective-permute-start | bytes 1572872 | tf_op jit(solution)/shard_map/ppermute | solution.py:496
  50.7 19.3 %all-to-all-done.1 = bf16[32,16,1536]{2,1,0:T(8,128)(2,1)} async-done(((bf16[32,16,1536]{2,1,0:T(8,128)(2,1)}), bf16[32,16,1536]{2,1,0:T(8,128)(2,1)}, u32[]{:S(2)}, u32[]{:S(2)}) %all-to-all-start.1) | async-done | bytes 1572896 | tf_op jit(solution)/shard_map/all_to_all | solution.py:484
  70.1 3.4 %column_forward.1 = bf16[32,2,8,512]{3,2,1,0:T(8,128)(2,1)S(1)} custom-call(bf16[32,2,8,1536]{3,2,1,0:T(8,128)(2,1)} %bitcast.12.r_ref), custom_call_target="tpu_custom_call" | custom-call | flops 99999997952 | bytes 2097152 | tf_op jit(solution)/shard_map/column_forward/pallas_call | solution.py:130
  74.3 2.2 %collective-permute-done.4.a_ref = bf16[256,1024]{1,0:T(8,128)(2,1)} collective-permute-done((bf16[256,1024]{1,0:T(8,128)(2,1)}, bf16[256,1024]{1,0:T(8,128)(2,1)}, u32[]{:S(2)}, u32[]{:S(2)}) %collective-permute-start.4) | collective-permute-done | bytes 524320 | tf_op jit(solution)/shard_map/ppermute | solution.py:496
  76.5 3.0 %gather_x.1.mine_ref = bf16[1024,1024]{1,0:T(8,128)(2,1)} custom-call(s32[5]{0:T(128)S(1)} %stack.23.place.core_ref, bf16[256,1024]{1,0:T(8,128)(2,1)} %gather_y.1.own_ref, bf16[256,1024]{1,0:T(8,128)(2,1)} %collective-permute-done.4.a_ref, bf16[256,1024]{1,0:T(8,128)(2,1)} %collective-permute-done.5.b_ref, bf16[256,1024]{1,0:T(8,128)(2,1)} %collective-permute-done.6.c_ref), custom_call_target="tpu_custom_call" | custom-call | bytes 4194304 | tf_op jit(solution)/shard_map/gather_x/pallas_call | solution.py:400
  80.0 9.4 %all-to-all-start.2 = ((bf16[32,16,512]{2,1,0:T(8,128)(2,1)}), bf16[32,16,512]{2,1,0:T(8,128)(2,1)}, u32[]{:S(2)}, u32[]{:S(2)}) async-start(bf16[32,16,512]{2,1,0:T(8,128)(2,1)} %bitcast.39), calls=%async_computation.2 | async-start | bytes 1048576 | tf_op jit(solution)/shard_map/all_to_all | solution.py:484
  89.5 6.2 %attn_grad.1 = (bf16[512,512]{1,0:T(8,128)(2,1)S(1)}, bf16[512,512]{1,0:T(8,128)(2,1)}) custom-call(s32[5]{0:T(128)S(1)} %stack.23.place.core_ref, bf16[512,2048]{1,0:T(8,128)(2,1)S(1)} %bitcast.26, bf16[512,2048]{1,0:T(8,128)(2,1)S(1)} %bitcast.27, bf16[1024,1024]{1,0:T(8,128)(2,1)} %gather_x.1.mine_ref, bf16[1024,1024]{1,0:T(8,128)(2,1)} %collective-permute-done.7.theirs_ref), custom_call_target="tpu_custom_call" | custom-call | flops 2147483648 | bytes 7340032 | tf_op jit(solution)/shard_map/attn_grad/pallas_call | solution.py:277
  95.7 9.1 %row_backward.1 = (bf16[512,1024]{1,0:T(8,128)(2,1)}, bf16[512,1024]{1,0:T(8,128)(2,1)}, bf16[512,1024]{1,0:T(8,128)(2,1)}) custom-call(s32[4,4]{1,0:T(4,128)S(1)} %copy-done.14, bf16[512,1024]{1,0:T(8,128)(2,1)S(1)} %bitcast.30, bf16[512,1024]{1,0:T(8,128)(2,1)S(1)} %bitcast.33, bf16[512,1024]{1,0:T(8,128)(2,1)S(1)} %bitcast.36, ...), custom_call_target="tpu_custom_call" | custom-call | flops 671088640 | bytes 3670016 | tf_op jit(solution)/shard_map/row_backward/pallas_call | solution.py:222
  107.0 7.8 %all-to-all-start.3 = ((bf16[32,16,512]{2,1,0:T(8,128)(2,1)}), bf16[32,16,512]{2,1,0:T(8,128)(2,1)S(1)}, u32[]{:S(2)}, u32[]{:S(2)}) async-start(bf16[32,16,512]{2,1,0:T(8,128)(2,1)} %bitcast.16), calls=%async_computation.3 | async-start | bytes 1048576 | tf_op jit(solution)/shard_map/all_to_all | solution.py:484
  114.8 7.1 %weight_grad.1 = (f32[256,1024]{1,0:T(8,128)}, bf16[256,1024]{1,0:T(8,128)(2,1)}, bf16[256,1024]{1,0:T(8,128)(2,1)S(1)}, bf16[256,1024]{1,0:T(8,128)(2,1)S(1)}) custom-call(s32[5]{0:T(128)S(1)} %stack.23.place.core_ref, bf16[512,512]{1,0:T(8,128)(2,1)} %row_forward.1.row_ref.row_mine, bf16[512,512]{1,0:T(8,128)(2,1)} %collective-permute-done.row_theirs, ...), custom_call_target="tpu_custom_call" | custom-call | flops 2147483648 | bytes 7340032 | tf_op jit(solution)/shard_map/weight_grad/pallas_call | solution.py:363
  122.8 2.7 %collective-permute-start.11 = (bf16[256,1024]{1,0:T(8,128)(2,1)S(1)}, bf16[256,1024]{1,0:T(8,128)(2,1)S(1)}, u32[]{:S(2)}, u32[]{:S(2)}) collective-permute-start(bf16[256,1024]{1,0:T(8,128)(2,1)S(1)} %get-tuple-element.86), channel_id=1, source_target_pairs={{0,192},{64,0},{128,64},{192,128},{1,193},{65,1},{129,65},{193,129... | collective-permute-start | bytes 1572872 | tf_op jit(solution)/shard_map/ppermute | solution.py:496
  125.4 5.8 %all-to-all-done.3 = bf16[32,16,512]{2,1,0:T(8,128)(2,1)S(1)} async-done(((bf16[32,16,512]{2,1,0:T(8,128)(2,1)}), bf16[32,16,512]{2,1,0:T(8,128)(2,1)S(1)}, u32[]{:S(2)}, u32[]{:S(2)}) %all-to-all-start.3) | async-done | bytes 524320 | tf_op jit(solution)/shard_map/all_to_all | solution.py:484
  131.3 7.2 %column_backward.1 = bf16[32,2,8,1536]{3,2,1,0:T(8,128)(2,1)} custom-call(bf16[32,2,8,1536]{3,2,1,0:T(8,128)(2,1)} %bitcast.12.r_ref, bf16[32,2,8,512]{3,2,1,0:T(8,128)(2,1)S(1)} %bitcast.38), custom_call_target="tpu_custom_call" | custom-call | flops 671088640 | bytes 3670016 | tf_op jit(solution)/shard_map/column_backward/pallas_call | solution.py:156
  139.3 9.4 %all-to-all-start.4 = ((bf16[32,16,1536]{2,1,0:T(8,128)(2,1)}), bf16[32,16,1536]{2,1,0:T(8,128)(2,1)S(1)}, u32[]{:S(2)}, u32[]{:S(2)}) async-start(bf16[32,16,1536]{2,1,0:T(8,128)(2,1)} %bitcast.18), calls=%async_computation.4 | async-start | bytes 3145728 | tf_op jit(solution)/shard_map/all_to_all | solution.py:484
  149.8 14.0 %collective-permute-done.12.c_ref = bf16[256,1024]{1,0:T(8,128)(2,1)S(1)} collective-permute-done((bf16[256,1024]{1,0:T(8,128)(2,1)}, bf16[256,1024]{1,0:T(8,128)(2,1)S(1)}, u32[]{:S(2)}, u32[]{:S(2)}) %collective-permute-start.12) | collective-permute-done | bytes 524320 | tf_op jit(solution)/shard_map/ppermute | solution.py:496
  167.0 2.4 %collective-permute-start.14 = (bf16[64,1024]{1,0:T(8,128)(2,1)S(1)}, bf16[64,1024]{1,0:T(8,128)(2,1)S(1)}, u32[]{:S(2)}, u32[]{:S(2)}) collective-permute-start(bf16[64,1024]{1,0:T(8,128)(2,1)S(1)} %get-tuple-element.92), channel_id=1, source_target_pairs={{0,16},{8,24},{16,0},{24,8},{1,17},{9,25},{17,1},{25,9},{2,18},{10... | collective-permute-start | bytes 393224 | tf_op jit(solution)/shard_map/ppermute | solution.py:496
  170.6 6.6 %layer_out.1 = bf16[512,2048]{1,0:T(8,128)(2,1)} custom-call(s32[5]{0:T(128)S(1)} %stack.23.place.core_ref, bf16[512,512]{1,0:T(8,128)(2,1)} %row_forward.1.row_ref.row_mine, bf16[512,512]{1,0:T(8,128)(2,1)} %bitcast.15.col_ref.col_mine, bf16[1024,1024]{1,0:T(8,128)(2,1)S(1)} %copy-done.9, bf16[1024,1024]{1,0:T(8,128)(2,1)} %collective-permute-done.7.theirs_ref), custom_call_target="tpu_custom_call" | custom-call | flops 2147483648 | bytes 7340032 | tf_op jit(solution)/shard_map/layer_out/pallas_call | solution.py:317
  178.1 2.3 %collective-permute-start.16 = (bf16[8,1024]{1,0:T(8,128)(2,1)S(1)}, bf16[8,1024]{1,0:T(8,128)(2,1)S(1)}, u32[]{:S(2)}, u32[]{:S(2)}) collective-permute-start(bf16[8,1024]{1,0:T(8,128)(2,1)S(1)} %get-tuple-element.107), channel_id=1, source_target_pairs={{0,2},{2,4},{4,6},{6,0},{32,34},{34,36},{36,38},{38,32},{1,3},{3,5... | collective-permute-start | bytes 49160 | tf_op jit(solution)/shard_map/ppermute | solution.py:501
  180.4 4.1 %collective-permute-start.17 = (bf16[8,1024]{1,0:T(8,128)(2,1)S(1)}, bf16[8,1024]{1,0:T(8,128)(2,1)S(1)}, u32[]{:S(2)}, u32[]{:S(2)}) collective-permute-start(bf16[8,1024]{1,0:T(8,128)(2,1)S(1)} %get-tuple-element.108), channel_id=1, source_target_pairs={{0,4},{2,6},{4,0},{6,2},{32,36},{34,38},{36,32},{38,34},{1,5},{3,7... | collective-permute-start | bytes 49160 | tf_op jit(solution)/shard_map/ppermute | solution.py:501
  184.5 2.1 collective-permute-start.18
  186.6 12.9 %collective-permute-start.19 = (bf16[8,1024]{1,0:T(8,128)(2,1)S(1)}, bf16[8,1024]{1,0:T(8,128)(2,1)S(1)}, u32[]{:S(2)}, u32[]{:S(2)}) collective-permute-start(bf16[8,1024]{1,0:T(8,128)(2,1)S(1)} %get-tuple-element.110), channel_id=1, source_target_pairs={{0,32},{2,34},{4,36},{6,38},{32,0},{34,2},{36,4},{38,6},{1,33},{3,... | collective-permute-start | bytes 49160 | tf_op jit(solution)/shard_map/ppermute | solution.py:501
  200.2 1.5 collective-permute-start.21
  201.7 2.3 %collective-permute-start.22 = (bf16[8,1024]{1,0:T(8,128)(2,1)S(1)}, bf16[8,1024]{1,0:T(8,128)(2,1)S(1)}, u32[]{:S(2)}, u32[]{:S(2)}) collective-permute-start(bf16[8,1024]{1,0:T(8,128)(2,1)S(1)} %get-tuple-element.113), channel_id=1, source_target_pairs={{0,38},{2,32},{4,34},{6,36},{32,6},{34,0},{36,2},{38,4},{1,39},{3,... | collective-permute-start | bytes 49160 | tf_op jit(solution)/shard_map/ppermute | solution.py:501
  204.0 2.6 %finish.1 = (bf16[512,1024]{1,0:T(8,128)(2,1)}, bf16[512,1024]{1,0:T(8,128)(2,1)}, bf16[512,1024]{1,0:T(8,128)(2,1)}) custom-call(s32[4]{0:T(128)S(1)} %copy-done.16, bf16[512,1536]{1,0:T(8,128)(2,1)S(1)} %bitcast.37, bf16[512,1024]{1,0:T(8,128)(2,1)} %get-tuple-element.96.dq_in, ...), custom_call_target="tpu_custom_call", output_to_operand_aliasing={{0}: (2, {}), {1}: (3, {}), {2}: (4, {})} | custom-call | flops 536870912 | bytes 3145728 | tf_op jit(solution)/shard_map/finish/pallas_call | solution.py:248
  207.2 2.9 %collective-permute-start.23 = (f32[4,1024]{1,0:T(4,128)S(1)}, f32[4,1024]{1,0:T(4,128)S(1)}, u32[]{:S(2)}, u32[]{:S(2)}) collective-permute-start(f32[4,1024]{1,0:T(4,128)S(1)} %get-tuple-element.126), channel_id=1, source_target_pairs={{0,1},{1,0},{2,3},{3,2},{4,5},{5,4},{6,7},{7,6},{8,9},{9,8},{10,11... | collective-permute-start | bytes 49160 | tf_op jit(solution)/shard_map/ppermute | solution.py:488
  (84 shorter events, 29.2 us)
Async XLA Ops:
  2.1 19.1 %all-to-all-start = ((bf16[16,4,1024]{2,1,0:T(4,128)(2,1)}), bf16[16,4,1024]{2,1,0:T(4,128)(2,1)S(1)}, u32[]{:S(2)}, u32[]{:S(2)}) async-start(bf16[16,4,1024]{2,1,0:T(4,128)(2,1)} %bitcast.6), calls=%async_computation | async-start | bytes 262144 | tf_op jit(solution)/shard_map/all_to_all | solution.py:484
  21.2 48.8 %all-to-all-start.1 = ((bf16[32,16,1536]{2,1,0:T(8,128)(2,1)}), bf16[32,16,1536]{2,1,0:T(8,128)(2,1)}, u32[]{:S(2)}, u32[]{:S(2)}) async-start(bf16[32,16,1536]{2,1,0:T(8,128)(2,1)} %bitcast.40), calls=%async_computation.1 | async-start | bytes 3145728 | tf_op jit(solution)/shard_map/all_to_all | solution.py:484
  30.2 10.5 %collective-permute-start.3 = (bf16[64,1024]{1,0:T(8,128)(2,1)S(1)}, bf16[64,1024]{1,0:T(8,128)(2,1)S(1)}, u32[]{:S(2)}, u32[]{:S(2)}) collective-permute-start(bf16[64,1024]{1,0:T(8,128)(2,1)S(1)} %reshape.77.own_ref), channel_id=1, source_target_pairs={{0,24},{8,0},{16,8},{24,16},{1,25},{9,1},{17,9},{25,17},{2,26},{10... | collective-permute-start | bytes 393224 | tf_op jit(solution)/shard_map/ppermute | solution.py:496
  32.9 8.8 %collective-permute-start.2 = (bf16[64,1024]{1,0:T(8,128)(2,1)S(1)}, bf16[64,1024]{1,0:T(8,128)(2,1)S(1)}, u32[]{:S(2)}, u32[]{:S(2)}) collective-permute-start(bf16[64,1024]{1,0:T(8,128)(2,1)S(1)} %reshape.77.own_ref), channel_id=1, source_target_pairs={{0,16},{8,24},{16,0},{24,8},{1,17},{9,25},{17,1},{25,9},{2,18},{10... | collective-permute-start | bytes 393224 | tf_op jit(solution)/shard_map/ppermute | solution.py:496
  33.4 12.0 %collective-permute-start.1 = (bf16[64,1024]{1,0:T(8,128)(2,1)S(1)}, bf16[64,1024]{1,0:T(8,128)(2,1)}, u32[]{:S(2)}, u32[]{:S(2)}) collective-permute-start(bf16[64,1024]{1,0:T(8,128)(2,1)S(1)} %reshape.77.own_ref), channel_id=1, source_target_pairs={{0,8},{8,16},{16,24},{24,0},{1,9},{9,17},{17,25},{25,1},{2,10},{10... | collective-permute-start | bytes 393224 | tf_op jit(solution)/shard_map/ppermute | solution.py:496
  39.4 34.9 %collective-permute-start = (bf16[512,512]{1,0:T(8,128)(2,1)}, bf16[512,512]{1,0:T(8,128)(2,1)}, u32[]{:S(2)}, u32[]{:S(2)}) collective-permute-start(bf16[512,512]{1,0:T(8,128)(2,1)} %row_forward.1.row_ref.row_mine), channel_id=1, source_target_pairs={{0,1},{1,0},{2,3},{3,2},{4,5},{5,4},{6,7},{7,6},{8,9},{9,8},{10,11... | collective-permute-start | bytes 1572872 | tf_op jit(solution)/shard_map/ppermute | solution.py:488
  47.1 27.1 %collective-permute-start.6 = (bf16[256,1024]{1,0:T(8,128)(2,1)}, bf16[256,1024]{1,0:T(8,128)(2,1)}, u32[]{:S(2)}, u32[]{:S(2)}) collective-permute-start(bf16[256,1024]{1,0:T(8,128)(2,1)} %gather_y.1.own_ref), channel_id=1, source_target_pairs={{0,192},{64,0},{128,64},{192,128},{1,193},{65,1},{129,65},{193,129... | collective-permute-start | bytes 1572872 | tf_op jit(solution)/shard_map/ppermute | solution.py:496
  49.6 24.7 %collective-permute-start.5 = (bf16[256,1024]{1,0:T(8,128)(2,1)}, bf16[256,1024]{1,0:T(8,128)(2,1)}, u32[]{:S(2)}, u32[]{:S(2)}) collective-permute-start(bf16[256,1024]{1,0:T(8,128)(2,1)} %gather_y.1.own_ref), channel_id=1, source_target_pairs={{0,128},{64,192},{128,0},{192,64},{1,129},{65,193},{129,1},{193,65... | collective-permute-start | bytes 1572872 | tf_op jit(solution)/shard_map/ppermute | solution.py:496
  50.1 26.4 %collective-permute-start.4 = (bf16[256,1024]{1,0:T(8,128)(2,1)}, bf16[256,1024]{1,0:T(8,128)(2,1)}, u32[]{:S(2)}, u32[]{:S(2)}) collective-permute-start(bf16[256,1024]{1,0:T(8,128)(2,1)} %gather_y.1.own_ref), channel_id=1, source_target_pairs={{0,64},{64,128},{128,192},{192,0},{1,65},{65,129},{129,193},{193,1... | collective-permute-start | bytes 1572872 | tf_op jit(solution)/shard_map/ppermute | solution.py:496
  79.5 9.9 %collective-permute-start.7 = (bf16[1024,1024]{1,0:T(8,128)(2,1)}, bf16[1024,1024]{1,0:T(8,128)(2,1)}, u32[]{:S(2)}, u32[]{:S(2)}) collective-permute-start(bf16[1024,1024]{1,0:T(8,128)(2,1)} %gather_x.1.mine_ref), channel_id=1, source_target_pairs={{0,1},{1,0},{2,3},{3,2},{4,5},{5,4},{6,7},{7,6},{8,9},{9,8},{10,11... | collective-permute-start | bytes 6291464 | tf_op jit(solution)/shard_map/ppermute | solution.py:488
  80.0 24.9 %collective-permute-start.8 = (bf16[512,1024]{1,0:T(8,128)(2,1)}, bf16[512,1024]{1,0:T(8,128)(2,1)}, u32[]{:S(2)}, u32[]{:S(2)}) collective-permute-start(bf16[512,1024]{1,0:T(8,128)(2,1)} %dynamic-slice_bitcast_fusion), channel_id=1, source_target_pairs={{0,1},{1,0},{2,3},{3,2},{4,5},{5,4},{6,7},{7,6},{8,9},{9,8},{10,11... | collective-permute-start | bytes 3145736 | tf_op jit(solution)/shard_map/ppermute | solution.py:488
  80.0 25.9 %all-to-all-start.2 = ((bf16[32,16,512]{2,1,0:T(8,128)(2,1)}), bf16[32,16,512]{2,1,0:T(8,128)(2,1)}, u32[]{:S(2)}, u32[]{:S(2)}) async-start(bf16[32,16,512]{2,1,0:T(8,128)(2,1)} %bitcast.39), calls=%async_computation.2 | async-start | bytes 1048576 | tf_op jit(solution)/shard_map/all_to_all | solution.py:484
  105.9 8.9 %collective-permute-start.9 = (bf16[512,512]{1,0:T(8,128)(2,1)}, bf16[512,512]{1,0:T(8,128)(2,1)S(1)}, u32[]{:S(2)}, u32[]{:S(2)}) collective-permute-start(bf16[512,512]{1,0:T(8,128)(2,1)} %bitcast.15.col_ref.col_mine), channel_id=1, source_target_pairs={{0,1},{1,0},{2,3},{3,2},{4,5},{5,4},{6,7},{7,6},{8,9},{9,8},{10,11... | collective-permute-start | bytes 1572872 | tf_op jit(solution)/shard_map/ppermute | solution.py:488
  107.0 24.3 %all-to-all-start.3 = ((bf16[32,16,512]{2,1,0:T(8,128)(2,1)}), bf16[32,16,512]{2,1,0:T(8,128)(2,1)S(1)}, u32[]{:S(2)}, u32[]{:S(2)}) async-start(bf16[32,16,512]{2,1,0:T(8,128)(2,1)} %bitcast.16), calls=%async_computation.3 | async-start | bytes 1048576 | tf_op jit(solution)/shard_map/all_to_all | solution.py:484
  122.8 15.7 %collective-permute-start.10 = (bf16[256,1024]{1,0:T(8,128)(2,1)}, bf16[256,1024]{1,0:T(8,128)(2,1)S(1)}, u32[]{:S(2)}, u32[]{:S(2)}) collective-permute-start(bf16[256,1024]{1,0:T(8,128)(2,1)} %get-tuple-element.85), channel_id=1, source_target_pairs={{0,64},{64,128},{128,192},{192,0},{1,65},{65,129},{129,193},{193,1... | collective-permute-start | bytes 1572872 | tf_op jit(solution)/shard_map/ppermute | solution.py:496
  122.8 15.7 %collective-permute-start.11 = (bf16[256,1024]{1,0:T(8,128)(2,1)S(1)}, bf16[256,1024]{1,0:T(8,128)(2,1)S(1)}, u32[]{:S(2)}, u32[]{:S(2)}) collective-permute-start(bf16[256,1024]{1,0:T(8,128)(2,1)S(1)} %get-tuple-element.86), channel_id=1, source_target_pairs={{0,192},{64,0},{128,64},{192,128},{1,193},{65,1},{129,65},{193,129... | collective-permute-start | bytes 1572872 | tf_op jit(solution)/shard_map/ppermute | solution.py:496
  138.5 25.4 %copy-start.10 = (f32[256,1024]{1,0:T(8,128)S(1)}, f32[256,1024]{1,0:T(8,128)}, u32[]{:S(2)}) copy-start(f32[256,1024]{1,0:T(8,128)} %get-tuple-element.83.a_ref) | copy-start | bytes 3145732
  139.3 64.7 %all-to-all-start.4 = ((bf16[32,16,1536]{2,1,0:T(8,128)(2,1)}), bf16[32,16,1536]{2,1,0:T(8,128)(2,1)S(1)}, u32[]{:S(2)}, u32[]{:S(2)}) async-start(bf16[32,16,1536]{2,1,0:T(8,128)(2,1)} %bitcast.18), calls=%async_computation.4 | async-start | bytes 3145728 | tf_op jit(solution)/shard_map/all_to_all | solution.py:484
  148.8 21.8 %copy-start.9 = (bf16[1024,1024]{1,0:T(8,128)(2,1)S(1)}, bf16[1024,1024]{1,0:T(8,128)(2,1)}, u32[]{:S(2)}) copy-start(bf16[1024,1024]{1,0:T(8,128)(2,1)} %gather_x.1.mine_ref) | copy-start | bytes 6291460
  148.8 15.1 %collective-permute-start.12 = (bf16[256,1024]{1,0:T(8,128)(2,1)}, bf16[256,1024]{1,0:T(8,128)(2,1)S(1)}, u32[]{:S(2)}, u32[]{:S(2)}) collective-permute-start(bf16[256,1024]{1,0:T(8,128)(2,1)} %copy-done.17), channel_id=1, source_target_pairs={{0,128},{64,192},{128,0},{192,64},{1,129},{65,193},{129,1},{193,65... | collective-permute-start | bytes 1572872 | tf_op jit(solution)/shard_map/ppermute | solution.py:496
  165.7 11.5 %collective-permute-start.13 = (bf16[64,1024]{1,0:T(8,128)(2,1)S(1)}, bf16[64,1024]{1,0:T(8,128)(2,1)S(1)}, u32[]{:S(2)}, u32[]{:S(2)}) collective-permute-start(bf16[64,1024]{1,0:T(8,128)(2,1)S(1)} %get-tuple-element.91), channel_id=1, source_target_pairs={{0,8},{8,16},{16,24},{24,0},{1,9},{9,17},{17,25},{25,1},{2,10},{10... | collective-permute-start | bytes 393224 | tf_op jit(solution)/shard_map/ppermute | solution.py:496
  167.0 10.5 %collective-permute-start.14 = (bf16[64,1024]{1,0:T(8,128)(2,1)S(1)}, bf16[64,1024]{1,0:T(8,128)(2,1)S(1)}, u32[]{:S(2)}, u32[]{:S(2)}) collective-permute-start(bf16[64,1024]{1,0:T(8,128)(2,1)S(1)} %get-tuple-element.92), channel_id=1, source_target_pairs={{0,16},{8,24},{16,0},{24,8},{1,17},{9,25},{17,1},{25,9},{2,18},{10... | collective-permute-start | bytes 393224 | tf_op jit(solution)/shard_map/ppermute | solution.py:496
  169.5 34.6 %copy-start.16 = (s32[4]{0:T(128)S(1)}, s32[4]{0:T(128)}, u32[]{:S(2)}) copy-start(s32[4]{0:T(128)} %off_ref.3) | copy-start | bytes 52
  169.5 8.0 %collective-permute-start.15 = (bf16[64,1024]{1,0:T(8,128)(2,1)S(1)}, bf16[64,1024]{1,0:T(8,128)(2,1)S(1)}, u32[]{:S(2)}, u32[]{:S(2)}) collective-permute-start(bf16[64,1024]{1,0:T(8,128)(2,1)S(1)} %get-tuple-element.93), channel_id=1, source_target_pairs={{0,24},{8,0},{16,8},{24,16},{1,25},{9,1},{17,9},{25,17},{2,26},{10... | collective-permute-start | bytes 393224 | tf_op jit(solution)/shard_map/ppermute | solution.py:496
  178.1 22.0 %collective-permute-start.16 = (bf16[8,1024]{1,0:T(8,128)(2,1)S(1)}, bf16[8,1024]{1,0:T(8,128)(2,1)S(1)}, u32[]{:S(2)}, u32[]{:S(2)}) collective-permute-start(bf16[8,1024]{1,0:T(8,128)(2,1)S(1)} %get-tuple-element.107), channel_id=1, source_target_pairs={{0,2},{2,4},{4,6},{6,0},{32,34},{34,36},{36,38},{38,32},{1,3},{3,5... | collective-permute-start | bytes 49160 | tf_op jit(solution)/shard_map/ppermute | solution.py:501
  180.4 21.2 %collective-permute-start.17 = (bf16[8,1024]{1,0:T(8,128)(2,1)S(1)}, bf16[8,1024]{1,0:T(8,128)(2,1)S(1)}, u32[]{:S(2)}, u32[]{:S(2)}) collective-permute-start(bf16[8,1024]{1,0:T(8,128)(2,1)S(1)} %get-tuple-element.108), channel_id=1, source_target_pairs={{0,4},{2,6},{4,0},{6,2},{32,36},{34,38},{36,32},{38,34},{1,5},{3,7... | collective-permute-start | bytes 49160 | tf_op jit(solution)/shard_map/ppermute | solution.py:501
  184.5 22.1 %collective-permute-start.18 = (bf16[8,1024]{1,0:T(8,128)(2,1)S(1)}, bf16[8,1024]{1,0:T(8,128)(2,1)S(1)}, u32[]{:S(2)}, u32[]{:S(2)}) collective-permute-start(bf16[8,1024]{1,0:T(8,128)(2,1)S(1)} %get-tuple-element.109), channel_id=1, source_target_pairs={{0,6},{2,0},{4,2},{6,4},{32,38},{34,32},{36,34},{38,36},{1,7},{3,1... | collective-permute-start | bytes 49160 | tf_op jit(solution)/shard_map/ppermute | solution.py:501
  186.6 20.0 %collective-permute-start.19 = (bf16[8,1024]{1,0:T(8,128)(2,1)S(1)}, bf16[8,1024]{1,0:T(8,128)(2,1)S(1)}, u32[]{:S(2)}, u32[]{:S(2)}) collective-permute-start(bf16[8,1024]{1,0:T(8,128)(2,1)S(1)} %get-tuple-element.110), channel_id=1, source_target_pairs={{0,32},{2,34},{4,36},{6,38},{32,0},{34,2},{36,4},{38,6},{1,33},{3,... | collective-permute-start | bytes 49160 | tf_op jit(solution)/shard_map/ppermute | solution.py:501
  199.5 7.1 %collective-permute-start.20 = (bf16[8,1024]{1,0:T(8,128)(2,1)S(1)}, bf16[8,1024]{1,0:T(8,128)(2,1)S(1)}, u32[]{:S(2)}, u32[]{:S(2)}) collective-permute-start(bf16[8,1024]{1,0:T(8,128)(2,1)S(1)} %get-tuple-element.111), channel_id=1, source_target_pairs={{0,34},{2,36},{4,38},{6,32},{32,2},{34,4},{36,6},{38,0},{1,35},{3,... | collective-permute-start | bytes 49160 | tf_op jit(solution)/shard_map/ppermute | solution.py:501
  200.2 6.4 %collective-permute-start.21 = (bf16[8,1024]{1,0:T(8,128)(2,1)S(1)}, bf16[8,1024]{1,0:T(8,128)(2,1)S(1)}, u32[]{:S(2)}, u32[]{:S(2)}) collective-permute-start(bf16[8,1024]{1,0:T(8,128)(2,1)S(1)} %get-tuple-element.112), channel_id=1, source_target_pairs={{0,36},{2,38},{4,32},{6,34},{32,4},{34,6},{36,0},{38,2},{1,37},{3,... | collective-permute-start | bytes 49160 | tf_op jit(solution)/shard_map/ppermute | solution.py:501
  201.7 5.0 %collective-permute-start.22 = (bf16[8,1024]{1,0:T(8,128)(2,1)S(1)}, bf16[8,1024]{1,0:T(8,128)(2,1)S(1)}, u32[]{:S(2)}, u32[]{:S(2)}) collective-permute-start(bf16[8,1024]{1,0:T(8,128)(2,1)S(1)} %get-tuple-element.113), channel_id=1, source_target_pairs={{0,38},{2,32},{4,34},{6,36},{32,6},{34,0},{36,2},{38,4},{1,39},{3,... | collective-permute-start | bytes 49160 | tf_op jit(solution)/shard_map/ppermute | solution.py:501
  207.2 3.7 %collective-permute-start.23 = (f32[4,1024]{1,0:T(4,128)S(1)}, f32[4,1024]{1,0:T(4,128)S(1)}, u32[]{:S(2)}, u32[]{:S(2)}) collective-permute-start(f32[4,1024]{1,0:T(4,128)S(1)} %get-tuple-element.126), channel_id=1, source_target_pairs={{0,1},{1,0},{2,3},{3,2},{4,5},{5,4},{6,7},{7,6},{8,9},{9,8},{10,11... | collective-permute-start | bytes 49160 | tf_op jit(solution)/shard_map/ppermute | solution.py:488
  (15 other events, 53.4 us)

commit v8 on v7

--- a/solution.py
+++ b/solution.py
@@ -334,16 +334,20 @@
     )(core, row_out, col_out, mine, theirs)
 
 
-def weight_grad_kernel(place, row_mine, row_theirs, col_mine, col_theirs, og_mine, og_theirs, *refs):
+def weight_grad_kernel(low, place, a_mine, a_theirs, og_mine, og_theirs, *refs):
     outs, total = refs[:4], refs[4]
     step = pl.program_id(0)
-    block = lax.rem(place[1] + step, 4)
-
-    def product(a_ref, b_ref):
-        total[...] = t_mm(a_ref[...], og_mine[...]) + t_mm(b_ref[...], og_theirs[...])
-
-    pl.when(block < 2)(lambda: product(row_mine, row_theirs))
-    pl.when(block >= 2)(lambda: product(col_mine, col_theirs))
+    local = lax.rem(place[1] + step, 4) - low
+    inside = jnp.logical_and(local >= 0, local < 2)
+
+    @pl.when(inside)
+    def _():
+        total[...] = t_mm(a_mine[...], og_mine[...]) + t_mm(a_theirs[...], og_theirs[...])
+
+    @pl.when(jnp.logical_not(inside))
+    def _():
+        total[...] = jnp.zeros_like(total)
+
     for target, out in enumerate(outs):
 
         @pl.when(step == target)
@@ -351,25 +355,20 @@
             out[...] = total[...].astype(out.dtype)
 
 
-def weight_grad_of(row_mine, row_theirs, col_mine, col_theirs, og, og_theirs, place):
+def weight_grad_of(mine, theirs, og, og_theirs, place, low):
     rows = 2 * HALF // 4
 
-    def row_block(i, at):
-        return (0, jnp.minimum(lax.rem(at[1] + i, 4), 1))
-
-    def col_block(i, at):
-        return (0, jnp.maximum(lax.rem(at[1] + i, 4), 2) - 2)
-
-    return pl.pallas_call(
-        weight_grad_kernel,
+    def block(i, at):
+        return (0, jnp.clip(lax.rem(at[1] + i, 4) - low, 0, 1))
+
+    return pl.pallas_call(
+        functools.partial(weight_grad_kernel, low),
         grid_spec=pltpu.PrefetchScalarGridSpec(
             num_scalar_prefetch=1,
             grid=(4,),
             in_specs=[
-                pl.BlockSpec((COLS, rows), row_block),
-                pl.BlockSpec((COLS, rows), row_block),
-                pl.BlockSpec((COLS, rows), col_block),
-                pl.BlockSpec((COLS, rows), col_block),
+                pl.BlockSpec((COLS, rows), block),
+                pl.BlockSpec((COLS, rows), block),
                 pl.BlockSpec((COLS, DH), lambda i, at: (0, at[0])),
                 pl.BlockSpec((COLS, DH), lambda i, at: (0, 0)),
             ],
@@ -378,9 +377,9 @@
         ),
         out_shape=(jax.ShapeDtypeStruct((rows, DH), F32),) + (jax.ShapeDtypeStruct((rows, DH), BF),) * 3,
         compiler_params=params(),
-        cost_estimate=cost(4 * COLS * 2 * HALF * DH, 7 * 2**20),
+        cost_estimate=cost(2 * COLS * 2 * HALF * DH, 6 * 2**20),
         name="weight_grad",
-    )(place, row_mine, row_theirs, col_mine, col_theirs, og, og_theirs)
+    )(place, mine, theirs, og, og_theirs)
 
 
 def gather_kernel(axis, pieces, place, own_ref, a_ref, b_ref, c_ref, o_ref):
@@ -408,15 +407,17 @@
     )(place, *blocks)
 
 
-def weight_sum_kernel(place, a_ref, b_ref, c_ref, d_ref, *outs):
+def weight_sum_kernel(place, *refs):
+    ins, outs = refs[:8], refs[8:]
     chunk = 2 * HD // 8
     for step, out in enumerate(outs):
         at_y = lax.rem(place[3] + step, 4)
         for at_z in range(2):
             rows = pl.ds(pl.multiple_of(at_z * HD + at_y * chunk, chunk), chunk)
-            near = a_ref[rows, :] + b_ref[rows, :].astype(F32)
-            far = c_ref[rows, :].astype(F32) + d_ref[rows, :].astype(F32)
-            out[at_z * chunk : (at_z + 1) * chunk, :] = (near + far).astype(out.dtype)
+            total = ins[0][rows, :] + ins[1][rows, :]
+            for ref in ins[2:]:
+                total = total + ref[rows, :].astype(F32)
+            out[at_z * chunk : (at_z + 1) * chunk, :] = total.astype(out.dtype)
 
 
 def weight_sum(parts, place):
@@ -424,10 +425,10 @@
     return pl.pallas_call(
         weight_sum_kernel,
         out_shape=(jax.ShapeDtypeStruct((rows, DH), F32),) + (jax.ShapeDtypeStruct((rows, DH), BF),) * 3,
-        in_specs=[SMEM_SPEC] + [VMEM_SPEC] * 4,
+        in_specs=[SMEM_SPEC] + [VMEM_SPEC] * 8,
         out_specs=(VMEM_SPEC,) * 4,
         compiler_params=params(),
-        cost_estimate=cost(16 * rows * DH, 4 * 2**20),
+        cost_estimate=cost(32 * rows * DH, 6 * 2**20),
         name="weight_sum",
     )(place, *parts)
 
@@ -496,6 +497,11 @@
     return lax.ppermute(tensor, axis, [(i, (i + step) % 4) for i in range(4)])
 
 
+def part_along_x(tensor, low, step):
+    pairs = [(i, (i + step) % 4) for i in range(4) if low <= (i + step) % 4 < low + 2]
+    return lax.ppermute(tensor, "x", pairs)
+
+
 def along_z(tensor, step):
     turns = [(z * 4 + h, (z + step // 4) % 2 * 4 + (h + step % 4) % 4) for z in range(2) for h in range(4)]
     return lax.ppermute(tensor, ("zl", "zh"), turns)
@@ -532,20 +538,23 @@
     theirs = other_core(mine)
     og_theirs = other_core(og_sent)
     grad_rows, grad_cols = attn_grad_of(og, mine, theirs, place)
-    dq, dk, dv = row_backward(q, k, v, grad_rows, block_pattern)
-    col_mine, grad_cols, og_theirs, dq, dk, dv = together(col_mine, grad_cols, og_theirs, dq, dk, dv)
+    early = weight_grad_of(row_out, row_theirs, og, og_theirs, place, 0)
+    col_mine, grad_cols, *early = together(col_mine, grad_cols, *early)
     col_mine = col_mine.reshape(COLS, HALF)
 
     col_grads = exchange(grad_cols.reshape(seq, COLS // seq, HALF), SEQ)
     col_theirs = other_core(col_mine)
-    parts = weight_grad_of(row_out, row_theirs, col_mine, col_theirs, og, og_theirs, place)
-    next_x, far_x, last_x = (along(parts[step], "x", step) for step in (1, 2, 3))
+    late = weight_grad_of(col_mine, col_theirs, og, og_theirs, place, 2)
+    early_x = [part_along_x(early[step], 0, step) for step in (1, 2, 3)]
+    late_x = [part_along_x(late[step], 2, step) for step in (1, 2, 3)]
+    dq, dk, dv = row_backward(q, k, v, grad_rows, block_pattern)
+    col_grads, dq, dk, dv, *early_x = together(col_grads, dq, dk, dv, *early_x)
 
     col_back = column_backward(received, col_grads.reshape(ROWS, 2, GRP, HALF)).reshape(seq, COLS // seq, 3 * HALF)
-    col_back, next_x, last_x = together(col_back, next_x, last_x)
+    col_back, *late_x = together(col_back, *late_x)
     back = exchange(col_back, SEQ).reshape(COLS, 3 * HALF)
 
-    parts = weight_sum([parts[0], next_x, far_x, last_x], place)
+    parts = weight_sum([early[0], late[0]] + early_x + late_x, place)
     layer = layer_out_of(row_out, col_mine, mine, theirs, place)
     parts = [parts[0]] + [along(parts[step], "y", step) for step in (1, 2, 3)]
     layer, *parts = together(layer, *parts)

time: 213 us -> 225 us (1.056)
  starting transfers between devices: 93.1 us -> 98.5 us
  local copies, waits for them, and re-layouts: 12.9 us -> 17.6 us
    ppermute x0 -> x6, starting transfers between devices: none -> 15 us  [part_along_x(): return lax.ppermute(tensor, 'x', pairs)]
    ppermute x0 -> x6, waiting for transfers between devices: none -> 8.58 us  [part_along_x(): return lax.ppermute(tensor, 'x', pairs)]
    ppermute x7, starting transfers between devices: 25.9 us -> 18.9 us  [along_z(): return lax.ppermute(tensor, ('zl', 'zh'), turns)]
    ppermute x12 -> x9, waiting for transfers between devices: 21.3 us -> 15.8 us  [along(): return lax.ppermute(tensor, axis, [(i, (i + step) % 4) for i in range(4)])]
    all_to_all x5, waiting for transfers between devices: 27.5 us -> 22.7 us  [exchange(): return lax.all_to_all(tensor, axes, split_axis=0, concat_axis=0, tiled=True)]
    unnamed x36 -> x60, local copies, waits for them, and re-layouts: 10.3 us -> 15 us
    ppermute x12 -> x9, starting transfers between devices: 16.1 us -> 12.6 us  [along(): return lax.ppermute(tensor, axis, [(i, (i + step) % 4) for i in range(4)])]
    pallas_call x1 -> x2, Pallas kernels: 7.09 us -> 9.73 us  [weight_grad_of(): pl.pallas_call(functools.partial(weight_grad_kernel, low), grid_spec=pltp...]
  transfers between devices with their start and end apart: 29 -> 32, of which waited for: 10 -> 12; matrix products, arithmetic and copies ran while one was open for 1% -> 1% of each run, Pallas kernels for 24% -> 24%
where the time goes in v8:
time: 225 us; the launch traced here: 223 us
  starting transfers between devices  98.5 us (44%)
  Pallas kernels  56.5 us (25%)
  waiting for transfers between devices  48.8 us (22%)
  local copies, waits for them, and re-layouts  17.6 us (8%)
    all_to_all x5, starting transfers between devices, exchange(): return lax.all_to_all(tensor, axes, split_axis=0, concat_axis=0, tiled=True)  46.6 us
    all_to_all x5, waiting for transfers between devices, exchange(): return lax.all_to_all(tensor, axes, split_axis=0, concat_axis=0, tiled=True)  22.7 us
    ppermute x7, starting transfers between devices, along_z(): return lax.ppermute(tensor, ('zl', 'zh'), turns)  18.9 us
    ppermute x9, waiting for transfers between devices, along(): return lax.ppermute(tensor, axis, [(i, (i + step) % 4) for i in range(4)])  15.8 us
    ppermute x6, starting transfers between devices, part_along_x(): return lax.ppermute(tensor, 'x', pairs)  15 us
    unnamed x60, local copies, waits for them, and re-layouts  15 us
    ppermute x9, starting transfers between devices, along(): return lax.ppermute(tensor, axis, [(i, (i + step) % 4) for i in range(4)])  12.6 us
    pallas_call x2, Pallas kernels, weight_grad_of(): pl.pallas_call(functools.partial(weight_grad_kernel, low), grid_spec=pltp...  9.73 us
  transfers between devices with their start and end apart: 32, of which 12 were waited for; matrix products, arithmetic and copies ran while one was open for 1% of the time, Pallas kernels for 24%

profile of v8, /device:TPU:1, one launch (start us, length us, event | category | flops | bytes accessed | tf_op | source)
XLA Modules:
  0.0 223.1 jit_solution(6757708884907138047)
XLA Ops:
  2.1 10.0 %all-to-all-start = ((bf16[16,4,1024]{2,1,0:T(4,128)(2,1)}), bf16[16,4,1024]{2,1,0:T(4,128)(2,1)S(1)}, u32[]{:S(2)}, u32[]{:S(2)}) async-start(bf16[16,4,1024]{2,1,0:T(4,128)(2,1)} %bitcast.6), calls=%async_computation | async-start | bytes 262144 | tf_op jit(solution)/shard_map/all_to_all | solution.py:485
  16.4 2.4 %pack.1 = bf16[512,1536]{1,0:T(8,128)(2,1)} custom-call(s32[4]{0:T(128)S(1)} %copy-done.24, bf16[512,1024]{1,0:T(8,128)(2,1)S(1)} %bitcast.29, bf16[512,1024]{1,0:T(8,128)(2,1)S(1)} %bitcast.32, bf16[512,1024]{1,0:T(8,128)(2,1)S(1)} %bitcast.35), custom_call_target="tpu_custom_call" | custom-call | flops 536870912 | bytes 3145728 | tf_op jit(solution)/shard_map/pack/pallas_call | solution.py:79
  21.2 9.0 %all-to-all-start.1 = ((bf16[32,16,1536]{2,1,0:T(8,128)(2,1)}), bf16[32,16,1536]{2,1,0:T(8,128)(2,1)}, u32[]{:S(2)}, u32[]{:S(2)}) async-start(bf16[32,16,1536]{2,1,0:T(8,128)(2,1)} %bitcast.45), calls=%async_computation.1 | async-start | bytes 3145728 | tf_op jit(solution)/shard_map/all_to_all | solution.py:485
  30.3 2.7 %collective-permute-start.3 = (bf16[64,1024]{1,0:T(8,128)(2,1)S(1)}, bf16[64,1024]{1,0:T(8,128)(2,1)S(1)}, u32[]{:S(2)}, u32[]{:S(2)}) collective-permute-start(bf16[64,1024]{1,0:T(8,128)(2,1)S(1)} %reshape.77.own_ref), channel_id=1, source_target_pairs={{0,24},{8,0},{16,8},{24,16},{1,25},{9,1},{17,9},{25,17},{2,26},{10... | collective-permute-start | bytes 393224 | tf_op jit(solution)/shard_map/ppermute | solution.py:497
  34.1 3.0 %row_forward.1.a_mine.row_ref = bf16[512,512]{1,0:T(8,128)(2,1)} custom-call(s32[4,4]{1,0:T(4,128)S(1)} %copy-done.23, bf16[512,1024]{1,0:T(8,128)(2,1)S(1)} %bitcast.30, bf16[512,1024]{1,0:T(8,128)(2,1)S(1)} %bitcast.33, bf16[512,1024]{1,0:T(8,128)(2,1)S(1)} %bitcast.36), custom_call_target="tpu_custom_call" | custom-call | flops 268435456 | bytes 2097152 | tf_op jit(solution)/shard_map/row_forward/pallas_call | solution.py:189
  41.8 3.8 %collective-permute-done.1.a_ref = bf16[64,1024]{1,0:T(8,128)(2,1)} collective-permute-done((bf16[64,1024]{1,0:T(8,128)(2,1)S(1)}, bf16[64,1024]{1,0:T(8,128)(2,1)}, u32[]{:S(2)}, u32[]{:S(2)}) %collective-permute-start.1) | collective-permute-done | bytes 131104 | tf_op jit(solution)/shard_map/ppermute | solution.py:497
  46.5 2.6 %collective-permute-start.6 = (bf16[256,1024]{1,0:T(8,128)(2,1)S(1)}, bf16[256,1024]{1,0:T(8,128)(2,1)S(1)}, u32[]{:S(2)}, u32[]{:S(2)}) collective-permute-start(bf16[256,1024]{1,0:T(8,128)(2,1)S(1)} %gather_y.1.own_ref), channel_id=1, source_target_pairs={{0,192},{64,0},{128,64},{192,128},{1,193},{65,1},{129,65},{193,129... | collective-permute-start | bytes 1572872 | tf_op jit(solution)/shard_map/ppermute | solution.py:497
  50.2 20.0 %all-to-all-done.1 = bf16[32,16,1536]{2,1,0:T(8,128)(2,1)} async-done(((bf16[32,16,1536]{2,1,0:T(8,128)(2,1)}), bf16[32,16,1536]{2,1,0:T(8,128)(2,1)}, u32[]{:S(2)}, u32[]{:S(2)}) %all-to-all-start.1) | async-done | bytes 1572896 | tf_op jit(solution)/shard_map/all_to_all | solution.py:485
  70.2 3.4 %column_forward.1 = bf16[32,2,8,512]{3,2,1,0:T(8,128)(2,1)S(1)} custom-call(bf16[32,2,8,1536]{3,2,1,0:T(8,128)(2,1)} %bitcast.12.r_ref), custom_call_target="tpu_custom_call" | custom-call | flops 99999997952 | bytes 2097152 | tf_op jit(solution)/shard_map/column_forward/pallas_call | solution.py:130
  75.7 2.5 %gather_x.1.mine_ref = bf16[1024,1024]{1,0:T(8,128)(2,1)} custom-call(s32[5]{0:T(128)S(1)} %stack.23.place.core_ref, bf16[256,1024]{1,0:T(8,128)(2,1)S(1)} %gather_y.1.own_ref, bf16[256,1024]{1,0:T(8,128)(2,1)} %collective-permute-done.4.a_ref, bf16[256,1024]{1,0:T(8,128)(2,1)S(1)} %collective-permute-done.5.b_ref, ...), custom_call_target="tpu_custom_call" | custom-call | bytes 4194304 | tf_op jit(solution)/shard_map/gather_x/pallas_call | solution.py:399
  78.8 9.4 %all-to-all-start.2 = ((bf16[32,16,512]{2,1,0:T(8,128)(2,1)}), bf16[32,16,512]{2,1,0:T(8,128)(2,1)S(1)}, u32[]{:S(2)}, u32[]{:S(2)}) async-start(bf16[32,16,512]{2,1,0:T(8,128)(2,1)} %bitcast.44), calls=%async_computation.2 | async-start | bytes 1048576 | tf_op jit(solution)/shard_map/all_to_all | solution.py:485
  89.1 4.3 %weight_grad.2 = (f32[256,1024]{1,0:T(8,128)S(1)}, bf16[256,1024]{1,0:T(8,128)(2,1)S(1)}, bf16[256,1024]{1,0:T(8,128)(2,1)S(1)}, bf16[256,1024]{1,0:T(8,128)(2,1)S(1)}) custom-call(s32[5]{0:T(128)S(1)} %stack.23.place.core_ref, bf16[512,512]{1,0:T(8,128)(2,1)} %row_forward.1.a_mine.row_ref, bf16[512,512]{1,0:T(8,128)(2,1)S(1)} %collective-permute-done.a_theirs, ...), custom_call_target="tpu_custom_call" | custom-call | flops 1073741824 | bytes 6291456 | tf_op jit(solution)/shard_map/weight_grad/pallas_call | solution.py:364
  96.8 5.5 %attn_grad.1 = (bf16[512,512]{1,0:T(8,128)(2,1)S(1)}, bf16[512,512]{1,0:T(8,128)(2,1)S(1)}) custom-call(s32[5]{0:T(128)S(1)} %stack.23.place.core_ref, bf16[512,2048]{1,0:T(8,128)(2,1)S(1)} %bitcast.27, bf16[512,2048]{1,0:T(8,128)(2,1)S(1)} %bitcast.28, bf16[1024,1024]{1,0:T(8,128)(2,1)} %gather_x.1.mine_ref, ...), custom_call_target="tpu_custom_call" | custom-call | flops 2147483648 | bytes 7340032 | tf_op jit(solution)/shard_map/attn_grad/pallas_call | solution.py:277
  105.6 7.5 %all-to-all-start.3 = ((bf16[32,16,512]{2,1,0:T(8,128)(2,1)}), bf16[32,16,512]{2,1,0:T(8,128)(2,1)S(1)}, u32[]{:S(2)}, u32[]{:S(2)}) async-start(bf16[32,16,512]{2,1,0:T(8,128)(2,1)} %bitcast.43), calls=%async_computation.3 | async-start | bytes 1048576 | tf_op jit(solution)/shard_map/all_to_all | solution.py:485
  117.8 5.4 %weight_grad.3 = (f32[256,1024]{1,0:T(8,128)S(1)}, bf16[256,1024]{1,0:T(8,128)(2,1)}, bf16[256,1024]{1,0:T(8,128)(2,1)}, bf16[256,1024]{1,0:T(8,128)(2,1)}) custom-call(s32[5]{0:T(128)S(1)} %stack.23.place.core_ref, bf16[512,512]{1,0:T(8,128)(2,1)S(1)} %bitcast.40, bf16[512,512]{1,0:T(8,128)(2,1)S(1)} %collective-permute-done.9.a_theirs, ...), custom_call_target="tpu_custom_call" | custom-call | flops 1073741824 | bytes 6291456 | tf_op jit(solution)/shard_map/weight_grad/pallas_call | solution.py:364
  124.9 7.6 %collective-permute-start.14 = (bf16[256,1024]{1,0:T(8,128)(2,1)}, bf16[256,1024]{1,0:T(8,128)(2,1)}, u32[]{:S(2)}, u32[]{:S(2)}) collective-permute-start(bf16[256,1024]{1,0:T(8,128)(2,1)} %get-tuple-element.109), channel_id=1, source_target_pairs={{0,128},{64,192},{1,129},{65,193},{2,130},{66,194},{3,131},{67,195... | collective-permute-start | bytes 1572872 | tf_op jit(solution)/shard_map/ppermute | solution.py:502
  132.6 8.6 %collective-permute-done.10.refs_2_ = bf16[256,1024]{1,0:T(8,128)(2,1)S(1)} collective-permute-done((bf16[256,1024]{1,0:T(8,128)(2,1)}, bf16[256,1024]{1,0:T(8,128)(2,1)S(1)}, u32[]{:S(2)}, u32[]{:S(2)}) %collective-permute-start.10) | collective-permute-done | bytes 524320 | tf_op jit(solution)/shard_map/ppermute | solution.py:502
  143.2 9.1 %row_backward.1 = (bf16[512,1024]{1,0:T(8,128)(2,1)}, bf16[512,1024]{1,0:T(8,128)(2,1)}, bf16[512,1024]{1,0:T(8,128)(2,1)}) custom-call(s32[4,4]{1,0:T(4,128)S(1)} %copy-done.23, bf16[512,1024]{1,0:T(8,128)(2,1)S(1)} %bitcast.31, bf16[512,1024]{1,0:T(8,128)(2,1)S(1)} %bitcast.34, bf16[512,1024]{1,0:T(8,128)(2,1)S(1)} %bitcast.37, ...), custom_call_target="tpu_custom_call" | custom-call | flops 671088640 | bytes 3670016 | tf_op jit(solution)/shard_map/row_backward/pallas_call | solution.py:222
  154.0 7.2 %column_backward.1 = bf16[32,2,8,1536]{3,2,1,0:T(8,128)(2,1)} custom-call(bf16[32,2,8,1536]{3,2,1,0:T(8,128)(2,1)} %bitcast.12.r_ref, bf16[32,2,8,512]{3,2,1,0:T(8,128)(2,1)S(1)} %bitcast.42), custom_call_target="tpu_custom_call" | custom-call | flops 671088640 | bytes 3670016 | tf_op jit(solution)/shard_map/column_backward/pallas_call | solution.py:156
  162.0 10.7 %all-to-all-start.4 = ((bf16[32,16,1536]{2,1,0:T(8,128)(2,1)}), bf16[32,16,1536]{2,1,0:T(8,128)(2,1)S(1)}, u32[]{:S(2)}, u32[]{:S(2)}) async-start(bf16[32,16,1536]{2,1,0:T(8,128)(2,1)} %bitcast.18), calls=%async_computation.4 | async-start | bytes 3145728 | tf_op jit(solution)/shard_map/all_to_all | solution.py:485
  174.9 2.5 %weight_sum.1 = (f32[64,1024]{1,0:T(8,128)S(1)}, bf16[64,1024]{1,0:T(8,128)(2,1)S(1)}, bf16[64,1024]{1,0:T(8,128)(2,1)S(1)}, bf16[64,1024]{1,0:T(8,128)(2,1)S(1)}) custom-call(s32[5]{0:T(128)S(1)} %stack.23.place.core_ref, f32[256,1024]{1,0:T(8,128)} %copy-done.11, f32[256,1024]{1,0:T(8,128)} %copy-done.12, bf16[256,1024]{1,0:T(8,128)(2,1)S(1)} %copy-done.16, ...), custom_call_target="tpu_custom_call" | custom-call | flops 2097152 | bytes 6291456 | tf_op jit(solution)/shard_map/weight_sum/pallas_call | solution.py:425
  178.8 2.4 %collective-permute-start.17 = (bf16[64,1024]{1,0:T(8,128)(2,1)S(1)}, bf16[64,1024]{1,0:T(8,128)(2,1)S(1)}, u32[]{:S(2)}, u32[]{:S(2)}) collective-permute-start(bf16[64,1024]{1,0:T(8,128)(2,1)S(1)} %get-tuple-element.116), channel_id=1, source_target_pairs={{0,16},{8,24},{16,0},{24,8},{1,17},{9,25},{17,1},{25,9},{2,18},{10... | collective-permute-start | bytes 393224 | tf_op jit(solution)/shard_map/ppermute | solution.py:497
  182.4 6.4 %layer_out.1 = bf16[512,2048]{1,0:T(8,128)(2,1)} custom-call(s32[5]{0:T(128)S(1)} %stack.23.place.core_ref, bf16[512,512]{1,0:T(8,128)(2,1)} %row_forward.1.a_mine.row_ref, bf16[512,512]{1,0:T(8,128)(2,1)S(1)} %bitcast.41, bf16[1024,1024]{1,0:T(8,128)(2,1)S(1)} %copy-done.10, bf16[1024,1024]{1,0:T(8,128)(2,1)} %collective-permute-done.7.theirs_ref), custom_call_target="tpu_custom_call" | custom-call | flops 2147483648 | bytes 7340032 | tf_op jit(solution)/shard_map/layer_out/pallas_call | solution.py:317
  188.8 2.6 %collective-permute-done.16.b_ref = bf16[64,1024]{1,0:T(8,128)(2,1)S(1)} collective-permute-done((bf16[64,1024]{1,0:T(8,128)(2,1)S(1)}, bf16[64,1024]{1,0:T(8,128)(2,1)S(1)}, u32[]{:S(2)}, u32[]{:S(2)}) %collective-permute-start.16) | collective-permute-done | bytes 131104 | tf_op jit(solution)/shard_map/ppermute | solution.py:497
  191.4 4.0 %collective-permute-done.17.c_ref = bf16[64,1024]{1,0:T(8,128)(2,1)S(1)} collective-permute-done((bf16[64,1024]{1,0:T(8,128)(2,1)S(1)}, bf16[64,1024]{1,0:T(8,128)(2,1)S(1)}, u32[]{:S(2)}, u32[]{:S(2)}) %collective-permute-start.17) | collective-permute-done | bytes 131104 | tf_op jit(solution)/shard_map/ppermute | solution.py:497
  196.0 3.7 %collective-permute-start.19 = (bf16[8,1024]{1,0:T(8,128)(2,1)S(1)}, bf16[8,1024]{1,0:T(8,128)(2,1)S(1)}, u32[]{:S(2)}, u32[]{:S(2)}) collective-permute-start(bf16[8,1024]{1,0:T(8,128)(2,1)S(1)} %get-tuple-element.131), channel_id=1, source_target_pairs={{0,2},{2,4},{4,6},{6,0},{32,34},{34,36},{36,38},{38,32},{1,3},{3,5... | collective-permute-start | bytes 49160 | tf_op jit(solution)/shard_map/ppermute | solution.py:507
  199.8 4.0 %collective-permute-start.20 = (bf16[8,1024]{1,0:T(8,128)(2,1)S(1)}, bf16[8,1024]{1,0:T(8,128)(2,1)S(1)}, u32[]{:S(2)}, u32[]{:S(2)}) collective-permute-start(bf16[8,1024]{1,0:T(8,128)(2,1)S(1)} %get-tuple-element.132), channel_id=1, source_target_pairs={{0,4},{2,6},{4,0},{6,2},{32,36},{34,38},{36,32},{38,34},{1,5},{3,7... | collective-permute-start | bytes 49160 | tf_op jit(solution)/shard_map/ppermute | solution.py:507
  203.8 3.5 %collective-permute-start.21 = (bf16[8,1024]{1,0:T(8,128)(2,1)S(1)}, bf16[8,1024]{1,0:T(8,128)(2,1)S(1)}, u32[]{:S(2)}, u32[]{:S(2)}) collective-permute-start(bf16[8,1024]{1,0:T(8,128)(2,1)S(1)} %get-tuple-element.133), channel_id=1, source_target_pairs={{0,6},{2,0},{4,2},{6,4},{32,38},{34,32},{36,34},{38,36},{1,7},{3,1... | collective-permute-start | bytes 49160 | tf_op jit(solution)/shard_map/ppermute | solution.py:507
  207.3 3.3 %collective-permute-start.22 = (bf16[8,1024]{1,0:T(8,128)(2,1)S(1)}, bf16[8,1024]{1,0:T(8,128)(2,1)S(1)}, u32[]{:S(2)}, u32[]{:S(2)}) collective-permute-start(bf16[8,1024]{1,0:T(8,128)(2,1)S(1)} %get-tuple-element.134), channel_id=1, source_target_pairs={{0,32},{2,34},{4,36},{6,38},{32,0},{34,2},{36,4},{38,6},{1,33},{3,... | collective-permute-start | bytes 49160 | tf_op jit(solution)/shard_map/ppermute | solution.py:507
  210.6 3.5 %collective-permute-start.24 = (bf16[8,1024]{1,0:T(8,128)(2,1)S(1)}, bf16[8,1024]{1,0:T(8,128)(2,1)S(1)}, u32[]{:S(2)}, u32[]{:S(2)}) collective-permute-start(bf16[8,1024]{1,0:T(8,128)(2,1)S(1)} %get-tuple-element.136), channel_id=1, source_target_pairs={{0,36},{2,38},{4,32},{6,34},{32,4},{34,6},{36,0},{38,2},{1,37},{3,... | collective-permute-start | bytes 49160 | tf_op jit(solution)/shard_map/ppermute | solution.py:507
  215.0 2.5 %finish.1 = (bf16[512,1024]{1,0:T(8,128)(2,1)}, bf16[512,1024]{1,0:T(8,128)(2,1)}, bf16[512,1024]{1,0:T(8,128)(2,1)}) custom-call(s32[4]{0:T(128)S(1)} %copy-done.25, bf16[512,1536]{1,0:T(8,128)(2,1)S(1)} %bitcast.38, bf16[512,1024]{1,0:T(8,128)(2,1)} %get-tuple-element.120.dq_in, ...), custom_call_target="tpu_custom_call", output_to_operand_aliasing={{0}: (2, {}), {1}: (3, {}), {2}: (4, {})} | custom-call | flops 536870912 | bytes 3145728 | tf_op jit(solution)/shard_map/finish/pallas_call | solution.py:248
  219.0 2.6 %collective-permute-start.26 = (f32[4,1024]{1,0:T(4,128)S(1)}, f32[4,1024]{1,0:T(4,128)S(1)}, u32[]{:S(2)}, u32[]{:S(2)}) collective-permute-start(f32[4,1024]{1,0:T(4,128)S(1)} %get-tuple-element.150), channel_id=1, source_target_pairs={{0,1},{1,0},{2,3},{3,2},{4,5},{5,4},{6,7},{7,6},{8,9},{9,8},{10,11... | collective-permute-start | bytes 49160 | tf_op jit(solution)/shard_map/ppermute | solution.py:489
  (115 shorter events, 46.3 us)
Async XLA Ops:
  2.1 19.1 %all-to-all-start = ((bf16[16,4,1024]{2,1,0:T(4,128)(2,1)}), bf16[16,4,1024]{2,1,0:T(4,128)(2,1)S(1)}, u32[]{:S(2)}, u32[]{:S(2)}) async-start(bf16[16,4,1024]{2,1,0:T(4,128)(2,1)} %bitcast.6), calls=%async_computation | async-start | bytes 262144 | tf_op jit(solution)/shard_map/all_to_all | solution.py:485
  21.2 49.0 %all-to-all-start.1 = ((bf16[32,16,1536]{2,1,0:T(8,128)(2,1)}), bf16[32,16,1536]{2,1,0:T(8,128)(2,1)}, u32[]{:S(2)}, u32[]{:S(2)}) async-start(bf16[32,16,1536]{2,1,0:T(8,128)(2,1)} %bitcast.45), calls=%async_computation.1 | async-start | bytes 3145728 | tf_op jit(solution)/shard_map/all_to_all | solution.py:485
  30.3 10.5 %collective-permute-start.3 = (bf16[64,1024]{1,0:T(8,128)(2,1)S(1)}, bf16[64,1024]{1,0:T(8,128)(2,1)S(1)}, u32[]{:S(2)}, u32[]{:S(2)}) collective-permute-start(bf16[64,1024]{1,0:T(8,128)(2,1)S(1)} %reshape.77.own_ref), channel_id=1, source_target_pairs={{0,24},{8,0},{16,8},{24,16},{1,25},{9,1},{17,9},{25,17},{2,26},{10... | collective-permute-start | bytes 393224 | tf_op jit(solution)/shard_map/ppermute | solution.py:497
  33.0 8.8 %collective-permute-start.2 = (bf16[64,1024]{1,0:T(8,128)(2,1)S(1)}, bf16[64,1024]{1,0:T(8,128)(2,1)S(1)}, u32[]{:S(2)}, u32[]{:S(2)}) collective-permute-start(bf16[64,1024]{1,0:T(8,128)(2,1)S(1)} %reshape.77.own_ref), channel_id=1, source_target_pairs={{0,16},{8,24},{16,0},{24,8},{1,17},{9,25},{17,1},{25,9},{2,18},{10... | collective-permute-start | bytes 393224 | tf_op jit(solution)/shard_map/ppermute | solution.py:497
  33.6 12.0 %collective-permute-start.1 = (bf16[64,1024]{1,0:T(8,128)(2,1)S(1)}, bf16[64,1024]{1,0:T(8,128)(2,1)}, u32[]{:S(2)}, u32[]{:S(2)}) collective-permute-start(bf16[64,1024]{1,0:T(8,128)(2,1)S(1)} %reshape.77.own_ref), channel_id=1, source_target_pairs={{0,8},{8,16},{16,24},{24,0},{1,9},{9,17},{17,25},{25,1},{2,10},{10... | collective-permute-start | bytes 393224 | tf_op jit(solution)/shard_map/ppermute | solution.py:497
  37.1 36.5 %collective-permute-start = (bf16[512,512]{1,0:T(8,128)(2,1)}, bf16[512,512]{1,0:T(8,128)(2,1)S(1)}, u32[]{:S(2)}, u32[]{:S(2)}) collective-permute-start(bf16[512,512]{1,0:T(8,128)(2,1)} %row_forward.1.a_mine.row_ref), channel_id=1, source_target_pairs={{0,1},{1,0},{2,3},{3,2},{4,5},{5,4},{6,7},{7,6},{8,9},{9,8},{10,11... | collective-permute-start | bytes 1572872 | tf_op jit(solution)/shard_map/ppermute | solution.py:489
  46.5 27.2 %collective-permute-start.6 = (bf16[256,1024]{1,0:T(8,128)(2,1)S(1)}, bf16[256,1024]{1,0:T(8,128)(2,1)S(1)}, u32[]{:S(2)}, u32[]{:S(2)}) collective-permute-start(bf16[256,1024]{1,0:T(8,128)(2,1)S(1)} %gather_y.1.own_ref), channel_id=1, source_target_pairs={{0,192},{64,0},{128,64},{192,128},{1,193},{65,1},{129,65},{193,129... | collective-permute-start | bytes 1572872 | tf_op jit(solution)/shard_map/ppermute | solution.py:497
  49.1 24.6 %collective-permute-start.5 = (bf16[256,1024]{1,0:T(8,128)(2,1)S(1)}, bf16[256,1024]{1,0:T(8,128)(2,1)S(1)}, u32[]{:S(2)}, u32[]{:S(2)}) collective-permute-start(bf16[256,1024]{1,0:T(8,128)(2,1)S(1)} %gather_y.1.own_ref), channel_id=1, source_target_pairs={{0,128},{64,192},{128,0},{192,64},{1,129},{65,193},{129,1},{193,65... | collective-permute-start | bytes 1572872 | tf_op jit(solution)/shard_map/ppermute | solution.py:497
  49.6 26.2 %collective-permute-start.4 = (bf16[256,1024]{1,0:T(8,128)(2,1)S(1)}, bf16[256,1024]{1,0:T(8,128)(2,1)}, u32[]{:S(2)}, u32[]{:S(2)}) collective-permute-start(bf16[256,1024]{1,0:T(8,128)(2,1)S(1)} %gather_y.1.own_ref), channel_id=1, source_target_pairs={{0,64},{64,128},{128,192},{192,0},{1,65},{65,129},{129,193},{193,1... | collective-permute-start | bytes 1572872 | tf_op jit(solution)/shard_map/ppermute | solution.py:497
  78.3 17.8 %collective-permute-start.7 = (bf16[1024,1024]{1,0:T(8,128)(2,1)}, bf16[1024,1024]{1,0:T(8,128)(2,1)}, u32[]{:S(2)}, u32[]{:S(2)}) collective-permute-start(bf16[1024,1024]{1,0:T(8,128)(2,1)} %gather_x.1.mine_ref), channel_id=1, source_target_pairs={{0,1},{1,0},{2,3},{3,2},{4,5},{5,4},{6,7},{7,6},{8,9},{9,8},{10,11... | collective-permute-start | bytes 6291464 | tf_op jit(solution)/shard_map/ppermute | solution.py:489
  78.8 9.4 %collective-permute-start.8 = (bf16[512,1024]{1,0:T(8,128)(2,1)}, bf16[512,1024]{1,0:T(8,128)(2,1)S(1)}, u32[]{:S(2)}, u32[]{:S(2)}) collective-permute-start(bf16[512,1024]{1,0:T(8,128)(2,1)} %dynamic-slice_bitcast_fusion), channel_id=1, source_target_pairs={{0,1},{1,0},{2,3},{3,2},{4,5},{5,4},{6,7},{7,6},{8,9},{9,8},{10,11... | collective-permute-start | bytes 3145736 | tf_op jit(solution)/shard_map/ppermute | solution.py:489
  78.8 25.8 %all-to-all-start.2 = ((bf16[32,16,512]{2,1,0:T(8,128)(2,1)}), bf16[32,16,512]{2,1,0:T(8,128)(2,1)S(1)}, u32[]{:S(2)}, u32[]{:S(2)}) async-start(bf16[32,16,512]{2,1,0:T(8,128)(2,1)} %bitcast.44), calls=%async_computation.2 | async-start | bytes 1048576 | tf_op jit(solution)/shard_map/all_to_all | solution.py:485
  104.6 13.3 %collective-permute-start.9 = (bf16[512,512]{1,0:T(8,128)(2,1)S(1)}, bf16[512,512]{1,0:T(8,128)(2,1)S(1)}, u32[]{:S(2)}, u32[]{:S(2)}) collective-permute-start(bf16[512,512]{1,0:T(8,128)(2,1)S(1)} %bitcast.39), channel_id=1, source_target_pairs={{0,1},{1,0},{2,3},{3,2},{4,5},{5,4},{6,7},{7,6},{8,9},{9,8},{10,11... | collective-permute-start | bytes 1572872 | tf_op jit(solution)/shard_map/ppermute | solution.py:489
  105.6 48.4 %all-to-all-start.3 = ((bf16[32,16,512]{2,1,0:T(8,128)(2,1)}), bf16[32,16,512]{2,1,0:T(8,128)(2,1)S(1)}, u32[]{:S(2)}, u32[]{:S(2)}) async-start(bf16[32,16,512]{2,1,0:T(8,128)(2,1)} %bitcast.43), calls=%async_computation.3 | async-start | bytes 1048576 | tf_op jit(solution)/shard_map/all_to_all | solution.py:485
  113.2 28.0 %collective-permute-start.10 = (bf16[256,1024]{1,0:T(8,128)(2,1)}, bf16[256,1024]{1,0:T(8,128)(2,1)S(1)}, u32[]{:S(2)}, u32[]{:S(2)}) collective-permute-start(bf16[256,1024]{1,0:T(8,128)(2,1)} %copy-done.28), channel_id=1, source_target_pairs={{0,64},{192,0},{1,65},{193,1},{2,66},{194,2},{3,67},{195,3},{4,68}... | collective-permute-start | bytes 1572872 | tf_op jit(solution)/shard_map/ppermute | solution.py:502
  115.2 37.2 %collective-permute-start.11 = (bf16[256,1024]{1,0:T(8,128)(2,1)}, bf16[256,1024]{1,0:T(8,128)(2,1)S(1)}, u32[]{:S(2)}, u32[]{:S(2)}) collective-permute-start(bf16[256,1024]{1,0:T(8,128)(2,1)} %copy-done.27), channel_id=1, source_target_pairs={{128,0},{192,64},{129,1},{193,65},{130,2},{194,66},{131,3},{195,67... | collective-permute-start | bytes 1572872 | tf_op jit(solution)/shard_map/ppermute | solution.py:502
  116.5 36.7 %collective-permute-start.12 = (bf16[256,1024]{1,0:T(8,128)(2,1)}, bf16[256,1024]{1,0:T(8,128)(2,1)S(1)}, u32[]{:S(2)}, u32[]{:S(2)}) collective-permute-start(bf16[256,1024]{1,0:T(8,128)(2,1)} %copy-done.26), channel_id=1, source_target_pairs={{64,0},{128,64},{65,1},{129,65},{66,2},{130,66},{67,3},{131,67},{6... | collective-permute-start | bytes 1572872 | tf_op jit(solution)/shard_map/ppermute | solution.py:502
  124.2 37.0 %collective-permute-start.13 = (bf16[256,1024]{1,0:T(8,128)(2,1)}, bf16[256,1024]{1,0:T(8,128)(2,1)S(1)}, u32[]{:S(2)}, u32[]{:S(2)}) collective-permute-start(bf16[256,1024]{1,0:T(8,128)(2,1)} %get-tuple-element.108), channel_id=1, source_target_pairs={{64,128},{128,192},{65,129},{129,193},{66,130},{130,194},{67,131},... | collective-permute-start | bytes 1572872 | tf_op jit(solution)/shard_map/ppermute | solution.py:502
  124.9 37.1 %collective-permute-start.14 = (bf16[256,1024]{1,0:T(8,128)(2,1)}, bf16[256,1024]{1,0:T(8,128)(2,1)}, u32[]{:S(2)}, u32[]{:S(2)}) collective-permute-start(bf16[256,1024]{1,0:T(8,128)(2,1)} %get-tuple-element.109), channel_id=1, source_target_pairs={{0,128},{64,192},{1,129},{65,193},{2,130},{66,194},{3,131},{67,195... | collective-permute-start | bytes 1572872 | tf_op jit(solution)/shard_map/ppermute | solution.py:502
  141.1 20.9 %collective-permute-start.15 = (bf16[256,1024]{1,0:T(8,128)(2,1)}, bf16[256,1024]{1,0:T(8,128)(2,1)}, u32[]{:S(2)}, u32[]{:S(2)}) collective-permute-start(bf16[256,1024]{1,0:T(8,128)(2,1)} %get-tuple-element.110), channel_id=1, source_target_pairs={{0,192},{192,128},{1,193},{193,129},{2,194},{194,130},{3,195},{195... | collective-permute-start | bytes 1572872 | tf_op jit(solution)/shard_map/ppermute | solution.py:502
  162.0 53.0 %all-to-all-start.4 = ((bf16[32,16,1536]{2,1,0:T(8,128)(2,1)}), bf16[32,16,1536]{2,1,0:T(8,128)(2,1)S(1)}, u32[]{:S(2)}, u32[]{:S(2)}) async-start(bf16[32,16,1536]{2,1,0:T(8,128)(2,1)} %bitcast.18), calls=%async_computation.4 | async-start | bytes 3145728 | tf_op jit(solution)/shard_map/all_to_all | solution.py:485
  177.4 14.0 %collective-permute-start.16 = (bf16[64,1024]{1,0:T(8,128)(2,1)S(1)}, bf16[64,1024]{1,0:T(8,128)(2,1)S(1)}, u32[]{:S(2)}, u32[]{:S(2)}) collective-permute-start(bf16[64,1024]{1,0:T(8,128)(2,1)S(1)} %get-tuple-element.115), channel_id=1, source_target_pairs={{0,8},{8,16},{16,24},{24,0},{1,9},{9,17},{17,25},{25,1},{2,10},{10... | collective-permute-start | bytes 393224 | tf_op jit(solution)/shard_map/ppermute | solution.py:497
  178.8 16.6 %collective-permute-start.17 = (bf16[64,1024]{1,0:T(8,128)(2,1)S(1)}, bf16[64,1024]{1,0:T(8,128)(2,1)S(1)}, u32[]{:S(2)}, u32[]{:S(2)}) collective-permute-start(bf16[64,1024]{1,0:T(8,128)(2,1)S(1)} %get-tuple-element.116), channel_id=1, source_target_pairs={{0,16},{8,24},{16,0},{24,8},{1,17},{9,25},{17,1},{25,9},{2,18},{10... | collective-permute-start | bytes 393224 | tf_op jit(solution)/shard_map/ppermute | solution.py:497
  181.3 14.1 %collective-permute-start.18 = (bf16[64,1024]{1,0:T(8,128)(2,1)S(1)}, bf16[64,1024]{1,0:T(8,128)(2,1)S(1)}, u32[]{:S(2)}, u32[]{:S(2)}) collective-permute-start(bf16[64,1024]{1,0:T(8,128)(2,1)S(1)} %get-tuple-element.117), channel_id=1, source_target_pairs={{0,24},{8,0},{16,8},{24,16},{1,25},{9,1},{17,9},{25,17},{2,26},{10... | collective-permute-start | bytes 393224 | tf_op jit(solution)/shard_map/ppermute | solution.py:497
  196.0 14.5 %collective-permute-start.19 = (bf16[8,1024]{1,0:T(8,128)(2,1)S(1)}, bf16[8,1024]{1,0:T(8,128)(2,1)S(1)}, u32[]{:S(2)}, u32[]{:S(2)}) collective-permute-start(bf16[8,1024]{1,0:T(8,128)(2,1)S(1)} %get-tuple-element.131), channel_id=1, source_target_pairs={{0,2},{2,4},{4,6},{6,0},{32,34},{34,36},{36,38},{38,32},{1,3},{3,5... | collective-permute-start | bytes 49160 | tf_op jit(solution)/shard_map/ppermute | solution.py:507
  199.8 14.3 %collective-permute-start.20 = (bf16[8,1024]{1,0:T(8,128)(2,1)S(1)}, bf16[8,1024]{1,0:T(8,128)(2,1)S(1)}, u32[]{:S(2)}, u32[]{:S(2)}) collective-permute-start(bf16[8,1024]{1,0:T(8,128)(2,1)S(1)} %get-tuple-element.132), channel_id=1, source_target_pairs={{0,4},{2,6},{4,0},{6,2},{32,36},{34,38},{36,32},{38,34},{1,5},{3,7... | collective-permute-start | bytes 49160 | tf_op jit(solution)/shard_map/ppermute | solution.py:507
  203.8 13.7 %collective-permute-start.21 = (bf16[8,1024]{1,0:T(8,128)(2,1)S(1)}, bf16[8,1024]{1,0:T(8,128)(2,1)S(1)}, u32[]{:S(2)}, u32[]{:S(2)}) collective-permute-start(bf16[8,1024]{1,0:T(8,128)(2,1)S(1)} %get-tuple-element.133), channel_id=1, source_target_pairs={{0,6},{2,0},{4,2},{6,4},{32,38},{34,32},{36,34},{38,36},{1,7},{3,1... | collective-permute-start | bytes 49160 | tf_op jit(solution)/shard_map/ppermute | solution.py:507
  207.3 10.3 %collective-permute-start.22 = (bf16[8,1024]{1,0:T(8,128)(2,1)S(1)}, bf16[8,1024]{1,0:T(8,128)(2,1)S(1)}, u32[]{:S(2)}, u32[]{:S(2)}) collective-permute-start(bf16[8,1024]{1,0:T(8,128)(2,1)S(1)} %get-tuple-element.134), channel_id=1, source_target_pairs={{0,32},{2,34},{4,36},{6,38},{32,0},{34,2},{36,4},{38,6},{1,33},{3,... | collective-permute-start | bytes 49160 | tf_op jit(solution)/shard_map/ppermute | solution.py:507
  210.6 7.0 %collective-permute-start.23 = (bf16[8,1024]{1,0:T(8,128)(2,1)S(1)}, bf16[8,1024]{1,0:T(8,128)(2,1)S(1)}, u32[]{:S(2)}, u32[]{:S(2)}) collective-permute-start(bf16[8,1024]{1,0:T(8,128)(2,1)S(1)} %get-tuple-element.135), channel_id=1, source_target_pairs={{0,34},{2,36},{4,38},{6,32},{32,2},{34,4},{36,6},{38,0},{1,35},{3,... | collective-permute-start | bytes 49160 | tf_op jit(solution)/shard_map/ppermute | solution.py:507
  210.6 7.0 %collective-permute-start.24 = (bf16[8,1024]{1,0:T(8,128)(2,1)S(1)}, bf16[8,1024]{1,0:T(8,128)(2,1)S(1)}, u32[]{:S(2)}, u32[]{:S(2)}) collective-permute-start(bf16[8,1024]{1,0:T(8,128)(2,1)S(1)} %get-tuple-element.136), channel_id=1, source_target_pairs={{0,36},{2,38},{4,32},{6,34},{32,4},{34,6},{36,0},{38,2},{1,37},{3,... | collective-permute-start | bytes 49160 | tf_op jit(solution)/shard_map/ppermute | solution.py:507
  214.1 4.4 %collective-permute-start.25 = (bf16[8,1024]{1,0:T(8,128)(2,1)S(1)}, bf16[8,1024]{1,0:T(8,128)(2,1)S(1)}, u32[]{:S(2)}, u32[]{:S(2)}) collective-permute-start(bf16[8,1024]{1,0:T(8,128)(2,1)S(1)} %get-tuple-element.137), channel_id=1, source_target_pairs={{0,38},{2,32},{4,34},{6,36},{32,6},{34,0},{36,2},{38,4},{1,39},{3,... | collective-permute-start | bytes 49160 | tf_op jit(solution)/shard_map/ppermute | solution.py:507
  219.0 3.5 %collective-permute-start.26 = (f32[4,1024]{1,0:T(4,128)S(1)}, f32[4,1024]{1,0:T(4,128)S(1)}, u32[]{:S(2)}, u32[]{:S(2)}) collective-permute-start(f32[4,1024]{1,0:T(4,128)S(1)} %get-tuple-element.150), channel_id=1, source_target_pairs={{0,1},{1,0},{2,3},{3,2},{4,5},{5,4},{6,7},{7,6},{8,9},{9,8},{10,11... | collective-permute-start | bytes 49160 | tf_op jit(solution)/shard_map/ppermute | solution.py:489
  (30 other events, 222.5 us)

commit v9 on v8

--- a/solution.py
+++ b/solution.py
@@ -335,7 +335,7 @@
 
 
 def weight_grad_kernel(low, place, a_mine, a_theirs, og_mine, og_theirs, *refs):
-    outs, total = refs[:4], refs[4]
+    early, outs, total = refs[:-5], refs[-5:-1], refs[-1]
     step = pl.program_id(0)
     local = lax.rem(place[1] + step, 4) - low
     inside = jnp.logical_and(local >= 0, local < 2)
@@ -344,23 +344,26 @@
     def _():
         total[...] = t_mm(a_mine[...], og_mine[...]) + t_mm(a_theirs[...], og_theirs[...])
 
-    @pl.when(jnp.logical_not(inside))
-    def _():
-        total[...] = jnp.zeros_like(total)
-
     for target, out in enumerate(outs):
 
-        @pl.when(step == target)
+        @pl.when(jnp.logical_and(step == target, inside))
         def _(out=out):
             out[...] = total[...].astype(out.dtype)
 
-
-def weight_grad_of(mine, theirs, og, og_theirs, place, low):
+        if early:
+
+            @pl.when(jnp.logical_and(step == target, jnp.logical_not(inside)))
+            def _(out=out, kept=early[target]):
+                out[...] = kept[...]
+
+
+def weight_grad_of(mine, theirs, og, og_theirs, place, low, early=()):
     rows = 2 * HALF // 4
 
     def block(i, at):
         return (0, jnp.clip(lax.rem(at[1] + i, 4) - low, 0, 1))
 
+    whole = pl.BlockSpec((rows, DH), lambda i, at: (0, 0))
     return pl.pallas_call(
         functools.partial(weight_grad_kernel, low),
         grid_spec=pltpu.PrefetchScalarGridSpec(
@@ -371,15 +374,16 @@
                 pl.BlockSpec((COLS, rows), block),
                 pl.BlockSpec((COLS, DH), lambda i, at: (0, at[0])),
                 pl.BlockSpec((COLS, DH), lambda i, at: (0, 0)),
-            ],
-            out_specs=(pl.BlockSpec((rows, DH), lambda i, at: (0, 0)),) * 4,
+            ]
+            + [whole] * len(early),
+            out_specs=(whole,) * 4,
             scratch_shapes=[pltpu.VMEM((rows, DH), F32)],
         ),
         out_shape=(jax.ShapeDtypeStruct((rows, DH), F32),) + (jax.ShapeDtypeStruct((rows, DH), BF),) * 3,
         compiler_params=params(),
         cost_estimate=cost(2 * COLS * 2 * HALF * DH, 6 * 2**20),
         name="weight_grad",
-    )(place, mine, theirs, og, og_theirs)
+    )(place, mine, theirs, og, og_theirs, *early)
 
 
 def gather_kernel(axis, pieces, place, own_ref, a_ref, b_ref, c_ref, o_ref):
@@ -407,17 +411,15 @@
     )(place, *blocks)
 
 
-def weight_sum_kernel(place, *refs):
-    ins, outs = refs[:8], refs[8:]
+def weight_sum_kernel(place, a_ref, b_ref, c_ref, d_ref, *outs):
     chunk = 2 * HD // 8
     for step, out in enumerate(outs):
         at_y = lax.rem(place[3] + step, 4)
         for at_z in range(2):
             rows = pl.ds(pl.multiple_of(at_z * HD + at_y * chunk, chunk), chunk)
-            total = ins[0][rows, :] + ins[1][rows, :]
-            for ref in ins[2:]:
-                total = total + ref[rows, :].astype(F32)
-            out[at_z * chunk : (at_z + 1) * chunk, :] = total.astype(out.dtype)
+            near = a_ref[rows, :] + b_ref[rows, :].astype(F32)
+            far = c_ref[rows, :].astype(F32) + d_ref[rows, :].astype(F32)
+            out[at_z * chunk : (at_z + 1) * chunk, :] = (near + far).astype(out.dtype)
 
 
 def weight_sum(parts, place):
@@ -425,10 +427,10 @@
     return pl.pallas_call(
         weight_sum_kernel,
         out_shape=(jax.ShapeDtypeStruct((rows, DH), F32),) + (jax.ShapeDtypeStruct((rows, DH), BF),) * 3,
-        in_specs=[SMEM_SPEC] + [VMEM_SPEC] * 8,
+        in_specs=[SMEM_SPEC] + [VMEM_SPEC] * 4,
         out_specs=(VMEM_SPEC,) * 4,
         compiler_params=params(),
-        cost_estimate=cost(32 * rows * DH, 6 * 2**20),
+        cost_estimate=cost(16 * rows * DH, 4 * 2**20),
         name="weight_sum",
     )(place, *parts)
 
@@ -495,11 +497,6 @@
 
 def along(tensor, axis, step):
     return lax.ppermute(tensor, axis, [(i, (i + step) % 4) for i in range(4)])
-
-
-def part_along_x(tensor, low, step):
-    pairs = [(i, (i + step) % 4) for i in range(4) if low <= (i + step) % 4 < low + 2]
-    return lax.ppermute(tensor, "x", pairs)
 
 
 def along_z(tensor, step):
@@ -544,17 +541,16 @@
 
     col_grads = exchange(grad_cols.reshape(seq, COLS // seq, HALF), SEQ)
     col_theirs = other_core(col_mine)
-    late = weight_grad_of(col_mine, col_theirs, og, og_theirs, place, 2)
-    early_x = [part_along_x(early[step], 0, step) for step in (1, 2, 3)]
-    late_x = [part_along_x(late[step], 2, step) for step in (1, 2, 3)]
+    parts = weight_grad_of(col_mine, col_theirs, og, og_theirs, place, 2, early)
+    x_parts = [parts[0]] + [along(parts[step], "x", step) for step in (1, 3, 2)]
     dq, dk, dv = row_backward(q, k, v, grad_rows, block_pattern)
-    col_grads, dq, dk, dv, *early_x = together(col_grads, dq, dk, dv, *early_x)
+    col_grads, dq, dk, dv = together(col_grads, dq, dk, dv)
 
     col_back = column_backward(received, col_grads.reshape(ROWS, 2, GRP, HALF)).reshape(seq, COLS // seq, 3 * HALF)
-    col_back, *late_x = together(col_back, *late_x)
+    col_back, *x_parts = together(col_back, *x_parts)
     back = exchange(col_back, SEQ).reshape(COLS, 3 * HALF)
 
-    parts = weight_sum([early[0], late[0]] + early_x + late_x, place)
+    parts = weight_sum(x_parts, place)
     layer = layer_out_of(row_out, col_mine, mine, theirs, place)
     parts = [parts[0]] + [along(parts[step], "y", step) for step in (1, 2, 3)]
     layer, *parts = together(layer, *parts)

time: 225 us -> 208 us (0.924)
  starting transfers between devices: 98.5 us -> 84.9 us
  local copies, waits for them, and re-layouts: 17.6 us -> 12.8 us
    ppermute x6 -> x0, starting transfers between devices: 15 us -> none  [part_along_x(): return lax.ppermute(tensor, 'x', pairs)]
    ppermute x9 -> x12, waiting for transfers between devices: 15.8 us -> 24.6 us  [along(): return lax.ppermute(tensor, axis, [(i, (i + step) % 4) for i in range(4)])]
    ppermute x6 -> x0, waiting for transfers between devices: 8.58 us -> none  [part_along_x(): return lax.ppermute(tensor, 'x', pairs)]
    unnamed x60 -> x46, local copies, waits for them, and re-layouts: 15 us -> 10.2 us
    ppermute x9 -> x12, starting transfers between devices: 12.6 us -> 15.2 us  [along(): return lax.ppermute(tensor, axis, [(i, (i + step) % 4) for i in range(4)])]
  transfers between devices with their start and end apart: 32 -> 29, of which waited for: 12 -> 11; matrix products, arithmetic and copies ran while one was open for 1% -> 1% of each run, Pallas kernels for 24% -> 26%
where the time goes in v9:
time: 208 us; the launch traced here: 206 us
  starting transfers between devices  84.9 us (41%)
  Pallas kernels  57 us (27%)
  waiting for transfers between devices  50.2 us (24%)
  local copies, waits for them, and re-layouts  12.8 us (6%)
    all_to_all x5, starting transfers between devices, exchange(): return lax.all_to_all(tensor, axes, split_axis=0, concat_axis=0, tiled=True)  44.5 us
    all_to_all x5, waiting for transfers between devices, exchange(): return lax.all_to_all(tensor, axes, split_axis=0, concat_axis=0, tiled=True)  24.7 us
    ppermute x12, waiting for transfers between devices, along(): return lax.ppermute(tensor, axis, [(i, (i + step) % 4) for i in range(4)])  24.6 us
    ppermute x7, starting transfers between devices, along_z(): return lax.ppermute(tensor, ('zl', 'zh'), turns)  20.4 us
    ppermute x12, starting transfers between devices, along(): return lax.ppermute(tensor, axis, [(i, (i + step) % 4) for i in range(4)])  15.2 us
    pallas_call x2, Pallas kernels, weight_grad_of(): pl.pallas_call(functools.partial(weight_grad_kernel, low), grid_spec=pltp...  10.4 us
    unnamed x46, local copies, waits for them, and re-layouts  10.2 us
    pallas_call x1, Pallas kernels, row_backward(): pl.pallas_call(row_backward_kernel, grid=(1,), out_shape=(whole, whole, w...  9.14 us
  transfers between devices with their start and end apart: 29, of which 11 were waited for; matrix products, arithmetic and copies ran while one was open for 1% of the time, Pallas kernels for 26%

profile of v9, /device:TPU:1, one launch (start us, length us, event | category | flops | bytes accessed | tf_op | source)
XLA Modules:
  0.0 206.4 jit_solution(9091853622137215417)
XLA Ops:
  2.1 10.0 %all-to-all-start = ((bf16[16,4,1024]{2,1,0:T(4,128)(2,1)}), bf16[16,4,1024]{2,1,0:T(4,128)(2,1)S(1)}, u32[]{:S(2)}, u32[]{:S(2)}) async-start(bf16[16,4,1024]{2,1,0:T(4,128)(2,1)} %bitcast.6), calls=%async_computation | async-start | bytes 262144 | tf_op jit(solution)/shard_map/all_to_all | solution.py:487
  16.4 2.4 %pack.1 = bf16[512,1536]{1,0:T(8,128)(2,1)} custom-call(s32[4]{0:T(128)S(1)} %copy-done.20, bf16[512,1024]{1,0:T(8,128)(2,1)S(1)} %bitcast.29, bf16[512,1024]{1,0:T(8,128)(2,1)S(1)} %bitcast.32, bf16[512,1024]{1,0:T(8,128)(2,1)S(1)} %bitcast.35), custom_call_target="tpu_custom_call" | custom-call | flops 536870912 | bytes 3145728 | tf_op jit(solution)/shard_map/pack/pallas_call | solution.py:79
  21.2 9.0 %all-to-all-start.1 = ((bf16[32,16,1536]{2,1,0:T(8,128)(2,1)}), bf16[32,16,1536]{2,1,0:T(8,128)(2,1)}, u32[]{:S(2)}, u32[]{:S(2)}) async-start(bf16[32,16,1536]{2,1,0:T(8,128)(2,1)} %bitcast.44), calls=%async_computation.1 | async-start | bytes 3145728 | tf_op jit(solution)/shard_map/all_to_all | solution.py:487
  30.3 2.7 %collective-permute-start.3 = (bf16[64,1024]{1,0:T(8,128)(2,1)S(1)}, bf16[64,1024]{1,0:T(8,128)(2,1)S(1)}, u32[]{:S(2)}, u32[]{:S(2)}) collective-permute-start(bf16[64,1024]{1,0:T(8,128)(2,1)S(1)} %reshape.77.own_ref), channel_id=1, source_target_pairs={{0,24},{8,0},{16,8},{24,16},{1,25},{9,1},{17,9},{25,17},{2,26},{10... | collective-permute-start | bytes 393224 | tf_op jit(solution)/shard_map/ppermute | solution.py:499
  34.1 2.9 %row_forward.1.a_mine.row_ref = bf16[512,512]{1,0:T(8,128)(2,1)} custom-call(s32[4,4]{1,0:T(4,128)S(1)} %copy-done.19, bf16[512,1024]{1,0:T(8,128)(2,1)S(1)} %bitcast.30, bf16[512,1024]{1,0:T(8,128)(2,1)S(1)} %bitcast.33, bf16[512,1024]{1,0:T(8,128)(2,1)S(1)} %bitcast.36), custom_call_target="tpu_custom_call" | custom-call | flops 268435456 | bytes 2097152 | tf_op jit(solution)/shard_map/row_forward/pallas_call | solution.py:189
  41.8 3.8 %collective-permute-done.1.a_ref = bf16[64,1024]{1,0:T(8,128)(2,1)} collective-permute-done((bf16[64,1024]{1,0:T(8,128)(2,1)S(1)}, bf16[64,1024]{1,0:T(8,128)(2,1)}, u32[]{:S(2)}, u32[]{:S(2)}) %collective-permute-start.1) | collective-permute-done | bytes 131104 | tf_op jit(solution)/shard_map/ppermute | solution.py:499
  46.5 2.6 %collective-permute-start.6 = (bf16[256,1024]{1,0:T(8,128)(2,1)S(1)}, bf16[256,1024]{1,0:T(8,128)(2,1)S(1)}, u32[]{:S(2)}, u32[]{:S(2)}) collective-permute-start(bf16[256,1024]{1,0:T(8,128)(2,1)S(1)} %gather_y.1.own_ref), channel_id=1, source_target_pairs={{0,192},{64,0},{128,64},{192,128},{1,193},{65,1},{129,65},{193,129... | collective-permute-start | bytes 1572872 | tf_op jit(solution)/shard_map/ppermute | solution.py:499
  50.2 20.0 %all-to-all-done.1 = bf16[32,16,1536]{2,1,0:T(8,128)(2,1)} async-done(((bf16[32,16,1536]{2,1,0:T(8,128)(2,1)}), bf16[32,16,1536]{2,1,0:T(8,128)(2,1)}, u32[]{:S(2)}, u32[]{:S(2)}) %all-to-all-start.1) | async-done | bytes 1572896 | tf_op jit(solution)/shard_map/all_to_all | solution.py:487
  70.2 3.4 %column_forward.1 = bf16[32,2,8,512]{3,2,1,0:T(8,128)(2,1)S(1)} custom-call(bf16[32,2,8,1536]{3,2,1,0:T(8,128)(2,1)} %bitcast.12.r_ref), custom_call_target="tpu_custom_call" | custom-call | flops 99999997952 | bytes 2097152 | tf_op jit(solution)/shard_map/column_forward/pallas_call | solution.py:130
  75.7 2.5 %gather_x.1.mine_ref = bf16[1024,1024]{1,0:T(8,128)(2,1)} custom-call(s32[5]{0:T(128)S(1)} %stack.23.place.core_ref, bf16[256,1024]{1,0:T(8,128)(2,1)S(1)} %gather_y.1.own_ref, bf16[256,1024]{1,0:T(8,128)(2,1)} %collective-permute-done.4.a_ref, bf16[256,1024]{1,0:T(8,128)(2,1)S(1)} %collective-permute-done.5.b_ref, ...), custom_call_target="tpu_custom_call" | custom-call | bytes 4194304 | tf_op jit(solution)/shard_map/gather_x/pallas_call | solution.py:403
  78.8 9.4 %all-to-all-start.2 = ((bf16[32,16,512]{2,1,0:T(8,128)(2,1)}), bf16[32,16,512]{2,1,0:T(8,128)(2,1)S(1)}, u32[]{:S(2)}, u32[]{:S(2)}) async-start(bf16[32,16,512]{2,1,0:T(8,128)(2,1)} %bitcast.43), calls=%async_computation.2 | async-start | bytes 1048576 | tf_op jit(solution)/shard_map/all_to_all | solution.py:487
  89.1 4.1 %weight_grad.2 = (f32[256,1024]{1,0:T(8,128)S(1)}, bf16[256,1024]{1,0:T(8,128)(2,1)S(1)}, bf16[256,1024]{1,0:T(8,128)(2,1)S(1)}, bf16[256,1024]{1,0:T(8,128)(2,1)S(1)}) custom-call(s32[5]{0:T(128)S(1)} %stack.23.place.core_ref, bf16[512,512]{1,0:T(8,128)(2,1)} %row_forward.1.a_mine.row_ref, bf16[512,512]{1,0:T(8,128)(2,1)S(1)} %collective-permute-done.a_theirs, ...), custom_call_target="tpu_custom_call" | custom-call | flops 1073741824 | bytes 6291456 | tf_op jit(solution)/shard_map/weight_grad/pallas_call | solution.py:367
  95.0 6.2 %attn_grad.1 = (bf16[512,512]{1,0:T(8,128)(2,1)S(1)}, bf16[512,512]{1,0:T(8,128)(2,1)}) custom-call(s32[5]{0:T(128)S(1)} %stack.23.place.core_ref, bf16[512,2048]{1,0:T(8,128)(2,1)S(1)} %bitcast.27, bf16[512,2048]{1,0:T(8,128)(2,1)S(1)} %bitcast.28, bf16[1024,1024]{1,0:T(8,128)(2,1)} %gather_x.1.mine_ref, bf16[1024,1024]{1,0:T(8,128)(2,1)} %collective-permute-done.7.theirs_ref), custom_call_target="tpu_custom_call" | custom-call | flops 2147483648 | bytes 7340032 | tf_op jit(solution)/shard_map/attn_grad/pallas_call | solution.py:277
  101.2 3.3 %all-to-all-done.2 = bf16[32,16,512]{2,1,0:T(8,128)(2,1)S(1)} async-done(((bf16[32,16,512]{2,1,0:T(8,128)(2,1)}), bf16[32,16,512]{2,1,0:T(8,128)(2,1)S(1)}, u32[]{:S(2)}, u32[]{:S(2)}) %all-to-all-start.2) | async-done | bytes 524320 | tf_op jit(solution)/shard_map/all_to_all | solution.py:487
  105.6 5.6 %all-to-all-start.3 = ((bf16[32,16,512]{2,1,0:T(8,128)(2,1)}), bf16[32,16,512]{2,1,0:T(8,128)(2,1)S(1)}, u32[]{:S(2)}, u32[]{:S(2)}) async-start(bf16[32,16,512]{2,1,0:T(8,128)(2,1)} %bitcast.16), calls=%async_computation.3 | async-start | bytes 1048576 | tf_op jit(solution)/shard_map/all_to_all | solution.py:487
  112.5 6.3 %weight_grad.3 = (f32[256,1024]{1,0:T(8,128)}, bf16[256,1024]{1,0:T(8,128)(2,1)}, bf16[256,1024]{1,0:T(8,128)(2,1)}, bf16[256,1024]{1,0:T(8,128)(2,1)}) custom-call(s32[5]{0:T(128)S(1)} %stack.23.place.core_ref, bf16[512,512]{1,0:T(8,128)(2,1)S(1)} %bitcast.41, bf16[512,512]{1,0:T(8,128)(2,1)} %collective-permute-done.9.a_theirs, ...), custom_call_target="tpu_custom_call" | custom-call | flops 1073741824 | bytes 6291456 | tf_op jit(solution)/shard_map/weight_grad/pallas_call | solution.py:367
  118.8 2.7 %collective-permute-start.11 = (bf16[256,1024]{1,0:T(8,128)(2,1)}, bf16[256,1024]{1,0:T(8,128)(2,1)}, u32[]{:S(2)}, u32[]{:S(2)}) collective-permute-start(bf16[256,1024]{1,0:T(8,128)(2,1)} %get-tuple-element.104), channel_id=1, source_target_pairs={{0,192},{64,0},{128,64},{192,128},{1,193},{65,1},{129,65},{193,129... | collective-permute-start | bytes 1572872 | tf_op jit(solution)/shard_map/ppermute | solution.py:499
  121.5 9.1 %row_backward.1 = (bf16[512,1024]{1,0:T(8,128)(2,1)}, bf16[512,1024]{1,0:T(8,128)(2,1)}, bf16[512,1024]{1,0:T(8,128)(2,1)}) custom-call(s32[4,4]{1,0:T(4,128)S(1)} %copy-done.19, bf16[512,1024]{1,0:T(8,128)(2,1)S(1)} %bitcast.31, bf16[512,1024]{1,0:T(8,128)(2,1)S(1)} %bitcast.34, bf16[512,1024]{1,0:T(8,128)(2,1)S(1)} %bitcast.37, ...), custom_call_target="tpu_custom_call" | custom-call | flops 671088640 | bytes 3670016 | tf_op jit(solution)/shard_map/row_backward/pallas_call | solution.py:222
  130.7 7.2 %column_backward.1 = bf16[32,2,8,1536]{3,2,1,0:T(8,128)(2,1)} custom-call(bf16[32,2,8,1536]{3,2,1,0:T(8,128)(2,1)} %bitcast.12.r_ref, bf16[32,2,8,512]{3,2,1,0:T(8,128)(2,1)S(1)} %bitcast.39), custom_call_target="tpu_custom_call" | custom-call | flops 671088640 | bytes 3670016 | tf_op jit(solution)/shard_map/column_backward/pallas_call | solution.py:156
  137.9 6.9 %collective-permute-done.10.b_ref = bf16[256,1024]{1,0:T(8,128)(2,1)S(1)} collective-permute-done((bf16[256,1024]{1,0:T(8,128)(2,1)}, bf16[256,1024]{1,0:T(8,128)(2,1)S(1)}, u32[]{:S(2)}, u32[]{:S(2)}) %collective-permute-start.10) | collective-permute-done | bytes 524320 | tf_op jit(solution)/shard_map/ppermute | solution.py:499
  145.6 10.5 %all-to-all-start.4 = ((bf16[32,16,1536]{2,1,0:T(8,128)(2,1)}), bf16[32,16,1536]{2,1,0:T(8,128)(2,1)S(1)}, u32[]{:S(2)}, u32[]{:S(2)}) async-start(bf16[32,16,1536]{2,1,0:T(8,128)(2,1)} %bitcast.18), calls=%async_computation.4 | async-start | bytes 3145728 | tf_op jit(solution)/shard_map/all_to_all | solution.py:487
  160.2 2.4 %collective-permute-start.14 = (bf16[64,1024]{1,0:T(8,128)(2,1)S(1)}, bf16[64,1024]{1,0:T(8,128)(2,1)S(1)}, u32[]{:S(2)}, u32[]{:S(2)}) collective-permute-start(bf16[64,1024]{1,0:T(8,128)(2,1)S(1)} %get-tuple-element.112), channel_id=1, source_target_pairs={{0,16},{8,24},{16,0},{24,8},{1,17},{9,25},{17,1},{25,9},{2,18},{10... | collective-permute-start | bytes 393224 | tf_op jit(solution)/shard_map/ppermute | solution.py:499
  163.8 6.4 %layer_out.1 = bf16[512,2048]{1,0:T(8,128)(2,1)} custom-call(s32[5]{0:T(128)S(1)} %stack.23.place.core_ref, bf16[512,512]{1,0:T(8,128)(2,1)} %row_forward.1.a_mine.row_ref, bf16[512,512]{1,0:T(8,128)(2,1)S(1)} %bitcast.42, bf16[1024,1024]{1,0:T(8,128)(2,1)S(1)} %copy-done.10, bf16[1024,1024]{1,0:T(8,128)(2,1)} %collective-permute-done.7.theirs_ref), custom_call_target="tpu_custom_call" | custom-call | flops 2147483648 | bytes 7340032 | tf_op jit(solution)/shard_map/layer_out/pallas_call | solution.py:317
  170.2 4.2 %collective-permute-done.13.b_ref = bf16[64,1024]{1,0:T(8,128)(2,1)S(1)} collective-permute-done((bf16[64,1024]{1,0:T(8,128)(2,1)S(1)}, bf16[64,1024]{1,0:T(8,128)(2,1)S(1)}, u32[]{:S(2)}, u32[]{:S(2)}) %collective-permute-start.13) | collective-permute-done | bytes 131104 | tf_op jit(solution)/shard_map/ppermute | solution.py:499
  174.4 4.3 %collective-permute-done.14.c_ref = bf16[64,1024]{1,0:T(8,128)(2,1)S(1)} collective-permute-done((bf16[64,1024]{1,0:T(8,128)(2,1)S(1)}, bf16[64,1024]{1,0:T(8,128)(2,1)S(1)}, u32[]{:S(2)}, u32[]{:S(2)}) %collective-permute-start.14) | collective-permute-done | bytes 131104 | tf_op jit(solution)/shard_map/ppermute | solution.py:499
  179.4 3.7 %collective-permute-start.16 = (bf16[8,1024]{1,0:T(8,128)(2,1)S(1)}, bf16[8,1024]{1,0:T(8,128)(2,1)S(1)}, u32[]{:S(2)}, u32[]{:S(2)}) collective-permute-start(bf16[8,1024]{1,0:T(8,128)(2,1)S(1)} %get-tuple-element.127), channel_id=1, source_target_pairs={{0,2},{2,4},{4,6},{6,0},{32,34},{34,36},{36,38},{38,32},{1,3},{3,5... | collective-permute-start | bytes 49160 | tf_op jit(solution)/shard_map/ppermute | solution.py:504
  183.1 4.0 %collective-permute-start.17 = (bf16[8,1024]{1,0:T(8,128)(2,1)S(1)}, bf16[8,1024]{1,0:T(8,128)(2,1)S(1)}, u32[]{:S(2)}, u32[]{:S(2)}) collective-permute-start(bf16[8,1024]{1,0:T(8,128)(2,1)S(1)} %get-tuple-element.128), channel_id=1, source_target_pairs={{0,4},{2,6},{4,0},{6,2},{32,36},{34,38},{36,32},{38,34},{1,5},{3,7... | collective-permute-start | bytes 49160 | tf_op jit(solution)/shard_map/ppermute | solution.py:504
  187.1 3.5 %collective-permute-start.18 = (bf16[8,1024]{1,0:T(8,128)(2,1)S(1)}, bf16[8,1024]{1,0:T(8,128)(2,1)S(1)}, u32[]{:S(2)}, u32[]{:S(2)}) collective-permute-start(bf16[8,1024]{1,0:T(8,128)(2,1)S(1)} %get-tuple-element.129), channel_id=1, source_target_pairs={{0,6},{2,0},{4,2},{6,4},{32,38},{34,32},{36,34},{38,36},{1,7},{3,1... | collective-permute-start | bytes 49160 | tf_op jit(solution)/shard_map/ppermute | solution.py:504
  190.6 3.3 %collective-permute-start.19 = (bf16[8,1024]{1,0:T(8,128)(2,1)S(1)}, bf16[8,1024]{1,0:T(8,128)(2,1)S(1)}, u32[]{:S(2)}, u32[]{:S(2)}) collective-permute-start(bf16[8,1024]{1,0:T(8,128)(2,1)S(1)} %get-tuple-element.130), channel_id=1, source_target_pairs={{0,32},{2,34},{4,36},{6,38},{32,0},{34,2},{36,4},{38,6},{1,33},{3,... | collective-permute-start | bytes 49160 | tf_op jit(solution)/shard_map/ppermute | solution.py:504
  193.9 3.4 %collective-permute-start.21 = (bf16[8,1024]{1,0:T(8,128)(2,1)S(1)}, bf16[8,1024]{1,0:T(8,128)(2,1)S(1)}, u32[]{:S(2)}, u32[]{:S(2)}) collective-permute-start(bf16[8,1024]{1,0:T(8,128)(2,1)S(1)} %get-tuple-element.132), channel_id=1, source_target_pairs={{0,36},{2,38},{4,32},{6,34},{32,4},{34,6},{36,0},{38,2},{1,37},{3,... | collective-permute-start | bytes 49160 | tf_op jit(solution)/shard_map/ppermute | solution.py:504
  197.4 2.4 %collective-permute-start.22 = (bf16[8,1024]{1,0:T(8,128)(2,1)S(1)}, bf16[8,1024]{1,0:T(8,128)(2,1)S(1)}, u32[]{:S(2)}, u32[]{:S(2)}) collective-permute-start(bf16[8,1024]{1,0:T(8,128)(2,1)S(1)} %get-tuple-element.133), channel_id=1, source_target_pairs={{0,38},{2,32},{4,34},{6,36},{32,6},{34,0},{36,2},{38,4},{1,39},{3,... | collective-permute-start | bytes 49160 | tf_op jit(solution)/shard_map/ppermute | solution.py:504
  199.8 2.5 %finish.1 = (bf16[512,1024]{1,0:T(8,128)(2,1)}, bf16[512,1024]{1,0:T(8,128)(2,1)}, bf16[512,1024]{1,0:T(8,128)(2,1)}) custom-call(s32[4]{0:T(128)S(1)} %copy-done.21, bf16[512,1536]{1,0:T(8,128)(2,1)S(1)} %bitcast.38, bf16[512,1024]{1,0:T(8,128)(2,1)} %get-tuple-element.116.dq_in, ...), custom_call_target="tpu_custom_call", output_to_operand_aliasing={{0}: (2, {}), {1}: (3, {}), {2}: (4, {})} | custom-call | flops 536870912 | bytes 3145728 | tf_op jit(solution)/shard_map/finish/pallas_call | solution.py:248
  (95 shorter events, 34.5 us)
Async XLA Ops:
  2.1 19.1 %all-to-all-start = ((bf16[16,4,1024]{2,1,0:T(4,128)(2,1)}), bf16[16,4,1024]{2,1,0:T(4,128)(2,1)S(1)}, u32[]{:S(2)}, u32[]{:S(2)}) async-start(bf16[16,4,1024]{2,1,0:T(4,128)(2,1)} %bitcast.6), calls=%async_computation | async-start | bytes 262144 | tf_op jit(solution)/shard_map/all_to_all | solution.py:487
  19.9 14.2 %copy-start.19 = (s32[4,4]{1,0:T(4,128)S(1)}, s32[4,4]{1,0:T(4,128)}, u32[]{:S(2)}) copy-start(s32[4,4]{1,0:T(4,128)} %pat_ref.3) | copy-start | bytes 196
  21.2 49.0 %all-to-all-start.1 = ((bf16[32,16,1536]{2,1,0:T(8,128)(2,1)}), bf16[32,16,1536]{2,1,0:T(8,128)(2,1)}, u32[]{:S(2)}, u32[]{:S(2)}) async-start(bf16[32,16,1536]{2,1,0:T(8,128)(2,1)} %bitcast.44), calls=%async_computation.1 | async-start | bytes 3145728 | tf_op jit(solution)/shard_map/all_to_all | solution.py:487
  30.3 10.5 %collective-permute-start.3 = (bf16[64,1024]{1,0:T(8,128)(2,1)S(1)}, bf16[64,1024]{1,0:T(8,128)(2,1)S(1)}, u32[]{:S(2)}, u32[]{:S(2)}) collective-permute-start(bf16[64,1024]{1,0:T(8,128)(2,1)S(1)} %reshape.77.own_ref), channel_id=1, source_target_pairs={{0,24},{8,0},{16,8},{24,16},{1,25},{9,1},{17,9},{25,17},{2,26},{10... | collective-permute-start | bytes 393224 | tf_op jit(solution)/shard_map/ppermute | solution.py:499
  33.0 8.8 %collective-permute-start.2 = (bf16[64,1024]{1,0:T(8,128)(2,1)S(1)}, bf16[64,1024]{1,0:T(8,128)(2,1)S(1)}, u32[]{:S(2)}, u32[]{:S(2)}) collective-permute-start(bf16[64,1024]{1,0:T(8,128)(2,1)S(1)} %reshape.77.own_ref), channel_id=1, source_target_pairs={{0,16},{8,24},{16,0},{24,8},{1,17},{9,25},{17,1},{25,9},{2,18},{10... | collective-permute-start | bytes 393224 | tf_op jit(solution)/shard_map/ppermute | solution.py:499
  33.6 12.0 %collective-permute-start.1 = (bf16[64,1024]{1,0:T(8,128)(2,1)S(1)}, bf16[64,1024]{1,0:T(8,128)(2,1)}, u32[]{:S(2)}, u32[]{:S(2)}) collective-permute-start(bf16[64,1024]{1,0:T(8,128)(2,1)S(1)} %reshape.77.own_ref), channel_id=1, source_target_pairs={{0,8},{8,16},{16,24},{24,0},{1,9},{9,17},{17,25},{25,1},{2,10},{10... | collective-permute-start | bytes 393224 | tf_op jit(solution)/shard_map/ppermute | solution.py:499
  37.1 36.6 %collective-permute-start = (bf16[512,512]{1,0:T(8,128)(2,1)}, bf16[512,512]{1,0:T(8,128)(2,1)S(1)}, u32[]{:S(2)}, u32[]{:S(2)}) collective-permute-start(bf16[512,512]{1,0:T(8,128)(2,1)} %row_forward.1.a_mine.row_ref), channel_id=1, source_target_pairs={{0,1},{1,0},{2,3},{3,2},{4,5},{5,4},{6,7},{7,6},{8,9},{9,8},{10,11... | collective-permute-start | bytes 1572872 | tf_op jit(solution)/shard_map/ppermute | solution.py:491
  46.5 27.2 %collective-permute-start.6 = (bf16[256,1024]{1,0:T(8,128)(2,1)S(1)}, bf16[256,1024]{1,0:T(8,128)(2,1)S(1)}, u32[]{:S(2)}, u32[]{:S(2)}) collective-permute-start(bf16[256,1024]{1,0:T(8,128)(2,1)S(1)} %gather_y.1.own_ref), channel_id=1, source_target_pairs={{0,192},{64,0},{128,64},{192,128},{1,193},{65,1},{129,65},{193,129... | collective-permute-start | bytes 1572872 | tf_op jit(solution)/shard_map/ppermute | solution.py:499
  49.1 24.6 %collective-permute-start.5 = (bf16[256,1024]{1,0:T(8,128)(2,1)S(1)}, bf16[256,1024]{1,0:T(8,128)(2,1)S(1)}, u32[]{:S(2)}, u32[]{:S(2)}) collective-permute-start(bf16[256,1024]{1,0:T(8,128)(2,1)S(1)} %gather_y.1.own_ref), channel_id=1, source_target_pairs={{0,128},{64,192},{128,0},{192,64},{1,129},{65,193},{129,1},{193,65... | collective-permute-start | bytes 1572872 | tf_op jit(solution)/shard_map/ppermute | solution.py:499
  49.6 26.2 %collective-permute-start.4 = (bf16[256,1024]{1,0:T(8,128)(2,1)S(1)}, bf16[256,1024]{1,0:T(8,128)(2,1)}, u32[]{:S(2)}, u32[]{:S(2)}) collective-permute-start(bf16[256,1024]{1,0:T(8,128)(2,1)S(1)} %gather_y.1.own_ref), channel_id=1, source_target_pairs={{0,64},{64,128},{128,192},{192,0},{1,65},{65,129},{129,193},{193,1... | collective-permute-start | bytes 1572872 | tf_op jit(solution)/shard_map/ppermute | solution.py:499
  78.3 16.7 %collective-permute-start.7 = (bf16[1024,1024]{1,0:T(8,128)(2,1)}, bf16[1024,1024]{1,0:T(8,128)(2,1)}, u32[]{:S(2)}, u32[]{:S(2)}) collective-permute-start(bf16[1024,1024]{1,0:T(8,128)(2,1)} %gather_x.1.mine_ref), channel_id=1, source_target_pairs={{0,1},{1,0},{2,3},{3,2},{4,5},{5,4},{6,7},{7,6},{8,9},{9,8},{10,11... | collective-permute-start | bytes 6291464 | tf_op jit(solution)/shard_map/ppermute | solution.py:491
  78.8 9.4 %collective-permute-start.8 = (bf16[512,1024]{1,0:T(8,128)(2,1)}, bf16[512,1024]{1,0:T(8,128)(2,1)S(1)}, u32[]{:S(2)}, u32[]{:S(2)}) collective-permute-start(bf16[512,1024]{1,0:T(8,128)(2,1)} %dynamic-slice_bitcast_fusion), channel_id=1, source_target_pairs={{0,1},{1,0},{2,3},{3,2},{4,5},{5,4},{6,7},{7,6},{8,9},{9,8},{10,11... | collective-permute-start | bytes 3145736 | tf_op jit(solution)/shard_map/ppermute | solution.py:491
  78.8 25.8 %all-to-all-start.2 = ((bf16[32,16,512]{2,1,0:T(8,128)(2,1)}), bf16[32,16,512]{2,1,0:T(8,128)(2,1)S(1)}, u32[]{:S(2)}, u32[]{:S(2)}) async-start(bf16[32,16,512]{2,1,0:T(8,128)(2,1)} %bitcast.43), calls=%async_computation.2 | async-start | bytes 1048576 | tf_op jit(solution)/shard_map/all_to_all | solution.py:487
  104.6 6.7 %collective-permute-start.9 = (bf16[512,512]{1,0:T(8,128)(2,1)S(1)}, bf16[512,512]{1,0:T(8,128)(2,1)}, u32[]{:S(2)}, u32[]{:S(2)}) collective-permute-start(bf16[512,512]{1,0:T(8,128)(2,1)S(1)} %bitcast.40), channel_id=1, source_target_pairs={{0,1},{1,0},{2,3},{3,2},{4,5},{5,4},{6,7},{7,6},{8,9},{9,8},{10,11... | collective-permute-start | bytes 1572872 | tf_op jit(solution)/shard_map/ppermute | solution.py:491
  105.6 25.0 %all-to-all-start.3 = ((bf16[32,16,512]{2,1,0:T(8,128)(2,1)}), bf16[32,16,512]{2,1,0:T(8,128)(2,1)S(1)}, u32[]{:S(2)}, u32[]{:S(2)}) async-start(bf16[32,16,512]{2,1,0:T(8,128)(2,1)} %bitcast.16), calls=%async_computation.3 | async-start | bytes 1048576 | tf_op jit(solution)/shard_map/all_to_all | solution.py:487
  118.8 25.9 %collective-permute-start.10 = (bf16[256,1024]{1,0:T(8,128)(2,1)}, bf16[256,1024]{1,0:T(8,128)(2,1)S(1)}, u32[]{:S(2)}, u32[]{:S(2)}) collective-permute-start(bf16[256,1024]{1,0:T(8,128)(2,1)} %get-tuple-element.103), channel_id=1, source_target_pairs={{0,64},{64,128},{128,192},{192,0},{1,65},{65,129},{129,193},{193,1... | collective-permute-start | bytes 1572872 | tf_op jit(solution)/shard_map/ppermute | solution.py:499
  118.8 26.8 %collective-permute-start.11 = (bf16[256,1024]{1,0:T(8,128)(2,1)}, bf16[256,1024]{1,0:T(8,128)(2,1)}, u32[]{:S(2)}, u32[]{:S(2)}) collective-permute-start(bf16[256,1024]{1,0:T(8,128)(2,1)} %get-tuple-element.104), channel_id=1, source_target_pairs={{0,192},{64,0},{128,64},{192,128},{1,193},{65,1},{129,65},{193,129... | collective-permute-start | bytes 1572872 | tf_op jit(solution)/shard_map/ppermute | solution.py:499
  121.5 24.1 %collective-permute-start.12 = (bf16[256,1024]{1,0:T(8,128)(2,1)}, bf16[256,1024]{1,0:T(8,128)(2,1)}, u32[]{:S(2)}, u32[]{:S(2)}) collective-permute-start(bf16[256,1024]{1,0:T(8,128)(2,1)} %get-tuple-element.105), channel_id=1, source_target_pairs={{0,128},{64,192},{128,0},{192,64},{1,129},{65,193},{129,1},{193,65... | collective-permute-start | bytes 1572872 | tf_op jit(solution)/shard_map/ppermute | solution.py:499
  137.9 18.2 %copy-start.11 = (f32[256,1024]{1,0:T(8,128)S(1)}, f32[256,1024]{1,0:T(8,128)}, u32[]{:S(2)}) copy-start(f32[256,1024]{1,0:T(8,128)} %get-tuple-element.106.a_ref) | copy-start | bytes 3145732
  145.6 54.2 %all-to-all-start.4 = ((bf16[32,16,1536]{2,1,0:T(8,128)(2,1)}), bf16[32,16,1536]{2,1,0:T(8,128)(2,1)S(1)}, u32[]{:S(2)}, u32[]{:S(2)}) async-start(bf16[32,16,1536]{2,1,0:T(8,128)(2,1)} %bitcast.18), calls=%async_computation.4 | async-start | bytes 3145728 | tf_op jit(solution)/shard_map/all_to_all | solution.py:487
  158.8 15.7 %collective-permute-start.13 = (bf16[64,1024]{1,0:T(8,128)(2,1)S(1)}, bf16[64,1024]{1,0:T(8,128)(2,1)S(1)}, u32[]{:S(2)}, u32[]{:S(2)}) collective-permute-start(bf16[64,1024]{1,0:T(8,128)(2,1)S(1)} %get-tuple-element.111), channel_id=1, source_target_pairs={{0,8},{8,16},{16,24},{24,0},{1,9},{9,17},{17,25},{25,1},{2,10},{10... | collective-permute-start | bytes 393224 | tf_op jit(solution)/shard_map/ppermute | solution.py:499
  160.2 18.5 %collective-permute-start.14 = (bf16[64,1024]{1,0:T(8,128)(2,1)S(1)}, bf16[64,1024]{1,0:T(8,128)(2,1)S(1)}, u32[]{:S(2)}, u32[]{:S(2)}) collective-permute-start(bf16[64,1024]{1,0:T(8,128)(2,1)S(1)} %get-tuple-element.112), channel_id=1, source_target_pairs={{0,16},{8,24},{16,0},{24,8},{1,17},{9,25},{17,1},{25,9},{2,18},{10... | collective-permute-start | bytes 393224 | tf_op jit(solution)/shard_map/ppermute | solution.py:499
  162.7 37.1 %copy-start.21 = (s32[4]{0:T(128)S(1)}, s32[4]{0:T(128)}, u32[]{:S(2)}) copy-start(s32[4]{0:T(128)} %off_ref.3) | copy-start | bytes 52
  162.7 16.1 %collective-permute-start.15 = (bf16[64,1024]{1,0:T(8,128)(2,1)S(1)}, bf16[64,1024]{1,0:T(8,128)(2,1)S(1)}, u32[]{:S(2)}, u32[]{:S(2)}) collective-permute-start(bf16[64,1024]{1,0:T(8,128)(2,1)S(1)} %get-tuple-element.113), channel_id=1, source_target_pairs={{0,24},{8,0},{16,8},{24,16},{1,25},{9,1},{17,9},{25,17},{2,26},{10... | collective-permute-start | bytes 393224 | tf_op jit(solution)/shard_map/ppermute | solution.py:499
  179.4 14.5 %collective-permute-start.16 = (bf16[8,1024]{1,0:T(8,128)(2,1)S(1)}, bf16[8,1024]{1,0:T(8,128)(2,1)S(1)}, u32[]{:S(2)}, u32[]{:S(2)}) collective-permute-start(bf16[8,1024]{1,0:T(8,128)(2,1)S(1)} %get-tuple-element.127), channel_id=1, source_target_pairs={{0,2},{2,4},{4,6},{6,0},{32,34},{34,36},{36,38},{38,32},{1,3},{3,5... | collective-permute-start | bytes 49160 | tf_op jit(solution)/shard_map/ppermute | solution.py:504
  183.1 14.2 %collective-permute-start.17 = (bf16[8,1024]{1,0:T(8,128)(2,1)S(1)}, bf16[8,1024]{1,0:T(8,128)(2,1)S(1)}, u32[]{:S(2)}, u32[]{:S(2)}) collective-permute-start(bf16[8,1024]{1,0:T(8,128)(2,1)S(1)} %get-tuple-element.128), channel_id=1, source_target_pairs={{0,4},{2,6},{4,0},{6,2},{32,36},{34,38},{36,32},{38,34},{1,5},{3,7... | collective-permute-start | bytes 49160 | tf_op jit(solution)/shard_map/ppermute | solution.py:504
  187.1 15.2 %collective-permute-start.18 = (bf16[8,1024]{1,0:T(8,128)(2,1)S(1)}, bf16[8,1024]{1,0:T(8,128)(2,1)S(1)}, u32[]{:S(2)}, u32[]{:S(2)}) collective-permute-start(bf16[8,1024]{1,0:T(8,128)(2,1)S(1)} %get-tuple-element.129), channel_id=1, source_target_pairs={{0,6},{2,0},{4,2},{6,4},{32,38},{34,32},{36,34},{38,36},{1,7},{3,1... | collective-permute-start | bytes 49160 | tf_op jit(solution)/shard_map/ppermute | solution.py:504
  190.6 11.7 %collective-permute-start.19 = (bf16[8,1024]{1,0:T(8,128)(2,1)S(1)}, bf16[8,1024]{1,0:T(8,128)(2,1)S(1)}, u32[]{:S(2)}, u32[]{:S(2)}) collective-permute-start(bf16[8,1024]{1,0:T(8,128)(2,1)S(1)} %get-tuple-element.130), channel_id=1, source_target_pairs={{0,32},{2,34},{4,36},{6,38},{32,0},{34,2},{36,4},{38,6},{1,33},{3,... | collective-permute-start | bytes 49160 | tf_op jit(solution)/shard_map/ppermute | solution.py:504
  193.9 8.5 %collective-permute-start.20 = (bf16[8,1024]{1,0:T(8,128)(2,1)S(1)}, bf16[8,1024]{1,0:T(8,128)(2,1)S(1)}, u32[]{:S(2)}, u32[]{:S(2)}) collective-permute-start(bf16[8,1024]{1,0:T(8,128)(2,1)S(1)} %get-tuple-element.131), channel_id=1, source_target_pairs={{0,34},{2,36},{4,38},{6,32},{32,2},{34,4},{36,6},{38,0},{1,35},{3,... | collective-permute-start | bytes 49160 | tf_op jit(solution)/shard_map/ppermute | solution.py:504
  193.9 8.5 %collective-permute-start.21 = (bf16[8,1024]{1,0:T(8,128)(2,1)S(1)}, bf16[8,1024]{1,0:T(8,128)(2,1)S(1)}, u32[]{:S(2)}, u32[]{:S(2)}) collective-permute-start(bf16[8,1024]{1,0:T(8,128)(2,1)S(1)} %get-tuple-element.132), channel_id=1, source_target_pairs={{0,36},{2,38},{4,32},{6,34},{32,4},{34,6},{36,0},{38,2},{1,37},{3,... | collective-permute-start | bytes 49160 | tf_op jit(solution)/shard_map/ppermute | solution.py:504
  197.4 5.0 %collective-permute-start.22 = (bf16[8,1024]{1,0:T(8,128)(2,1)S(1)}, bf16[8,1024]{1,0:T(8,128)(2,1)S(1)}, u32[]{:S(2)}, u32[]{:S(2)}) collective-permute-start(bf16[8,1024]{1,0:T(8,128)(2,1)S(1)} %get-tuple-element.133), channel_id=1, source_target_pairs={{0,38},{2,32},{4,34},{6,36},{32,6},{34,0},{36,2},{38,4},{1,39},{3,... | collective-permute-start | bytes 49160 | tf_op jit(solution)/shard_map/ppermute | solution.py:504
  203.0 2.9 %collective-permute-start.23 = (f32[4,1024]{1,0:T(4,128)S(1)}, f32[4,1024]{1,0:T(4,128)S(1)}, u32[]{:S(2)}, u32[]{:S(2)}) collective-permute-start(f32[4,1024]{1,0:T(4,128)S(1)} %get-tuple-element.146), channel_id=1, source_target_pairs={{0,1},{1,0},{2,3},{3,2},{4,5},{5,4},{6,7},{7,6},{8,9},{9,8},{10,11... | collective-permute-start | bytes 49160 | tf_op jit(solution)/shard_map/ppermute | solution.py:491
  (20 other events, 99.2 us)
